TPU v7x, 128 devices: a whole 4x4x4 slice. The times are simulated.
128 devices in a mesh: paths: 16 (over z, y_lo, core), stocks: 8 (over x, y_hi).
Axes of the slice: x: 4, y: 4 (y_hi: 2, y_lo: 2; y = y_hi * 2 + y_lo), z: 4, core: 2. Of those that a mesh axis runs over, the one named last changes fastest.
Arguments:
- prices: bfloat16 [256, 262144], P('stocks', 'paths'), may hold values from -18 to 18
- loadings: bfloat16 [256, 32], P('stocks'), may hold values from -0.25 to 0.25
- basis_w: float32 [32, 512], replicated, may hold values from -1 to 1
- basis_bias: float32 [512], replicated, may hold values from -1 to 1
- payoff: bfloat16 [262144], P('paths'), may hold values from -4 to 4
- in_fit: int32 [262144], P('paths'), may hold values 0 or 1
- cotangent: bfloat16 [256, 262144], P('stocks', 'paths'), may hold values from -6 to 6
- shocks: bfloat16 [4, 256, 262144], P(None, 'stocks', 'paths'), may hold values from -6 to 6
- corr_gen: bfloat16 [256, 256], replicated, may hold values from -0.375 to 0.375
- basket: float32 [256], replicated, may hold values from 0.2 to 2
- exercise: int32 [4, 262144], P(None, 'paths'), may hold values 0 or 1
- bucket: int32 [4, 262144], P(None, 'paths'), may hold values from 0 to 255
Outputs:
- delta_out: float32 [256, 262144], P('stocks', 'paths')
- surface: float32 [256, 256], P('stocks', 'paths')
All inputs are finite; a program needn't handle non-finite values. No bound on the sum of `in_fit` or of `exercise` on one device may be relied on, other than what follows from the above.
Results may differ from a plain program's by a relative error of at most 0.003.
Values may be sent and summed in bfloat16 or wider, within the bound.
No kernel may reach another device: no remote copies, remote signals or barrier semaphores. Data moves between devices by JAX's collectives and lax.ppermute only.
A program may use at most 192 MiB of HBM per device.

v0:
```python
import jax
import jax.numpy as jnp
from jax import lax
from jax.sharding import PartitionSpec as P

NK = 256
STEPS = 4


time_step = 0.25
ridge_weight = 0.1


def split_up(x, dim, size):
    lengths = x.shape
    pieces = x.reshape(*lengths[:dim], size, lengths[dim] // size, *lengths[dim + 1 :])
    return jnp.moveaxis(pieces, dim, 0)


def sum_at_owner(x, axis, dim):
    size = lax.axis_size(axis)
    pieces = lax.all_to_all(split_up(x, dim, size), axis, 0, 0, tiled=True)
    return jnp.sum(pieces, axis=0)


def piece_ends(length, count):
    unit = 8 if length >= 8 * count else 1
    return [length // unit * k // count * unit for k in range(1, count)]


def joined_along(pieces, dim):
    pieces = jnp.moveaxis(pieces, 0, dim)
    lengths = pieces.shape
    return pieces.reshape(*lengths[:dim], lengths[dim] * lengths[dim + 1], *lengths[dim + 2 :])


def several_exchanges(x, axis, pieces, split_dim, concat_dim):
    blocks = split_up(x, split_dim, lax.axis_size(axis))
    cut = max(range(1, max(2, blocks.ndim - 1)), key=lambda d: blocks.shape[d])
    gathered = []
    for share in jnp.split(blocks, piece_ends(blocks.shape[cut], pieces), axis=cut):
        if share.size:
            gathered.append(lax.all_to_all(share, axis, split_axis=0, concat_axis=0, tiled=True))
    return joined_along(jnp.concatenate(gathered, axis=cut), concat_dim)


def make_basis(factors, basis_w, basis_bias):
    raised = (
        jnp.dot(
            basis_w.T, factors, preferred_element_type=jnp.float32, precision=lax.Precision.HIGHEST
        )
        + basis_bias[:, None]
    )
    return jnp.tanh(raised).astype(jnp.bfloat16)


def regression_sums(basis, payoff, in_fit):
    picked = basis * in_fit.astype(jnp.bfloat16)[None, :]
    gram_sums = lax.dot_general(
        picked, basis, (((1,), (1,)), ((), ())), preferred_element_type=jnp.float32
    )
    moment = jnp.dot(picked, payoff, preferred_element_type=jnp.float32)
    return (gram_sums, moment)


def solve_coefficients(gram_sums, moment, path_count):
    system = gram_sums / path_count + ridge_weight * jnp.eye(gram_sums.shape[0], dtype=jnp.float32)
    cholesky_factor = jnp.linalg.cholesky(system)
    return jax.scipy.linalg.cho_solve((cholesky_factor, True), moment / path_count)


def per_device(
    prices,
    loadings,
    basis_w,
    basis_bias,
    payoff,
    in_fit,
    cotangent,
    shocks,
    corr_gen,
    basket,
    exercise,
    bucket,
):
    stock_count = lax.axis_size("stocks")
    local_paths = prices.shape[1]
    slab_part = local_paths // stock_count
    path_count = float(local_paths * lax.axis_size("paths"))
    offset = lax.axis_index("stocks") * slab_part
    partial_value = lax.dot_general(
        loadings, prices, (((0,), (0,)), ((), ())), preferred_element_type=jnp.float32
    )
    factors_own = sum_at_owner(partial_value, "stocks", 1)
    basis = make_basis(factors_own, basis_w, basis_bias)
    payoff_own = lax.dynamic_slice_in_dim(payoff, offset, slab_part, 0)
    fit_own = lax.dynamic_slice_in_dim(in_fit, offset, slab_part, 0)
    gram_sums, moment = regression_sums(basis, payoff_own, fit_own)
    gram_sums, moment = lax.psum((gram_sums, moment), ("paths", "stocks"))
    coefficients = solve_coefficients(gram_sums, moment, path_count)
    continuation_own = jnp.dot(
        coefficients, basis, preferred_element_type=jnp.float32, precision=lax.Precision.HIGHEST
    )
    strikes = jnp.arange(NK, dtype=jnp.int32)
    stacked = jnp.concatenate([cotangent[None], shocks], axis=0)
    exchanged = several_exchanges(stacked, "stocks", 2, 2, 1)
    exercise_own = lax.dynamic_slice_in_dim(exercise, offset, slab_part, 1)
    bucket_own = lax.dynamic_slice_in_dim(bucket, offset, slab_part, 1)
    adjoint = exchanged[0].astype(jnp.float32)
    partial_surface = jnp.zeros((corr_gen.shape[0], NK), jnp.float32)
    for date_index in range(STEPS - 1, -1, -1):
        mixed_rows = jnp.dot(
            corr_gen, adjoint.astype(jnp.bfloat16), preferred_element_type=jnp.float32
        )
        adjoint = (
            adjoint
            + time_step * mixed_rows
            + exercise_own[date_index].astype(jnp.float32)[None, :]
            * continuation_own[None, :]
            * basket[:, None]
        )
        vega_terms = (adjoint * exchanged[date_index + 1].astype(jnp.float32)).astype(jnp.bfloat16)
        one_hot = (bucket_own[date_index][:, None] == strikes[None, :]).astype(jnp.bfloat16)
        partial_surface = partial_surface + jnp.dot(
            vega_terms, one_hot, preferred_element_type=jnp.float32
        )
    strike_share = sum_at_owner(partial_surface, "paths", 1)
    surface = sum_at_owner(strike_share, "stocks", 0)
    delta_out = lax.all_to_all(adjoint, "stocks", split_axis=0, concat_axis=1, tiled=True)
    return (delta_out, surface)


def solution(mesh):
    return jax.shard_map(
        per_device,
        mesh=mesh,
        in_specs=(
            P("stocks", "paths"),
            P("stocks", None),
            P(),
            P(),
            P("paths"),
            P("paths"),
            P("stocks", "paths"),
            P(None, "stocks", "paths"),
            P(),
            P(),
            P(None, "paths"),
            P(None, "paths"),
        ),
        out_specs=(P("stocks", "paths"), P("stocks", "paths")),
        check_vma=False,
    )
```

profile of v0, /device:TPU:1, one launch (start us, length us, event | category | flops | bytes accessed | tf_op | source)
XLA Modules:
  0.0 492.1 jit_solution(14408656979231489318)
XLA Ops:
  7.2 1.2 copy-done
  8.4 1.2 fusion.108
  9.6 1.5 copy.65
  11.0 7.5 %all-to-all-start.2 = ((f32[8,32,2048]{2,1,0:T(8,128)}), f32[8,32,2048]{2,1,0:T(8,128)}, u32[]{:S(2)}, u32[]{:S(2)}) async-start(f32[8,32,2048]{2,1,0:T(8,128)} %bitcast.220), calls=%async_computation.2 | async-start | bytes 4194304 | tf_op jit(solution)/shard_map/all_to_all | solution.py:22
  18.5 5.1 %copy.62 = bf16[16,8,8,2048]{3,2,1,0:T(8,128)(2,1)S(1)} copy(bf16[16,8,8,2048]{3,1,2,0:T(8,128)(2,1)} %bitcast.237) | data formatting | bytes 8388608
  24.6 2.0 fusion.106
  26.6 2.9 copy.40
  29.5 19.5 %all-to-all-done.2 = f32[8,32,2048]{2,1,0:T(8,128)} async-done(((f32[8,32,2048]{2,1,0:T(8,128)}), f32[8,32,2048]{2,1,0:T(8,128)}, u32[]{:S(2)}, u32[]{:S(2)}) %all-to-all-start.2) | async-done | bytes 2097184 | tf_op jit(solution)/shard_map/all_to_all | solution.py:22
  49.1 3.6 all-to-all-start
  52.7 4.7 copy.41
  57.4 32.4 %all-to-all-done = bf16[8,5,16,2048]{3,2,1,0:T(8,128)(2,1)S(1)} async-done(((bf16[8,5,16,2048]{3,2,1,0:T(8,128)(2,1)}), bf16[8,5,16,2048]{3,2,1,0:T(8,128)(2,1)S(1)}, u32[]{:S(2)}, u32[]{:S(2)}) %all-to-all-start) | async-done | bytes 2621472 | tf_op jit(solution)/shard_map/all_to_all | solution.py:43
  89.8 4.4 all-to-all-start.1
  94.4 0.7 dynamic_slice.14
  95.2 0.7 dynamic-slice_convert_fusion.4
  95.9 1.7 dynamic-slice_convert_fusion
  97.6 1.7 reduce_sum.27
  99.3 3.9 tanh_convert_fusion
  103.2 1.3 copy-done.9
  104.5 2.5 fusion.19
  107.0 2.0 fusion.18
  109.0 78.7 %psum.15 = f32[512]{0:T(512)S(1)} all-reduce(f32[512]{0:T(512)S(1)} %bitcast.256), channel_id=1, replica_groups=mesh['paths'=16,'stocks'=8] {'paths','stocks'}, use_global_device_ids=true, to_apply=%region_10.11 | all-reduce | flops 512 | bytes 4096 | tf_op jit(solution)/shard_map/psum | solution.py:99
  187.8 2.2 maximum_bitcast_fusion.1
  190.0 2.1 fusion.105
  192.0 74.5 %all-reduce.3.cloned.1.call-done = f32[512,512]{0,1:T(8,128)} async-done(((f32[512,512]{0,1:T(8,128)}), f32[512,512]{0,1:T(8,128)}) %all-reduce.3.cloned.1.call-update) | async-done | bytes 1048592 | tf_op jit(solution)/shard_map/psum | solution.py:99
  266.5 2.4 select_add_fusion
  268.9 1.6 copy.44
  270.7 1.0 copy-done.7
  271.7 11.7 %cholesky.103 = f32[128,128]{1,0:T(8,128)S(1)} custom-call(f32[128,128]{1,0:T(8,128)S(1)} %cholesky.263), custom_call_target="Cholesky" | custom-call | tf_op jit(solution)/shard_map/jit(cholesky)/cholesky | solution.py:68
  283.4 9.8 %custom-call.34 = f32[1,128,128]{1,2,0:T(8,128)S(1)} custom-call(f32[1,128,128]{2,1,0:T(8,128)S(1)} %get-tuple-element.52), custom_call_target="InvertDiagBlocksLowerTriangular" | custom-call | tf_op jit(solution)/shard_map/jit(cholesky)/cholesky | solution.py:68
  293.3 1.2 fusion.57
  294.5 1.3 convolution_subtract_fusion
  295.8 11.7 %cholesky.215 = f32[128,128]{1,0:T(8,128)S(1)} custom-call(f32[128,128]{1,0:T(8,128)S(1)} %cholesky.267), custom_call_target="Cholesky" | custom-call | tf_op jit(solution)/shard_map/jit(cholesky)/cholesky | solution.py:68
  308.4 9.8 %custom-call.35 = f32[1,128,128]{1,2,0:T(8,128)S(1)} custom-call(f32[1,128,128]{2,1,0:T(8,128)S(1)} %get-tuple-element.50), custom_call_target="InvertDiagBlocksLowerTriangular" | custom-call | tf_op jit(solution)/shard_map/jit(cholesky)/cholesky | solution.py:68
  318.6 1.5 convolution_subtract_fusion.1
  320.1 11.7 %cholesky.236 = f32[128,128]{1,0:T(8,128)S(1)} custom-call(f32[128,128]{1,0:T(8,128)S(1)} %cholesky.272), custom_call_target="Cholesky" | custom-call | tf_op jit(solution)/shard_map/jit(cholesky)/cholesky | solution.py:68
  331.9 9.8 %custom-call.36 = f32[1,128,128]{1,2,0:T(8,128)S(1)} custom-call(f32[1,128,128]{2,1,0:T(8,128)S(1)} %get-tuple-element.48), custom_call_target="InvertDiagBlocksLowerTriangular" | custom-call | tf_op jit(solution)/shard_map/jit(cholesky)/cholesky | solution.py:68
  342.1 1.3 convolution_subtract_fusion.2
  343.4 11.9 %cholesky.253 = f32[128,128]{1,0:T(8,128)S(1)} custom-call(f32[128,128]{1,0:T(8,128)S(1)} %convolution_subtract_fusion.2), custom_call_target="Cholesky" | custom-call | tf_op jit(solution)/shard_map/jit(cholesky)/cholesky | solution.py:68
  355.4 0.7 compare_reduce_fusion.1
  356.1 0.7 compare_reduce_fusion
  356.8 0.6 compare_reduce_fusion.2
  360.0 11.2 %while.1 = (s32[]{:T(128)}, f32[512,512]{0,1:T(8,128)S(1)}, s32[4,2]{0,1:T(2,128)S(1)}, f32[4,128,128]{2,1,0:T(8,128)}, s32[]{:T(128)}) while((s32[]{:T(128)}, f32[512,512]{0,1:T(8,128)S(1)}, s32[4,2]{0,1:T(2,128)S(1)}, f32[4,128,128]{2,1,0:T(8,128)}, s32[]{:T(128)}) %tuple.48), condition=%wide.while_cond, body=%wide.while_body.sunk | while | flops 2 | bytes 393829 | solution.py:69
  360.7 1.4 dynamic-slice.23
  362.2 0.6 bitcast_dynamic-update-slice_fusion.2
  363.5 1.4 dynamic-slice.23
  365.0 0.6 bitcast_dynamic-update-slice_fusion.2
  366.3 1.4 dynamic-slice.23
  367.8 0.6 bitcast_dynamic-update-slice_fusion.2
  369.1 1.4 dynamic-slice.23
  370.5 0.6 bitcast_dynamic-update-slice_fusion.2
  371.2 40.2 %custom-call.37 = f32[4,128,128]{1,2,0:T(8,128)S(1)} custom-call(f32[4,128,128]{2,1,0:T(8,128)} %get-tuple-element.9), custom_call_target="InvertDiagBlocksLowerTriangular" | custom-call | tf_op jit(solution)/shard_map/jit(_cho_solve)/triangular_solve | solution.py:69
  414.4 3.4 fusion.16
  418.9 0.7 copy-done.4
  419.6 1.1 fusion.20
  421.2 1.8 fusion.2
  423.0 1.1 fusion.26
  424.2 1.1 fusion.25
  425.3 2.6 fusion.24
  428.0 11.6 %all_to_all.44 = f32[16,256,16]{1,2,0:T(8,128)S(1)} all-to-all(f32[16,256,16]{1,2,0:T(8,128)S(1)} %bitcast.239), channel_id=1, replica_groups=mesh['paths'=16,'stocks'=8] {'paths'}, dimensions={0} | all-to-all | bytes 524288 | tf_op jit(solution)/shard_map/all_to_all | solution.py:22
  439.8 11.4 %all_to_all.45 = f32[8,1,512]{2,1,0:T(1,128)S(1)} all-to-all(f32[8,1,512]{2,1,0:T(1,128)S(1)} %reshape.229), channel_id=1, replica_groups=mesh['paths'=16,'stocks'=8] {'stocks'}, dimensions={0} | all-to-all | bytes 32768 | tf_op jit(solution)/shard_map/all_to_all | solution.py:22
  451.2 3.6 all-to-all-start.3
  455.3 0.7 reduce.24
  456.7 26.8 %all-to-all-done.3 = f32[8,32,2048]{2,1,0:T(8,128)S(1)} async-done(((f32[8,32,2048]{2,1,0:T(8,128)}), f32[8,32,2048]{2,1,0:T(8,128)S(1)}, u32[]{:S(2)}, u32[]{:S(2)}) %all-to-all-start.3) | async-done | bytes 2097184 | tf_op jit(solution)/shard_map/all_to_all | solution.py:129
  483.5 1.5 copy.60
  (106 shorter events, 12.8 us)
Async XLA Ops:
  7.2 1.2 copy-start
  11.0 38.1 %all-to-all-start.2 = ((f32[8,32,2048]{2,1,0:T(8,128)}), f32[8,32,2048]{2,1,0:T(8,128)}, u32[]{:S(2)}, u32[]{:S(2)}) async-start(f32[8,32,2048]{2,1,0:T(8,128)} %bitcast.220), calls=%async_computation.2 | async-start | bytes 4194304 | tf_op jit(solution)/shard_map/all_to_all | solution.py:22
  18.5 5.1 %copy-start.10 = (bf16[32,16384]{1,0:T(8,128)(2,1)S(1)}, bf16[32,16384]{1,0:T(8,128)(2,1)}, u32[]{:S(2)}) copy-start(bf16[32,16384]{1,0:T(8,128)(2,1)} %param.18) | copy-start | bytes 3145732
  49.1 40.7 %all-to-all-start = ((bf16[8,5,16,2048]{3,2,1,0:T(8,128)(2,1)}), bf16[8,5,16,2048]{3,2,1,0:T(8,128)(2,1)S(1)}, u32[]{:S(2)}, u32[]{:S(2)}) async-start(bf16[8,5,16,2048]{3,2,1,0:T(8,128)(2,1)} %copy.40), calls=%async_computation | async-start | bytes 5242880 | tf_op jit(solution)/shard_map/all_to_all | solution.py:43
  89.8 98.0 %all-to-all-start.1 = ((bf16[8,5,16,2048]{3,2,1,0:T(8,128)(2,1)}), bf16[8,5,16,2048]{3,2,1,0:T(8,128)(2,1)}, u32[]{:S(2)}, u32[]{:S(2)}) async-start(bf16[8,5,16,2048]{3,2,1,0:T(8,128)(2,1)} %copy.41), calls=%async_computation.1 | async-start | bytes 5242880 | tf_op jit(solution)/shard_map/all_to_all | solution.py:43
  94.2 5.1 %copy-start.19 = (f32[32,512]{1,0:T(8,128)S(1)}, f32[32,512]{1,0:T(8,128)}, u32[]{:S(2)}) copy-start(f32[32,512]{1,0:T(8,128)} %param.14) | copy-start | bytes 196612
  94.2 5.1 %copy-start.20 = (f32[512]{0:T(512)S(1)}, f32[512]{0:T(512)}, u32[]{:S(2)}) copy-start(f32[512]{0:T(512)} %param.15) | copy-start | bytes 6148
  94.2 172.3 %all-reduce.3.cloned.1.call-start = ((), (), s32[]{:S(2)}) async-start(), calls=%async_computation.6 | async-start | bytes 2097152 | tf_op jit(solution)/shard_map/psum | solution.py:99
  103.2 1.3 copy-start.9
  266.5 4.0 copy-start.6
  270.7 1.0 copy-start.7
  371.2 46.6 %copy-start.5 = (bf16[1,8,32,2048]{3,2,0,1:T(8,128)(2,1)S(1)}, bf16[1,8,32,2048]{3,2,0,1:T(8,128)(2,1)}, u32[]{:S(2)}) copy-start(bf16[1,8,32,2048]{3,2,0,1:T(8,128)(2,1)} %get-tuple-element.36) | copy-start | bytes 3145732
  371.2 46.6 %copy-start.8 = (bf16[256,256]{1,0:T(8,128)(2,1)S(1)}, bf16[256,256]{1,0:T(8,128)(2,1)}, u32[]{:S(2)}) copy-start(bf16[256,256]{1,0:T(8,128)(2,1)} %param.20) | copy-start | bytes 393220
  371.2 46.6 %copy-start.18 = (f32[256]{0:T(256)S(1)}, f32[256]{0:T(256)}, u32[]{:S(2)}) copy-start(f32[256]{0:T(256)} %param.21) | copy-start | bytes 3076
  411.4 6.3 %copy-start.14 = (f32[1,2048]{1,0:T(1,128)S(1)}, f32[1,2048]{1,0:T(1,128)}, u32[]{:S(2)}) copy-start(f32[1,2048]{1,0:T(1,128)} %get-tuple-element.43) | copy-start | bytes 24580
  411.4 6.3 %copy-start.15 = (f32[1,2048]{1,0:T(1,128)S(1)}, f32[1,2048]{1,0:T(1,128)}, u32[]{:S(2)}) copy-start(f32[1,2048]{1,0:T(1,128)} %get-tuple-element.44) | copy-start | bytes 24580
  411.4 6.3 %copy-start.16 = (f32[1,2048]{1,0:T(1,128)S(1)}, f32[1,2048]{1,0:T(1,128)}, u32[]{:S(2)}) copy-start(f32[1,2048]{1,0:T(1,128)} %get-tuple-element.45) | copy-start | bytes 24580
  411.4 6.3 %copy-start.17 = (f32[1,2048]{1,0:T(1,128)S(1)}, f32[1,2048]{1,0:T(1,128)}, u32[]{:S(2)}) copy-start(f32[1,2048]{1,0:T(1,128)} %get-tuple-element.46) | copy-start | bytes 24580
  418.4 1.2 copy-start.4
  418.4 1.2 copy-start.13
  421.2 1.9 copy-start.3
  421.2 1.8 copy-start.12
  423.0 1.2 copy-start.2
  423.0 1.2 copy-start.11
  451.2 32.3 %all-to-all-start.3 = ((f32[8,32,2048]{2,1,0:T(8,128)}), f32[8,32,2048]{2,1,0:T(8,128)S(1)}, u32[]{:S(2)}, u32[]{:S(2)}) async-start(f32[8,32,2048]{2,1,0:T(8,128)} %bitcast.60), calls=%async_computation.3 | async-start | bytes 4194304 | tf_op jit(solution)/shard_map/all_to_all | solution.py:129
  483.5 1.6 copy-start.1
Sparse Core Ops, SparseCore 0:
  107.1 159.3 all-reduce.2
where the time goes:
time: 501 us; the launch traced here: 492 us
  waiting for transfers between devices  153 us (31%)
  other arithmetic  130 us (26%)
  blocking collectives  102 us (20%)
  local copies, waits for them, and re-layouts  40 us (8%)
  matrix products  30.9 us (6%)
  starting transfers between devices  19.3 us (4%)
  between operations  17.2 us (3%)
    psum x1, blocking collectives, per_device(): gram_sums, moment = lax.psum((gram_sums, moment), ('paths', 'stocks'))  78.7 us
    another operation x14, other arithmetic, solve_coefficients(): cholesky_factor = jnp.linalg.cholesky(system)  78.6 us
    psum x1, waiting for transfers between devices, per_device(): gram_sums, moment = lax.psum((gram_sums, moment), ('paths', 'stocks'))  74.5 us
    another operation x3, other arithmetic, solve_coefficients(): jax.scipy.linalg.cho_solve((cholesky_factor, True), moment / path_count)  40.3 us
    all_to_all x2, waiting for transfers between devices, several_exchanges(): lax.all_to_all(share, axis, split_axis=0, concat_axis=0, tiled=True)  32.4 us
    all_to_all x1, waiting for transfers between devices, per_device(): lax.all_to_all(adjoint, 'stocks', split_axis=0, concat_axis=1, tiled=True)  26.8 us
    all_to_all x2, blocking collectives, sum_at_owner(): pieces = lax.all_to_all(split_up(x, dim, size), axis, 0, 0, tiled=True)  23 us
    all_to_all x1, waiting for transfers between devices, sum_at_owner(): pieces = lax.all_to_all(split_up(x, dim, size), axis, 0, 0, tiled=True)  19.5 us
  transfers between devices with their start and end apart: 5, of which 4 were waited for; matrix products, arithmetic and copies ran while one was open for 7% of the time, Pallas kernels for 0%

commit v1 on v0

v1 whole, which is shorter than its diff:
```python
import jax
import jax.numpy as jnp
from jax import lax
from jax.experimental import pallas as pl
from jax.experimental.pallas import tpu as pltpu
from jax.sharding import Mesh
from jax.sharding import PartitionSpec as P

NK = 256
STEPS = 4
TIME_STEP = 0.25
RIDGE = 0.1
LANES = 128
BLOCK = 128
TILE = 512
PATH_AXES = ("z", "ylo", "core")
STOCK_AXES = ("x", "yhi")
ALL_AXES = PATH_AXES + STOCK_AXES
FINE = (4, 2, 2, 4, 2)
f32 = jnp.float32
bf16 = jnp.bfloat16


def three_terms(x):
    high = x.astype(bf16)
    rest = x - high.astype(f32)
    middle = rest.astype(bf16)
    low = (rest - middle.astype(f32)).astype(bf16)
    return high, middle, low


def left_terms(x, axis):
    high, middle, low = three_terms(x)
    return jnp.concatenate([high, high, middle, high, low, middle], axis=axis)


def right_terms(x, axis):
    high, middle, low = three_terms(x)
    return jnp.concatenate([high, middle, high, low, high, middle], axis=axis)


def exact_dot(left, right):
    return jnp.dot(left_terms(left, 1), right_terms(right, 0), preferred_element_type=f32)


GRAM_BLOCKS = tuple((i, j) for i in range(4) for j in range(i + 1))
MOMENT_ROW = len(GRAM_BLOCKS) * BLOCK
SUM_ROWS = 1344
PIECE = SUM_ROWS // 8


def gram_kernel(slab_ref, moved_ref, table_ref, weight_ref, bias_ref, payoff_ref, fit_ref,
                basis_ref, sums_ref, gram_ref, moment_ref):
    step = pl.program_id(0)
    tile = moved_ref[...].reshape(256, TILE)
    loads = table_ref[...].reshape(256, LANES)[:, :32]
    factors = lax.dot_general(loads, tile, (((0,), (0,)), ((), ())), preferred_element_type=f32)
    raised = lax.dot_general(
        weight_ref[...], right_terms(factors, 0), (((0,), (0,)), ((), ())), preferred_element_type=f32
    )
    basis = jnp.tanh(raised + bias_ref[...]).astype(bf16)
    basis_ref[...] = basis
    picked = basis * fit_ref[...].astype(f32).astype(bf16)
    paid = jnp.broadcast_to(payoff_ref[...].astype(f32), (16, TILE)).astype(bf16)
    contract = (((1,), (1,)), ((), ()))
    first = lax.dot_general(picked[:256], basis[:256], contract, preferred_element_type=f32)
    second = lax.dot_general(picked[256:], basis, contract, preferred_element_type=f32)
    moment = lax.dot_general(paid, picked, contract, preferred_element_type=f32)

    @pl.when(step == 0)
    def _():
        gram_ref[:256, :256] = first
        gram_ref[256:, :] = second
        moment_ref[...] = moment

    @pl.when(step > 0)
    def _():
        gram_ref[:256, :256] += first
        gram_ref[256:, :] += second
        moment_ref[...] += moment

    @pl.when(step == pl.num_programs(0) - 1)
    def _():
        for at, (i, j) in enumerate(GRAM_BLOCKS):
            sums_ref[at * BLOCK:(at + 1) * BLOCK, :] = gram_ref[
                i * BLOCK:(i + 1) * BLOCK, j * BLOCK:(j + 1) * BLOCK
            ]
        sums_ref[MOMENT_ROW:, :] = jnp.zeros((SUM_ROWS - MOMENT_ROW, LANES), f32)
        for i in range(4):
            sums_ref[MOMENT_ROW + 8 * i:MOMENT_ROW + 8 * i + 8, :] = moment_ref[
                :8, i * BLOCK:(i + 1) * BLOCK
            ]


def regression_sums(slab, moved, weights, bias, payoff, fit, slab_part):
    tiles = slab_part // TILE
    table_at = slab_part // LANES

    def own(step, slab_ref):
        return (0, slab_ref[0] * tiles + step)

    return pl.pallas_call(
        gram_kernel,
        out_shape=(
            jax.ShapeDtypeStruct((512, slab_part), bf16),
            jax.ShapeDtypeStruct((SUM_ROWS, LANES), f32),
        ),
        grid_spec=pltpu.PrefetchScalarGridSpec(
            num_scalar_prefetch=1,
            grid=(tiles,),
            in_specs=[
                pl.BlockSpec((8, 32, TILE), lambda i, s: (0, 0, i)),
                pl.BlockSpec((8, 32, LANES), lambda i, s: (0, 0, table_at)),
                pl.BlockSpec((192, 512), lambda i, s: (0, 0)),
                pl.BlockSpec((512, 1), lambda i, s: (0, 0)),
                pl.BlockSpec((1, TILE), own),
                pl.BlockSpec((1, TILE), own),
            ],
            out_specs=(
                pl.BlockSpec((512, TILE), lambda i, s: (0, i)),
                pl.BlockSpec((SUM_ROWS, LANES), lambda i, s: (0, 0)),
            ),
            scratch_shapes=[pltpu.VMEM((512, 512), f32), pltpu.VMEM((16, 512), f32)],
        ),
        compiler_params=pltpu.CompilerParams(vmem_limit_bytes=40 << 20),
        name="regression_sums",
    )(slab, moved, moved, weights, bias, payoff, fit)


def exchange_with_others(x, axes, count, piece_of=None):
    received = []
    for flip in range(1, count):
        sent = x if piece_of is None else piece_of(flip)
        received.append(lax.ppermute(sent, axes, [(i, i ^ flip) for i in range(count)]))
    return received


def all_device_sum(sums):
    core = lax.axis_index("core")
    z = lax.axis_index("z")
    halves = sums.reshape(2, 4, PIECE, LANES)
    mine = lax.dynamic_index_in_dim(halves, core, 0, False)
    other = lax.dynamic_index_in_dim(halves, 1 - core, 0, False)
    mine = mine + exchange_with_others(other, "core", 2)[0]

    def piece_of(flip):
        return lax.dynamic_index_in_dim(mine, z ^ flip, 0, False)

    share = piece_of(0)
    for part in exchange_with_others(None, "z", 4, piece_of):
        share = share + part
    for axes in ("x", ("ylo", "yhi")):
        parts = exchange_with_others(share, axes, 4)
        share = (share + parts[0]) + (parts[1] + parts[2])
    column = jnp.stack([share] + exchange_with_others(share, "z", 4))
    return column, exchange_with_others(column, "core", 2)[0]


def lane_column(x, j):
    return jnp.broadcast_to(x[:, j:j + 1], (8, LANES))


def sublane_row(x, j):
    return jnp.broadcast_to(x[j:j + 1, :], (8, LANES))


def pivot_rows(panel, base, lane, sub):
    inside = (lane >= base) & (lane < base + 8)
    columns = [lane_column(panel, base + j) for j in range(8)]
    d = {(i, j): sublane_row(columns[j], i) for j in range(8) for i in range(j, 8)}
    marked = jnp.where(inside, jnp.where(lane - base == sub, 1.0, 0.0), panel)
    y = [sublane_row(marked, j) for j in range(8)]
    lower = {}
    inverse = []
    for j in range(8):
        inverse.append(1.0 / d[j, j])
        for i in range(j + 1, 8):
            lower[i, j] = d[i, j] * inverse[j]
        for k in range(j + 1, 8):
            for i in range(k, 8):
                d[i, k] = d[i, k] - lower[i, j] * d[k, j]
        for i in range(j + 1, 8):
            y[i] = y[i] - lower[i, j] * y[j]
    y = [y[j] * inverse[j] for j in range(8)]
    for j in range(7, -1, -1):
        for i in range(j):
            y[i] = y[i] - lower[j, i] * y[j]
    return y


def eliminated(x, rows, base, lane):
    inside = (lane >= base) & (lane < base + 8)
    t = [lane_column(x, base + j) * rows[j] for j in range(8)]
    total = ((t[0] + t[1]) + (t[2] + t[3])) + ((t[4] + t[5]) + (t[6] + t[7]))
    return jnp.where(inside, 0.0, x) - total


def inverse_of_block(rows):
    lane = lax.broadcasted_iota(jnp.int32, (8, LANES), 1)
    sub = lax.broadcasted_iota(jnp.int32, (8, LANES), 0)
    rows = list(rows)
    for g in range(16):
        pivots = pivot_rows(rows[g], 8 * g, lane, sub)
        for t in range(1, 16):
            h = (g + t) % 16
            rows[h] = eliminated(rows[h], pivots, 8 * g, lane)
        own = pivots[0]
        for j in range(1, 8):
            own = jnp.where(sub == j, pivots[j], own)
        rows[g] = own
    return rows


def solve_kernel(at_ref, near_ref, far_ref, out_ref, sums_ref, system_ref, inverse_ref, *, scale):
    core = at_ref[0]
    z = at_ref[1]
    for flip in range(4):
        at = pl.multiple_of((core * 4 + (z ^ flip)) * PIECE, 8)
        sums_ref[pl.ds(at, PIECE), :] = near_ref[flip]
        at = pl.multiple_of(((1 - core) * 4 + (z ^ flip)) * PIECE, 8)
        sums_ref[pl.ds(at, PIECE), :] = far_ref[flip]
    diagonal = (
        lax.broadcasted_iota(jnp.int32, (BLOCK, BLOCK), 0)
        == lax.broadcasted_iota(jnp.int32, (BLOCK, BLOCK), 1)
    )
    for at, (i, j) in enumerate(GRAM_BLOCKS):
        block = sums_ref[at * BLOCK:(at + 1) * BLOCK, :] * scale
        if i == j:
            block = block + jnp.where(diagonal, RIDGE, 0.0)
        else:
            system_ref[j * BLOCK:(j + 1) * BLOCK, i * BLOCK:(i + 1) * BLOCK] = block.T
        system_ref[i * BLOCK:(i + 1) * BLOCK, j * BLOCK:(j + 1) * BLOCK] = block
    for i in range(4):
        row = sums_ref[MOMENT_ROW + 8 * i:MOMENT_ROW + 8 * i + 1, :] * scale
        system_ref[i * BLOCK:(i + 1) * BLOCK, 512:] = jnp.broadcast_to(row, (BLOCK, BLOCK)).T

    for i in range(4):
        lo = i * BLOCK
        inverse = inverse_of_block(
            [system_ref[lo + 8 * g:lo + 8 * g + 8, lo:lo + BLOCK] for g in range(16)]
        )
        inverse = jnp.concatenate(inverse, axis=0)
        solved = exact_dot(inverse, system_ref[lo:lo + BLOCK, lo + BLOCK:])
        for j in range(4):
            if j != i:
                system_ref[j * BLOCK:(j + 1) * BLOCK, lo + BLOCK:] -= exact_dot(
                    system_ref[j * BLOCK:(j + 1) * BLOCK, lo:lo + BLOCK], solved
                )
        system_ref[lo:lo + BLOCK, lo + BLOCK:] = solved
    out_ref[...] = system_ref[:, 512:]


def solve_coefficients(near, far, path_count):
    at = jnp.stack([lax.axis_index("core"), lax.axis_index("z")]).astype(jnp.int32)
    whole = pl.BlockSpec((4, PIECE, LANES), lambda i, s: (0, 0, 0))
    return pl.pallas_call(
        lambda *refs: solve_kernel(*refs, scale=1.0 / path_count),
        out_shape=jax.ShapeDtypeStruct((512, LANES), f32),
        grid_spec=pltpu.PrefetchScalarGridSpec(
            num_scalar_prefetch=1,
            grid=(1,),
            in_specs=[whole, whole],
            out_specs=pl.BlockSpec((512, LANES), lambda i, s: (0, 0)),
            scratch_shapes=[
                pltpu.VMEM((SUM_ROWS, LANES), f32),
                pltpu.VMEM((512, 512 + LANES), f32),
                pltpu.VMEM((BLOCK, BLOCK), f32),
            ],
        ),
        compiler_params=pltpu.CompilerParams(vmem_limit_bytes=40 << 20),
        name="solve_coefficients",
    )(at, near, far)


def dates_kernel(slab_ref, coefficient_ref, basis_ref, moved_ref, mixer_ref, basket_ref, exercise_ref,
                 bucket_ref, delta_ref, surface_ref, total_ref):
    step = pl.program_id(0)
    parts = [jnp.zeros((8, TILE), f32) for _ in range(4)]
    for b in range(64):
        weight = jnp.broadcast_to(coefficient_ref[8 * b:8 * b + 8, :1], (8, TILE))
        parts[b % 4] += weight * basis_ref[8 * b:8 * b + 8, :].astype(f32)
    continuation = jnp.sum((parts[0] + parts[1]) + (parts[2] + parts[3]), axis=0, keepdims=True)
    adjoint = moved_ref[:, 0].reshape(256, TILE).astype(f32)
    basket = basket_ref[...]
    strikes = lax.broadcasted_iota(jnp.int32, (NK, TILE), 0)
    total = jnp.zeros((NK, 256), f32)
    for date in range(STEPS - 1, -1, -1):
        mixed = jnp.dot(mixer_ref[...], adjoint.astype(bf16), preferred_element_type=f32)
        held = exercise_ref[date:date + 1, :].astype(f32) * continuation
        adjoint = adjoint + TIME_STEP * mixed + held * basket
        terms = (adjoint * moved_ref[:, date + 1].reshape(256, TILE).astype(f32)).astype(bf16)
        chosen = jnp.where(strikes == bucket_ref[date:date + 1, :], 1.0, 0.0).astype(bf16)
        total = total + lax.dot_general(
            chosen, terms, (((1,), (1,)), ((), ())), preferred_element_type=f32
        )
    delta_ref[...] = adjoint.astype(bf16).reshape(8, 32, TILE)

    @pl.when(step == 0)
    def _():
        total_ref[...] = total

    @pl.when(step > 0)
    def _():
        total_ref[...] += total

    @pl.when(step == pl.num_programs(0) - 1)
    def _():
        grouped = total_ref[...].reshape(16, 16, 256)
        for s in range(8):
            for q in range(4):
                surface_ref[:, s, :, 32 * q:32 * q + 32] = grouped[
                    :, 4 * q:4 * q + 4, 32 * s:32 * s + 32
                ]


def date_loop(slab, coefficients, basis, moved, mixer, basket, exercise, bucket, slab_part):
    tiles = slab_part // TILE

    def own(step, slab_ref):
        return (0, slab_ref[0] * tiles + step)

    return pl.pallas_call(
        dates_kernel,
        out_shape=(
            jax.ShapeDtypeStruct((8, 32, slab_part), bf16),
            jax.ShapeDtypeStruct((16, 8, 4, LANES), f32),
        ),
        grid_spec=pltpu.PrefetchScalarGridSpec(
            num_scalar_prefetch=1,
            grid=(tiles,),
            in_specs=[
                pl.BlockSpec((512, LANES), lambda i, s: (0, 0)),
                pl.BlockSpec((512, TILE), lambda i, s: (0, i)),
                pl.BlockSpec((8, 5, 32, TILE), lambda i, s: (0, 0, 0, i)),
                pl.BlockSpec((256, 256), lambda i, s: (0, 0)),
                pl.BlockSpec((256, 1), lambda i, s: (0, 0)),
                pl.BlockSpec((4, TILE), own),
                pl.BlockSpec((4, TILE), own),
            ],
            out_specs=(
                pl.BlockSpec((8, 32, TILE), lambda i, s: (0, 0, i)),
                pl.BlockSpec((16, 8, 4, LANES), lambda i, s: (0, 0, 0, 0)),
            ),
            scratch_shapes=[pltpu.VMEM((NK, 256), f32)],
        ),
        compiler_params=pltpu.CompilerParams(vmem_limit_bytes=48 << 20),
        name="date_loop",
    )(slab, coefficients, basis, moved, mixer, basket, exercise, bucket)


def per_device(prices, loadings, basis_w, basis_bias, payoff, in_fit, cotangent, shocks, corr_gen,
               basket, exercise, bucket):
    local_paths = prices.shape[1]
    slab_part = local_paths // 8
    path_count = float(local_paths * 16)
    slab = lax.axis_index(STOCK_AXES).astype(jnp.int32).reshape(1)

    pieces = jnp.moveaxis(prices.reshape(32, 8, slab_part), 1, 0)
    table = jnp.broadcast_to(jnp.pad(loadings, ((0, 0), (0, LANES - 32)))[None], (8, 32, LANES))
    moved_prices = lax.all_to_all(
        jnp.concatenate([pieces, table], axis=2), STOCK_AXES, 0, 0, tiled=True
    )
    stacked = jnp.concatenate([cotangent[None], shocks], axis=0)
    stacked = jnp.moveaxis(stacked.reshape(5, 32, 8, slab_part), 2, 0)
    stacked, moved_prices = lax.optimization_barrier((stacked, moved_prices))
    moved = lax.all_to_all(stacked, STOCK_AXES, 0, 0, tiled=True)

    basis, sums = regression_sums(
        slab, moved_prices, left_terms(basis_w, 0), basis_bias[:, None], payoff[None, :],
        in_fit[None, :], slab_part,
    )
    near, far = all_device_sum(sums)
    coefficients = solve_coefficients(near, far, path_count)
    delta, surface = date_loop(
        slab, coefficients, basis, moved, corr_gen, basket[:, None], exercise, bucket, slab_part
    )
    surface = lax.all_to_all(surface.reshape(128, 4, LANES), ALL_AXES, 0, 0, tiled=True)
    surface = jnp.sum(surface, axis=0).reshape(4, 4, 32)
    surface = jnp.transpose(surface, (2, 1, 0)).reshape(32, 16)
    delta = lax.all_to_all(delta, STOCK_AXES, 0, 0, tiled=True)
    delta = jnp.moveaxis(delta, 0, 1).reshape(32, local_paths).astype(f32)
    return delta, surface


def solution(mesh):
    fine = Mesh(mesh.devices.reshape(FINE), ALL_AXES)
    stocks, paths = STOCK_AXES, PATH_AXES
    return jax.shard_map(
        per_device,
        mesh=fine,
        in_specs=(
            P(stocks, paths),
            P(stocks, None),
            P(),
            P(),
            P(paths),
            P(paths),
            P(stocks, paths),
            P(None, stocks, paths),
            P(),
            P(),
            P(None, paths),
            P(None, paths),
        ),
        out_specs=(P(stocks, paths), P(stocks, paths)),
        check_vma=False,
    )
```

time: 501 us -> 199 us (0.40); the launches traced: 492 us -> 198 us
  other arithmetic: 130 us -> 5.52 us
  blocking collectives: 102 us -> 17.4 us
  waiting for transfers between devices: 153 us -> 91.1 us
  Pallas kernels: 0 us -> 31.4 us
  matrix products: 30.9 us -> 0 us
  local copies, waits for them, and re-layouts: 40 us -> 11.5 us
  starting transfers between devices: 19.3 us -> 40.1 us
  between operations: 17.2 us -> 0.93 us
    another operation x17 -> x2, other arithmetic: 119 us -> 0.11 us  [the longest x1 0.08 us: solve_coefficients(): jnp.stack([lax.axis_index('core'), lax.axis_index('z')]).astype(jnp.int32)]
    psum x1 -> x0, blocking collectives: 78.7 us -> none  [per_device(): gram_sums, moment = lax.psum((gram_sums, moment), ('paths', 'stocks'))]
    psum x1 -> x0, waiting for transfers between devices: 74.5 us -> none  [per_device(): gram_sums, moment = lax.psum((gram_sums, moment), ('paths', 'stocks'))]
    ppermute x0 -> x14, waiting for transfers between devices: none -> 65 us  [exchange_with_others(): lax.ppermute(sent, axes, [(i, i ^ flip) for i in range(count)])]
    all_to_all x4 -> x3, waiting for transfers between devices: 78.7 us -> 26.1 us  [the longest x1 15.2 us: per_device(): delta = lax.all_to_all(delta, STOCK_AXES, 0, 0, tiled=True)]
    pallas_call x0 -> x3, Pallas kernels: none -> 31.4 us  [the longest x1 20.4 us: solve_coefficients(): pl.pallas_call(lambda *refs: solve_kernel(*refs, scale=1.0 / path_count),...]
    ppermute x0 -> x14, starting transfers between devices: none -> 24.4 us  [exchange_with_others(): lax.ppermute(sent, axes, [(i, i ^ flip) for i in range(count)])]
    dot_general x13 -> x0, matrix products: 22.1 us -> none  [the longest x4 5.82 us: per_device(): jnp.dot(vega_terms, one_hot, preferred_element_type=jnp.float32)]
  transfers between devices with their start and end apart: 5 -> 17, of which waited for: 4 -> 14; matrix products, arithmetic and copies ran while one was open for 7% -> 3% of each run, Pallas kernels for 0% -> 12%
where the time goes in v1:
time: 199 us; the launch traced here: 198 us
  waiting for transfers between devices  91.1 us (46%)
  starting transfers between devices  40.1 us (20%)
  Pallas kernels  31.4 us (16%)
  blocking collectives  17.4 us (9%)
  local copies, waits for them, and re-layouts  11.5 us (6%)
  other arithmetic  5.52 us (3%)
    ppermute x14, waiting for transfers between devices, exchange_with_others(): lax.ppermute(sent, axes, [(i, i ^ flip) for i in range(count)])  65 us
    ppermute x14, starting transfers between devices, exchange_with_others(): lax.ppermute(sent, axes, [(i, i ^ flip) for i in range(count)])  24.4 us
    pallas_call x1, Pallas kernels, solve_coefficients(): pl.pallas_call(lambda *refs: solve_kernel(*refs, scale=1.0 / path_count),...  20.4 us
    all_to_all x1, blocking collectives, per_device(): lax.all_to_all(surface.reshape(128, 4, LANES), ALL_AXES, 0, 0, tiled=True)  17.4 us
    all_to_all x1, waiting for transfers between devices, per_device(): delta = lax.all_to_all(delta, STOCK_AXES, 0, 0, tiled=True)  15.2 us
    all_to_all x1, waiting for transfers between devices, per_device(): lax.all_to_all(jnp.concatenate([pieces, table], axis=2), STOCK_AXES, 0, 0...  10.9 us
    all_to_all x1, starting transfers between devices, per_device(): lax.all_to_all(jnp.concatenate([pieces, table], axis=2), STOCK_AXES, 0, 0...  7.48 us
    pallas_call x1, Pallas kernels, date_loop(): pl.pallas_call(dates_kernel, out_shape=(jax.ShapeDtypeStruct((8, 32, slab...  6.72 us
  transfers between devices with their start and end apart: 17, of which 14 were waited for; matrix products, arithmetic and copies ran while one was open for 3% of the time, Pallas kernels for 12%

profile of v1, /device:TPU:1, one launch (start us, length us, event | category | flops | bytes accessed | tf_op | source)
XLA Modules:
  0.0 198.0 jit_solution(13316094293627954931)
XLA Ops:
  0.6 1.3 copy.34
  2.0 0.7 pad.4
  2.7 0.0 copy-start.8
  2.7 1.1 pad_maximum_fusion
  3.8 7.5 %all-to-all-start = ((bf16[8,32,2176]{2,1,0:T(8,128)(2,1)}), bf16[8,32,2176]{2,1,0:T(8,128)(2,1)S(1)}, u32[]{:S(2)}, u32[]{:S(2)}) async-start(bf16[8,32,2176]{2,1,0:T(8,128)(2,1)} %pad_maximum_fusion), calls=%async_computation | async-start | bytes 2228224 | tf_op jit(solution)/shard_map/all_to_all | solution.py:360
  11.3 0.6 copy.30
  11.9 0.6 copy.20
  12.4 1.0 copy-done.6
  13.4 0.3 copy.33
  13.8 2.8 %maximum_bitcast_fusion = bf16[8,5,32,2048]{3,2,1,0:T(8,128)(2,1)} fusion(bf16[4,32,8,2048]{3,1,0,2:T(8,128)(2,1)S(1)} %bitcast.54, bf16[1,32,8,2048]{3,1,0,2:T(8,128)(2,1)S(1)} %copy.20), kind=kLoop, calls=%fused_computation | loop fusion | flops 2621440 | bytes 10485760 | tf_op jit(solution)/shard_map/transpose | solution.py:364
  16.6 10.9 %all-to-all-done.moved_ref.table_ref = bf16[8,32,2176]{2,1,0:T(8,128)(2,1)S(1)} async-done(((bf16[8,32,2176]{2,1,0:T(8,128)(2,1)}), bf16[8,32,2176]{2,1,0:T(8,128)(2,1)S(1)}, u32[]{:S(2)}, u32[]{:S(2)}) %all-to-all-start) | async-done | bytes 1114144 | tf_op jit(solution)/shard_map/all_to_all | solution.py:360
  27.5 4.7 %all-to-all-start.1 = ((bf16[8,5,32,2048]{3,2,1,0:T(8,128)(2,1)}), bf16[8,5,32,2048]{3,2,1,0:T(8,128)(2,1)}, u32[]{:S(2)}, u32[]{:S(2)}) async-start(bf16[8,5,32,2048]{3,2,1,0:T(8,128)(2,1)} %maximum_bitcast_fusion), calls=%async_computation.1 | async-start | bytes 10485760 | tf_op jit(solution)/shard_map/all_to_all | solution.py:366
  32.2 0.1 copy.23.bias_ref
  32.5 0.0 copy-start.5
  32.5 0.8 copy-done.5
  33.3 4.3 %regression_sums.1 = (bf16[512,2048]{1,0:T(8,128)(2,1)S(1)}, f32[1344,128]{1,0:T(8,128)S(1)}) custom-call(s32[1]{0:T(128)} %bitcast.slab_ref, bf16[8,32,2176]{2,1,0:T(8,128)(2,1)S(1)} %all-to-all-done.moved_ref.table_ref, bf16[8,32,2176]{2,1,0:T(8,128)(2,1)S(1)} %all-to-all-done.moved_ref.table_ref, bf16[192,512]{1,0:T(8,128)(2,1)S(1)} %fusion.5.weight_ref, ...), custom_call_target="tpu_custom_call" | custom-call | tf_op jit(solution)/shard_map/regression_sums/pallas_call | solution.py:102
  37.6 0.0 copy-start.1
  37.6 0.0 copy-start.11
  37.6 0.8 copy-done.1
  38.5 1.7 collective-permute-start
  40.2 1.3 collective-permute-done
  41.4 1.0 bitcast_add_fusion
  42.5 1.7 collective-permute-start.1
  44.2 2.2 %collective-permute-start.3 = (f32[168,128]{1,0:T(8,128)S(1)}, f32[168,128]{1,0:T(8,128)S(1)}, u32[]{:S(2)}, u32[]{:S(2)}) collective-permute-start(f32[168,128]{1,0:T(8,128)S(1)} %get-tuple-element.15), channel_id=1, source_target_pairs={{0,96},{32,64},{64,32},{96,0},{1,97},{33,65},{65,33},{97,1},{2,98}... | collective-permute-start | bytes 258056 | tf_op jit(solution)/shard_map/ppermute | solution.py:134
  46.5 1.1 collective-permute-start.2
  47.5 0.0 collective-permute-done.1
  47.5 1.6 collective-permute-done.3
  49.2 2.5 %collective-permute-done.2 = f32[168,128]{1,0:T(8,128)S(1)} collective-permute-done((f32[168,128]{1,0:T(8,128)S(1)}, f32[168,128]{1,0:T(8,128)S(1)}, u32[]{:S(2)}, u32[]{:S(2)}) %collective-permute-start.2) | collective-permute-done | bytes 86048 | tf_op jit(solution)/shard_map/ppermute | solution.py:134
  51.7 2.9 %collective-permute-start.6 = (f32[168,128]{1,0:T(8,128)S(1)}, f32[168,128]{1,0:T(8,128)S(1)}, u32[]{:S(2)}, u32[]{:S(2)}) collective-permute-start(f32[168,128]{1,0:T(8,128)S(1)} %fusion.1), channel_id=1, source_target_pairs={{0,6},{2,4},{4,2},{6,0},{1,7},{3,5},{5,3},{7,1},{8,14},{10,12},{12... | collective-permute-start | bytes 258056 | tf_op jit(solution)/shard_map/ppermute | solution.py:134
  54.6 0.6 collective-permute-start.5
  55.2 0.1 collective-permute-start.4
  55.3 15.4 %collective-permute-done.6 = f32[168,128]{1,0:T(8,128)S(1)} collective-permute-done((f32[168,128]{1,0:T(8,128)S(1)}, f32[168,128]{1,0:T(8,128)S(1)}, u32[]{:S(2)}, u32[]{:S(2)}) %collective-permute-start.6) | collective-permute-done | bytes 86048 | tf_op jit(solution)/shard_map/ppermute | solution.py:134
  70.7 35.8 %collective-permute-done.5 = f32[168,128]{1,0:T(8,128)S(1)} collective-permute-done((f32[168,128]{1,0:T(8,128)S(1)}, f32[168,128]{1,0:T(8,128)S(1)}, u32[]{:S(2)}, u32[]{:S(2)}) %collective-permute-start.5) | collective-permute-done | bytes 86048 | tf_op jit(solution)/shard_map/ppermute | solution.py:134
  106.5 0.2 collective-permute-done.4
  106.8 1.9 collective-permute-start.9
  108.7 0.0 collective-permute-start.8
  108.7 2.0 %collective-permute-start.7 = (f32[168,128]{1,0:T(8,128)S(1)}, f32[168,128]{1,0:T(8,128)S(1)}, u32[]{:S(2)}, u32[]{:S(2)}) collective-permute-start(f32[168,128]{1,0:T(8,128)S(1)} %add_add_fusion.1), channel_id=1, source_target_pairs={{0,1},{1,0},{16,17},{17,16},{2,3},{3,2},{18,19},{19,18},{4,5},{5,4... | collective-permute-start | bytes 258056 | tf_op jit(solution)/shard_map/ppermute | solution.py:134
  110.7 0.7 collective-permute-done.9
  111.4 0.6 collective-permute-done.8
  112.0 1.5 collective-permute-done.7
  113.6 3.8 %collective-permute-start.12 = (f32[168,128]{1,0:T(8,128)S(1)}, f32[168,128]{1,0:T(8,128)S(1)}, u32[]{:S(2)}, u32[]{:S(2)}) collective-permute-start(f32[168,128]{1,0:T(8,128)S(1)} %add_add_fusion), channel_id=1, source_target_pairs={{0,96},{32,64},{64,32},{96,0},{1,97},{33,65},{65,33},{97,1},{2,98}... | collective-permute-start | bytes 258056 | tf_op jit(solution)/shard_map/ppermute | solution.py:134
  117.4 0.7 collective-permute-start.10
  118.1 1.7 collective-permute-done.12
  119.8 2.5 %collective-permute-done.11 = f32[168,128]{1,0:T(8,128)S(1)} collective-permute-done((f32[168,128]{1,0:T(8,128)S(1)}, f32[168,128]{1,0:T(8,128)S(1)}, u32[]{:S(2)}, u32[]{:S(2)}) %collective-permute-start.11) | collective-permute-done | bytes 86048 | tf_op jit(solution)/shard_map/ppermute | solution.py:134
  122.3 5.7 %collective-permute-start.13 = (f32[4,168,128]{2,1,0:T(8,128)S(1)}, f32[4,168,128]{2,1,0:T(8,128)S(1)}, u32[]{:S(2)}, u32[]{:S(2)}) collective-permute-start(f32[4,168,128]{2,1,0:T(8,128)S(1)} %pad_maximum_fusion.1.refs_1_), channel_id=1, source_target_pairs={{0,8},{8,0},{1,9},{9,1},{2,10},{10,2},{3,11},{11,3},{4,12},{12,4},... | collective-permute-start | bytes 1032200 | tf_op jit(solution)/shard_map/ppermute | solution.py:134
  127.9 0.1 copy.24.basket_ref
  128.1 0.1 pad_add_fusion.refs_0_
  128.2 1.1 collective-permute-done.13.refs_2_
  129.2 20.4 %solve_coefficients.1.coefficient_ref = f32[512,128]{1,0:T(8,128)S(1)} custom-call(s32[2]{0:T(128)S(1)} %pad_add_fusion.refs_0_, f32[4,168,128]{2,1,0:T(8,128)S(1)} %pad_maximum_fusion.1.refs_1_, f32[4,168,128]{2,1,0:T(8,128)S(1)} %collective-permute-done.13.refs_2_), custom_call_target="tpu_custom_call" | custom-call | tf_op jit(solution)/shard_map/solve_coefficients/pallas_call | solution.py:256
  149.6 0.0 all-to-all-done.1.moved_ref
  149.7 0.0 copy-start.3
  149.7 0.9 copy-done.3
  150.6 0.9 copy-done.4
  151.5 6.7 %date_loop.1 = (bf16[8,32,2048]{2,1,0:T(8,128)(2,1)S(1)}, f32[16,8,4,128]{3,2,1,0:T(4,128)S(1)}) custom-call(s32[1]{0:T(128)} %bitcast.slab_ref, f32[512,128]{1,0:T(8,128)S(1)} %solve_coefficients.1.coefficient_ref, bf16[512,2048]{1,0:T(8,128)(2,1)S(1)} %get-tuple-element.10.basis_ref, bf16[8,5,32,2048]{3,2,1,0:T(8,128)(2,1)} %all-to-all-done.1.moved_ref, ...), custom_call_target="tpu_custom_call" | custom-call | tf_op jit(solution)/shard_map/date_loop/pallas_call | solution.py:322
  158.2 0.0 copy-start
  158.3 1.0 copy-done
  159.2 17.4 %all_to_all.20 = f32[128,4,128]{2,1,0:T(4,128)S(1)} all-to-all(f32[128,4,128]{2,1,0:T(4,128)S(1)} %bitcast.52), channel_id=1, replica_groups=mesh['z'=4,'ylo'=2,'core'=2,'x'=4,'yhi'=2] {'z','ylo','core','x','yhi'}, dimensions={0} | all-to-all | bytes 524288 | tf_op jit(solution)/shard_map/all_to_all | solution.py:377
  176.6 3.6 %all-to-all-start.2 = ((bf16[8,32,2048]{2,1,0:T(8,128)(2,1)}), bf16[8,32,2048]{2,1,0:T(8,128)(2,1)S(1)}, u32[]{:S(2)}, u32[]{:S(2)}) async-start(bf16[8,32,2048]{2,1,0:T(8,128)(2,1)} %copy-done), calls=%async_computation.2 | async-start | bytes 2097152 | tf_op jit(solution)/shard_map/all_to_all | solution.py:380
  180.2 0.1 reduce_sum.9
  180.4 0.1 reshape.34
  180.4 0.6 copy.26
  181.0 15.2 %all-to-all-done.2 = bf16[8,32,2048]{2,1,0:T(8,128)(2,1)S(1)} async-done(((bf16[8,32,2048]{2,1,0:T(8,128)(2,1)}), bf16[8,32,2048]{2,1,0:T(8,128)(2,1)S(1)}, u32[]{:S(2)}, u32[]{:S(2)}) %all-to-all-start.2) | async-done | bytes 1048608 | tf_op jit(solution)/shard_map/all_to_all | solution.py:380
  196.3 0.2 convert_bitcast_fusion
  196.5 1.5 copy.29
  (28 shorter events, 0.3 us)
Async XLA Ops:
  2.7 8.6 %copy-start.8 = (bf16[32,16384]{1,0:T(8,128)(2,1)S(1)}, bf16[32,16384]{1,0:T(8,128)(2,1)}, u32[]{:S(2)}) copy-start(bf16[32,16384]{1,0:T(8,128)(2,1)} %param.18) | copy-start | bytes 3145732
  3.8 23.7 %all-to-all-start = ((bf16[8,32,2176]{2,1,0:T(8,128)(2,1)}), bf16[8,32,2176]{2,1,0:T(8,128)(2,1)S(1)}, u32[]{:S(2)}, u32[]{:S(2)}) async-start(bf16[8,32,2176]{2,1,0:T(8,128)(2,1)} %pad_maximum_fusion), calls=%async_computation | async-start | bytes 2228224 | tf_op jit(solution)/shard_map/all_to_all | solution.py:360
  11.3 2.2 %copy-start.6 = (bf16[4,32,16384]{2,1,0:T(8,128)(2,1)S(1)}, bf16[4,32,16384]{2,1,0:T(8,128)(2,1)}, u32[]{:S(2)}) copy-start(bf16[4,32,16384]{2,1,0:T(8,128)(2,1)} %param.19) | copy-start | bytes 12582916
  16.6 15.6 %copy-start.9 = (bf16[16384]{0:T(1024)(128)(2,1)S(1)}, bf16[16384]{0:T(1024)(128)(2,1)}, u32[]{:S(2)}) copy-start(bf16[16384]{0:T(1024)(128)(2,1)} %param.16) | copy-start | bytes 98308
  16.6 15.6 %copy-start.10 = (f32[512]{0:T(512)S(1)}, f32[512]{0:T(512)}, u32[]{:S(2)}) copy-start(f32[512]{0:T(512)} %param.15) | copy-start | bytes 6148
  16.6 15.8 %copy-start.7 = (f32[32,512]{1,0:T(8,128)S(1)}, f32[32,512]{1,0:T(8,128)}, u32[]{:S(2)}) copy-start(f32[32,512]{1,0:T(8,128)} %param.14) | copy-start | bytes 196612
  27.5 122.2 %all-to-all-start.1 = ((bf16[8,5,32,2048]{3,2,1,0:T(8,128)(2,1)}), bf16[8,5,32,2048]{3,2,1,0:T(8,128)(2,1)}, u32[]{:S(2)}, u32[]{:S(2)}) async-start(bf16[8,5,32,2048]{3,2,1,0:T(8,128)(2,1)} %maximum_bitcast_fusion), calls=%async_computation.1 | async-start | bytes 10485760 | tf_op jit(solution)/shard_map/all_to_all | solution.py:366
  32.5 0.8 copy-start.5
  37.6 0.8 copy-start.1
  37.6 90.3 %copy-start.11 = (f32[256]{0:T(256)S(1)}, f32[256]{0:T(256)}, u32[]{:S(2)}) copy-start(f32[256]{0:T(256)} %param.21) | copy-start | bytes 3076
  38.5 3.0 %collective-permute-start = (f32[4,168,128]{2,1,0:T(8,128)S(1)}, f32[4,168,128]{2,1,0:T(8,128)S(1)}, u32[]{:S(2)}, u32[]{:S(2)}) collective-permute-start(f32[4,168,128]{2,1,0:T(8,128)S(1)} %dynamic-slice_bitcast_fusion), channel_id=1, source_target_pairs={{0,8},{8,0},{1,9},{9,1},{2,10},{10,2},{3,11},{11,3},{4,12},{12,4},... | collective-permute-start | bytes 1032200 | tf_op jit(solution)/shard_map/ppermute | solution.py:134
  40.2 109.5 %copy-start.2 = (s32[4,16384]{1,0:T(4,128)S(1)}, s32[4,16384]{1,0:T(4,128)}, u32[]{:S(2)}) copy-start(s32[4,16384]{1,0:T(4,128)} %exercise_ref.1) | copy-start | bytes 786436
  42.5 5.0 %collective-permute-start.1 = (f32[168,128]{1,0:T(8,128)S(1)}, f32[168,128]{1,0:T(8,128)S(1)}, u32[]{:S(2)}, u32[]{:S(2)}) collective-permute-start(f32[168,128]{1,0:T(8,128)S(1)} %get-tuple-element.14), channel_id=1, source_target_pairs={{0,32},{32,0},{64,96},{96,64},{1,33},{33,1},{65,97},{97,65},{2,34}... | collective-permute-start | bytes 258056 | tf_op jit(solution)/shard_map/ppermute | solution.py:134
  44.2 4.9 %collective-permute-start.3 = (f32[168,128]{1,0:T(8,128)S(1)}, f32[168,128]{1,0:T(8,128)S(1)}, u32[]{:S(2)}, u32[]{:S(2)}) collective-permute-start(f32[168,128]{1,0:T(8,128)S(1)} %get-tuple-element.15), channel_id=1, source_target_pairs={{0,96},{32,64},{64,32},{96,0},{1,97},{33,65},{65,33},{97,1},{2,98}... | collective-permute-start | bytes 258056 | tf_op jit(solution)/shard_map/ppermute | solution.py:134
  46.5 5.2 %collective-permute-start.2 = (f32[168,128]{1,0:T(8,128)S(1)}, f32[168,128]{1,0:T(8,128)S(1)}, u32[]{:S(2)}, u32[]{:S(2)}) collective-permute-start(f32[168,128]{1,0:T(8,128)S(1)} %get-tuple-element.16), channel_id=1, source_target_pairs={{0,64},{32,96},{64,0},{96,32},{1,65},{33,97},{65,1},{97,33},{2,66}... | collective-permute-start | bytes 258056 | tf_op jit(solution)/shard_map/ppermute | solution.py:134
  51.7 19.0 %collective-permute-start.6 = (f32[168,128]{1,0:T(8,128)S(1)}, f32[168,128]{1,0:T(8,128)S(1)}, u32[]{:S(2)}, u32[]{:S(2)}) collective-permute-start(f32[168,128]{1,0:T(8,128)S(1)} %fusion.1), channel_id=1, source_target_pairs={{0,6},{2,4},{4,2},{6,0},{1,7},{3,5},{5,3},{7,1},{8,14},{10,12},{12... | collective-permute-start | bytes 258056 | tf_op jit(solution)/shard_map/ppermute | solution.py:134
  54.6 51.9 %collective-permute-start.5 = (f32[168,128]{1,0:T(8,128)S(1)}, f32[168,128]{1,0:T(8,128)S(1)}, u32[]{:S(2)}, u32[]{:S(2)}) collective-permute-start(f32[168,128]{1,0:T(8,128)S(1)} %fusion.1), channel_id=1, source_target_pairs={{0,4},{2,6},{4,0},{6,2},{1,5},{3,7},{5,1},{7,3},{8,12},{10,14},{12... | collective-permute-start | bytes 258056 | tf_op jit(solution)/shard_map/ppermute | solution.py:134
  55.2 51.6 %collective-permute-start.4 = (f32[168,128]{1,0:T(8,128)S(1)}, f32[168,128]{1,0:T(8,128)S(1)}, u32[]{:S(2)}, u32[]{:S(2)}) collective-permute-start(f32[168,128]{1,0:T(8,128)S(1)} %fusion.1), channel_id=1, source_target_pairs={{0,2},{2,0},{4,6},{6,4},{1,3},{3,1},{5,7},{7,5},{8,10},{10,8},{12,... | collective-permute-start | bytes 258056 | tf_op jit(solution)/shard_map/ppermute | solution.py:134
  106.8 4.6 %collective-permute-start.9 = (f32[168,128]{1,0:T(8,128)S(1)}, f32[168,128]{1,0:T(8,128)S(1)}, u32[]{:S(2)}, u32[]{:S(2)}) collective-permute-start(f32[168,128]{1,0:T(8,128)S(1)} %add_add_fusion.1), channel_id=1, source_target_pairs={{0,17},{1,16},{16,1},{17,0},{2,19},{3,18},{18,3},{19,2},{4,21},{5,... | collective-permute-start | bytes 258056 | tf_op jit(solution)/shard_map/ppermute | solution.py:134
  108.7 3.3 %collective-permute-start.8 = (f32[168,128]{1,0:T(8,128)S(1)}, f32[168,128]{1,0:T(8,128)S(1)}, u32[]{:S(2)}, u32[]{:S(2)}) collective-permute-start(f32[168,128]{1,0:T(8,128)S(1)} %add_add_fusion.1), channel_id=1, source_target_pairs={{0,16},{1,17},{16,0},{17,1},{2,18},{3,19},{18,2},{19,3},{4,20},{5,... | collective-permute-start | bytes 258056 | tf_op jit(solution)/shard_map/ppermute | solution.py:134
  108.7 4.8 %collective-permute-start.7 = (f32[168,128]{1,0:T(8,128)S(1)}, f32[168,128]{1,0:T(8,128)S(1)}, u32[]{:S(2)}, u32[]{:S(2)}) collective-permute-start(f32[168,128]{1,0:T(8,128)S(1)} %add_add_fusion.1), channel_id=1, source_target_pairs={{0,1},{1,0},{16,17},{17,16},{2,3},{3,2},{18,19},{19,18},{4,5},{5,4... | collective-permute-start | bytes 258056 | tf_op jit(solution)/shard_map/ppermute | solution.py:134
  113.6 6.2 %collective-permute-start.12 = (f32[168,128]{1,0:T(8,128)S(1)}, f32[168,128]{1,0:T(8,128)S(1)}, u32[]{:S(2)}, u32[]{:S(2)}) collective-permute-start(f32[168,128]{1,0:T(8,128)S(1)} %add_add_fusion), channel_id=1, source_target_pairs={{0,96},{32,64},{64,32},{96,0},{1,97},{33,65},{65,33},{97,1},{2,98}... | collective-permute-start | bytes 258056 | tf_op jit(solution)/shard_map/ppermute | solution.py:134
  117.4 4.8 %collective-permute-start.11 = (f32[168,128]{1,0:T(8,128)S(1)}, f32[168,128]{1,0:T(8,128)S(1)}, u32[]{:S(2)}, u32[]{:S(2)}) collective-permute-start(f32[168,128]{1,0:T(8,128)S(1)} %add_add_fusion), channel_id=1, source_target_pairs={{0,64},{32,96},{64,0},{96,32},{1,65},{33,97},{65,1},{97,33},{2,66}... | collective-permute-start | bytes 258056 | tf_op jit(solution)/shard_map/ppermute | solution.py:134
  117.4 4.8 %collective-permute-start.10 = (f32[168,128]{1,0:T(8,128)S(1)}, f32[168,128]{1,0:T(8,128)S(1)}, u32[]{:S(2)}, u32[]{:S(2)}) collective-permute-start(f32[168,128]{1,0:T(8,128)S(1)} %add_add_fusion), channel_id=1, source_target_pairs={{0,32},{32,0},{64,96},{96,64},{1,33},{33,1},{65,97},{97,65},{2,34}... | collective-permute-start | bytes 258056 | tf_op jit(solution)/shard_map/ppermute | solution.py:134
  122.3 6.9 %collective-permute-start.13 = (f32[4,168,128]{2,1,0:T(8,128)S(1)}, f32[4,168,128]{2,1,0:T(8,128)S(1)}, u32[]{:S(2)}, u32[]{:S(2)}) collective-permute-start(f32[4,168,128]{2,1,0:T(8,128)S(1)} %pad_maximum_fusion.1.refs_1_), channel_id=1, source_target_pairs={{0,8},{8,0},{1,9},{9,1},{2,10},{10,2},{3,11},{11,3},{4,12},{12,4},... | collective-permute-start | bytes 1032200 | tf_op jit(solution)/shard_map/ppermute | solution.py:134
  149.7 1.0 copy-start.3
  150.6 0.9 copy-start.4
  158.2 1.0 copy-start
  176.6 19.6 %all-to-all-start.2 = ((bf16[8,32,2048]{2,1,0:T(8,128)(2,1)}), bf16[8,32,2048]{2,1,0:T(8,128)(2,1)S(1)}, u32[]{:S(2)}, u32[]{:S(2)}) async-start(bf16[8,32,2048]{2,1,0:T(8,128)(2,1)} %copy-done), calls=%async_computation.2 | async-start | bytes 2097152 | tf_op jit(solution)/shard_map/all_to_all | solution.py:380

commit v2 on v1

--- a/solution.py
+++ b/solution.py
@@ -13,6 +13,8 @@
 LANES = 128
 BLOCK = 128
 TILE = 512
+INCREMENT_TILE = 512
+DATE_TILE = 1024
 PATH_AXES = ("z", "ylo", "core")
 STOCK_AXES = ("x", "yhi")
 ALL_AXES = PATH_AXES + STOCK_AXES
@@ -135,7 +137,7 @@
     return received
 
 
-def all_device_sum(sums):
+def all_device_sum(sums, beside):
     core = lax.axis_index("core")
     z = lax.axis_index("z")
     halves = sums.reshape(2, 4, PIECE, LANES)
@@ -149,9 +151,14 @@
     share = piece_of(0)
     for part in exchange_with_others(None, "z", 4, piece_of):
         share = share + part
+    share, beside = lax.optimization_barrier((share, beside))
     for axes in ("x", ("ylo", "yhi")):
         parts = exchange_with_others(share, axes, 4)
         share = (share + parts[0]) + (parts[1] + parts[2])
+    return lax.optimization_barrier((share, beside))
+
+
+def gathered_sum(share):
     column = jnp.stack([share] + exchange_with_others(share, "z", 4))
     return column, exchange_with_others(column, "core", 2)[0]
 
@@ -211,7 +218,7 @@
     return rows
 
 
-def solve_kernel(at_ref, near_ref, far_ref, out_ref, sums_ref, system_ref, inverse_ref, *, scale):
+def solve_kernel(at_ref, near_ref, far_ref, basis_ref, out_ref, sums_ref, system_ref, *, scale):
     core = at_ref[0]
     z = at_ref[1]
     for flip in range(4):
@@ -247,105 +254,154 @@
                     system_ref[j * BLOCK:(j + 1) * BLOCK, lo:lo + BLOCK], solved
                 )
         system_ref[lo:lo + BLOCK, lo + BLOCK:] = solved
-    out_ref[...] = system_ref[:, 512:]
-
-
-def solve_coefficients(near, far, path_count):
+    width = basis_ref.shape[1]
+    for lo in range(0, width, 512):
+        parts = [jnp.zeros((8, 512), f32) for _ in range(4)]
+        for b in range(64):
+            coefficient = jnp.tile(system_ref[8 * b:8 * b + 8, 512:], (1, 4))
+            parts[b % 4] += coefficient * basis_ref[8 * b:8 * b + 8, lo:lo + 512].astype(f32)
+        out_ref[:, lo:lo + 512] = jnp.sum(
+            (parts[0] + parts[1]) + (parts[2] + parts[3]), axis=0, keepdims=True
+        )
+
+
+def solve_continuation(near, far, basis, path_count):
     at = jnp.stack([lax.axis_index("core"), lax.axis_index("z")]).astype(jnp.int32)
     whole = pl.BlockSpec((4, PIECE, LANES), lambda i, s: (0, 0, 0))
     return pl.pallas_call(
         lambda *refs: solve_kernel(*refs, scale=1.0 / path_count),
-        out_shape=jax.ShapeDtypeStruct((512, LANES), f32),
+        out_shape=jax.ShapeDtypeStruct((1, basis.shape[1]), f32),
         grid_spec=pltpu.PrefetchScalarGridSpec(
             num_scalar_prefetch=1,
             grid=(1,),
-            in_specs=[whole, whole],
-            out_specs=pl.BlockSpec((512, LANES), lambda i, s: (0, 0)),
+            in_specs=[whole, whole, pl.BlockSpec(basis.shape, lambda i, s: (0, 0))],
+            out_specs=pl.BlockSpec((1, basis.shape[1]), lambda i, s: (0, 0)),
             scratch_shapes=[
                 pltpu.VMEM((SUM_ROWS, LANES), f32),
                 pltpu.VMEM((512, 512 + LANES), f32),
-                pltpu.VMEM((BLOCK, BLOCK), f32),
             ],
         ),
         compiler_params=pltpu.CompilerParams(vmem_limit_bytes=40 << 20),
-        name="solve_coefficients",
-    )(at, near, far)
-
-
-def dates_kernel(slab_ref, coefficient_ref, basis_ref, moved_ref, mixer_ref, basket_ref, exercise_ref,
-                 bucket_ref, delta_ref, surface_ref, total_ref):
+        name="solve_continuation",
+    )(at, near, far, basis)
+
+
+def increments_kernel(moved_ref, mixer_ref, basket_ref, sent_ref, weights_ref):
+    adjoint = moved_ref[...].reshape(256, INCREMENT_TILE).astype(f32)
+    for date in range(STEPS - 1, -1, -1):
+        gain = TIME_STEP * jnp.dot(mixer_ref[...], adjoint.astype(bf16), preferred_element_type=f32)
+        sent_ref[:, date] = gain.astype(bf16).reshape(8, 32, INCREMENT_TILE)
+        if date:
+            adjoint = adjoint + gain
+
+    @pl.when(pl.program_id(0) == 0)
+    def _():
+        lane = lax.broadcasted_iota(jnp.int32, (256, LANES), 1)
+        weight = jnp.broadcast_to(basket_ref[...], (256, LANES))
+        table = weight
+        for later in range(1, STEPS):
+            gain = sum(
+                jnp.dot(mixer_ref[...], part, preferred_element_type=f32)
+                for part in three_terms(weight)
+            )
+            weight = weight + TIME_STEP * gain
+            table = jnp.where(lane == later, weight, table)
+        weights_ref[...] = table
+
+
+def increments(moved, mixer, basket, slab_part):
+    return pl.pallas_call(
+        increments_kernel,
+        out_shape=(
+            jax.ShapeDtypeStruct((8, STEPS, 32, slab_part), bf16),
+            jax.ShapeDtypeStruct((256, LANES), f32),
+        ),
+        grid=(slab_part // INCREMENT_TILE,),
+        in_specs=[
+            pl.BlockSpec((8, 32, INCREMENT_TILE), lambda i: (0, 0, i)),
+            pl.BlockSpec((256, 256), lambda i: (0, 0)),
+            pl.BlockSpec((256, 1), lambda i: (0, 0)),
+        ],
+        out_specs=(
+            pl.BlockSpec((8, STEPS, 32, INCREMENT_TILE), lambda i: (0, 0, 0, i)),
+            pl.BlockSpec((256, LANES), lambda i: (0, 0)),
+        ),
+        compiler_params=pltpu.CompilerParams(vmem_limit_bytes=40 << 20),
+        name="increments",
+    )(moved, mixer, basket)
+
+
+def surface_kernel(slab_ref, *refs):
+    continuation_refs = refs[:8]
+    (cotangent_ref, gain_ref, shock_ref, weight_ref, exercise_ref, bucket_ref, delta_ref, share_ref,
+     continuation_ref, total_ref) = refs[8:]
     step = pl.program_id(0)
-    parts = [jnp.zeros((8, TILE), f32) for _ in range(4)]
-    for b in range(64):
-        weight = jnp.broadcast_to(coefficient_ref[8 * b:8 * b + 8, :1], (8, TILE))
-        parts[b % 4] += weight * basis_ref[8 * b:8 * b + 8, :].astype(f32)
-    continuation = jnp.sum((parts[0] + parts[1]) + (parts[2] + parts[3]), axis=0, keepdims=True)
-    adjoint = moved_ref[:, 0].reshape(256, TILE).astype(f32)
-    basket = basket_ref[...]
-    strikes = lax.broadcasted_iota(jnp.int32, (NK, TILE), 0)
-    total = jnp.zeros((NK, 256), f32)
+
+    @pl.when(step == 0)
+    def _():
+        for flip in range(8):
+            at = slab_ref[0] ^ flip
+            for part in range(2):
+                continuation_ref[pl.ds(2 * at + part, 1), :] = continuation_refs[flip][
+                    :, part * DATE_TILE:(part + 1) * DATE_TILE
+                ]
+        total_ref[...] = jnp.zeros(total_ref.shape, f32)
+
+    continuation = continuation_ref[pl.ds(step, 1), :]
+    held = [exercise_ref[date:date + 1, :].astype(f32) * continuation for date in range(STEPS)]
+    weights = [weight_ref[:, later:later + 1] for later in range(STEPS)]
+    strikes = lax.broadcasted_iota(jnp.int32, (NK, DATE_TILE), 0)
+    base = cotangent_ref[...].astype(f32)
+    total = total_ref[...]
     for date in range(STEPS - 1, -1, -1):
-        mixed = jnp.dot(mixer_ref[...], adjoint.astype(bf16), preferred_element_type=f32)
-        held = exercise_ref[date:date + 1, :].astype(f32) * continuation
-        adjoint = adjoint + TIME_STEP * mixed + held * basket
-        terms = (adjoint * moved_ref[:, date + 1].reshape(256, TILE).astype(f32)).astype(bf16)
+        base = base + gain_ref[0, date].astype(f32)
+        adjoint = base
+        for later in range(STEPS - date):
+            adjoint = adjoint + held[date + later] * weights[later]
+        terms = (adjoint * shock_ref[date].astype(f32)).astype(bf16)
         chosen = jnp.where(strikes == bucket_ref[date:date + 1, :], 1.0, 0.0).astype(bf16)
         total = total + lax.dot_general(
             chosen, terms, (((1,), (1,)), ((), ())), preferred_element_type=f32
         )
-    delta_ref[...] = adjoint.astype(bf16).reshape(8, 32, TILE)
-
-    @pl.when(step == 0)
-    def _():
-        total_ref[...] = total
-
-    @pl.when(step > 0)
-    def _():
-        total_ref[...] += total
+    delta_ref[...] = adjoint
+    total_ref[...] = total
 
     @pl.when(step == pl.num_programs(0) - 1)
     def _():
-        grouped = total_ref[...].reshape(16, 16, 256)
-        for s in range(8):
-            for q in range(4):
-                surface_ref[:, s, :, 32 * q:32 * q + 32] = grouped[
-                    :, 4 * q:4 * q + 4, 32 * s:32 * s + 32
-                ]
-
-
-def date_loop(slab, coefficients, basis, moved, mixer, basket, exercise, bucket, slab_part):
-    tiles = slab_part // TILE
-
-    def own(step, slab_ref):
-        return (0, slab_ref[0] * tiles + step)
-
+        grouped = total.reshape(16, 16, 32)
+        for q in range(4):
+            share_ref[:, :, 32 * q:32 * q + 32] = grouped[:, 4 * q:4 * q + 4, :]
+
+
+def surface_and_delta(slab, continuations, cotangent, gains, shocks, weights, exercise, bucket):
+    local_paths = cotangent.shape[1]
+    whole = pl.BlockSpec((1, local_paths // 8), lambda i, s: (0, 0))
     return pl.pallas_call(
-        dates_kernel,
+        surface_kernel,
         out_shape=(
-            jax.ShapeDtypeStruct((8, 32, slab_part), bf16),
-            jax.ShapeDtypeStruct((16, 8, 4, LANES), f32),
+            jax.ShapeDtypeStruct((32, local_paths), f32),
+            jax.ShapeDtypeStruct((16, 4, LANES), f32),
         ),
         grid_spec=pltpu.PrefetchScalarGridSpec(
             num_scalar_prefetch=1,
-            grid=(tiles,),
-            in_specs=[
-                pl.BlockSpec((512, LANES), lambda i, s: (0, 0)),
-                pl.BlockSpec((512, TILE), lambda i, s: (0, i)),
-                pl.BlockSpec((8, 5, 32, TILE), lambda i, s: (0, 0, 0, i)),
-                pl.BlockSpec((256, 256), lambda i, s: (0, 0)),
-                pl.BlockSpec((256, 1), lambda i, s: (0, 0)),
-                pl.BlockSpec((4, TILE), own),
-                pl.BlockSpec((4, TILE), own),
+            grid=(local_paths // DATE_TILE,),
+            in_specs=[whole] * 8 + [
+                pl.BlockSpec((32, DATE_TILE), lambda i, s: (0, i)),
+                pl.BlockSpec((1, STEPS, 32, DATE_TILE), lambda i, s: (i // 2, 0, 0, i % 2)),
+                pl.BlockSpec((STEPS, 32, DATE_TILE), lambda i, s: (0, 0, i)),
+                pl.BlockSpec((32, LANES), lambda i, s: (s[0], 0)),
+                pl.BlockSpec((STEPS, DATE_TILE), lambda i, s: (0, i)),
+                pl.BlockSpec((STEPS, DATE_TILE), lambda i, s: (0, i)),
             ],
             out_specs=(
-                pl.BlockSpec((8, 32, TILE), lambda i, s: (0, 0, i)),
-                pl.BlockSpec((16, 8, 4, LANES), lambda i, s: (0, 0, 0, 0)),
+                pl.BlockSpec((32, DATE_TILE), lambda i, s: (0, i)),
+                pl.BlockSpec((16, 4, LANES), lambda i, s: (0, 0, 0)),
             ),
-            scratch_shapes=[pltpu.VMEM((NK, 256), f32)],
+            scratch_shapes=[pltpu.VMEM((16, DATE_TILE), f32), pltpu.VMEM((NK, 32), f32)],
         ),
         compiler_params=pltpu.CompilerParams(vmem_limit_bytes=48 << 20),
-        name="date_loop",
-    )(slab, coefficients, basis, moved, mixer, basket, exercise, bucket)
+        name="surface_and_delta",
+    )(slab, *continuations, cotangent, gains, shocks, weights, exercise, bucket)
 
 
 def per_device(prices, loadings, basis_w, basis_bias, payoff, in_fit, cotangent, shocks, corr_gen,
@@ -360,25 +416,25 @@
     moved_prices = lax.all_to_all(
         jnp.concatenate([pieces, table], axis=2), STOCK_AXES, 0, 0, tiled=True
     )
-    stacked = jnp.concatenate([cotangent[None], shocks], axis=0)
-    stacked = jnp.moveaxis(stacked.reshape(5, 32, 8, slab_part), 2, 0)
-    stacked, moved_prices = lax.optimization_barrier((stacked, moved_prices))
-    moved = lax.all_to_all(stacked, STOCK_AXES, 0, 0, tiled=True)
-
+    slabs = jnp.moveaxis(cotangent.reshape(32, 8, slab_part), 1, 0)
+    slabs, moved_prices = lax.optimization_barrier((slabs, moved_prices))
+    moved = lax.all_to_all(slabs, STOCK_AXES, 0, 0, tiled=True)
     basis, sums = regression_sums(
         slab, moved_prices, left_terms(basis_w, 0), basis_bias[:, None], payoff[None, :],
         in_fit[None, :], slab_part,
     )
-    near, far = all_device_sum(sums)
-    coefficients = solve_coefficients(near, far, path_count)
-    delta, surface = date_loop(
-        slab, coefficients, basis, moved, corr_gen, basket[:, None], exercise, bucket, slab_part
-    )
-    surface = lax.all_to_all(surface.reshape(128, 4, LANES), ALL_AXES, 0, 0, tiled=True)
+    sent, weights = increments(moved, corr_gen, basket[:, None], slab_part)
+    share, sent = all_device_sum(sums, sent)
+    gains = lax.all_to_all(sent, STOCK_AXES, 0, 0, tiled=True)
+    near, far = gathered_sum(share)
+    continuation = solve_continuation(near, far, basis, path_count)
+    continuations = [continuation] + exchange_with_others(continuation, STOCK_AXES, 8)
+    delta, surface = surface_and_delta(
+        slab, continuations, cotangent, gains, shocks, weights, exercise, bucket
+    )
+    surface = lax.all_to_all(surface, PATH_AXES, 0, 0, tiled=True)
     surface = jnp.sum(surface, axis=0).reshape(4, 4, 32)
     surface = jnp.transpose(surface, (2, 1, 0)).reshape(32, 16)
-    delta = lax.all_to_all(delta, STOCK_AXES, 0, 0, tiled=True)
-    delta = jnp.moveaxis(delta, 0, 1).reshape(32, local_paths).astype(f32)
     return delta, surface
 
 

time: 199 us -> 178 us (0.89)
  waiting for transfers between devices: 91.1 us -> 51.6 us
  Pallas kernels: 31.4 us -> 46.7 us
  starting transfers between devices: 40.1 us -> 51.5 us
  local copies, waits for them, and re-layouts: 11.5 us -> 7.78 us
  blocking collectives: 17.4 us -> 15 us
    ppermute x14 -> x21, waiting for transfers between devices: 65 us -> 33 us  [exchange_with_others(): lax.ppermute(sent, axes, [(i, i ^ flip) for i in range(count)])]
    pallas_call x2 -> x3, Pallas kernels: 27.1 us -> 42.4 us  [the longest x1 20.7 us: solve_continuation(): pl.pallas_call(lambda *refs: solve_kernel(*refs, scale=1.0 / path_count),...]
    all_to_all x2, waiting for transfers between devices: 15.2 us -> 3.86 us  [the longest x1 3.86 us: per_device(): moved = lax.all_to_all(slabs, STOCK_AXES, 0, 0, tiled=True)]
    ppermute x14 -> x21, starting transfers between devices: 24.4 us -> 35.6 us  [exchange_with_others(): lax.ppermute(sent, axes, [(i, i ^ flip) for i in range(count)])]
    all_to_all x1, waiting for transfers between devices: 10.9 us -> 14.8 us  [per_device(): lax.all_to_all(jnp.concatenate([pieces, table], axis=2), STOCK_AXES, 0, 0...]
    transpose x1 -> x0, other arithmetic: 2.82 us -> none  [per_device(): stacked = jnp.moveaxis(stacked.reshape(5, 32, 8, slab_part), 2, 0)]
    all_to_all x1, blocking collectives: 17.4 us -> 15 us  [per_device(): surface = lax.all_to_all(surface, PATH_AXES, 0, 0, tiled=True)]
    unnamed x25 -> x26, local copies, waits for them, and re-layouts: 6.09 us -> 4.28 us
  transfers between devices with their start and end apart: 17 -> 24, of which waited for: 14 -> 16; matrix products, arithmetic and copies ran while one was open for 3% -> 2% of each run, Pallas kernels for 12% -> 12%
where the time goes in v2:
time: 178 us; the launch traced here: 177 us
  waiting for transfers between devices  51.6 us (29%)
  starting transfers between devices  51.5 us (29%)
  Pallas kernels  46.7 us (26%)
  blocking collectives  15 us (8%)
  local copies, waits for them, and re-layouts  7.78 us (4%)
  other arithmetic  3.89 us (2%)
    ppermute x21, starting transfers between devices, exchange_with_others(): lax.ppermute(sent, axes, [(i, i ^ flip) for i in range(count)])  35.6 us
    ppermute x21, waiting for transfers between devices, exchange_with_others(): lax.ppermute(sent, axes, [(i, i ^ flip) for i in range(count)])  33 us
    pallas_call x1, Pallas kernels, solve_continuation(): pl.pallas_call(lambda *refs: solve_kernel(*refs, scale=1.0 / path_count),...  20.7 us
    pallas_call x1, Pallas kernels, surface_and_delta(): pl.pallas_call(surface_kernel, out_shape=(jax.ShapeDtypeStruct((32, local...  17 us
    all_to_all x1, blocking collectives, per_device(): surface = lax.all_to_all(surface, PATH_AXES, 0, 0, tiled=True)  15 us
    all_to_all x1, waiting for transfers between devices, per_device(): lax.all_to_all(jnp.concatenate([pieces, table], axis=2), STOCK_AXES, 0, 0...  14.8 us
    all_to_all x1, starting transfers between devices, per_device(): lax.all_to_all(jnp.concatenate([pieces, table], axis=2), STOCK_AXES, 0, 0...  7.61 us
    all_to_all x1, starting transfers between devices, per_device(): gains = lax.all_to_all(sent, STOCK_AXES, 0, 0, tiled=True)  4.68 us
  transfers between devices with their start and end apart: 24, of which 16 were waited for; matrix products, arithmetic and copies ran while one was open for 2% of the time, Pallas kernels for 12%

profile of v2, /device:TPU:1, one launch (start us, length us, event | category | flops | bytes accessed | tf_op | source)
XLA Modules:
  0.0 177.5 jit_solution(16724775572945288557)
XLA Ops:
  0.6 1.3 copy.27
  2.0 0.0 copy-start.8
  2.0 0.0 copy-start
  2.0 1.1 pad_maximum_fusion
  3.1 7.6 %all-to-all-start = ((bf16[8,32,2176]{2,1,0:T(8,128)(2,1)}), bf16[8,32,2176]{2,1,0:T(8,128)(2,1)S(1)}, u32[]{:S(2)}, u32[]{:S(2)}) async-start(bf16[8,32,2176]{2,1,0:T(8,128)(2,1)} %pad_maximum_fusion), calls=%async_computation | async-start | bytes 2228224 | tf_op jit(solution)/shard_map/all_to_all | solution.py:416
  10.7 0.0 copy-start.7
  10.8 1.1 copy.28
  11.9 0.1 copy.20.bias_ref
  12.2 14.8 %all-to-all-done.moved_ref.table_ref = bf16[8,32,2176]{2,1,0:T(8,128)(2,1)S(1)} async-done(((bf16[8,32,2176]{2,1,0:T(8,128)(2,1)}), bf16[8,32,2176]{2,1,0:T(8,128)(2,1)S(1)}, u32[]{:S(2)}, u32[]{:S(2)}) %all-to-all-start) | async-done | bytes 1114144 | tf_op jit(solution)/shard_map/all_to_all | solution.py:416
  26.9 4.3 %regression_sums.1 = (bf16[512,2048]{1,0:T(8,128)(2,1)S(1)}, f32[1344,128]{1,0:T(8,128)S(1)}) custom-call(s32[1]{0:T(128)} %bitcast.slab_ref, bf16[8,32,2176]{2,1,0:T(8,128)(2,1)S(1)} %all-to-all-done.moved_ref.table_ref, bf16[8,32,2176]{2,1,0:T(8,128)(2,1)S(1)} %all-to-all-done.moved_ref.table_ref, bf16[192,512]{1,0:T(8,128)(2,1)S(1)} %fusion.5.weight_ref, ...), custom_call_target="tpu_custom_call" | custom-call | tf_op jit(solution)/shard_map/regression_sums/pallas_call | solution.py:104
  31.2 0.0 copy-start.2
  31.2 1.3 copy-done.2
  32.6 0.0 copy-start.6
  32.6 1.7 collective-permute-start
  34.3 3.6 %all-to-all-start.1 = ((bf16[8,32,2048]{2,1,0:T(8,128)(2,1)}), bf16[8,32,2048]{2,1,0:T(8,128)(2,1)S(1)}, u32[]{:S(2)}, u32[]{:S(2)}) async-start(bf16[8,32,2048]{2,1,0:T(8,128)(2,1)} %bitcast.47), calls=%async_computation.1 | async-start | bytes 2097152 | tf_op jit(solution)/shard_map/all_to_all | solution.py:421
  37.9 1.0 bitcast_add_fusion
  38.9 1.7 collective-permute-start.1
  40.7 3.3 %collective-permute-start.2 = (f32[168,128]{1,0:T(8,128)S(1)}, f32[168,128]{1,0:T(8,128)S(1)}, u32[]{:S(2)}, u32[]{:S(2)}) collective-permute-start(f32[168,128]{1,0:T(8,128)S(1)} %get-tuple-element.28), channel_id=1, source_target_pairs={{0,64},{32,96},{64,0},{96,32},{1,65},{33,97},{65,1},{97,33},{2,66}... | collective-permute-start | bytes 258056 | tf_op jit(solution)/shard_map/ppermute | solution.py:136
  44.0 0.1 copy.21.basket_ref
  44.1 4.1 %collective-permute-done.2 = f32[168,128]{1,0:T(8,128)S(1)} collective-permute-done((f32[168,128]{1,0:T(8,128)S(1)}, f32[168,128]{1,0:T(8,128)S(1)}, u32[]{:S(2)}, u32[]{:S(2)}) %collective-permute-start.2) | collective-permute-done | bytes 86048 | tf_op jit(solution)/shard_map/ppermute | solution.py:136
  48.2 2.2 %collective-permute-done.3 = f32[168,128]{1,0:T(8,128)S(1)} collective-permute-done((f32[168,128]{1,0:T(8,128)S(1)}, f32[168,128]{1,0:T(8,128)S(1)}, u32[]{:S(2)}, u32[]{:S(2)}) %collective-permute-start.3) | collective-permute-done | bytes 86048 | tf_op jit(solution)/shard_map/ppermute | solution.py:136
  50.5 3.9 %all-to-all-done.1.moved_ref = bf16[8,32,2048]{2,1,0:T(8,128)(2,1)S(1)} async-done(((bf16[8,32,2048]{2,1,0:T(8,128)(2,1)}), bf16[8,32,2048]{2,1,0:T(8,128)(2,1)S(1)}, u32[]{:S(2)}, u32[]{:S(2)}) %all-to-all-start.1) | async-done | bytes 1048608 | tf_op jit(solution)/shard_map/all_to_all | solution.py:421
  54.4 4.6 %increments.1 = (bf16[8,4,32,2048]{3,2,1,0:T(8,128)(2,1)S(1)}, f32[256,128]{1,0:T(8,128)S(1)}) custom-call(bf16[8,32,2048]{2,1,0:T(8,128)(2,1)S(1)} %all-to-all-done.1.moved_ref, bf16[256,256]{1,0:T(8,128)(2,1)S(1)} %copy-done.6, f32[256,1]{1,0:T(8,128)S(1)} %copy.21.basket_ref), custom_call_target="tpu_custom_call" | custom-call | tf_op jit(solution)/shard_map/increments/pallas_call | solution.py:313
  59.0 2.0 %copy-done.1 = bf16[8,4,32,2048]{3,2,1,0:T(8,128)(2,1)} copy-done((bf16[8,4,32,2048]{3,2,1,0:T(8,128)(2,1)}, bf16[8,4,32,2048]{3,2,1,0:T(8,128)(2,1)S(1)}, u32[]{:S(2)}) %copy-start.1) | copy-done | bytes 4194328
  61.0 0.0 collective-permute-start.4
  61.0 2.2 %collective-permute-start.5 = (f32[168,128]{1,0:T(8,128)S(1)}, f32[168,128]{1,0:T(8,128)S(1)}, u32[]{:S(2)}, u32[]{:S(2)}) collective-permute-start(f32[168,128]{1,0:T(8,128)S(1)} %fusion.1), channel_id=1, source_target_pairs={{0,4},{2,6},{4,0},{6,2},{1,5},{3,7},{5,1},{7,3},{8,12},{10,14},{12... | collective-permute-start | bytes 258056 | tf_op jit(solution)/shard_map/ppermute | solution.py:136
  63.2 1.7 collective-permute-start.6
  64.9 0.0 collective-permute-done.4
  64.9 1.6 collective-permute-done.5
  66.5 2.2 %collective-permute-done.6 = f32[168,128]{1,0:T(8,128)S(1)} collective-permute-done((f32[168,128]{1,0:T(8,128)S(1)}, f32[168,128]{1,0:T(8,128)S(1)}, u32[]{:S(2)}, u32[]{:S(2)}) %collective-permute-start.6) | collective-permute-done | bytes 86048 | tf_op jit(solution)/shard_map/ppermute | solution.py:136
  68.7 2.1 %collective-permute-start.7 = (f32[168,128]{1,0:T(8,128)S(1)}, f32[168,128]{1,0:T(8,128)S(1)}, u32[]{:S(2)}, u32[]{:S(2)}) collective-permute-start(f32[168,128]{1,0:T(8,128)S(1)} %add_add_fusion.1), channel_id=1, source_target_pairs={{0,1},{1,0},{16,17},{17,16},{2,3},{3,2},{18,19},{19,18},{4,5},{5,4... | collective-permute-start | bytes 258056 | tf_op jit(solution)/shard_map/ppermute | solution.py:136
  70.8 0.4 collective-permute-start.8
  71.2 0.8 collective-permute-start.9
  72.0 1.6 collective-permute-done.7
  73.6 1.0 collective-permute-done.8
  74.6 2.0 %collective-permute-done.9 = f32[168,128]{1,0:T(8,128)S(1)} collective-permute-done((f32[168,128]{1,0:T(8,128)S(1)}, f32[168,128]{1,0:T(8,128)S(1)}, u32[]{:S(2)}, u32[]{:S(2)}) %collective-permute-start.9) | collective-permute-done | bytes 86048 | tf_op jit(solution)/shard_map/ppermute | solution.py:136
  76.6 0.7 add_add_fusion
  77.3 4.7 %all-to-all-start.2 = ((bf16[8,4,32,2048]{3,2,1,0:T(8,128)(2,1)}), bf16[8,4,32,2048]{3,2,1,0:T(8,128)(2,1)}, u32[]{:S(2)}, u32[]{:S(2)}) async-start(bf16[8,4,32,2048]{3,2,1,0:T(8,128)(2,1)} %copy-done.1), calls=%async_computation.2 | async-start | bytes 8388608 | tf_op jit(solution)/shard_map/all_to_all | solution.py:428
  82.0 0.0 copy-start.4
  82.0 1.8 collective-permute-start.10
  83.8 3.3 %collective-permute-start.11 = (f32[168,128]{1,0:T(8,128)}, f32[168,128]{1,0:T(8,128)S(1)}, u32[]{:S(2)}, u32[]{:S(2)}) collective-permute-start(f32[168,128]{1,0:T(8,128)} %add_add_fusion), channel_id=1, source_target_pairs={{0,64},{32,96},{64,0},{96,32},{1,65},{33,97},{65,1},{97,33},{2,66}... | collective-permute-start | bytes 258056 | tf_op jit(solution)/shard_map/ppermute | solution.py:136
  87.1 3.0 %collective-permute-done.11 = f32[168,128]{1,0:T(8,128)S(1)} collective-permute-done((f32[168,128]{1,0:T(8,128)}, f32[168,128]{1,0:T(8,128)S(1)}, u32[]{:S(2)}, u32[]{:S(2)}) %collective-permute-start.11) | collective-permute-done | bytes 86048 | tf_op jit(solution)/shard_map/ppermute | solution.py:136
  90.1 3.1 %collective-permute-done.12 = f32[168,128]{1,0:T(8,128)S(1)} collective-permute-done((f32[168,128]{1,0:T(8,128)}, f32[168,128]{1,0:T(8,128)S(1)}, u32[]{:S(2)}, u32[]{:S(2)}) %collective-permute-start.12) | collective-permute-done | bytes 86048 | tf_op jit(solution)/shard_map/ppermute | solution.py:136
  93.1 0.9 pad_maximum_fusion.1.refs_1_
  94.1 2.6 %collective-permute-start.13 = (f32[4,168,128]{2,1,0:T(8,128)S(1)}, f32[4,168,128]{2,1,0:T(8,128)S(1)}, u32[]{:S(2)}, u32[]{:S(2)}) collective-permute-start(f32[4,168,128]{2,1,0:T(8,128)S(1)} %pad_maximum_fusion.1.refs_1_), channel_id=1, source_target_pairs={{0,8},{8,0},{1,9},{9,1},{2,10},{10,2},{3,11},{11,3},{4,12},{12,4},... | collective-permute-start | bytes 1032200 | tf_op jit(solution)/shard_map/ppermute | solution.py:136
  96.7 0.1 pad_add_fusion.refs_0_
  96.8 1.2 collective-permute-done.13.refs_2_
  98.0 20.7 %solve_continuation.1.refs_0_ = f32[1,2048]{1,0:T(1,128)S(1)} custom-call(s32[2]{0:T(128)S(1)} %pad_add_fusion.refs_0_, f32[4,168,128]{2,1,0:T(8,128)S(1)} %pad_maximum_fusion.1.refs_1_, f32[4,168,128]{2,1,0:T(8,128)S(1)} %collective-permute-done.13.refs_2_, bf16[512,2048]{1,0:T(8,128)(2,1)S(1)} %copy-done.3), custom_call_target="tpu_custom_call" | custom-call | tf_op jit(solution)/shard_map/solve_continuation/pallas_call | solution.py:271
  118.7 3.1 %collective-permute-start.14 = (f32[1,2048]{1,0:T(1,128)S(1)}, f32[1,2048]{1,0:T(1,128)S(1)}, u32[]{:S(2)}, u32[]{:S(2)}) collective-permute-start(f32[1,2048]{1,0:T(1,128)S(1)} %solve_continuation.1.refs_0_), channel_id=1, source_target_pairs={{0,1},{1,0},{2,3},{3,2},{4,5},{5,4},{6,7},{7,6},{8,9},{9,8},{10,11... | collective-permute-start | bytes 24584 | tf_op jit(solution)/shard_map/ppermute | solution.py:136
  121.8 1.2 collective-permute-start.15
  123.0 0.1 collective-permute-start.16
  123.1 2.9 %collective-permute-start.17 = (f32[1,2048]{1,0:T(1,128)S(1)}, f32[1,2048]{1,0:T(1,128)S(1)}, u32[]{:S(2)}, u32[]{:S(2)}) collective-permute-start(f32[1,2048]{1,0:T(1,128)S(1)} %solve_continuation.1.refs_0_), channel_id=1, source_target_pairs={{0,4},{1,5},{2,6},{3,7},{4,0},{5,1},{6,2},{7,3},{8,12},{9,13},{10,... | collective-permute-start | bytes 24584 | tf_op jit(solution)/shard_map/ppermute | solution.py:136
  126.0 2.7 %collective-permute-start.18 = (f32[1,2048]{1,0:T(1,128)S(1)}, f32[1,2048]{1,0:T(1,128)S(1)}, u32[]{:S(2)}, u32[]{:S(2)}) collective-permute-start(f32[1,2048]{1,0:T(1,128)S(1)} %solve_continuation.1.refs_0_), channel_id=1, source_target_pairs={{0,5},{1,4},{2,7},{3,6},{4,1},{5,0},{6,3},{7,2},{8,13},{9,12},{10,... | collective-permute-start | bytes 24584 | tf_op jit(solution)/shard_map/ppermute | solution.py:136
  128.7 1.8 %collective-permute-done.14.refs_1_ = f32[1,2048]{1,0:T(1,128)S(1)} collective-permute-done((f32[1,2048]{1,0:T(1,128)S(1)}, f32[1,2048]{1,0:T(1,128)S(1)}, u32[]{:S(2)}, u32[]{:S(2)}) %collective-permute-start.14) | collective-permute-done | bytes 8224 | tf_op jit(solution)/shard_map/ppermute | solution.py:136
  130.5 1.0 collective-permute-start.19
  131.5 6.1 %collective-permute-done.15.refs_2_ = f32[1,2048]{1,0:T(1,128)S(1)} collective-permute-done((f32[1,2048]{1,0:T(1,128)S(1)}, f32[1,2048]{1,0:T(1,128)S(1)}, u32[]{:S(2)}, u32[]{:S(2)}) %collective-permute-start.15) | collective-permute-done | bytes 8224 | tf_op jit(solution)/shard_map/ppermute | solution.py:136
  137.6 3.1 %collective-permute-start.20 = (f32[1,2048]{1,0:T(1,128)S(1)}, f32[1,2048]{1,0:T(1,128)S(1)}, u32[]{:S(2)}, u32[]{:S(2)}) collective-permute-start(f32[1,2048]{1,0:T(1,128)S(1)} %solve_continuation.1.refs_0_), channel_id=1, source_target_pairs={{0,7},{1,6},{2,5},{3,4},{4,3},{5,2},{6,1},{7,0},{8,15},{9,14},{10,... | collective-permute-start | bytes 24584 | tf_op jit(solution)/shard_map/ppermute | solution.py:136
  140.7 0.2 collective-permute-done.17.refs_4_
  140.9 2.8 %collective-permute-done.20.refs_7_ = f32[1,2048]{1,0:T(1,128)S(1)} collective-permute-done((f32[1,2048]{1,0:T(1,128)S(1)}, f32[1,2048]{1,0:T(1,128)S(1)}, u32[]{:S(2)}, u32[]{:S(2)}) %collective-permute-start.20) | collective-permute-done | bytes 8224 | tf_op jit(solution)/shard_map/ppermute | solution.py:136
  143.8 0.9 copy-done.5
  144.7 17.0 %surface_and_delta.1 = (f32[32,16384]{1,0:T(8,128)}, f32[16,4,128]{2,1,0:T(4,128)S(1)}) custom-call(s32[1]{0:T(128)} %bitcast.slab_ref, f32[1,2048]{1,0:T(1,128)S(1)} %solve_continuation.1.refs_0_, f32[1,2048]{1,0:T(1,128)S(1)} %collective-permute-done.14.refs_1_, f32[1,2048]{1,0:T(1,128)S(1)} %collective-permute-done.15.refs_2_, ...), custom_call_target="tpu_custom_call" | custom-call | tf_op jit(solution)/shard_map/surface_and_delta/pallas_call | solution.py:379
  161.7 15.0 %all_to_all.20 = f32[16,4,128]{2,1,0:T(4,128)S(1)} all-to-all(f32[16,4,128]{2,1,0:T(4,128)S(1)} %get-tuple-element.25), channel_id=1, replica_groups=mesh['z'=4,'ylo'=2,'core'=2,'x'=4,'yhi'=2] {'z','ylo','core'}, dimensions={0} | all-to-all | bytes 65536 | tf_op jit(solution)/shard_map/all_to_all | solution.py:435
  176.8 0.1 reshape.27
  176.8 0.6 copy.22
  (40 shorter events, 0.3 us)
Async XLA Ops:
  0.6 1.3 copy-start.10
  2.0 8.7 %copy-start.8 = (f32[32,512]{1,0:T(8,128)S(1)}, f32[32,512]{1,0:T(8,128)}, u32[]{:S(2)}) copy-start(f32[32,512]{1,0:T(8,128)} %param.14) | copy-start | bytes 196612
  2.0 8.8 %copy-start = (bf16[32,16384]{1,0:T(8,128)(2,1)S(1)}, bf16[32,16384]{1,0:T(8,128)(2,1)}, u32[]{:S(2)}) copy-start(bf16[32,16384]{1,0:T(8,128)(2,1)} %refs_8_.1) | copy-start | bytes 3145732
  3.1 8.8 %copy-start.11 = (f32[512]{0:T(512)S(1)}, f32[512]{0:T(512)}, u32[]{:S(2)}) copy-start(f32[512]{0:T(512)} %param.15) | copy-start | bytes 6148
  3.1 8.9 %copy-start.9 = (bf16[16384]{0:T(1024)(128)(2,1)S(1)}, bf16[16384]{0:T(1024)(128)(2,1)}, u32[]{:S(2)}) copy-start(bf16[16384]{0:T(1024)(128)(2,1)} %param.16) | copy-start | bytes 98308
  3.1 23.8 %all-to-all-start = ((bf16[8,32,2176]{2,1,0:T(8,128)(2,1)}), bf16[8,32,2176]{2,1,0:T(8,128)(2,1)S(1)}, u32[]{:S(2)}, u32[]{:S(2)}) async-start(bf16[8,32,2176]{2,1,0:T(8,128)(2,1)} %pad_maximum_fusion), calls=%async_computation | async-start | bytes 2228224 | tf_op jit(solution)/shard_map/all_to_all | solution.py:416
  10.7 16.2 %copy-start.7 = (s32[16384]{0:T(1024)S(1)}, s32[16384]{0:T(1024)}, u32[]{:S(2)}) copy-start(s32[16384]{0:T(1024)} %param.17) | copy-start | bytes 196612
  31.2 1.3 copy-start.2
  32.5 11.4 %copy-start.12 = (f32[256]{0:T(256)S(1)}, f32[256]{0:T(256)}, u32[]{:S(2)}) copy-start(f32[256]{0:T(256)} %param.21) | copy-start | bytes 3076
  32.6 21.8 %copy-start.6 = (bf16[256,256]{1,0:T(8,128)(2,1)S(1)}, bf16[256,256]{1,0:T(8,128)(2,1)}, u32[]{:S(2)}) copy-start(bf16[256,256]{1,0:T(8,128)(2,1)} %mixer_ref.1) | copy-start | bytes 393220
  32.6 5.3 %collective-permute-start = (f32[4,168,128]{2,1,0:T(8,128)S(1)}, f32[4,168,128]{2,1,0:T(8,128)}, u32[]{:S(2)}, u32[]{:S(2)}) collective-permute-start(f32[4,168,128]{2,1,0:T(8,128)S(1)} %dynamic-slice_bitcast_fusion), channel_id=1, source_target_pairs={{0,8},{8,0},{1,9},{9,1},{2,10},{10,2},{3,11},{11,3},{4,12},{12,4},... | collective-permute-start | bytes 1032200 | tf_op jit(solution)/shard_map/ppermute | solution.py:136
  34.3 20.1 %all-to-all-start.1 = ((bf16[8,32,2048]{2,1,0:T(8,128)(2,1)}), bf16[8,32,2048]{2,1,0:T(8,128)(2,1)S(1)}, u32[]{:S(2)}, u32[]{:S(2)}) async-start(bf16[8,32,2048]{2,1,0:T(8,128)(2,1)} %bitcast.47), calls=%async_computation.1 | async-start | bytes 2097152 | tf_op jit(solution)/shard_map/all_to_all | solution.py:421
  38.9 5.2 %collective-permute-start.1 = (f32[168,128]{1,0:T(8,128)S(1)}, f32[168,128]{1,0:T(8,128)S(1)}, u32[]{:S(2)}, u32[]{:S(2)}) collective-permute-start(f32[168,128]{1,0:T(8,128)S(1)} %get-tuple-element.26), channel_id=1, source_target_pairs={{0,32},{32,0},{64,96},{96,64},{1,33},{33,1},{65,97},{97,65},{2,34}... | collective-permute-start | bytes 258056 | tf_op jit(solution)/shard_map/ppermute | solution.py:136
  40.7 7.6 %collective-permute-start.2 = (f32[168,128]{1,0:T(8,128)S(1)}, f32[168,128]{1,0:T(8,128)S(1)}, u32[]{:S(2)}, u32[]{:S(2)}) collective-permute-start(f32[168,128]{1,0:T(8,128)S(1)} %get-tuple-element.28), channel_id=1, source_target_pairs={{0,64},{32,96},{64,0},{96,32},{1,65},{33,97},{65,1},{97,33},{2,66}... | collective-permute-start | bytes 258056 | tf_op jit(solution)/shard_map/ppermute | solution.py:136
  44.0 6.5 %collective-permute-start.3 = (f32[168,128]{1,0:T(8,128)S(1)}, f32[168,128]{1,0:T(8,128)S(1)}, u32[]{:S(2)}, u32[]{:S(2)}) collective-permute-start(f32[168,128]{1,0:T(8,128)S(1)} %get-tuple-element.27), channel_id=1, source_target_pairs={{0,96},{32,64},{64,32},{96,0},{1,97},{33,65},{65,33},{97,1},{2,98}... | collective-permute-start | bytes 258056 | tf_op jit(solution)/shard_map/ppermute | solution.py:136
  59.0 2.0 %copy-start.1 = (bf16[8,4,32,2048]{3,2,1,0:T(8,128)(2,1)}, bf16[8,4,32,2048]{3,2,1,0:T(8,128)(2,1)S(1)}, u32[]{:S(2)}) copy-start(bf16[8,4,32,2048]{3,2,1,0:T(8,128)(2,1)S(1)} %get-tuple-element.22) | copy-start | bytes 12582916
  61.0 3.9 %collective-permute-start.4 = (f32[168,128]{1,0:T(8,128)S(1)}, f32[168,128]{1,0:T(8,128)S(1)}, u32[]{:S(2)}, u32[]{:S(2)}) collective-permute-start(f32[168,128]{1,0:T(8,128)S(1)} %fusion.1), channel_id=1, source_target_pairs={{0,2},{2,0},{4,6},{6,4},{1,3},{3,1},{5,7},{7,5},{8,10},{10,8},{12,... | collective-permute-start | bytes 258056 | tf_op jit(solution)/shard_map/ppermute | solution.py:136
  61.0 5.5 %collective-permute-start.5 = (f32[168,128]{1,0:T(8,128)S(1)}, f32[168,128]{1,0:T(8,128)S(1)}, u32[]{:S(2)}, u32[]{:S(2)}) collective-permute-start(f32[168,128]{1,0:T(8,128)S(1)} %fusion.1), channel_id=1, source_target_pairs={{0,4},{2,6},{4,0},{6,2},{1,5},{3,7},{5,1},{7,3},{8,12},{10,14},{12... | collective-permute-start | bytes 258056 | tf_op jit(solution)/shard_map/ppermute | solution.py:136
  63.2 5.5 %collective-permute-start.6 = (f32[168,128]{1,0:T(8,128)S(1)}, f32[168,128]{1,0:T(8,128)S(1)}, u32[]{:S(2)}, u32[]{:S(2)}) collective-permute-start(f32[168,128]{1,0:T(8,128)S(1)} %fusion.1), channel_id=1, source_target_pairs={{0,6},{2,4},{4,2},{6,0},{1,7},{3,5},{5,3},{7,1},{8,14},{10,12},{12... | collective-permute-start | bytes 258056 | tf_op jit(solution)/shard_map/ppermute | solution.py:136
  68.7 4.9 %collective-permute-start.7 = (f32[168,128]{1,0:T(8,128)S(1)}, f32[168,128]{1,0:T(8,128)S(1)}, u32[]{:S(2)}, u32[]{:S(2)}) collective-permute-start(f32[168,128]{1,0:T(8,128)S(1)} %add_add_fusion.1), channel_id=1, source_target_pairs={{0,1},{1,0},{16,17},{17,16},{2,3},{3,2},{18,19},{19,18},{4,5},{5,4... | collective-permute-start | bytes 258056 | tf_op jit(solution)/shard_map/ppermute | solution.py:136
  70.8 3.8 %collective-permute-start.8 = (f32[168,128]{1,0:T(8,128)S(1)}, f32[168,128]{1,0:T(8,128)S(1)}, u32[]{:S(2)}, u32[]{:S(2)}) collective-permute-start(f32[168,128]{1,0:T(8,128)S(1)} %add_add_fusion.1), channel_id=1, source_target_pairs={{0,16},{1,17},{16,0},{17,1},{2,18},{3,19},{18,2},{19,3},{4,20},{5,... | collective-permute-start | bytes 258056 | tf_op jit(solution)/shard_map/ppermute | solution.py:136
  71.2 5.4 %collective-permute-start.9 = (f32[168,128]{1,0:T(8,128)S(1)}, f32[168,128]{1,0:T(8,128)S(1)}, u32[]{:S(2)}, u32[]{:S(2)}) collective-permute-start(f32[168,128]{1,0:T(8,128)S(1)} %add_add_fusion.1), channel_id=1, source_target_pairs={{0,17},{1,16},{16,1},{17,0},{2,19},{3,18},{18,3},{19,2},{4,21},{5,... | collective-permute-start | bytes 258056 | tf_op jit(solution)/shard_map/ppermute | solution.py:136
  77.3 20.7 %copy-start.3 = (bf16[512,2048]{1,0:T(8,128)(2,1)S(1)}, bf16[512,2048]{1,0:T(8,128)(2,1)}, u32[]{:S(2)}) copy-start(bf16[512,2048]{1,0:T(8,128)(2,1)} %copy-done.2) | copy-start | bytes 6291460
  77.3 66.5 %all-to-all-start.2 = ((bf16[8,4,32,2048]{3,2,1,0:T(8,128)(2,1)}), bf16[8,4,32,2048]{3,2,1,0:T(8,128)(2,1)}, u32[]{:S(2)}, u32[]{:S(2)}) async-start(bf16[8,4,32,2048]{3,2,1,0:T(8,128)(2,1)} %copy-done.1), calls=%async_computation.2 | async-start | bytes 8388608 | tf_op jit(solution)/shard_map/all_to_all | solution.py:428
  82.0 61.8 %copy-start.4 = (s32[4,16384]{1,0:T(4,128)S(1)}, s32[4,16384]{1,0:T(4,128)}, u32[]{:S(2)}) copy-start(s32[4,16384]{1,0:T(4,128)} %refs_12_.1) | copy-start | bytes 786436
  82.0 5.1 %collective-permute-start.10 = (f32[168,128]{1,0:T(8,128)}, f32[168,128]{1,0:T(8,128)S(1)}, u32[]{:S(2)}, u32[]{:S(2)}) collective-permute-start(f32[168,128]{1,0:T(8,128)} %add_add_fusion), channel_id=1, source_target_pairs={{0,32},{32,0},{64,96},{96,64},{1,33},{33,1},{65,97},{97,65},{2,34}... | collective-permute-start | bytes 258056 | tf_op jit(solution)/shard_map/ppermute | solution.py:136
  83.8 6.3 %collective-permute-start.11 = (f32[168,128]{1,0:T(8,128)}, f32[168,128]{1,0:T(8,128)S(1)}, u32[]{:S(2)}, u32[]{:S(2)}) collective-permute-start(f32[168,128]{1,0:T(8,128)} %add_add_fusion), channel_id=1, source_target_pairs={{0,64},{32,96},{64,0},{96,32},{1,65},{33,97},{65,1},{97,33},{2,66}... | collective-permute-start | bytes 258056 | tf_op jit(solution)/shard_map/ppermute | solution.py:136
  87.1 6.1 %collective-permute-start.12 = (f32[168,128]{1,0:T(8,128)}, f32[168,128]{1,0:T(8,128)S(1)}, u32[]{:S(2)}, u32[]{:S(2)}) collective-permute-start(f32[168,128]{1,0:T(8,128)} %add_add_fusion), channel_id=1, source_target_pairs={{0,96},{32,64},{64,32},{96,0},{1,97},{33,65},{65,33},{97,1},{2,98}... | collective-permute-start | bytes 258056 | tf_op jit(solution)/shard_map/ppermute | solution.py:136
  94.1 3.9 %collective-permute-start.13 = (f32[4,168,128]{2,1,0:T(8,128)S(1)}, f32[4,168,128]{2,1,0:T(8,128)S(1)}, u32[]{:S(2)}, u32[]{:S(2)}) collective-permute-start(f32[4,168,128]{2,1,0:T(8,128)S(1)} %pad_maximum_fusion.1.refs_1_), channel_id=1, source_target_pairs={{0,8},{8,0},{1,9},{9,1},{2,10},{10,2},{3,11},{11,3},{4,12},{12,4},... | collective-permute-start | bytes 1032200 | tf_op jit(solution)/shard_map/ppermute | solution.py:136
  118.7 11.7 %collective-permute-start.14 = (f32[1,2048]{1,0:T(1,128)S(1)}, f32[1,2048]{1,0:T(1,128)S(1)}, u32[]{:S(2)}, u32[]{:S(2)}) collective-permute-start(f32[1,2048]{1,0:T(1,128)S(1)} %solve_continuation.1.refs_0_), channel_id=1, source_target_pairs={{0,1},{1,0},{2,3},{3,2},{4,5},{5,4},{6,7},{7,6},{8,9},{9,8},{10,11... | collective-permute-start | bytes 24584 | tf_op jit(solution)/shard_map/ppermute | solution.py:136
  121.8 15.8 %collective-permute-start.15 = (f32[1,2048]{1,0:T(1,128)S(1)}, f32[1,2048]{1,0:T(1,128)S(1)}, u32[]{:S(2)}, u32[]{:S(2)}) collective-permute-start(f32[1,2048]{1,0:T(1,128)S(1)} %solve_continuation.1.refs_0_), channel_id=1, source_target_pairs={{0,2},{1,3},{2,0},{3,1},{4,6},{5,7},{6,4},{7,5},{8,10},{9,11},{10,... | collective-permute-start | bytes 24584 | tf_op jit(solution)/shard_map/ppermute | solution.py:136
  123.0 17.7 %collective-permute-start.16 = (f32[1,2048]{1,0:T(1,128)S(1)}, f32[1,2048]{1,0:T(1,128)S(1)}, u32[]{:S(2)}, u32[]{:S(2)}) collective-permute-start(f32[1,2048]{1,0:T(1,128)S(1)} %solve_continuation.1.refs_0_), channel_id=1, source_target_pairs={{0,3},{1,2},{2,1},{3,0},{4,7},{5,6},{6,5},{7,4},{8,11},{9,10},{10,... | collective-permute-start | bytes 24584 | tf_op jit(solution)/shard_map/ppermute | solution.py:136
  123.1 17.8 %collective-permute-start.17 = (f32[1,2048]{1,0:T(1,128)S(1)}, f32[1,2048]{1,0:T(1,128)S(1)}, u32[]{:S(2)}, u32[]{:S(2)}) collective-permute-start(f32[1,2048]{1,0:T(1,128)S(1)} %solve_continuation.1.refs_0_), channel_id=1, source_target_pairs={{0,4},{1,5},{2,6},{3,7},{4,0},{5,1},{6,2},{7,3},{8,12},{9,13},{10,... | collective-permute-start | bytes 24584 | tf_op jit(solution)/shard_map/ppermute | solution.py:136
  126.0 14.9 %collective-permute-start.18 = (f32[1,2048]{1,0:T(1,128)S(1)}, f32[1,2048]{1,0:T(1,128)S(1)}, u32[]{:S(2)}, u32[]{:S(2)}) collective-permute-start(f32[1,2048]{1,0:T(1,128)S(1)} %solve_continuation.1.refs_0_), channel_id=1, source_target_pairs={{0,5},{1,4},{2,7},{3,6},{4,1},{5,0},{6,3},{7,2},{8,13},{9,12},{10,... | collective-permute-start | bytes 24584 | tf_op jit(solution)/shard_map/ppermute | solution.py:136
  130.5 10.5 %collective-permute-start.19 = (f32[1,2048]{1,0:T(1,128)S(1)}, f32[1,2048]{1,0:T(1,128)S(1)}, u32[]{:S(2)}, u32[]{:S(2)}) collective-permute-start(f32[1,2048]{1,0:T(1,128)S(1)} %solve_continuation.1.refs_0_), channel_id=1, source_target_pairs={{0,6},{1,7},{2,4},{3,5},{4,2},{5,3},{6,0},{7,1},{8,14},{9,15},{10,... | collective-permute-start | bytes 24584 | tf_op jit(solution)/shard_map/ppermute | solution.py:136
  137.6 6.1 %collective-permute-start.20 = (f32[1,2048]{1,0:T(1,128)S(1)}, f32[1,2048]{1,0:T(1,128)S(1)}, u32[]{:S(2)}, u32[]{:S(2)}) collective-permute-start(f32[1,2048]{1,0:T(1,128)S(1)} %solve_continuation.1.refs_0_), channel_id=1, source_target_pairs={{0,7},{1,6},{2,5},{3,4},{4,3},{5,2},{6,1},{7,0},{8,15},{9,14},{10,... | collective-permute-start | bytes 24584 | tf_op jit(solution)/shard_map/ppermute | solution.py:136
  143.8 1.0 copy-start.5

commit v3 on v2

--- a/solution.py
+++ b/solution.py
@@ -14,7 +14,7 @@
 BLOCK = 128
 TILE = 512
 INCREMENT_TILE = 512
-DATE_TILE = 1024
+DATE_TILE = 2048
 PATH_AXES = ("z", "ylo", "core")
 STOCK_AXES = ("x", "yhi")
 ALL_AXES = PATH_AXES + STOCK_AXES
@@ -148,14 +148,13 @@
     def piece_of(flip):
         return lax.dynamic_index_in_dim(mine, z ^ flip, 0, False)
 
-    share = piece_of(0)
-    for part in exchange_with_others(None, "z", 4, piece_of):
-        share = share + part
-    share, beside = lax.optimization_barrier((share, beside))
-    for axes in ("x", ("ylo", "yhi")):
-        parts = exchange_with_others(share, axes, 4)
-        share = (share + parts[0]) + (parts[1] + parts[2])
-    return lax.optimization_barrier((share, beside))
+    parts, beside = lax.optimization_barrier((exchange_with_others(None, "z", 4, piece_of), beside))
+    share = (piece_of(0) + parts[0]) + (parts[1] + parts[2])
+    parts = exchange_with_others(share, "x", 4)
+    share = (share + parts[0]) + (parts[1] + parts[2])
+    parts = exchange_with_others(share, ("ylo", "yhi"), 4)
+    parts, beside = lax.optimization_barrier((parts, beside))
+    return (share + parts[0]) + (parts[1] + parts[2]), beside
 
 
 def gathered_sum(share):
@@ -332,19 +331,17 @@
 
 
 def surface_kernel(slab_ref, *refs):
-    continuation_refs = refs[:8]
+    continuation_refs = refs[:4]
     (cotangent_ref, gain_ref, shock_ref, weight_ref, exercise_ref, bucket_ref, delta_ref, share_ref,
-     continuation_ref, total_ref) = refs[8:]
+     continuation_ref, total_ref) = refs[4:]
     step = pl.program_id(0)
 
     @pl.when(step == 0)
     def _():
         for flip in range(8):
-            at = slab_ref[0] ^ flip
-            for part in range(2):
-                continuation_ref[pl.ds(2 * at + part, 1), :] = continuation_refs[flip][
-                    :, part * DATE_TILE:(part + 1) * DATE_TILE
-                ]
+            continuation_ref[pl.ds(slab_ref[0] ^ flip, 1), :] = continuation_refs[flip // 2][
+                flip % 2:flip % 2 + 1, :
+            ]
         total_ref[...] = jnp.zeros(total_ref.shape, f32)
 
     continuation = continuation_ref[pl.ds(step, 1), :]
@@ -375,7 +372,7 @@
 
 def surface_and_delta(slab, continuations, cotangent, gains, shocks, weights, exercise, bucket):
     local_paths = cotangent.shape[1]
-    whole = pl.BlockSpec((1, local_paths // 8), lambda i, s: (0, 0))
+    whole = pl.BlockSpec((2, DATE_TILE), lambda i, s: (0, 0))
     return pl.pallas_call(
         surface_kernel,
         out_shape=(
@@ -385,9 +382,9 @@
         grid_spec=pltpu.PrefetchScalarGridSpec(
             num_scalar_prefetch=1,
             grid=(local_paths // DATE_TILE,),
-            in_specs=[whole] * 8 + [
+            in_specs=[whole] * 4 + [
                 pl.BlockSpec((32, DATE_TILE), lambda i, s: (0, i)),
-                pl.BlockSpec((1, STEPS, 32, DATE_TILE), lambda i, s: (i // 2, 0, 0, i % 2)),
+                pl.BlockSpec((1, STEPS, 32, DATE_TILE), lambda i, s: (i, 0, 0, 0)),
                 pl.BlockSpec((STEPS, 32, DATE_TILE), lambda i, s: (0, 0, i)),
                 pl.BlockSpec((32, LANES), lambda i, s: (s[0], 0)),
                 pl.BlockSpec((STEPS, DATE_TILE), lambda i, s: (0, i)),
@@ -397,7 +394,7 @@
                 pl.BlockSpec((32, DATE_TILE), lambda i, s: (0, i)),
                 pl.BlockSpec((16, 4, LANES), lambda i, s: (0, 0, 0)),
             ),
-            scratch_shapes=[pltpu.VMEM((16, DATE_TILE), f32), pltpu.VMEM((NK, 32), f32)],
+            scratch_shapes=[pltpu.VMEM((8, DATE_TILE), f32), pltpu.VMEM((NK, 32), f32)],
         ),
         compiler_params=pltpu.CompilerParams(vmem_limit_bytes=48 << 20),
         name="surface_and_delta",
@@ -428,7 +425,8 @@
     gains = lax.all_to_all(sent, STOCK_AXES, 0, 0, tiled=True)
     near, far = gathered_sum(share)
     continuation = solve_continuation(near, far, basis, path_count)
-    continuations = [continuation] + exchange_with_others(continuation, STOCK_AXES, 8)
+    pair = jnp.concatenate([continuation] + exchange_with_others(continuation, "yhi", 2), axis=0)
+    continuations = [pair] + exchange_with_others(pair, "x", 4)
     delta, surface = surface_and_delta(
         slab, continuations, cotangent, gains, shocks, weights, exercise, bucket
     )

time: 178 us -> 166 us (0.933)
  waiting for transfers between devices: 51.6 us -> 46.1 us
  local copies, waits for them, and re-layouts: 7.78 us -> 12.5 us
  starting transfers between devices: 51.5 us -> 46.8 us
  Pallas kernels: 46.7 us -> 43.1 us
  blocking collectives: 15 us -> 12.5 us
    ppermute x21 -> x18, starting transfers between devices: 35.6 us -> 30.4 us  [exchange_with_others(): lax.ppermute(sent, axes, [(i, i ^ flip) for i in range(count)])]
    unnamed x26 -> x36, local copies, waits for them, and re-layouts: 4.28 us -> 8.21 us
    all_to_all x1, waiting for transfers between devices: 3.86 us -> 0.01 us  [per_device(): moved = lax.all_to_all(slabs, STOCK_AXES, 0, 0, tiled=True)]
    pallas_call x1, Pallas kernels: 17 us -> 13.4 us  [surface_and_delta(): pl.pallas_call(surface_kernel, out_shape=(jax.ShapeDtypeStruct((32, local...]
    all_to_all x1, blocking collectives: 15 us -> 12.5 us  [per_device(): surface = lax.all_to_all(surface, PATH_AXES, 0, 0, tiled=True)]
    ppermute x21 -> x18, waiting for transfers between devices: 33 us -> 31.1 us  [exchange_with_others(): lax.ppermute(sent, axes, [(i, i ^ flip) for i in range(count)])]
  transfers between devices with their start and end apart: 24 -> 21, of which waited for: 16 -> 13; matrix products, arithmetic and copies ran while one was open for 2% -> 3% of each run, Pallas kernels for 12% -> 18%
where the time goes in v3:
time: 166 us; the launch traced here: 165 us
  starting transfers between devices  46.8 us (28%)
  waiting for transfers between devices  46.1 us (28%)
  Pallas kernels  43.1 us (26%)
  local copies, waits for them, and re-layouts  12.5 us (8%)
  blocking collectives  12.5 us (8%)
  other arithmetic  3.43 us (2%)
    ppermute x18, waiting for transfers between devices, exchange_with_others(): lax.ppermute(sent, axes, [(i, i ^ flip) for i in range(count)])  31.1 us
    ppermute x18, starting transfers between devices, exchange_with_others(): lax.ppermute(sent, axes, [(i, i ^ flip) for i in range(count)])  30.4 us
    pallas_call x1, Pallas kernels, solve_continuation(): pl.pallas_call(lambda *refs: solve_kernel(*refs, scale=1.0 / path_count),...  20.7 us
    all_to_all x1, waiting for transfers between devices, per_device(): lax.all_to_all(jnp.concatenate([pieces, table], axis=2), STOCK_AXES, 0, 0...  15 us
    pallas_call x1, Pallas kernels, surface_and_delta(): pl.pallas_call(surface_kernel, out_shape=(jax.ShapeDtypeStruct((32, local...  13.4 us
    all_to_all x1, blocking collectives, per_device(): surface = lax.all_to_all(surface, PATH_AXES, 0, 0, tiled=True)  12.5 us
    unnamed x36, local copies, waits for them, and re-layouts  8.21 us
    all_to_all x1, starting transfers between devices, per_device(): lax.all_to_all(jnp.concatenate([pieces, table], axis=2), STOCK_AXES, 0, 0...  7.48 us
  transfers between devices with their start and end apart: 21, of which 13 were waited for; matrix products, arithmetic and copies ran while one was open for 3% of the time, Pallas kernels for 18%

profile of v3, /device:TPU:1, one launch (start us, length us, event | category | flops | bytes accessed | tf_op | source)
XLA Modules:
  0.0 165.3 jit_solution(2179659062334903332)
XLA Ops:
  0.6 1.3 copy.27
  2.0 0.0 copy-start.11
  2.0 0.0 copy-start
  2.0 1.1 pad_maximum_fusion
  3.1 7.5 %all-to-all-start = ((bf16[8,32,2176]{2,1,0:T(8,128)(2,1)}), bf16[8,32,2176]{2,1,0:T(8,128)(2,1)S(1)}, u32[]{:S(2)}, u32[]{:S(2)}) async-start(bf16[8,32,2176]{2,1,0:T(8,128)(2,1)} %pad_maximum_fusion), calls=%async_computation | async-start | bytes 2228224 | tf_op jit(solution)/shard_map/all_to_all | solution.py:413
  10.6 0.0 copy-start.16
  10.6 1.1 copy.28
  11.8 15.0 %all-to-all-done.moved_ref.table_ref = bf16[8,32,2176]{2,1,0:T(8,128)(2,1)S(1)} async-done(((bf16[8,32,2176]{2,1,0:T(8,128)(2,1)}), bf16[8,32,2176]{2,1,0:T(8,128)(2,1)S(1)}, u32[]{:S(2)}, u32[]{:S(2)}) %all-to-all-start) | async-done | bytes 1114144 | tf_op jit(solution)/shard_map/all_to_all | solution.py:413
  26.8 4.2 %all-to-all-start.1 = ((bf16[8,32,2048]{2,1,0:T(8,128)(2,1)}), bf16[8,32,2048]{2,1,0:T(8,128)(2,1)S(1)}, u32[]{:S(2)}, u32[]{:S(2)}) async-start(bf16[8,32,2048]{2,1,0:T(8,128)(2,1)} %bitcast.45), calls=%async_computation.1 | async-start | bytes 2097152 | tf_op jit(solution)/shard_map/all_to_all | solution.py:418
  31.0 0.0 copy-start.5
  31.0 0.7 copy-done.5
  31.7 0.1 copy.20.bias_ref
  31.9 0.8 broadcast_in_dim.20.payoff_ref
  32.7 0.0 copy-start.6
  32.7 0.9 copy-done.6
  33.6 0.8 copy-done.10
  34.4 4.3 %regression_sums.1 = (bf16[512,2048]{1,0:T(8,128)(2,1)S(1)}, f32[1344,128]{1,0:T(8,128)S(1)}) custom-call(s32[1]{0:T(128)} %bitcast.slab_ref, bf16[8,32,2176]{2,1,0:T(8,128)(2,1)S(1)} %all-to-all-done.moved_ref.table_ref, bf16[8,32,2176]{2,1,0:T(8,128)(2,1)S(1)} %all-to-all-done.moved_ref.table_ref, bf16[192,512]{1,0:T(8,128)(2,1)S(1)} %copy-done.6, ...), custom_call_target="tpu_custom_call" | custom-call | tf_op jit(solution)/shard_map/regression_sums/pallas_call | solution.py:104
  38.7 0.0 copy-start.2
  38.7 1.3 copy-done.2
  40.0 0.9 copy-done.4
  40.9 1.3 collective-permute-start
  42.2 1.3 collective-permute-done
  43.5 1.0 bitcast_add_fusion
  44.6 1.7 %collective-permute-start.1 = (f32[168,128]{1,0:T(8,128)S(1)}, f32[168,128]{1,0:T(8,128)S(1)}, u32[]{:S(2)}, u32[]{:S(2)}) collective-permute-start(f32[168,128]{1,0:T(8,128)S(1)} %get-tuple-element.36), channel_id=1, source_target_pairs={{0,32},{32,0},{64,96},{96,64},{1,33},{33,1},{65,97},{97,65},{2,34}... | collective-permute-start | bytes 258056 | tf_op jit(solution)/shard_map/ppermute | solution.py:136
  46.3 3.3 %collective-permute-start.2 = (f32[168,128]{1,0:T(8,128)S(1)}, f32[168,128]{1,0:T(8,128)S(1)}, u32[]{:S(2)}, u32[]{:S(2)}) collective-permute-start(f32[168,128]{1,0:T(8,128)S(1)} %get-tuple-element.35), channel_id=1, source_target_pairs={{0,64},{32,96},{64,0},{96,32},{1,65},{33,97},{65,1},{97,33},{2,66}... | collective-permute-start | bytes 258056 | tf_op jit(solution)/shard_map/ppermute | solution.py:136
  49.6 0.1 copy.21.basket_ref
  49.8 4.7 %increments.1 = (bf16[8,4,32,2048]{3,2,1,0:T(8,128)(2,1)S(1)}, f32[256,128]{1,0:T(8,128)S(1)}) custom-call(bf16[8,32,2048]{2,1,0:T(8,128)(2,1)S(1)} %all-to-all-done.1.moved_ref, bf16[256,256]{1,0:T(8,128)(2,1)S(1)} %copy-done.9, f32[256,1]{1,0:T(8,128)S(1)} %copy.21.basket_ref), custom_call_target="tpu_custom_call" | custom-call | tf_op jit(solution)/shard_map/increments/pallas_call | solution.py:312
  54.5 2.0 %copy-done.1 = bf16[8,4,32,2048]{3,2,1,0:T(8,128)(2,1)} copy-done((bf16[8,4,32,2048]{3,2,1,0:T(8,128)(2,1)}, bf16[8,4,32,2048]{3,2,1,0:T(8,128)(2,1)S(1)}, u32[]{:S(2)}) %copy-start.1) | copy-done | bytes 4194328
  56.5 1.8 %collective-permute-start.4 = (f32[168,128]{1,0:T(8,128)S(1)}, f32[168,128]{1,0:T(8,128)S(1)}, u32[]{:S(2)}, u32[]{:S(2)}) collective-permute-start(f32[168,128]{1,0:T(8,128)S(1)} %fusion), channel_id=1, source_target_pairs={{0,2},{2,0},{4,6},{6,4},{1,3},{3,1},{5,7},{7,5},{8,10},{10,8},{12,... | collective-permute-start | bytes 258056 | tf_op jit(solution)/shard_map/ppermute | solution.py:136
  58.3 2.4 %collective-permute-start.5 = (f32[168,128]{1,0:T(8,128)S(1)}, f32[168,128]{1,0:T(8,128)S(1)}, u32[]{:S(2)}, u32[]{:S(2)}) collective-permute-start(f32[168,128]{1,0:T(8,128)S(1)} %fusion), channel_id=1, source_target_pairs={{0,4},{2,6},{4,0},{6,2},{1,5},{3,7},{5,1},{7,3},{8,12},{10,14},{12... | collective-permute-start | bytes 258056 | tf_op jit(solution)/shard_map/ppermute | solution.py:136
  60.6 0.1 collective-permute-start.6
  60.8 3.0 %collective-permute-done.5 = f32[168,128]{1,0:T(8,128)S(1)} collective-permute-done((f32[168,128]{1,0:T(8,128)S(1)}, f32[168,128]{1,0:T(8,128)S(1)}, u32[]{:S(2)}, u32[]{:S(2)}) %collective-permute-start.5) | collective-permute-done | bytes 86048 | tf_op jit(solution)/shard_map/ppermute | solution.py:136
  63.8 2.3 %collective-permute-done.6 = f32[168,128]{1,0:T(8,128)S(1)} collective-permute-done((f32[168,128]{1,0:T(8,128)S(1)}, f32[168,128]{1,0:T(8,128)S(1)}, u32[]{:S(2)}, u32[]{:S(2)}) %collective-permute-start.6) | collective-permute-done | bytes 86048 | tf_op jit(solution)/shard_map/ppermute | solution.py:136
  66.1 2.8 %collective-permute-start.7 = (f32[168,128]{1,0:T(8,128)S(1)}, f32[168,128]{1,0:T(8,128)S(1)}, u32[]{:S(2)}, u32[]{:S(2)}) collective-permute-start(f32[168,128]{1,0:T(8,128)S(1)} %add_add_fusion.1), channel_id=1, source_target_pairs={{0,1},{1,0},{16,17},{17,16},{2,3},{3,2},{18,19},{19,18},{4,5},{5,4... | collective-permute-start | bytes 258056 | tf_op jit(solution)/shard_map/ppermute | solution.py:136
  69.0 0.4 collective-permute-start.8
  69.3 0.1 collective-permute-start.9
  69.5 1.6 collective-permute-done.7
  71.1 1.5 collective-permute-done.8
  72.6 0.6 copy-done.14
  73.2 1.1 collective-permute-done.9
  74.3 4.7 %all-to-all-start.2 = ((bf16[8,4,32,2048]{3,2,1,0:T(8,128)(2,1)}), bf16[8,4,32,2048]{3,2,1,0:T(8,128)(2,1)}, u32[]{:S(2)}, u32[]{:S(2)}) async-start(bf16[8,4,32,2048]{3,2,1,0:T(8,128)(2,1)} %copy-done.1), calls=%async_computation.2 | async-start | bytes 8388608 | tf_op jit(solution)/shard_map/all_to_all | solution.py:425
  79.0 0.0 copy-start.7
  79.0 1.1 add_add_fusion
  80.1 0.1 collective-permute-start.10
  80.2 4.1 %collective-permute-start.11 = (f32[168,128]{1,0:T(8,128)S(1)}, f32[168,128]{1,0:T(8,128)S(1)}, u32[]{:S(2)}, u32[]{:S(2)}) collective-permute-start(f32[168,128]{1,0:T(8,128)S(1)} %add_add_fusion), channel_id=1, source_target_pairs={{0,64},{32,96},{64,0},{96,32},{1,65},{33,97},{65,1},{97,33},{2,66}... | collective-permute-start | bytes 258056 | tf_op jit(solution)/shard_map/ppermute | solution.py:136
  84.3 2.8 %collective-permute-done.11 = f32[168,128]{1,0:T(8,128)S(1)} collective-permute-done((f32[168,128]{1,0:T(8,128)S(1)}, f32[168,128]{1,0:T(8,128)S(1)}, u32[]{:S(2)}, u32[]{:S(2)}) %collective-permute-start.11) | collective-permute-done | bytes 86048 | tf_op jit(solution)/shard_map/ppermute | solution.py:136
  87.1 1.8 %collective-permute-done.12 = f32[168,128]{1,0:T(8,128)S(1)} collective-permute-done((f32[168,128]{1,0:T(8,128)S(1)}, f32[168,128]{1,0:T(8,128)S(1)}, u32[]{:S(2)}, u32[]{:S(2)}) %collective-permute-start.12) | collective-permute-done | bytes 86048 | tf_op jit(solution)/shard_map/ppermute | solution.py:136
  88.9 5.1 %collective-permute-start.13 = (f32[4,168,128]{2,1,0:T(8,128)S(1)}, f32[4,168,128]{2,1,0:T(8,128)S(1)}, u32[]{:S(2)}, u32[]{:S(2)}) collective-permute-start(f32[4,168,128]{2,1,0:T(8,128)S(1)} %pad_maximum_fusion.1.refs_1_), channel_id=1, source_target_pairs={{0,8},{8,0},{1,9},{9,1},{2,10},{10,2},{3,11},{11,3},{4,12},{12,4},... | collective-permute-start | bytes 1032200 | tf_op jit(solution)/shard_map/ppermute | solution.py:136
  94.0 0.1 pad_add_fusion.refs_0_
  94.1 1.2 collective-permute-done.13.refs_2_
  95.3 20.7 %solve_continuation.1 = f32[1,2048]{1,0:T(1,128)S(1)} custom-call(s32[2]{0:T(128)S(1)} %pad_add_fusion.refs_0_, f32[4,168,128]{2,1,0:T(8,128)S(1)} %pad_maximum_fusion.1.refs_1_, f32[4,168,128]{2,1,0:T(8,128)S(1)} %collective-permute-done.13.refs_2_, bf16[512,2048]{1,0:T(8,128)(2,1)S(1)} %copy-done.3), custom_call_target="tpu_custom_call" | custom-call | tf_op jit(solution)/shard_map/solve_continuation/pallas_call | solution.py:270
  116.0 3.2 %collective-permute-start.14 = (f32[1,2048]{1,0:T(1,128)S(1)}, f32[1,2048]{1,0:T(1,128)S(1)}, u32[]{:S(2)}, u32[]{:S(2)}) collective-permute-start(f32[1,2048]{1,0:T(1,128)S(1)} %solve_continuation.1), channel_id=1, source_target_pairs={{0,1},{1,0},{2,3},{3,2},{4,5},{5,4},{6,7},{7,6},{8,9},{9,8},{10,11... | collective-permute-start | bytes 24584 | tf_op jit(solution)/shard_map/ppermute | solution.py:136
  119.2 8.6 %collective-permute-done.14 = f32[1,2048]{1,0:T(1,128)S(1)} collective-permute-done((f32[1,2048]{1,0:T(1,128)S(1)}, f32[1,2048]{1,0:T(1,128)S(1)}, u32[]{:S(2)}, u32[]{:S(2)}) %collective-permute-start.14) | collective-permute-done | bytes 8224 | tf_op jit(solution)/shard_map/ppermute | solution.py:136
  127.8 0.1 collective-permute-start.15
  127.9 2.9 %collective-permute-start.16 = (f32[2,2048]{1,0:T(2,128)S(1)}, f32[2,2048]{1,0:T(2,128)S(1)}, u32[]{:S(2)}, u32[]{:S(2)}) collective-permute-start(f32[2,2048]{1,0:T(2,128)S(1)} %pad_maximum_fusion.2.refs_0_), channel_id=1, source_target_pairs={{0,4},{2,6},{4,0},{6,2},{1,5},{3,7},{5,1},{7,3},{8,12},{10,14},{12... | collective-permute-start | bytes 49160 | tf_op jit(solution)/shard_map/ppermute | solution.py:136
  130.8 1.0 collective-permute-start.17
  131.8 1.8 %collective-permute-done.15.refs_1_ = f32[2,2048]{1,0:T(2,128)S(1)} collective-permute-done((f32[2,2048]{1,0:T(2,128)S(1)}, f32[2,2048]{1,0:T(2,128)S(1)}, u32[]{:S(2)}, u32[]{:S(2)}) %collective-permute-start.15) | collective-permute-done | bytes 16416 | tf_op jit(solution)/shard_map/ppermute | solution.py:136
  133.5 4.2 %collective-permute-done.16.refs_2_ = f32[2,2048]{1,0:T(2,128)S(1)} collective-permute-done((f32[2,2048]{1,0:T(2,128)S(1)}, f32[2,2048]{1,0:T(2,128)S(1)}, u32[]{:S(2)}, u32[]{:S(2)}) %collective-permute-start.16) | collective-permute-done | bytes 16416 | tf_op jit(solution)/shard_map/ppermute | solution.py:136
  137.7 0.0 copy-start.8
  137.7 0.9 copy-done.8
  138.7 13.4 %surface_and_delta.1 = (f32[32,16384]{1,0:T(8,128)}, f32[16,4,128]{2,1,0:T(4,128)S(1)}) custom-call(s32[1]{0:T(128)} %bitcast.slab_ref, f32[2,2048]{1,0:T(2,128)S(1)} %pad_maximum_fusion.2.refs_0_, f32[2,2048]{1,0:T(2,128)S(1)} %collective-permute-done.15.refs_1_, f32[2,2048]{1,0:T(2,128)S(1)} %collective-permute-done.16.refs_2_, ...), custom_call_target="tpu_custom_call" | custom-call | tf_op jit(solution)/shard_map/surface_and_delta/pallas_call | solution.py:376
  152.1 12.5 %all_to_all.20 = f32[16,4,128]{2,1,0:T(4,128)S(1)} all-to-all(f32[16,4,128]{2,1,0:T(4,128)S(1)} %get-tuple-element.33), channel_id=1, replica_groups=mesh['z'=4,'ylo'=2,'core'=2,'x'=4,'yhi'=2] {'z','ylo','core'}, dimensions={0} | all-to-all | bytes 65536 | tf_op jit(solution)/shard_map/all_to_all | solution.py:433
  164.6 0.1 reshape.27
  164.7 0.6 copy.22
  (45 shorter events, 0.3 us)
Async XLA Ops:
  0.6 1.3 copy-start.15
  2.0 8.6 %copy-start.11 = (f32[32,512]{1,0:T(8,128)S(1)}, f32[32,512]{1,0:T(8,128)}, u32[]{:S(2)}) copy-start(f32[32,512]{1,0:T(8,128)} %param.14) | copy-start | bytes 196612
  2.0 8.6 %copy-start = (bf16[32,16384]{1,0:T(8,128)(2,1)S(1)}, bf16[32,16384]{1,0:T(8,128)(2,1)}, u32[]{:S(2)}) copy-start(bf16[32,16384]{1,0:T(8,128)(2,1)} %refs_4_.1) | copy-start | bytes 3145732
  3.1 23.7 %all-to-all-start = ((bf16[8,32,2176]{2,1,0:T(8,128)(2,1)}), bf16[8,32,2176]{2,1,0:T(8,128)(2,1)S(1)}, u32[]{:S(2)}, u32[]{:S(2)}) async-start(bf16[8,32,2176]{2,1,0:T(8,128)(2,1)} %pad_maximum_fusion), calls=%async_computation | async-start | bytes 2228224 | tf_op jit(solution)/shard_map/all_to_all | solution.py:413
  10.6 21.1 %copy-start.16 = (f32[512]{0:T(512)S(1)}, f32[512]{0:T(512)}, u32[]{:S(2)}) copy-start(f32[512]{0:T(512)} %param.15) | copy-start | bytes 6148
  26.8 22.9 %all-to-all-start.1 = ((bf16[8,32,2048]{2,1,0:T(8,128)(2,1)}), bf16[8,32,2048]{2,1,0:T(8,128)(2,1)S(1)}, u32[]{:S(2)}, u32[]{:S(2)}) async-start(bf16[8,32,2048]{2,1,0:T(8,128)(2,1)} %bitcast.45), calls=%async_computation.1 | async-start | bytes 2097152 | tf_op jit(solution)/shard_map/all_to_all | solution.py:418
  31.0 0.7 copy-start.5
  32.7 0.9 copy-start.6
  33.6 0.8 copy-start.10
  34.4 15.2 %copy-start.17 = (f32[256]{0:T(256)S(1)}, f32[256]{0:T(256)}, u32[]{:S(2)}) copy-start(f32[256]{0:T(256)} %param.21) | copy-start | bytes 3076
  38.7 1.3 copy-start.2
  40.0 0.9 copy-start.4
  40.0 9.7 %copy-start.9 = (bf16[256,256]{1,0:T(8,128)(2,1)S(1)}, bf16[256,256]{1,0:T(8,128)(2,1)}, u32[]{:S(2)}) copy-start(bf16[256,256]{1,0:T(8,128)(2,1)} %mixer_ref.1) | copy-start | bytes 393220
  40.9 2.6 %collective-permute-start = (f32[4,168,128]{2,1,0:T(8,128)S(1)}, f32[4,168,128]{2,1,0:T(8,128)S(1)}, u32[]{:S(2)}, u32[]{:S(2)}) collective-permute-start(f32[4,168,128]{2,1,0:T(8,128)S(1)} %dynamic-slice_bitcast_fusion), channel_id=1, source_target_pairs={{0,8},{8,0},{1,9},{9,1},{2,10},{10,2},{3,11},{11,3},{4,12},{12,4},... | collective-permute-start | bytes 1032200 | tf_op jit(solution)/shard_map/ppermute | solution.py:136
  44.6 11.8 %collective-permute-start.1 = (f32[168,128]{1,0:T(8,128)S(1)}, f32[168,128]{1,0:T(8,128)S(1)}, u32[]{:S(2)}, u32[]{:S(2)}) collective-permute-start(f32[168,128]{1,0:T(8,128)S(1)} %get-tuple-element.36), channel_id=1, source_target_pairs={{0,32},{32,0},{64,96},{96,64},{1,33},{33,1},{65,97},{97,65},{2,34}... | collective-permute-start | bytes 258056 | tf_op jit(solution)/shard_map/ppermute | solution.py:136
  46.3 10.1 %collective-permute-start.2 = (f32[168,128]{1,0:T(8,128)S(1)}, f32[168,128]{1,0:T(8,128)S(1)}, u32[]{:S(2)}, u32[]{:S(2)}) collective-permute-start(f32[168,128]{1,0:T(8,128)S(1)} %get-tuple-element.35), channel_id=1, source_target_pairs={{0,64},{32,96},{64,0},{96,32},{1,65},{33,97},{65,1},{97,33},{2,66}... | collective-permute-start | bytes 258056 | tf_op jit(solution)/shard_map/ppermute | solution.py:136
  49.6 6.8 %collective-permute-start.3 = (f32[168,128]{1,0:T(8,128)S(1)}, f32[168,128]{1,0:T(8,128)S(1)}, u32[]{:S(2)}, u32[]{:S(2)}) collective-permute-start(f32[168,128]{1,0:T(8,128)S(1)} %get-tuple-element.34), channel_id=1, source_target_pairs={{0,96},{32,64},{64,32},{96,0},{1,97},{33,65},{65,33},{97,1},{2,98}... | collective-permute-start | bytes 258056 | tf_op jit(solution)/shard_map/ppermute | solution.py:136
  54.4 2.0 %copy-start.1 = (bf16[8,4,32,2048]{3,2,1,0:T(8,128)(2,1)}, bf16[8,4,32,2048]{3,2,1,0:T(8,128)(2,1)S(1)}, u32[]{:S(2)}) copy-start(bf16[8,4,32,2048]{3,2,1,0:T(8,128)(2,1)S(1)} %get-tuple-element.30) | copy-start | bytes 12582916
  56.5 4.3 %collective-permute-start.4 = (f32[168,128]{1,0:T(8,128)S(1)}, f32[168,128]{1,0:T(8,128)S(1)}, u32[]{:S(2)}, u32[]{:S(2)}) collective-permute-start(f32[168,128]{1,0:T(8,128)S(1)} %fusion), channel_id=1, source_target_pairs={{0,2},{2,0},{4,6},{6,4},{1,3},{3,1},{5,7},{7,5},{8,10},{10,8},{12,... | collective-permute-start | bytes 258056 | tf_op jit(solution)/shard_map/ppermute | solution.py:136
  58.3 5.5 %collective-permute-start.5 = (f32[168,128]{1,0:T(8,128)S(1)}, f32[168,128]{1,0:T(8,128)S(1)}, u32[]{:S(2)}, u32[]{:S(2)}) collective-permute-start(f32[168,128]{1,0:T(8,128)S(1)} %fusion), channel_id=1, source_target_pairs={{0,4},{2,6},{4,0},{6,2},{1,5},{3,7},{5,1},{7,3},{8,12},{10,14},{12... | collective-permute-start | bytes 258056 | tf_op jit(solution)/shard_map/ppermute | solution.py:136
  60.6 5.5 %collective-permute-start.6 = (f32[168,128]{1,0:T(8,128)S(1)}, f32[168,128]{1,0:T(8,128)S(1)}, u32[]{:S(2)}, u32[]{:S(2)}) collective-permute-start(f32[168,128]{1,0:T(8,128)S(1)} %fusion), channel_id=1, source_target_pairs={{0,6},{2,4},{4,2},{6,0},{1,7},{3,5},{5,3},{7,1},{8,14},{10,12},{12... | collective-permute-start | bytes 258056 | tf_op jit(solution)/shard_map/ppermute | solution.py:136
  66.1 6.4 %copy-start.12 = (f32[168,128]{1,0:T(8,128)}, f32[168,128]{1,0:T(8,128)S(1)}, u32[]{:S(2)}) copy-start(f32[168,128]{1,0:T(8,128)S(1)} %add_add_fusion.1) | copy-start | bytes 258052
  66.1 4.9 %collective-permute-start.7 = (f32[168,128]{1,0:T(8,128)S(1)}, f32[168,128]{1,0:T(8,128)S(1)}, u32[]{:S(2)}, u32[]{:S(2)}) collective-permute-start(f32[168,128]{1,0:T(8,128)S(1)} %add_add_fusion.1), channel_id=1, source_target_pairs={{0,1},{1,0},{16,17},{17,16},{2,3},{3,2},{18,19},{19,18},{4,5},{5,4... | collective-permute-start | bytes 258056 | tf_op jit(solution)/shard_map/ppermute | solution.py:136
  69.0 3.6 %collective-permute-start.8 = (f32[168,128]{1,0:T(8,128)S(1)}, f32[168,128]{1,0:T(8,128)S(1)}, u32[]{:S(2)}, u32[]{:S(2)}) collective-permute-start(f32[168,128]{1,0:T(8,128)S(1)} %add_add_fusion.1), channel_id=1, source_target_pairs={{0,16},{1,17},{16,0},{17,1},{2,18},{3,19},{18,2},{19,3},{4,20},{5,... | collective-permute-start | bytes 258056 | tf_op jit(solution)/shard_map/ppermute | solution.py:136
  69.3 5.0 %collective-permute-start.9 = (f32[168,128]{1,0:T(8,128)S(1)}, f32[168,128]{1,0:T(8,128)}, u32[]{:S(2)}, u32[]{:S(2)}) collective-permute-start(f32[168,128]{1,0:T(8,128)S(1)} %add_add_fusion.1), channel_id=1, source_target_pairs={{0,17},{1,16},{16,1},{17,0},{2,19},{3,18},{18,3},{19,2},{4,21},{5,... | collective-permute-start | bytes 258056 | tf_op jit(solution)/shard_map/ppermute | solution.py:136
  71.1 1.5 copy-start.13
  72.6 0.6 copy-start.14
  74.3 21.0 %copy-start.3 = (bf16[512,2048]{1,0:T(8,128)(2,1)S(1)}, bf16[512,2048]{1,0:T(8,128)(2,1)}, u32[]{:S(2)}) copy-start(bf16[512,2048]{1,0:T(8,128)(2,1)} %copy-done.2) | copy-start | bytes 6291460
  74.3 63.4 %all-to-all-start.2 = ((bf16[8,4,32,2048]{3,2,1,0:T(8,128)(2,1)}), bf16[8,4,32,2048]{3,2,1,0:T(8,128)(2,1)}, u32[]{:S(2)}, u32[]{:S(2)}) async-start(bf16[8,4,32,2048]{3,2,1,0:T(8,128)(2,1)} %copy-done.1), calls=%async_computation.2 | async-start | bytes 8388608 | tf_op jit(solution)/shard_map/all_to_all | solution.py:425
  79.0 58.7 %copy-start.7 = (s32[4,16384]{1,0:T(4,128)S(1)}, s32[4,16384]{1,0:T(4,128)}, u32[]{:S(2)}) copy-start(s32[4,16384]{1,0:T(4,128)} %refs_8_.1) | copy-start | bytes 786436
  80.1 4.2 %collective-permute-start.10 = (f32[168,128]{1,0:T(8,128)S(1)}, f32[168,128]{1,0:T(8,128)S(1)}, u32[]{:S(2)}, u32[]{:S(2)}) collective-permute-start(f32[168,128]{1,0:T(8,128)S(1)} %add_add_fusion), channel_id=1, source_target_pairs={{0,32},{32,0},{64,96},{96,64},{1,33},{33,1},{65,97},{97,65},{2,34}... | collective-permute-start | bytes 258056 | tf_op jit(solution)/shard_map/ppermute | solution.py:136
  80.2 6.9 %collective-permute-start.11 = (f32[168,128]{1,0:T(8,128)S(1)}, f32[168,128]{1,0:T(8,128)S(1)}, u32[]{:S(2)}, u32[]{:S(2)}) collective-permute-start(f32[168,128]{1,0:T(8,128)S(1)} %add_add_fusion), channel_id=1, source_target_pairs={{0,64},{32,96},{64,0},{96,32},{1,65},{33,97},{65,1},{97,33},{2,66}... | collective-permute-start | bytes 258056 | tf_op jit(solution)/shard_map/ppermute | solution.py:136
  84.3 4.5 %collective-permute-start.12 = (f32[168,128]{1,0:T(8,128)S(1)}, f32[168,128]{1,0:T(8,128)S(1)}, u32[]{:S(2)}, u32[]{:S(2)}) collective-permute-start(f32[168,128]{1,0:T(8,128)S(1)} %add_add_fusion), channel_id=1, source_target_pairs={{0,96},{32,64},{64,32},{96,0},{1,97},{33,65},{65,33},{97,1},{2,98}... | collective-permute-start | bytes 258056 | tf_op jit(solution)/shard_map/ppermute | solution.py:136
  88.9 6.4 %collective-permute-start.13 = (f32[4,168,128]{2,1,0:T(8,128)S(1)}, f32[4,168,128]{2,1,0:T(8,128)S(1)}, u32[]{:S(2)}, u32[]{:S(2)}) collective-permute-start(f32[4,168,128]{2,1,0:T(8,128)S(1)} %pad_maximum_fusion.1.refs_1_), channel_id=1, source_target_pairs={{0,8},{8,0},{1,9},{9,1},{2,10},{10,2},{3,11},{11,3},{4,12},{12,4},... | collective-permute-start | bytes 1032200 | tf_op jit(solution)/shard_map/ppermute | solution.py:136
  116.0 11.8 %collective-permute-start.14 = (f32[1,2048]{1,0:T(1,128)S(1)}, f32[1,2048]{1,0:T(1,128)S(1)}, u32[]{:S(2)}, u32[]{:S(2)}) collective-permute-start(f32[1,2048]{1,0:T(1,128)S(1)} %solve_continuation.1), channel_id=1, source_target_pairs={{0,1},{1,0},{2,3},{3,2},{4,5},{5,4},{6,7},{7,6},{8,9},{9,8},{10,11... | collective-permute-start | bytes 24584 | tf_op jit(solution)/shard_map/ppermute | solution.py:136
  127.8 5.7 %collective-permute-start.15 = (f32[2,2048]{1,0:T(2,128)S(1)}, f32[2,2048]{1,0:T(2,128)S(1)}, u32[]{:S(2)}, u32[]{:S(2)}) collective-permute-start(f32[2,2048]{1,0:T(2,128)S(1)} %pad_maximum_fusion.2.refs_0_), channel_id=1, source_target_pairs={{0,2},{2,0},{4,6},{6,4},{1,3},{3,1},{5,7},{7,5},{8,10},{10,8},{12,... | collective-permute-start | bytes 49160 | tf_op jit(solution)/shard_map/ppermute | solution.py:136
  127.9 9.8 %collective-permute-start.16 = (f32[2,2048]{1,0:T(2,128)S(1)}, f32[2,2048]{1,0:T(2,128)S(1)}, u32[]{:S(2)}, u32[]{:S(2)}) collective-permute-start(f32[2,2048]{1,0:T(2,128)S(1)} %pad_maximum_fusion.2.refs_0_), channel_id=1, source_target_pairs={{0,4},{2,6},{4,0},{6,2},{1,5},{3,7},{5,1},{7,3},{8,12},{10,14},{12... | collective-permute-start | bytes 49160 | tf_op jit(solution)/shard_map/ppermute | solution.py:136
  130.8 6.9 %collective-permute-start.17 = (f32[2,2048]{1,0:T(2,128)S(1)}, f32[2,2048]{1,0:T(2,128)S(1)}, u32[]{:S(2)}, u32[]{:S(2)}) collective-permute-start(f32[2,2048]{1,0:T(2,128)S(1)} %pad_maximum_fusion.2.refs_0_), channel_id=1, source_target_pairs={{0,6},{2,4},{4,2},{6,0},{1,7},{3,5},{5,3},{7,1},{8,14},{10,12},{12... | collective-permute-start | bytes 49160 | tf_op jit(solution)/shard_map/ppermute | solution.py:136
  137.7 1.0 copy-start.8

commit v4 on v3

--- a/solution.py
+++ b/solution.py
@@ -15,6 +15,8 @@
 TILE = 512
 INCREMENT_TILE = 512
 DATE_TILE = 2048
+STRIKE_BITS = 7
+STRIKE_ROWS = 1 << STRIKE_BITS
 PATH_AXES = ("z", "ylo", "core")
 STOCK_AXES = ("x", "yhi")
 ALL_AXES = PATH_AXES + STOCK_AXES
@@ -52,7 +54,7 @@
 
 
 def gram_kernel(slab_ref, moved_ref, table_ref, weight_ref, bias_ref, payoff_ref, fit_ref,
-                basis_ref, sums_ref, gram_ref, moment_ref):
+                basis_ref, kept_ref, sent_ref, gram_ref, moment_ref, sums_ref):
     step = pl.program_id(0)
     tile = moved_ref[...].reshape(256, TILE)
     loads = table_ref[...].reshape(256, LANES)[:, :32]
@@ -92,6 +94,9 @@
             sums_ref[MOMENT_ROW + 8 * i:MOMENT_ROW + 8 * i + 8, :] = moment_ref[
                 :8, i * BLOCK:(i + 1) * BLOCK
             ]
+        half = 4 * PIECE
+        kept_ref[...] = sums_ref[pl.ds(pl.multiple_of(slab_ref[1] * half, 8), half), :]
+        sent_ref[...] = sums_ref[pl.ds(pl.multiple_of((1 - slab_ref[1]) * half, 8), half), :]
 
 
 def regression_sums(slab, moved, weights, bias, payoff, fit, slab_part):
@@ -105,7 +110,8 @@
         gram_kernel,
         out_shape=(
             jax.ShapeDtypeStruct((512, slab_part), bf16),
-            jax.ShapeDtypeStruct((SUM_ROWS, LANES), f32),
+            jax.ShapeDtypeStruct((SUM_ROWS // 2, LANES), f32),
+            jax.ShapeDtypeStruct((SUM_ROWS // 2, LANES), f32),
         ),
         grid_spec=pltpu.PrefetchScalarGridSpec(
             num_scalar_prefetch=1,
@@ -120,9 +126,14 @@
             ],
             out_specs=(
                 pl.BlockSpec((512, TILE), lambda i, s: (0, i)),
-                pl.BlockSpec((SUM_ROWS, LANES), lambda i, s: (0, 0)),
+                pl.BlockSpec((SUM_ROWS // 2, LANES), lambda i, s: (0, 0)),
+                pl.BlockSpec((SUM_ROWS // 2, LANES), lambda i, s: (0, 0)),
             ),
-            scratch_shapes=[pltpu.VMEM((512, 512), f32), pltpu.VMEM((16, 512), f32)],
+            scratch_shapes=[
+                pltpu.VMEM((512, 512), f32),
+                pltpu.VMEM((16, 512), f32),
+                pltpu.VMEM((SUM_ROWS, LANES), f32),
+            ],
         ),
         compiler_params=pltpu.CompilerParams(vmem_limit_bytes=40 << 20),
         name="regression_sums",
@@ -137,23 +148,19 @@
     return received
 
 
-def all_device_sum(sums, beside):
-    core = lax.axis_index("core")
+def sum_over_cores_and_z(kept, sent, beside):
     z = lax.axis_index("z")
-    halves = sums.reshape(2, 4, PIECE, LANES)
-    mine = lax.dynamic_index_in_dim(halves, core, 0, False)
-    other = lax.dynamic_index_in_dim(halves, 1 - core, 0, False)
-    mine = mine + exchange_with_others(other, "core", 2)[0]
+    mine = (kept + exchange_with_others(sent, "core", 2)[0]).reshape(4, PIECE, LANES)
 
     def piece_of(flip):
         return lax.dynamic_index_in_dim(mine, z ^ flip, 0, False)
 
     parts, beside = lax.optimization_barrier((exchange_with_others(None, "z", 4, piece_of), beside))
-    share = (piece_of(0) + parts[0]) + (parts[1] + parts[2])
-    parts = exchange_with_others(share, "x", 4)
-    share = (share + parts[0]) + (parts[1] + parts[2])
-    parts = exchange_with_others(share, ("ylo", "yhi"), 4)
-    parts, beside = lax.optimization_barrier((parts, beside))
+    return (piece_of(0) + parts[0]) + (parts[1] + parts[2]), beside
+
+
+def sum_over_others(share, axes, beside):
+    parts, beside = lax.optimization_barrier((exchange_with_others(share, axes, 4), beside))
     return (share + parts[0]) + (parts[1] + parts[2]), beside
 
 
@@ -285,69 +292,75 @@
     )(at, near, far, basis)
 
 
-def increments_kernel(moved_ref, mixer_ref, basket_ref, sent_ref, weights_ref):
-    adjoint = moved_ref[...].reshape(256, INCREMENT_TILE).astype(f32)
-    for date in range(STEPS - 1, -1, -1):
-        gain = TIME_STEP * jnp.dot(mixer_ref[...], adjoint.astype(bf16), preferred_element_type=f32)
-        sent_ref[:, date] = gain.astype(bf16).reshape(8, 32, INCREMENT_TILE)
-        if date:
-            adjoint = adjoint + gain
-
-    @pl.when(pl.program_id(0) == 0)
-    def _():
-        lane = lax.broadcasted_iota(jnp.int32, (256, LANES), 1)
-        weight = jnp.broadcast_to(basket_ref[...], (256, LANES))
-        table = weight
-        for later in range(1, STEPS):
-            gain = sum(
-                jnp.dot(mixer_ref[...], part, preferred_element_type=f32)
-                for part in three_terms(weight)
+def increments_kernel(moved_ref, mixer_ref, basket_ref, sent_ref, weights_ref, buffer_ref, copied):
+    copies = []
+    for tile in range(moved_ref.shape[2] // INCREMENT_TILE):
+        span = pl.ds(tile * INCREMENT_TILE, INCREMENT_TILE)
+        adjoint = moved_ref[:, :, span].reshape(256, INCREMENT_TILE).astype(f32)
+        for date in range(STEPS - 1, -1, -1):
+            gain = TIME_STEP * jnp.dot(
+                mixer_ref[...], adjoint.astype(bf16), preferred_element_type=f32
             )
-            weight = weight + TIME_STEP * gain
-            table = jnp.where(lane == later, weight, table)
-        weights_ref[...] = table
+            buffer_ref[tile, :, date] = gain.astype(bf16).reshape(8, 32, INCREMENT_TILE)
+            if date:
+                adjoint = adjoint + gain
+        copies.append(
+            pltpu.make_async_copy(buffer_ref.at[tile], sent_ref.at[:, :, :, span], copied.at[tile])
+        )
+        copies[-1].start()
+    lane = lax.broadcasted_iota(jnp.int32, (256, LANES), 1)
+    weight = jnp.broadcast_to(basket_ref[...], (256, LANES))
+    table = weight
+    for later in range(1, STEPS):
+        gain = sum(
+            jnp.dot(mixer_ref[...], part, preferred_element_type=f32) for part in three_terms(weight)
+        )
+        weight = weight + TIME_STEP * gain
+        table = jnp.where(lane == later, weight, table)
+    weights_ref[...] = table
+    for copy in copies:
+        copy.wait()
 
 
 def increments(moved, mixer, basket, slab_part):
+    tiles = slab_part // INCREMENT_TILE
     return pl.pallas_call(
         increments_kernel,
         out_shape=(
-            jax.ShapeDtypeStruct((8, STEPS, 32, slab_part), bf16),
+            pltpu.HBM((8, STEPS, 32, slab_part), bf16),
             jax.ShapeDtypeStruct((256, LANES), f32),
         ),
-        grid=(slab_part // INCREMENT_TILE,),
-        in_specs=[
-            pl.BlockSpec((8, 32, INCREMENT_TILE), lambda i: (0, 0, i)),
-            pl.BlockSpec((256, 256), lambda i: (0, 0)),
-            pl.BlockSpec((256, 1), lambda i: (0, 0)),
+        out_specs=(
+            pl.BlockSpec(memory_space=pltpu.HBM),
+            pl.BlockSpec(memory_space=pltpu.VMEM),
+        ),
+        scratch_shapes=[
+            pltpu.VMEM((tiles, 8, STEPS, 32, INCREMENT_TILE), bf16),
+            pltpu.SemaphoreType.DMA((tiles,)),
         ],
-        out_specs=(
-            pl.BlockSpec((8, STEPS, 32, INCREMENT_TILE), lambda i: (0, 0, 0, i)),
-            pl.BlockSpec((256, LANES), lambda i: (0, 0)),
-        ),
         compiler_params=pltpu.CompilerParams(vmem_limit_bytes=40 << 20),
         name="increments",
     )(moved, mixer, basket)
 
 
 def surface_kernel(slab_ref, *refs):
-    continuation_refs = refs[:4]
+    continuation_refs = refs[:2]
     (cotangent_ref, gain_ref, shock_ref, weight_ref, exercise_ref, bucket_ref, delta_ref, share_ref,
-     continuation_ref, total_ref) = refs[4:]
+     continuation_ref, total_ref) = refs[2:]
     step = pl.program_id(0)
 
     @pl.when(step == 0)
     def _():
         for flip in range(8):
-            continuation_ref[pl.ds(slab_ref[0] ^ flip, 1), :] = continuation_refs[flip // 2][
-                flip % 2:flip % 2 + 1, :
+            continuation_ref[pl.ds(slab_ref[0] ^ flip, 1), :] = continuation_refs[flip % 2][
+                flip // 2:flip // 2 + 1, :
             ]
         total_ref[...] = jnp.zeros(total_ref.shape, f32)
 
     continuation = continuation_ref[pl.ds(step, 1), :]
     held = [exercise_ref[date:date + 1, :].astype(f32) * continuation for date in range(STEPS)]
     weights = [weight_ref[:, later:later + 1] for later in range(STEPS)]
-    strikes = lax.broadcasted_iota(jnp.int32, (NK, DATE_TILE), 0)
+    strikes = lax.broadcasted_iota(jnp.int32, (STRIKE_ROWS, DATE_TILE), 0).astype(f32).astype(bf16)
     base = cotangent_ref[...].astype(f32)
     total = total_ref[...]
     for date in range(STEPS - 1, -1, -1):
@@ -355,8 +368,14 @@
         adjoint = base
         for later in range(STEPS - date):
             adjoint = adjoint + held[date + later] * weights[later]
-        terms = (adjoint * shock_ref[date].astype(f32)).astype(bf16)
-        chosen = jnp.where(strikes == bucket_ref[date:date + 1, :], 1.0, 0.0).astype(bf16)
+        terms = (adjoint * shock_ref[date].astype(f32)).astype(bf16).astype(f32)
+        bucket = bucket_ref[date:date + 1, :]
+        column = (bucket & (STRIKE_ROWS - 1)).astype(f32).astype(bf16)
+        chosen = jnp.where(strikes == column, jnp.bfloat16(1), jnp.bfloat16(0))
+        group = bucket >> STRIKE_BITS
+        terms = jnp.concatenate(
+            [jnp.where(group == g, terms, 0.0).astype(bf16) for g in range(NK // STRIKE_ROWS)], axis=0
+        )
         total = total + lax.dot_general(
             chosen, terms, (((1,), (1,)), ((), ())), preferred_element_type=f32
         )
@@ -365,14 +384,18 @@
 
     @pl.when(step == pl.num_programs(0) - 1)
     def _():
-        grouped = total.reshape(16, 16, 32)
-        for q in range(4):
-            share_ref[:, :, 32 * q:32 * q + 32] = grouped[:, 4 * q:4 * q + 4, :]
+        owners = STRIKE_ROWS // 16
+        for g in range(NK // STRIKE_ROWS):
+            grouped = total[:, 32 * g:32 * g + 32].reshape(owners, 16, 32)
+            for q in range(4):
+                share_ref[g * owners:(g + 1) * owners, :, 32 * q:32 * q + 32] = grouped[
+                    :, 4 * q:4 * q + 4, :
+                ]
 
 
 def surface_and_delta(slab, continuations, cotangent, gains, shocks, weights, exercise, bucket):
     local_paths = cotangent.shape[1]
-    whole = pl.BlockSpec((2, DATE_TILE), lambda i, s: (0, 0))
+    whole = pl.BlockSpec((4, DATE_TILE), lambda i, s: (0, 0))
     return pl.pallas_call(
         surface_kernel,
         out_shape=(
@@ -382,7 +405,7 @@
         grid_spec=pltpu.PrefetchScalarGridSpec(
             num_scalar_prefetch=1,
             grid=(local_paths // DATE_TILE,),
-            in_specs=[whole] * 4 + [
+            in_specs=[whole] * 2 + [
                 pl.BlockSpec((32, DATE_TILE), lambda i, s: (0, i)),
                 pl.BlockSpec((1, STEPS, 32, DATE_TILE), lambda i, s: (i, 0, 0, 0)),
                 pl.BlockSpec((STEPS, 32, DATE_TILE), lambda i, s: (0, 0, i)),
@@ -394,7 +417,7 @@
                 pl.BlockSpec((32, DATE_TILE), lambda i, s: (0, i)),
                 pl.BlockSpec((16, 4, LANES), lambda i, s: (0, 0, 0)),
             ),
-            scratch_shapes=[pltpu.VMEM((8, DATE_TILE), f32), pltpu.VMEM((NK, 32), f32)],
+            scratch_shapes=[pltpu.VMEM((8, DATE_TILE), f32), pltpu.VMEM((STRIKE_ROWS, 32 * (NK // STRIKE_ROWS)), f32)],
         ),
         compiler_params=pltpu.CompilerParams(vmem_limit_bytes=48 << 20),
         name="surface_and_delta",
@@ -414,19 +437,24 @@
         jnp.concatenate([pieces, table], axis=2), STOCK_AXES, 0, 0, tiled=True
     )
     slabs = jnp.moveaxis(cotangent.reshape(32, 8, slab_part), 1, 0)
-    slabs, moved_prices = lax.optimization_barrier((slabs, moved_prices))
+    small = (left_terms(basis_w, 0), basis_bias[:, None], payoff[None, :], in_fit[None, :],
+             basket[:, None])
+    slabs, moved_prices, small = lax.optimization_barrier((slabs, moved_prices, small))
+    weight_terms, bias, payoff, in_fit, basket = small
     moved = lax.all_to_all(slabs, STOCK_AXES, 0, 0, tiled=True)
-    basis, sums = regression_sums(
-        slab, moved_prices, left_terms(basis_w, 0), basis_bias[:, None], payoff[None, :],
-        in_fit[None, :], slab_part,
-    )
-    sent, weights = increments(moved, corr_gen, basket[:, None], slab_part)
-    share, sent = all_device_sum(sums, sent)
+    place = jnp.stack([slab[0], lax.axis_index("core").astype(jnp.int32)])
+    basis, kept, other = regression_sums(
+        place, moved_prices, weight_terms, bias, payoff, in_fit, slab_part
+    )
+    share, moved = sum_over_cores_and_z(kept, other, moved)
+    sent, weights = increments(moved, corr_gen, basket, slab_part)
+    share, sent = sum_over_others(share, "x", sent)
+    share, sent = sum_over_others(share, ("ylo", "yhi"), sent)
     gains = lax.all_to_all(sent, STOCK_AXES, 0, 0, tiled=True)
     near, far = gathered_sum(share)
     continuation = solve_continuation(near, far, basis, path_count)
-    pair = jnp.concatenate([continuation] + exchange_with_others(continuation, "yhi", 2), axis=0)
-    continuations = [pair] + exchange_with_others(pair, "x", 4)
+    column = jnp.concatenate([continuation] + exchange_with_others(continuation, "x", 4), axis=0)
+    continuations = [column] + exchange_with_others(column, "yhi", 2)
     delta, surface = surface_and_delta(
         slab, continuations, cotangent, gains, shocks, weights, exercise, bucket
     )

time: 166 us -> 164 us (0.988)
  waiting for transfers between devices: 46.1 us -> 55.2 us
  starting transfers between devices: 46.8 us -> 43.3 us
  local copies, waits for them, and re-layouts: 12.5 us -> 9.62 us
  Pallas kernels: 43.1 us -> 40.5 us
    ppermute x18, waiting for transfers between devices: 31.1 us -> 40.9 us  [exchange_with_others(): lax.ppermute(sent, axes, [(i, i ^ flip) for i in range(count)])]
    ppermute x18, starting transfers between devices: 30.4 us -> 26.9 us  [exchange_with_others(): lax.ppermute(sent, axes, [(i, i ^ flip) for i in range(count)])]
    pallas_call x1, Pallas kernels: 13.4 us -> 10.3 us  [surface_and_delta(): pl.pallas_call(surface_kernel, out_shape=(jax.ShapeDtypeStruct((32, local...]
    unnamed x36 -> x30, local copies, waits for them, and re-layouts: 8.21 us -> 6.16 us
  transfers between devices with their start and end apart: 21 -> 21, of which waited for: 13 -> 14; matrix products, arithmetic and copies ran while one was open for 3% -> 2% of each run, Pallas kernels for 18% -> 18%
where the time goes in v4:
time: 164 us
  waiting for transfers between devices  55.2 us (34%)
  starting transfers between devices  43.3 us (26%)
  Pallas kernels  40.5 us (25%)
  blocking collectives  11.9 us (7%)
  local copies, waits for them, and re-layouts  9.62 us (6%)
  other arithmetic  2.47 us (2%)
    ppermute x18, waiting for transfers between devices, exchange_with_others(): lax.ppermute(sent, axes, [(i, i ^ flip) for i in range(count)])  40.9 us
    ppermute x18, starting transfers between devices, exchange_with_others(): lax.ppermute(sent, axes, [(i, i ^ flip) for i in range(count)])  26.9 us
    pallas_call x1, Pallas kernels, solve_continuation(): pl.pallas_call(lambda *refs: solve_kernel(*refs, scale=1.0 / path_count),...  20.7 us
    all_to_all x1, waiting for transfers between devices, per_device(): lax.all_to_all(jnp.concatenate([pieces, table], axis=2), STOCK_AXES, 0, 0...  14.3 us
    all_to_all x1, blocking collectives, per_device(): surface = lax.all_to_all(surface, PATH_AXES, 0, 0, tiled=True)  11.9 us
    pallas_call x1, Pallas kernels, surface_and_delta(): pl.pallas_call(surface_kernel, out_shape=(jax.ShapeDtypeStruct((32, local...  10.3 us
    all_to_all x1, starting transfers between devices, per_device(): lax.all_to_all(jnp.concatenate([pieces, table], axis=2), STOCK_AXES, 0, 0...  7.61 us
    unnamed x30, local copies, waits for them, and re-layouts  6.16 us
  transfers between devices with their start and end apart: 21, of which 14 were waited for; matrix products, arithmetic and copies ran while one was open for 2% of the time, Pallas kernels for 18%

profile of v4, /device:TPU:1, one launch (start us, length us, event | category | flops | bytes accessed | tf_op | source)
XLA Modules:
  0.0 163.8 jit_solution(277688038679103909)
XLA Ops:
  0.6 1.3 copy.27
  2.0 0.0 copy-start.10
  2.0 0.0 copy-start
  2.0 1.1 pad_maximum_fusion
  3.1 7.6 %all-to-all-start = ((bf16[8,32,2176]{2,1,0:T(8,128)(2,1)}), bf16[8,32,2176]{2,1,0:T(8,128)(2,1)S(1)}, u32[]{:S(2)}, u32[]{:S(2)}) async-start(bf16[8,32,2176]{2,1,0:T(8,128)(2,1)} %pad_maximum_fusion), calls=%async_computation | async-start | bytes 2228224 | tf_op jit(solution)/shard_map/all_to_all | solution.py:436
  10.8 0.0 copy-start.13
  10.8 1.1 copy.28
  12.0 0.7 copy-done.4
  12.7 14.3 %all-to-all-done.moved_ref.table_ref = bf16[8,32,2176]{2,1,0:T(8,128)(2,1)S(1)} async-done(((bf16[8,32,2176]{2,1,0:T(8,128)(2,1)}), bf16[8,32,2176]{2,1,0:T(8,128)(2,1)S(1)}, u32[]{:S(2)}, u32[]{:S(2)}) %all-to-all-start) | async-done | bytes 1114144 | tf_op jit(solution)/shard_map/all_to_all | solution.py:436
  26.9 4.2 %all-to-all-start.1 = ((bf16[8,32,2048]{2,1,0:T(8,128)(2,1)}), bf16[8,32,2048]{2,1,0:T(8,128)(2,1)S(1)}, u32[]{:S(2)}, u32[]{:S(2)}) async-start(bf16[8,32,2048]{2,1,0:T(8,128)(2,1)} %bitcast.39), calls=%async_computation.1 | async-start | bytes 2097152 | tf_op jit(solution)/shard_map/all_to_all | solution.py:444
  31.1 0.1 pad_add_fusion.1.slab_ref
  31.2 0.1 copy.20.bias_ref
  31.4 0.9 copy-done.5
  32.3 0.8 copy-done.9
  33.2 5.6 %regression_sums.1 = (bf16[512,2048]{1,0:T(8,128)(2,1)S(1)}, f32[672,128]{1,0:T(8,128)S(1)}, f32[672,128]{1,0:T(8,128)}) custom-call(s32[2]{0:T(128)S(1)} %pad_add_fusion.1.slab_ref, bf16[8,32,2176]{2,1,0:T(8,128)(2,1)S(1)} %all-to-all-done.moved_ref.table_ref, bf16[8,32,2176]{2,1,0:T(8,128)(2,1)S(1)} %all-to-all-done.moved_ref.table_ref, ...), custom_call_target="tpu_custom_call" | custom-call | tf_op jit(solution)/shard_map/regression_sums/pallas_call | solution.py:109
  38.8 1.3 copy-done.1
  40.1 0.8 copy-done.3
  40.8 1.2 collective-permute-start
  42.1 1.5 collective-permute-done
  43.6 1.0 add.49
  44.6 1.7 %collective-permute-start.1 = (f32[168,128]{1,0:T(8,128)S(1)}, f32[168,128]{1,0:T(8,128)S(1)}, u32[]{:S(2)}, u32[]{:S(2)}) collective-permute-start(f32[168,128]{1,0:T(8,128)S(1)} %get-tuple-element.56), channel_id=1, source_target_pairs={{0,32},{32,0},{64,96},{96,64},{1,33},{33,1},{65,97},{97,65},{2,34}... | collective-permute-start | bytes 258056 | tf_op jit(solution)/shard_map/ppermute | solution.py:147
  46.3 3.3 %collective-permute-start.2 = (f32[168,128]{1,0:T(8,128)S(1)}, f32[168,128]{1,0:T(8,128)S(1)}, u32[]{:S(2)}, u32[]{:S(2)}) collective-permute-start(f32[168,128]{1,0:T(8,128)S(1)} %get-tuple-element.55), channel_id=1, source_target_pairs={{0,64},{32,96},{64,0},{96,32},{1,65},{33,97},{65,1},{97,33},{2,66}... | collective-permute-start | bytes 258056 | tf_op jit(solution)/shard_map/ppermute | solution.py:147
  49.6 0.0 collective-permute-start.3
  49.6 0.0 collective-permute-done.1
  49.6 4.1 %collective-permute-done.2 = f32[168,128]{1,0:T(8,128)S(1)} collective-permute-done((f32[168,128]{1,0:T(8,128)S(1)}, f32[168,128]{1,0:T(8,128)S(1)}, u32[]{:S(2)}, u32[]{:S(2)}) %collective-permute-start.2) | collective-permute-done | bytes 86048 | tf_op jit(solution)/shard_map/ppermute | solution.py:147
  53.8 2.2 %collective-permute-done.3 = f32[168,128]{1,0:T(8,128)S(1)} collective-permute-done((f32[168,128]{1,0:T(8,128)S(1)}, f32[168,128]{1,0:T(8,128)S(1)}, u32[]{:S(2)}, u32[]{:S(2)}) %collective-permute-start.3) | collective-permute-done | bytes 86048 | tf_op jit(solution)/shard_map/ppermute | solution.py:147
  56.0 1.8 %collective-permute-start.4 = (f32[168,128]{1,0:T(8,128)S(1)}, f32[168,128]{1,0:T(8,128)S(1)}, u32[]{:S(2)}, u32[]{:S(2)}) collective-permute-start(f32[168,128]{1,0:T(8,128)S(1)} %fusion), channel_id=1, source_target_pairs={{0,2},{2,0},{4,6},{6,4},{1,3},{3,1},{5,7},{7,5},{8,10},{10,8},{12,... | collective-permute-start | bytes 258056 | tf_op jit(solution)/shard_map/ppermute | solution.py:147
  57.8 2.4 %collective-permute-start.5 = (f32[168,128]{1,0:T(8,128)S(1)}, f32[168,128]{1,0:T(8,128)S(1)}, u32[]{:S(2)}, u32[]{:S(2)}) collective-permute-start(f32[168,128]{1,0:T(8,128)S(1)} %fusion), channel_id=1, source_target_pairs={{0,4},{2,6},{4,0},{6,2},{1,5},{3,7},{5,1},{7,3},{8,12},{10,14},{12... | collective-permute-start | bytes 258056 | tf_op jit(solution)/shard_map/ppermute | solution.py:147
  60.2 0.1 collective-permute-start.6
  60.3 0.1 copy.21.basket_ref
  60.5 3.8 %increments.1 = (bf16[8,4,32,2048]{3,2,1,0:T(8,128)(2,1)}, f32[256,128]{1,0:T(8,128)S(1)}) custom-call(bf16[8,32,2048]{2,1,0:T(8,128)(2,1)S(1)} %all-to-all-done.1.moved_ref, bf16[256,256]{1,0:T(8,128)(2,1)S(1)} %copy-done.8, f32[256,1]{1,0:T(8,128)S(1)} %copy.21.basket_ref), custom_call_target="tpu_custom_call" | custom-call | tf_op jit(solution)/shard_map/increments/pallas_call | solution.py:327
  64.3 0.0 collective-permute-done.5
  64.3 1.4 collective-permute-done.6
  65.7 2.8 %collective-permute-start.7 = (f32[168,128]{1,0:T(8,128)S(1)}, f32[168,128]{1,0:T(8,128)S(1)}, u32[]{:S(2)}, u32[]{:S(2)}) collective-permute-start(f32[168,128]{1,0:T(8,128)S(1)} %add_add_fusion.1), channel_id=1, source_target_pairs={{0,1},{1,0},{16,17},{17,16},{2,3},{3,2},{18,19},{19,18},{4,5},{5,4... | collective-permute-start | bytes 258056 | tf_op jit(solution)/shard_map/ppermute | solution.py:147
  68.5 0.4 collective-permute-start.8
  68.9 0.2 collective-permute-start.9
  69.0 1.6 collective-permute-done.7
  70.6 1.5 collective-permute-done.8
  72.1 1.5 collective-permute-done.9
  73.6 4.6 %all-to-all-start.2 = ((bf16[8,4,32,2048]{3,2,1,0:T(8,128)(2,1)}), bf16[8,4,32,2048]{3,2,1,0:T(8,128)(2,1)}, u32[]{:S(2)}, u32[]{:S(2)}) async-start(bf16[8,4,32,2048]{3,2,1,0:T(8,128)(2,1)} %get-tuple-element.50), calls=%async_computation.2 | async-start | bytes 8388608 | tf_op jit(solution)/shard_map/all_to_all | solution.py:453
  78.2 0.0 copy-start.6
  78.2 0.0 copy-start.7
  78.3 0.1 collective-permute-start.10
  78.3 1.7 %collective-permute-start.11 = (f32[168,128]{1,0:T(8,128)S(1)}, f32[168,128]{1,0:T(8,128)S(1)}, u32[]{:S(2)}, u32[]{:S(2)}) collective-permute-start(f32[168,128]{1,0:T(8,128)S(1)} %add_add_fusion), channel_id=1, source_target_pairs={{0,64},{32,96},{64,0},{96,32},{1,65},{33,97},{65,1},{97,33},{2,66}... | collective-permute-start | bytes 258056 | tf_op jit(solution)/shard_map/ppermute | solution.py:147
  80.0 2.2 %collective-permute-start.12 = (f32[168,128]{1,0:T(8,128)S(1)}, f32[168,128]{1,0:T(8,128)S(1)}, u32[]{:S(2)}, u32[]{:S(2)}) collective-permute-start(f32[168,128]{1,0:T(8,128)S(1)} %add_add_fusion), channel_id=1, source_target_pairs={{0,96},{32,64},{64,32},{96,0},{1,97},{33,65},{65,33},{97,1},{2,98}... | collective-permute-start | bytes 258056 | tf_op jit(solution)/shard_map/ppermute | solution.py:147
  82.2 1.1 collective-permute-done.11
  83.3 1.3 collective-permute-done.12
  84.6 4.8 %collective-permute-start.13 = (f32[4,168,128]{2,1,0:T(8,128)S(1)}, f32[4,168,128]{2,1,0:T(8,128)S(1)}, u32[]{:S(2)}, u32[]{:S(2)}) collective-permute-start(f32[4,168,128]{2,1,0:T(8,128)S(1)} %pad_maximum_fusion.1.refs_1_), channel_id=1, source_target_pairs={{0,8},{8,0},{1,9},{9,1},{2,10},{10,2},{3,11},{11,3},{4,12},{12,4},... | collective-permute-start | bytes 1032200 | tf_op jit(solution)/shard_map/ppermute | solution.py:147
  89.4 0.1 pad_add_fusion.refs_0_
  89.5 1.2 collective-permute-done.13.refs_2_
  90.7 1.6 copy-done.2
  92.3 20.7 %solve_continuation.1 = f32[1,2048]{1,0:T(1,128)S(1)} custom-call(s32[2]{0:T(128)S(1)} %pad_add_fusion.refs_0_, f32[4,168,128]{2,1,0:T(8,128)S(1)} %pad_maximum_fusion.1.refs_1_, f32[4,168,128]{2,1,0:T(8,128)S(1)} %collective-permute-done.13.refs_2_, bf16[512,2048]{1,0:T(8,128)(2,1)S(1)} %copy-done.2), custom_call_target="tpu_custom_call" | custom-call | tf_op jit(solution)/shard_map/solve_continuation/pallas_call | solution.py:277
  113.1 1.7 %collective-permute-start.14 = (f32[1,2048]{1,0:T(1,128)S(1)}, f32[1,2048]{1,0:T(1,128)S(1)}, u32[]{:S(2)}, u32[]{:S(2)}) collective-permute-start(f32[1,2048]{1,0:T(1,128)S(1)} %solve_continuation.1), channel_id=1, source_target_pairs={{0,2},{2,0},{4,6},{6,4},{1,3},{3,1},{5,7},{7,5},{8,10},{10,8},{12,... | collective-permute-start | bytes 24584 | tf_op jit(solution)/shard_map/ppermute | solution.py:147
  114.7 2.4 %collective-permute-start.15 = (f32[1,2048]{1,0:T(1,128)S(1)}, f32[1,2048]{1,0:T(1,128)S(1)}, u32[]{:S(2)}, u32[]{:S(2)}) collective-permute-start(f32[1,2048]{1,0:T(1,128)S(1)} %solve_continuation.1), channel_id=1, source_target_pairs={{0,4},{2,6},{4,0},{6,2},{1,5},{3,7},{5,1},{7,3},{8,12},{10,14},{12... | collective-permute-start | bytes 24584 | tf_op jit(solution)/shard_map/ppermute | solution.py:147
  117.2 0.1 collective-permute-start.16
  117.2 15.4 %collective-permute-done.14 = f32[1,2048]{1,0:T(1,128)S(1)} collective-permute-done((f32[1,2048]{1,0:T(1,128)S(1)}, f32[1,2048]{1,0:T(1,128)S(1)}, u32[]{:S(2)}, u32[]{:S(2)}) %collective-permute-start.14) | collective-permute-done | bytes 8224 | tf_op jit(solution)/shard_map/ppermute | solution.py:147
  132.6 3.9 %collective-permute-done.15 = f32[1,2048]{1,0:T(1,128)S(1)} collective-permute-done((f32[1,2048]{1,0:T(1,128)S(1)}, f32[1,2048]{1,0:T(1,128)S(1)}, u32[]{:S(2)}, u32[]{:S(2)}) %collective-permute-start.15) | collective-permute-done | bytes 8224 | tf_op jit(solution)/shard_map/ppermute | solution.py:147
  136.5 0.0 collective-permute-done.16
  136.5 0.1 collective-permute-start.17
  136.6 4.3 %collective-permute-done.17.refs_1_ = f32[4,2048]{1,0:T(4,128)S(1)} collective-permute-done((f32[4,2048]{1,0:T(4,128)S(1)}, f32[4,2048]{1,0:T(4,128)S(1)}, u32[]{:S(2)}, u32[]{:S(2)}) %collective-permute-start.17) | collective-permute-done | bytes 32800 | tf_op jit(solution)/shard_map/ppermute | solution.py:147
  140.9 10.3 %surface_and_delta.1 = (f32[32,16384]{1,0:T(8,128)}, f32[16,4,128]{2,1,0:T(4,128)S(1)}) custom-call(s32[1]{0:T(128)} %bitcast.slab_ref, f32[4,2048]{1,0:T(4,128)S(1)} %pad_maximum_fusion.2.refs_0_, f32[4,2048]{1,0:T(4,128)S(1)} %collective-permute-done.17.refs_1_, bf16[32,16384]{1,0:T(8,128)(2,1)S(1)} %copy-done, ...), custom_call_target="tpu_custom_call" | custom-call | tf_op jit(solution)/shard_map/surface_and_delta/pallas_call | solution.py:399
  151.2 11.9 %all_to_all.20 = f32[16,4,128]{2,1,0:T(4,128)S(1)} all-to-all(f32[16,4,128]{2,1,0:T(4,128)S(1)} %get-tuple-element.53), channel_id=1, replica_groups=mesh['z'=4,'ylo'=2,'core'=2,'x'=4,'yhi'=2] {'z','ylo','core'}, dimensions={0} | all-to-all | bytes 65536 | tf_op jit(solution)/shard_map/all_to_all | solution.py:461
  163.1 0.1 reshape.27
  163.1 0.6 copy.22
  (39 shorter events, 0.3 us)
Async XLA Ops:
  0.6 1.3 copy-start.12
  2.0 8.7 %copy-start.10 = (f32[32,512]{1,0:T(8,128)S(1)}, f32[32,512]{1,0:T(8,128)}, u32[]{:S(2)}) copy-start(f32[32,512]{1,0:T(8,128)} %param.14) | copy-start | bytes 196612
  2.0 8.7 %copy-start = (bf16[32,16384]{1,0:T(8,128)(2,1)S(1)}, bf16[32,16384]{1,0:T(8,128)(2,1)}, u32[]{:S(2)}) copy-start(bf16[32,16384]{1,0:T(8,128)(2,1)} %refs_2_.1) | copy-start | bytes 3145732
  3.1 8.8 %copy-start.11 = (bf16[16384]{0:T(1024)(128)(2,1)S(1)}, bf16[16384]{0:T(1024)(128)(2,1)}, u32[]{:S(2)}) copy-start(bf16[16384]{0:T(1024)(128)(2,1)} %param.16) | copy-start | bytes 98308
  3.1 23.8 %all-to-all-start = ((bf16[8,32,2176]{2,1,0:T(8,128)(2,1)}), bf16[8,32,2176]{2,1,0:T(8,128)(2,1)S(1)}, u32[]{:S(2)}, u32[]{:S(2)}) async-start(bf16[8,32,2176]{2,1,0:T(8,128)(2,1)} %pad_maximum_fusion), calls=%async_computation | async-start | bytes 2228224 | tf_op jit(solution)/shard_map/all_to_all | solution.py:436
  10.8 20.4 %copy-start.13 = (f32[512]{0:T(512)S(1)}, f32[512]{0:T(512)}, u32[]{:S(2)}) copy-start(f32[512]{0:T(512)} %param.15) | copy-start | bytes 6148
  12.0 0.7 copy-start.4
  26.9 29.0 %all-to-all-start.1 = ((bf16[8,32,2048]{2,1,0:T(8,128)(2,1)}), bf16[8,32,2048]{2,1,0:T(8,128)(2,1)S(1)}, u32[]{:S(2)}, u32[]{:S(2)}) async-start(bf16[8,32,2048]{2,1,0:T(8,128)(2,1)} %bitcast.39), calls=%async_computation.1 | async-start | bytes 2097152 | tf_op jit(solution)/shard_map/all_to_all | solution.py:444
  31.4 0.9 copy-start.5
  32.3 0.8 copy-start.9
  33.2 27.1 %copy-start.14 = (f32[256]{0:T(256)S(1)}, f32[256]{0:T(256)}, u32[]{:S(2)}) copy-start(f32[256]{0:T(256)} %param.21) | copy-start | bytes 3076
  38.8 1.3 copy-start.1
  40.1 0.8 copy-start.3
  40.8 19.6 %copy-start.8 = (bf16[256,256]{1,0:T(8,128)(2,1)S(1)}, bf16[256,256]{1,0:T(8,128)(2,1)}, u32[]{:S(2)}) copy-start(bf16[256,256]{1,0:T(8,128)(2,1)} %mixer_ref.1) | copy-start | bytes 393220
  40.8 2.7 %collective-permute-start = (f32[672,128]{1,0:T(8,128)}, f32[672,128]{1,0:T(8,128)S(1)}, u32[]{:S(2)}, u32[]{:S(2)}) collective-permute-start(f32[672,128]{1,0:T(8,128)} %get-tuple-element.34), channel_id=1, source_target_pairs={{0,8},{8,0},{1,9},{9,1},{2,10},{10,2},{3,11},{11,3},{4,12},{12,4},... | collective-permute-start | bytes 1032200 | tf_op jit(solution)/shard_map/ppermute | solution.py:147
  44.6 5.0 %collective-permute-start.1 = (f32[168,128]{1,0:T(8,128)S(1)}, f32[168,128]{1,0:T(8,128)S(1)}, u32[]{:S(2)}, u32[]{:S(2)}) collective-permute-start(f32[168,128]{1,0:T(8,128)S(1)} %get-tuple-element.56), channel_id=1, source_target_pairs={{0,32},{32,0},{64,96},{96,64},{1,33},{33,1},{65,97},{97,65},{2,34}... | collective-permute-start | bytes 258056 | tf_op jit(solution)/shard_map/ppermute | solution.py:147
  46.3 7.4 %collective-permute-start.2 = (f32[168,128]{1,0:T(8,128)S(1)}, f32[168,128]{1,0:T(8,128)S(1)}, u32[]{:S(2)}, u32[]{:S(2)}) collective-permute-start(f32[168,128]{1,0:T(8,128)S(1)} %get-tuple-element.55), channel_id=1, source_target_pairs={{0,64},{32,96},{64,0},{96,32},{1,65},{33,97},{65,1},{97,33},{2,66}... | collective-permute-start | bytes 258056 | tf_op jit(solution)/shard_map/ppermute | solution.py:147
  49.6 6.3 %collective-permute-start.3 = (f32[168,128]{1,0:T(8,128)S(1)}, f32[168,128]{1,0:T(8,128)S(1)}, u32[]{:S(2)}, u32[]{:S(2)}) collective-permute-start(f32[168,128]{1,0:T(8,128)S(1)} %get-tuple-element.54), channel_id=1, source_target_pairs={{0,96},{32,64},{64,32},{96,0},{1,97},{33,65},{65,33},{97,1},{2,98}... | collective-permute-start | bytes 258056 | tf_op jit(solution)/shard_map/ppermute | solution.py:147
  56.0 8.3 %collective-permute-start.4 = (f32[168,128]{1,0:T(8,128)S(1)}, f32[168,128]{1,0:T(8,128)S(1)}, u32[]{:S(2)}, u32[]{:S(2)}) collective-permute-start(f32[168,128]{1,0:T(8,128)S(1)} %fusion), channel_id=1, source_target_pairs={{0,2},{2,0},{4,6},{6,4},{1,3},{3,1},{5,7},{7,5},{8,10},{10,8},{12,... | collective-permute-start | bytes 258056 | tf_op jit(solution)/shard_map/ppermute | solution.py:147
  57.8 6.5 %collective-permute-start.5 = (f32[168,128]{1,0:T(8,128)S(1)}, f32[168,128]{1,0:T(8,128)S(1)}, u32[]{:S(2)}, u32[]{:S(2)}) collective-permute-start(f32[168,128]{1,0:T(8,128)S(1)} %fusion), channel_id=1, source_target_pairs={{0,4},{2,6},{4,0},{6,2},{1,5},{3,7},{5,1},{7,3},{8,12},{10,14},{12... | collective-permute-start | bytes 258056 | tf_op jit(solution)/shard_map/ppermute | solution.py:147
  60.2 5.5 %collective-permute-start.6 = (f32[168,128]{1,0:T(8,128)S(1)}, f32[168,128]{1,0:T(8,128)S(1)}, u32[]{:S(2)}, u32[]{:S(2)}) collective-permute-start(f32[168,128]{1,0:T(8,128)S(1)} %fusion), channel_id=1, source_target_pairs={{0,6},{2,4},{4,2},{6,0},{1,7},{3,5},{5,3},{7,1},{8,14},{10,12},{12... | collective-permute-start | bytes 258056 | tf_op jit(solution)/shard_map/ppermute | solution.py:147
  65.7 4.9 %collective-permute-start.7 = (f32[168,128]{1,0:T(8,128)S(1)}, f32[168,128]{1,0:T(8,128)S(1)}, u32[]{:S(2)}, u32[]{:S(2)}) collective-permute-start(f32[168,128]{1,0:T(8,128)S(1)} %add_add_fusion.1), channel_id=1, source_target_pairs={{0,1},{1,0},{16,17},{17,16},{2,3},{3,2},{18,19},{19,18},{4,5},{5,4... | collective-permute-start | bytes 258056 | tf_op jit(solution)/shard_map/ppermute | solution.py:147
  68.5 3.6 %collective-permute-start.8 = (f32[168,128]{1,0:T(8,128)S(1)}, f32[168,128]{1,0:T(8,128)S(1)}, u32[]{:S(2)}, u32[]{:S(2)}) collective-permute-start(f32[168,128]{1,0:T(8,128)S(1)} %add_add_fusion.1), channel_id=1, source_target_pairs={{0,16},{1,17},{16,0},{17,1},{2,18},{3,19},{18,2},{19,3},{4,20},{5,... | collective-permute-start | bytes 258056 | tf_op jit(solution)/shard_map/ppermute | solution.py:147
  68.9 4.8 %collective-permute-start.9 = (f32[168,128]{1,0:T(8,128)S(1)}, f32[168,128]{1,0:T(8,128)S(1)}, u32[]{:S(2)}, u32[]{:S(2)}) collective-permute-start(f32[168,128]{1,0:T(8,128)S(1)} %add_add_fusion.1), channel_id=1, source_target_pairs={{0,17},{1,16},{16,1},{17,0},{2,19},{3,18},{18,3},{19,2},{4,21},{5,... | collective-permute-start | bytes 258056 | tf_op jit(solution)/shard_map/ppermute | solution.py:147
  73.6 67.2 %all-to-all-start.2 = ((bf16[8,4,32,2048]{3,2,1,0:T(8,128)(2,1)}), bf16[8,4,32,2048]{3,2,1,0:T(8,128)(2,1)}, u32[]{:S(2)}, u32[]{:S(2)}) async-start(bf16[8,4,32,2048]{3,2,1,0:T(8,128)(2,1)} %get-tuple-element.50), calls=%async_computation.2 | async-start | bytes 8388608 | tf_op jit(solution)/shard_map/all_to_all | solution.py:453
  78.2 62.7 %copy-start.6 = (s32[4,16384]{1,0:T(4,128)S(1)}, s32[4,16384]{1,0:T(4,128)}, u32[]{:S(2)}) copy-start(s32[4,16384]{1,0:T(4,128)} %refs_6_.1) | copy-start | bytes 786436
  78.2 62.7 %copy-start.7 = (s32[4,16384]{1,0:T(4,128)S(1)}, s32[4,16384]{1,0:T(4,128)}, u32[]{:S(2)}) copy-start(s32[4,16384]{1,0:T(4,128)} %refs_7_.1) | copy-start | bytes 786436
  78.3 3.9 %collective-permute-start.10 = (f32[168,128]{1,0:T(8,128)S(1)}, f32[168,128]{1,0:T(8,128)S(1)}, u32[]{:S(2)}, u32[]{:S(2)}) collective-permute-start(f32[168,128]{1,0:T(8,128)S(1)} %add_add_fusion), channel_id=1, source_target_pairs={{0,32},{32,0},{64,96},{96,64},{1,33},{33,1},{65,97},{97,65},{2,34}... | collective-permute-start | bytes 258056 | tf_op jit(solution)/shard_map/ppermute | solution.py:147
  78.3 4.9 %collective-permute-start.11 = (f32[168,128]{1,0:T(8,128)S(1)}, f32[168,128]{1,0:T(8,128)S(1)}, u32[]{:S(2)}, u32[]{:S(2)}) collective-permute-start(f32[168,128]{1,0:T(8,128)S(1)} %add_add_fusion), channel_id=1, source_target_pairs={{0,64},{32,96},{64,0},{96,32},{1,65},{33,97},{65,1},{97,33},{2,66}... | collective-permute-start | bytes 258056 | tf_op jit(solution)/shard_map/ppermute | solution.py:147
  80.0 4.5 %collective-permute-start.12 = (f32[168,128]{1,0:T(8,128)S(1)}, f32[168,128]{1,0:T(8,128)S(1)}, u32[]{:S(2)}, u32[]{:S(2)}) collective-permute-start(f32[168,128]{1,0:T(8,128)S(1)} %add_add_fusion), channel_id=1, source_target_pairs={{0,96},{32,64},{64,32},{96,0},{1,97},{33,65},{65,33},{97,1},{2,98}... | collective-permute-start | bytes 258056 | tf_op jit(solution)/shard_map/ppermute | solution.py:147
  84.6 6.1 %collective-permute-start.13 = (f32[4,168,128]{2,1,0:T(8,128)S(1)}, f32[4,168,128]{2,1,0:T(8,128)S(1)}, u32[]{:S(2)}, u32[]{:S(2)}) collective-permute-start(f32[4,168,128]{2,1,0:T(8,128)S(1)} %pad_maximum_fusion.1.refs_1_), channel_id=1, source_target_pairs={{0,8},{8,0},{1,9},{9,1},{2,10},{10,2},{3,11},{11,3},{4,12},{12,4},... | collective-permute-start | bytes 1032200 | tf_op jit(solution)/shard_map/ppermute | solution.py:147
  90.7 1.6 copy-start.2
  113.1 19.5 %collective-permute-start.14 = (f32[1,2048]{1,0:T(1,128)S(1)}, f32[1,2048]{1,0:T(1,128)S(1)}, u32[]{:S(2)}, u32[]{:S(2)}) collective-permute-start(f32[1,2048]{1,0:T(1,128)S(1)} %solve_continuation.1), channel_id=1, source_target_pairs={{0,2},{2,0},{4,6},{6,4},{1,3},{3,1},{5,7},{7,5},{8,10},{10,8},{12,... | collective-permute-start | bytes 24584 | tf_op jit(solution)/shard_map/ppermute | solution.py:147
  114.7 21.8 %collective-permute-start.15 = (f32[1,2048]{1,0:T(1,128)S(1)}, f32[1,2048]{1,0:T(1,128)S(1)}, u32[]{:S(2)}, u32[]{:S(2)}) collective-permute-start(f32[1,2048]{1,0:T(1,128)S(1)} %solve_continuation.1), channel_id=1, source_target_pairs={{0,4},{2,6},{4,0},{6,2},{1,5},{3,7},{5,1},{7,3},{8,12},{10,14},{12... | collective-permute-start | bytes 24584 | tf_op jit(solution)/shard_map/ppermute | solution.py:147
  117.2 19.3 %collective-permute-start.16 = (f32[1,2048]{1,0:T(1,128)S(1)}, f32[1,2048]{1,0:T(1,128)S(1)}, u32[]{:S(2)}, u32[]{:S(2)}) collective-permute-start(f32[1,2048]{1,0:T(1,128)S(1)} %solve_continuation.1), channel_id=1, source_target_pairs={{0,6},{2,4},{4,2},{6,0},{1,7},{3,5},{5,3},{7,1},{8,14},{10,12},{12... | collective-permute-start | bytes 24584 | tf_op jit(solution)/shard_map/ppermute | solution.py:147
  136.5 4.3 %collective-permute-start.17 = (f32[4,2048]{1,0:T(4,128)S(1)}, f32[4,2048]{1,0:T(4,128)S(1)}, u32[]{:S(2)}, u32[]{:S(2)}) collective-permute-start(f32[4,2048]{1,0:T(4,128)S(1)} %pad_maximum_fusion.2.refs_0_), channel_id=1, source_target_pairs={{0,1},{1,0},{2,3},{3,2},{4,5},{5,4},{6,7},{7,6},{8,9},{9,8},{10,11... | collective-permute-start | bytes 98312 | tf_op jit(solution)/shard_map/ppermute | solution.py:147

commit v5 on v4

--- a/solution.py
+++ b/solution.py
@@ -60,7 +60,7 @@
     loads = table_ref[...].reshape(256, LANES)[:, :32]
     factors = lax.dot_general(loads, tile, (((0,), (0,)), ((), ())), preferred_element_type=f32)
     raised = lax.dot_general(
-        weight_ref[...], right_terms(factors, 0), (((0,), (0,)), ((), ())), preferred_element_type=f32
+        left_terms(weight_ref[...], 0), right_terms(factors, 0), (((0,), (0,)), ((), ())), preferred_element_type=f32
     )
     basis = jnp.tanh(raised + bias_ref[...]).astype(bf16)
     basis_ref[...] = basis
@@ -109,9 +109,9 @@
     return pl.pallas_call(
         gram_kernel,
         out_shape=(
-            jax.ShapeDtypeStruct((512, slab_part), bf16),
-            jax.ShapeDtypeStruct((SUM_ROWS // 2, LANES), f32),
-            jax.ShapeDtypeStruct((SUM_ROWS // 2, LANES), f32),
+            pltpu.HBM((512, slab_part), bf16),
+            pltpu.HBM((SUM_ROWS // 2, LANES), f32),
+            pltpu.HBM((SUM_ROWS // 2, LANES), f32),
         ),
         grid_spec=pltpu.PrefetchScalarGridSpec(
             num_scalar_prefetch=1,
@@ -119,7 +119,7 @@
             in_specs=[
                 pl.BlockSpec((8, 32, TILE), lambda i, s: (0, 0, i)),
                 pl.BlockSpec((8, 32, LANES), lambda i, s: (0, 0, table_at)),
-                pl.BlockSpec((192, 512), lambda i, s: (0, 0)),
+                pl.BlockSpec((32, 512), lambda i, s: (0, 0)),
                 pl.BlockSpec((512, 1), lambda i, s: (0, 0)),
                 pl.BlockSpec((1, TILE), own),
                 pl.BlockSpec((1, TILE), own),
@@ -135,7 +135,7 @@
                 pltpu.VMEM((SUM_ROWS, LANES), f32),
             ],
         ),
-        compiler_params=pltpu.CompilerParams(vmem_limit_bytes=40 << 20),
+        compiler_params=pltpu.CompilerParams(vmem_limit_bytes=20 << 20),
         name="regression_sums",
     )(slab, moved, moved, weights, bias, payoff, fit)
 
@@ -287,7 +287,7 @@
                 pltpu.VMEM((512, 512 + LANES), f32),
             ],
         ),
-        compiler_params=pltpu.CompilerParams(vmem_limit_bytes=40 << 20),
+        compiler_params=pltpu.CompilerParams(vmem_limit_bytes=20 << 20),
         name="solve_continuation",
     )(at, near, far, basis)
 
@@ -338,22 +338,22 @@
             pltpu.VMEM((tiles, 8, STEPS, 32, INCREMENT_TILE), bf16),
             pltpu.SemaphoreType.DMA((tiles,)),
         ],
-        compiler_params=pltpu.CompilerParams(vmem_limit_bytes=40 << 20),
+        compiler_params=pltpu.CompilerParams(vmem_limit_bytes=20 << 20),
         name="increments",
     )(moved, mixer, basket)
 
 
 def surface_kernel(slab_ref, *refs):
-    continuation_refs = refs[:2]
+    continuation_refs = refs[:4]
     (cotangent_ref, gain_ref, shock_ref, weight_ref, exercise_ref, bucket_ref, delta_ref, share_ref,
-     continuation_ref, total_ref) = refs[2:]
+     continuation_ref, total_ref) = refs[4:]
     step = pl.program_id(0)
 
     @pl.when(step == 0)
     def _():
         for flip in range(8):
-            continuation_ref[pl.ds(slab_ref[0] ^ flip, 1), :] = continuation_refs[flip % 2][
-                flip // 2:flip // 2 + 1, :
+            continuation_ref[pl.ds(slab_ref[0] ^ flip, 1), :] = continuation_refs[flip // 2][
+                flip % 2:flip % 2 + 1, :
             ]
         total_ref[...] = jnp.zeros(total_ref.shape, f32)
 
@@ -395,7 +395,7 @@
 
 def surface_and_delta(slab, continuations, cotangent, gains, shocks, weights, exercise, bucket):
     local_paths = cotangent.shape[1]
-    whole = pl.BlockSpec((4, DATE_TILE), lambda i, s: (0, 0))
+    whole = pl.BlockSpec((2, DATE_TILE), lambda i, s: (0, 0))
     return pl.pallas_call(
         surface_kernel,
         out_shape=(
@@ -405,7 +405,7 @@
         grid_spec=pltpu.PrefetchScalarGridSpec(
             num_scalar_prefetch=1,
             grid=(local_paths // DATE_TILE,),
-            in_specs=[whole] * 2 + [
+            in_specs=[whole] * 4 + [
                 pl.BlockSpec((32, DATE_TILE), lambda i, s: (0, i)),
                 pl.BlockSpec((1, STEPS, 32, DATE_TILE), lambda i, s: (i, 0, 0, 0)),
                 pl.BlockSpec((STEPS, 32, DATE_TILE), lambda i, s: (0, 0, i)),
@@ -419,7 +419,7 @@
             ),
             scratch_shapes=[pltpu.VMEM((8, DATE_TILE), f32), pltpu.VMEM((STRIKE_ROWS, 32 * (NK // STRIKE_ROWS)), f32)],
         ),
-        compiler_params=pltpu.CompilerParams(vmem_limit_bytes=48 << 20),
+        compiler_params=pltpu.CompilerParams(vmem_limit_bytes=32 << 20),
         name="surface_and_delta",
     )(slab, *continuations, cotangent, gains, shocks, weights, exercise, bucket)
 
@@ -437,14 +437,16 @@
         jnp.concatenate([pieces, table], axis=2), STOCK_AXES, 0, 0, tiled=True
     )
     slabs = jnp.moveaxis(cotangent.reshape(32, 8, slab_part), 1, 0)
-    small = (left_terms(basis_w, 0), basis_bias[:, None], payoff[None, :], in_fit[None, :],
+    small = (basis_w, basis_bias[:, None], payoff[None, :], in_fit[None, :],
              basket[:, None])
     slabs, moved_prices, small = lax.optimization_barrier((slabs, moved_prices, small))
-    weight_terms, bias, payoff, in_fit, basket = small
+    basis_w, bias, payoff, in_fit, basket = small
     moved = lax.all_to_all(slabs, STOCK_AXES, 0, 0, tiled=True)
+    basis_w = pltpu.with_memory_space_constraint(basis_w, pltpu.HBM)
+    in_fit = pltpu.with_memory_space_constraint(in_fit, pltpu.HBM)
     place = jnp.stack([slab[0], lax.axis_index("core").astype(jnp.int32)])
     basis, kept, other = regression_sums(
-        place, moved_prices, weight_terms, bias, payoff, in_fit, slab_part
+        place, moved_prices, basis_w, bias, payoff, in_fit, slab_part
     )
     share, moved = sum_over_cores_and_z(kept, other, moved)
     sent, weights = increments(moved, corr_gen, basket, slab_part)
@@ -453,8 +455,8 @@
     gains = lax.all_to_all(sent, STOCK_AXES, 0, 0, tiled=True)
     near, far = gathered_sum(share)
     continuation = solve_continuation(near, far, basis, path_count)
-    column = jnp.concatenate([continuation] + exchange_with_others(continuation, "x", 4), axis=0)
-    continuations = [column] + exchange_with_others(column, "yhi", 2)
+    pair = jnp.concatenate([continuation] + exchange_with_others(continuation, "yhi", 2), axis=0)
+    continuations = [pair] + exchange_with_others(pair, "x", 4)
     delta, surface = surface_and_delta(
         slab, continuations, cotangent, gains, shocks, weights, exercise, bucket
     )

time: 164 us -> 158 us (0.963)
  waiting for transfers between devices: 55.2 us -> 49.1 us
  starting transfers between devices: 43.3 us -> 46.1 us
  local copies, waits for them, and re-layouts: 9.62 us -> 7.29 us
    ppermute x18, waiting for transfers between devices: 40.9 us -> 34.1 us  [exchange_with_others(): lax.ppermute(sent, axes, [(i, i ^ flip) for i in range(count)])]
    ppermute x18, starting transfers between devices: 26.9 us -> 29.8 us  [exchange_with_others(): lax.ppermute(sent, axes, [(i, i ^ flip) for i in range(count)])]
    unnamed x30 -> x20, local copies, waits for them, and re-layouts: 6.16 us -> 3.82 us
  transfers between devices with their start and end apart: 21 -> 21, of which waited for: 14 -> 14; matrix products, arithmetic and copies ran while one was open for 2% -> 2% of each run, Pallas kernels for 18% -> 20%
where the time goes in v5:
time: 158 us; the launch traced here: 157 us
  waiting for transfers between devices  49.1 us (31%)
  starting transfers between devices  46.1 us (29%)
  Pallas kernels  40.8 us (26%)
  blocking collectives  10.7 us (7%)
  local copies, waits for them, and re-layouts  7.29 us (5%)
  other arithmetic  2.4 us (2%)
    ppermute x18, waiting for transfers between devices, exchange_with_others(): lax.ppermute(sent, axes, [(i, i ^ flip) for i in range(count)])  34.1 us
    ppermute x18, starting transfers between devices, exchange_with_others(): lax.ppermute(sent, axes, [(i, i ^ flip) for i in range(count)])  29.8 us
    pallas_call x1, Pallas kernels, solve_continuation(): pl.pallas_call(lambda *refs: solve_kernel(*refs, scale=1.0 / path_count),...  20.7 us
    all_to_all x1, waiting for transfers between devices, per_device(): lax.all_to_all(jnp.concatenate([pieces, table], axis=2), STOCK_AXES, 0, 0...  15 us
    all_to_all x1, blocking collectives, per_device(): surface = lax.all_to_all(surface, PATH_AXES, 0, 0, tiled=True)  10.7 us
    pallas_call x1, Pallas kernels, surface_and_delta(): pl.pallas_call(surface_kernel, out_shape=(jax.ShapeDtypeStruct((32, local...  9.54 us
    all_to_all x1, starting transfers between devices, per_device(): lax.all_to_all(jnp.concatenate([pieces, table], axis=2), STOCK_AXES, 0, 0...  7.61 us
    pallas_call x1, Pallas kernels, regression_sums(): pl.pallas_call(gram_kernel, out_shape=(pltpu.HBM((512, slab_part), bf16),...  6.69 us
  transfers between devices with their start and end apart: 21, of which 14 were waited for; matrix products, arithmetic and copies ran while one was open for 2% of the time, Pallas kernels for 20%

profile of v5, /device:TPU:1, one launch (start us, length us, event | category | flops | bytes accessed | tf_op | source)
XLA Modules:
  0.0 157.3 jit_solution(7789902061604208858)
XLA Ops:
  0.6 1.3 copy.27
  2.0 0.0 copy-start.1
  2.0 1.1 pad_maximum_fusion
  3.1 7.6 %all-to-all-start = ((bf16[8,32,2176]{2,1,0:T(8,128)(2,1)}), bf16[8,32,2176]{2,1,0:T(8,128)(2,1)S(1)}, u32[]{:S(2)}, u32[]{:S(2)}) async-start(bf16[8,32,2176]{2,1,0:T(8,128)(2,1)} %pad_maximum_fusion), calls=%async_computation | async-start | bytes 2228224 | tf_op jit(solution)/shard_map/all_to_all | solution.py:436
  10.7 0.0 copy-start.8
  10.7 1.1 copy.28
  11.9 15.0 %all-to-all-done.moved_ref.table_ref = bf16[8,32,2176]{2,1,0:T(8,128)(2,1)S(1)} async-done(((bf16[8,32,2176]{2,1,0:T(8,128)(2,1)}), bf16[8,32,2176]{2,1,0:T(8,128)(2,1)S(1)}, u32[]{:S(2)}, u32[]{:S(2)}) %all-to-all-start) | async-done | bytes 1114144 | tf_op jit(solution)/shard_map/all_to_all | solution.py:436
  26.9 4.2 %all-to-all-start.1 = ((bf16[8,32,2048]{2,1,0:T(8,128)(2,1)}), bf16[8,32,2048]{2,1,0:T(8,128)(2,1)S(1)}, u32[]{:S(2)}, u32[]{:S(2)}) async-start(bf16[8,32,2048]{2,1,0:T(8,128)(2,1)} %bitcast.38), calls=%async_computation.1 | async-start | bytes 2097152 | tf_op jit(solution)/shard_map/all_to_all | solution.py:444
  31.1 0.1 pad_add_fusion.1.slab_ref
  31.2 0.1 copy.20.bias_ref
  31.4 0.0 copy-start.9
  31.4 6.7 %regression_sums.1 = (bf16[512,2048]{1,0:T(8,128)(2,1)}, f32[672,128]{1,0:T(8,128)}, f32[672,128]{1,0:T(8,128)}) custom-call(s32[2]{0:T(128)S(1)} %pad_add_fusion.1.slab_ref, bf16[8,32,2176]{2,1,0:T(8,128)(2,1)S(1)} %all-to-all-done.moved_ref.table_ref, bf16[8,32,2176]{2,1,0:T(8,128)(2,1)S(1)} %all-to-all-done.moved_ref.table_ref, f32[32,512]{1,0:T(8,128)} %weight_ref, ...), custom_call_target="tpu_custom_call" | custom-call | tf_op jit(solution)/shard_map/regression_sums/pallas_call | solution.py:109
  38.1 1.3 collective-permute-start
  39.3 1.5 collective-permute-done
  40.8 1.0 add.49
  41.9 1.7 %collective-permute-start.1 = (f32[168,128]{1,0:T(8,128)S(1)}, f32[168,128]{1,0:T(8,128)S(1)}, u32[]{:S(2)}, u32[]{:S(2)}) collective-permute-start(f32[168,128]{1,0:T(8,128)S(1)} %get-tuple-element.56), channel_id=1, source_target_pairs={{0,32},{32,0},{64,96},{96,64},{1,33},{33,1},{65,97},{97,65},{2,34}... | collective-permute-start | bytes 258056 | tf_op jit(solution)/shard_map/ppermute | solution.py:147
  43.6 3.3 %collective-permute-start.2 = (f32[168,128]{1,0:T(8,128)S(1)}, f32[168,128]{1,0:T(8,128)S(1)}, u32[]{:S(2)}, u32[]{:S(2)}) collective-permute-start(f32[168,128]{1,0:T(8,128)S(1)} %get-tuple-element.55), channel_id=1, source_target_pairs={{0,64},{32,96},{64,0},{96,32},{1,65},{33,97},{65,1},{97,33},{2,66}... | collective-permute-start | bytes 258056 | tf_op jit(solution)/shard_map/ppermute | solution.py:147
  46.9 0.0 collective-permute-start.3
  46.9 0.0 collective-permute-done.1
  46.9 4.1 %collective-permute-done.2 = f32[168,128]{1,0:T(8,128)S(1)} collective-permute-done((f32[168,128]{1,0:T(8,128)S(1)}, f32[168,128]{1,0:T(8,128)S(1)}, u32[]{:S(2)}, u32[]{:S(2)}) %collective-permute-start.2) | collective-permute-done | bytes 86048 | tf_op jit(solution)/shard_map/ppermute | solution.py:147
  51.0 2.2 %collective-permute-done.3 = f32[168,128]{1,0:T(8,128)S(1)} collective-permute-done((f32[168,128]{1,0:T(8,128)S(1)}, f32[168,128]{1,0:T(8,128)S(1)}, u32[]{:S(2)}, u32[]{:S(2)}) %collective-permute-start.3) | collective-permute-done | bytes 86048 | tf_op jit(solution)/shard_map/ppermute | solution.py:147
  53.2 0.0 all-to-all-done.1.moved_ref
  53.3 1.8 %collective-permute-start.4 = (f32[168,128]{1,0:T(8,128)S(1)}, f32[168,128]{1,0:T(8,128)S(1)}, u32[]{:S(2)}, u32[]{:S(2)}) collective-permute-start(f32[168,128]{1,0:T(8,128)S(1)} %fusion), channel_id=1, source_target_pairs={{0,2},{2,0},{4,6},{6,4},{1,3},{3,1},{5,7},{7,5},{8,10},{10,8},{12,... | collective-permute-start | bytes 258056 | tf_op jit(solution)/shard_map/ppermute | solution.py:147
  55.1 2.4 %collective-permute-start.5 = (f32[168,128]{1,0:T(8,128)S(1)}, f32[168,128]{1,0:T(8,128)S(1)}, u32[]{:S(2)}, u32[]{:S(2)}) collective-permute-start(f32[168,128]{1,0:T(8,128)S(1)} %fusion), channel_id=1, source_target_pairs={{0,4},{2,6},{4,0},{6,2},{1,5},{3,7},{5,1},{7,3},{8,12},{10,14},{12... | collective-permute-start | bytes 258056 | tf_op jit(solution)/shard_map/ppermute | solution.py:147
  57.5 0.1 collective-permute-start.6
  57.6 0.1 copy.21.basket_ref
  57.7 3.8 %increments.1 = (bf16[8,4,32,2048]{3,2,1,0:T(8,128)(2,1)}, f32[256,128]{1,0:T(8,128)S(1)}) custom-call(bf16[8,32,2048]{2,1,0:T(8,128)(2,1)S(1)} %all-to-all-done.1.moved_ref, bf16[256,256]{1,0:T(8,128)(2,1)S(1)} %copy-done.5, f32[256,1]{1,0:T(8,128)S(1)} %copy.21.basket_ref), custom_call_target="tpu_custom_call" | custom-call | tf_op jit(solution)/shard_map/increments/pallas_call | solution.py:327
  61.5 0.0 collective-permute-done.4
  61.6 0.0 collective-permute-done.5
  61.6 1.4 collective-permute-done.6
  63.0 2.8 %collective-permute-start.7 = (f32[168,128]{1,0:T(8,128)S(1)}, f32[168,128]{1,0:T(8,128)S(1)}, u32[]{:S(2)}, u32[]{:S(2)}) collective-permute-start(f32[168,128]{1,0:T(8,128)S(1)} %add_add_fusion.1), channel_id=1, source_target_pairs={{0,1},{1,0},{16,17},{17,16},{2,3},{3,2},{18,19},{19,18},{4,5},{5,4... | collective-permute-start | bytes 258056 | tf_op jit(solution)/shard_map/ppermute | solution.py:147
  65.7 0.4 collective-permute-start.8
  66.1 0.2 collective-permute-start.9
  66.3 1.6 %collective-permute-done.7 = f32[168,128]{1,0:T(8,128)S(1)} collective-permute-done((f32[168,128]{1,0:T(8,128)S(1)}, f32[168,128]{1,0:T(8,128)S(1)}, u32[]{:S(2)}, u32[]{:S(2)}) %collective-permute-start.7) | collective-permute-done | bytes 86048 | tf_op jit(solution)/shard_map/ppermute | solution.py:147
  67.9 1.5 collective-permute-done.8
  69.4 1.5 collective-permute-done.9
  70.9 4.5 %all-to-all-start.2 = ((bf16[8,4,32,2048]{3,2,1,0:T(8,128)(2,1)}), bf16[8,4,32,2048]{3,2,1,0:T(8,128)(2,1)}, u32[]{:S(2)}, u32[]{:S(2)}) async-start(bf16[8,4,32,2048]{3,2,1,0:T(8,128)(2,1)} %get-tuple-element.50), calls=%async_computation.2 | async-start | bytes 8388608 | tf_op jit(solution)/shard_map/all_to_all | solution.py:455
  75.4 0.0 copy-start.3
  75.5 0.0 copy-start.4
  75.5 0.1 collective-permute-start.10
  75.6 1.7 %collective-permute-start.11 = (f32[168,128]{1,0:T(8,128)S(1)}, f32[168,128]{1,0:T(8,128)S(1)}, u32[]{:S(2)}, u32[]{:S(2)}) collective-permute-start(f32[168,128]{1,0:T(8,128)S(1)} %add_add_fusion), channel_id=1, source_target_pairs={{0,64},{32,96},{64,0},{96,32},{1,65},{33,97},{65,1},{97,33},{2,66}... | collective-permute-start | bytes 258056 | tf_op jit(solution)/shard_map/ppermute | solution.py:147
  77.3 2.2 %collective-permute-start.12 = (f32[168,128]{1,0:T(8,128)S(1)}, f32[168,128]{1,0:T(8,128)S(1)}, u32[]{:S(2)}, u32[]{:S(2)}) collective-permute-start(f32[168,128]{1,0:T(8,128)S(1)} %add_add_fusion), channel_id=1, source_target_pairs={{0,96},{32,64},{64,32},{96,0},{1,97},{33,65},{65,33},{97,1},{2,98}... | collective-permute-start | bytes 258056 | tf_op jit(solution)/shard_map/ppermute | solution.py:147
  79.4 0.0 collective-permute-done.10
  79.4 1.1 collective-permute-done.11
  80.5 1.3 collective-permute-done.12
  81.9 4.8 %collective-permute-start.13 = (f32[4,168,128]{2,1,0:T(8,128)S(1)}, f32[4,168,128]{2,1,0:T(8,128)S(1)}, u32[]{:S(2)}, u32[]{:S(2)}) collective-permute-start(f32[4,168,128]{2,1,0:T(8,128)S(1)} %pad_maximum_fusion.1.refs_1_), channel_id=1, source_target_pairs={{0,8},{8,0},{1,9},{9,1},{2,10},{10,2},{3,11},{11,3},{4,12},{12,4},... | collective-permute-start | bytes 1032200 | tf_op jit(solution)/shard_map/ppermute | solution.py:147
  86.7 0.1 pad_add_fusion.refs_0_
  86.8 1.2 collective-permute-done.13.refs_2_
  88.0 1.6 %copy-done.2 = bf16[512,2048]{1,0:T(8,128)(2,1)S(1)} copy-done((bf16[512,2048]{1,0:T(8,128)(2,1)S(1)}, bf16[512,2048]{1,0:T(8,128)(2,1)}, u32[]{:S(2)}) %copy-start.2) | copy-done | bytes 2097176
  89.6 20.7 %solve_continuation.1 = f32[1,2048]{1,0:T(1,128)S(1)} custom-call(s32[2]{0:T(128)S(1)} %pad_add_fusion.refs_0_, f32[4,168,128]{2,1,0:T(8,128)S(1)} %pad_maximum_fusion.1.refs_1_, f32[4,168,128]{2,1,0:T(8,128)S(1)} %collective-permute-done.13.refs_2_, bf16[512,2048]{1,0:T(8,128)(2,1)S(1)} %copy-done.2), custom_call_target="tpu_custom_call" | custom-call | tf_op jit(solution)/shard_map/solve_continuation/pallas_call | solution.py:277
  110.3 3.2 %collective-permute-start.14 = (f32[1,2048]{1,0:T(1,128)S(1)}, f32[1,2048]{1,0:T(1,128)S(1)}, u32[]{:S(2)}, u32[]{:S(2)}) collective-permute-start(f32[1,2048]{1,0:T(1,128)S(1)} %solve_continuation.1), channel_id=1, source_target_pairs={{0,1},{1,0},{2,3},{3,2},{4,5},{5,4},{6,7},{7,6},{8,9},{9,8},{10,11... | collective-permute-start | bytes 24584 | tf_op jit(solution)/shard_map/ppermute | solution.py:147
  113.5 10.8 %collective-permute-done.14 = f32[1,2048]{1,0:T(1,128)S(1)} collective-permute-done((f32[1,2048]{1,0:T(1,128)S(1)}, f32[1,2048]{1,0:T(1,128)S(1)}, u32[]{:S(2)}, u32[]{:S(2)}) %collective-permute-start.14) | collective-permute-done | bytes 8224 | tf_op jit(solution)/shard_map/ppermute | solution.py:147
  124.3 0.1 collective-permute-start.15
  124.4 2.9 %collective-permute-start.16 = (f32[2,2048]{1,0:T(2,128)S(1)}, f32[2,2048]{1,0:T(2,128)S(1)}, u32[]{:S(2)}, u32[]{:S(2)}) collective-permute-start(f32[2,2048]{1,0:T(2,128)S(1)} %pad_maximum_fusion.2.refs_0_), channel_id=1, source_target_pairs={{0,4},{2,6},{4,0},{6,2},{1,5},{3,7},{5,1},{7,3},{8,12},{10,14},{12... | collective-permute-start | bytes 49160 | tf_op jit(solution)/shard_map/ppermute | solution.py:147
  127.3 0.9 collective-permute-start.17
  128.2 1.7 %collective-permute-done.15.refs_1_ = f32[2,2048]{1,0:T(2,128)S(1)} collective-permute-done((f32[2,2048]{1,0:T(2,128)S(1)}, f32[2,2048]{1,0:T(2,128)S(1)}, u32[]{:S(2)}, u32[]{:S(2)}) %collective-permute-start.15) | collective-permute-done | bytes 16416 | tf_op jit(solution)/shard_map/ppermute | solution.py:147
  129.9 4.2 %collective-permute-done.16.refs_2_ = f32[2,2048]{1,0:T(2,128)S(1)} collective-permute-done((f32[2,2048]{1,0:T(2,128)S(1)}, f32[2,2048]{1,0:T(2,128)S(1)}, u32[]{:S(2)}, u32[]{:S(2)}) %collective-permute-start.16) | collective-permute-done | bytes 16416 | tf_op jit(solution)/shard_map/ppermute | solution.py:147
  134.1 0.0 collective-permute-done.17.refs_3_
  134.2 0.0 copy-start
  134.2 2.2 %copy-done = bf16[4,32,16384]{2,1,0:T(8,128)(2,1)S(1)} copy-done((bf16[4,32,16384]{2,1,0:T(8,128)(2,1)S(1)}, bf16[4,32,16384]{2,1,0:T(8,128)(2,1)}, u32[]{:S(2)}) %copy-start) | copy-done | bytes 4194328
  136.3 9.5 %surface_and_delta.1 = (f32[32,16384]{1,0:T(8,128)}, f32[16,4,128]{2,1,0:T(4,128)S(1)}) custom-call(s32[1]{0:T(128)} %bitcast.slab_ref, f32[2,2048]{1,0:T(2,128)S(1)} %pad_maximum_fusion.2.refs_0_, f32[2,2048]{1,0:T(2,128)S(1)} %collective-permute-done.15.refs_1_, f32[2,2048]{1,0:T(2,128)S(1)} %collective-permute-done.16.refs_2_, ...), custom_call_target="tpu_custom_call" | custom-call | tf_op jit(solution)/shard_map/surface_and_delta/pallas_call | solution.py:399
  145.9 10.7 %all_to_all.20 = f32[16,4,128]{2,1,0:T(4,128)S(1)} all-to-all(f32[16,4,128]{2,1,0:T(4,128)S(1)} %get-tuple-element.53), channel_id=1, replica_groups=mesh['z'=4,'ylo'=2,'core'=2,'x'=4,'yhi'=2] {'z','ylo','core'}, dimensions={0} | all-to-all | bytes 65536 | tf_op jit(solution)/shard_map/all_to_all | solution.py:463
  156.6 0.1 reshape.27
  156.7 0.6 copy.22
  (23 shorter events, 0.3 us)
Async XLA Ops:
  0.6 1.3 copy-start.7
  2.0 8.7 %copy-start.1 = (bf16[32,16384]{1,0:T(8,128)(2,1)S(1)}, bf16[32,16384]{1,0:T(8,128)(2,1)}, u32[]{:S(2)}) copy-start(bf16[32,16384]{1,0:T(8,128)(2,1)} %refs_4_.1) | copy-start | bytes 3145732
  3.1 8.7 %copy-start.6 = (bf16[16384]{0:T(1024)(128)(2,1)S(1)}, bf16[16384]{0:T(1024)(128)(2,1)}, u32[]{:S(2)}) copy-start(bf16[16384]{0:T(1024)(128)(2,1)} %param.16) | copy-start | bytes 98308
  3.1 23.8 %all-to-all-start = ((bf16[8,32,2176]{2,1,0:T(8,128)(2,1)}), bf16[8,32,2176]{2,1,0:T(8,128)(2,1)S(1)}, u32[]{:S(2)}, u32[]{:S(2)}) async-start(bf16[8,32,2176]{2,1,0:T(8,128)(2,1)} %pad_maximum_fusion), calls=%async_computation | async-start | bytes 2228224 | tf_op jit(solution)/shard_map/all_to_all | solution.py:436
  10.7 20.5 %copy-start.8 = (f32[512]{0:T(512)S(1)}, f32[512]{0:T(512)}, u32[]{:S(2)}) copy-start(f32[512]{0:T(512)} %param.15) | copy-start | bytes 6148
  26.9 26.3 %all-to-all-start.1 = ((bf16[8,32,2048]{2,1,0:T(8,128)(2,1)}), bf16[8,32,2048]{2,1,0:T(8,128)(2,1)S(1)}, u32[]{:S(2)}, u32[]{:S(2)}) async-start(bf16[8,32,2048]{2,1,0:T(8,128)(2,1)} %bitcast.38), calls=%async_computation.1 | async-start | bytes 2097152 | tf_op jit(solution)/shard_map/all_to_all | solution.py:444
  31.4 26.2 %copy-start.9 = (f32[256]{0:T(256)S(1)}, f32[256]{0:T(256)}, u32[]{:S(2)}) copy-start(f32[256]{0:T(256)} %param.21) | copy-start | bytes 3076
  38.1 19.6 %copy-start.5 = (bf16[256,256]{1,0:T(8,128)(2,1)S(1)}, bf16[256,256]{1,0:T(8,128)(2,1)}, u32[]{:S(2)}) copy-start(bf16[256,256]{1,0:T(8,128)(2,1)} %mixer_ref.1) | copy-start | bytes 393220
  38.1 2.8 %collective-permute-start = (f32[672,128]{1,0:T(8,128)}, f32[672,128]{1,0:T(8,128)S(1)}, u32[]{:S(2)}, u32[]{:S(2)}) collective-permute-start(f32[672,128]{1,0:T(8,128)} %get-tuple-element.34), channel_id=1, source_target_pairs={{0,8},{8,0},{1,9},{9,1},{2,10},{10,2},{3,11},{11,3},{4,12},{12,4},... | collective-permute-start | bytes 1032200 | tf_op jit(solution)/shard_map/ppermute | solution.py:147
  41.9 5.0 %collective-permute-start.1 = (f32[168,128]{1,0:T(8,128)S(1)}, f32[168,128]{1,0:T(8,128)S(1)}, u32[]{:S(2)}, u32[]{:S(2)}) collective-permute-start(f32[168,128]{1,0:T(8,128)S(1)} %get-tuple-element.56), channel_id=1, source_target_pairs={{0,32},{32,0},{64,96},{96,64},{1,33},{33,1},{65,97},{97,65},{2,34}... | collective-permute-start | bytes 258056 | tf_op jit(solution)/shard_map/ppermute | solution.py:147
  43.6 7.4 %collective-permute-start.2 = (f32[168,128]{1,0:T(8,128)S(1)}, f32[168,128]{1,0:T(8,128)S(1)}, u32[]{:S(2)}, u32[]{:S(2)}) collective-permute-start(f32[168,128]{1,0:T(8,128)S(1)} %get-tuple-element.55), channel_id=1, source_target_pairs={{0,64},{32,96},{64,0},{96,32},{1,65},{33,97},{65,1},{97,33},{2,66}... | collective-permute-start | bytes 258056 | tf_op jit(solution)/shard_map/ppermute | solution.py:147
  46.9 6.3 %collective-permute-start.3 = (f32[168,128]{1,0:T(8,128)S(1)}, f32[168,128]{1,0:T(8,128)S(1)}, u32[]{:S(2)}, u32[]{:S(2)}) collective-permute-start(f32[168,128]{1,0:T(8,128)S(1)} %get-tuple-element.54), channel_id=1, source_target_pairs={{0,96},{32,64},{64,32},{96,0},{1,97},{33,65},{65,33},{97,1},{2,98}... | collective-permute-start | bytes 258056 | tf_op jit(solution)/shard_map/ppermute | solution.py:147
  53.3 8.3 %collective-permute-start.4 = (f32[168,128]{1,0:T(8,128)S(1)}, f32[168,128]{1,0:T(8,128)S(1)}, u32[]{:S(2)}, u32[]{:S(2)}) collective-permute-start(f32[168,128]{1,0:T(8,128)S(1)} %fusion), channel_id=1, source_target_pairs={{0,2},{2,0},{4,6},{6,4},{1,3},{3,1},{5,7},{7,5},{8,10},{10,8},{12,... | collective-permute-start | bytes 258056 | tf_op jit(solution)/shard_map/ppermute | solution.py:147
  55.1 6.5 %collective-permute-start.5 = (f32[168,128]{1,0:T(8,128)S(1)}, f32[168,128]{1,0:T(8,128)S(1)}, u32[]{:S(2)}, u32[]{:S(2)}) collective-permute-start(f32[168,128]{1,0:T(8,128)S(1)} %fusion), channel_id=1, source_target_pairs={{0,4},{2,6},{4,0},{6,2},{1,5},{3,7},{5,1},{7,3},{8,12},{10,14},{12... | collective-permute-start | bytes 258056 | tf_op jit(solution)/shard_map/ppermute | solution.py:147
  57.5 5.5 %collective-permute-start.6 = (f32[168,128]{1,0:T(8,128)S(1)}, f32[168,128]{1,0:T(8,128)S(1)}, u32[]{:S(2)}, u32[]{:S(2)}) collective-permute-start(f32[168,128]{1,0:T(8,128)S(1)} %fusion), channel_id=1, source_target_pairs={{0,6},{2,4},{4,2},{6,0},{1,7},{3,5},{5,3},{7,1},{8,14},{10,12},{12... | collective-permute-start | bytes 258056 | tf_op jit(solution)/shard_map/ppermute | solution.py:147
  63.0 4.9 %collective-permute-start.7 = (f32[168,128]{1,0:T(8,128)S(1)}, f32[168,128]{1,0:T(8,128)S(1)}, u32[]{:S(2)}, u32[]{:S(2)}) collective-permute-start(f32[168,128]{1,0:T(8,128)S(1)} %add_add_fusion.1), channel_id=1, source_target_pairs={{0,1},{1,0},{16,17},{17,16},{2,3},{3,2},{18,19},{19,18},{4,5},{5,4... | collective-permute-start | bytes 258056 | tf_op jit(solution)/shard_map/ppermute | solution.py:147
  65.7 3.6 %collective-permute-start.8 = (f32[168,128]{1,0:T(8,128)S(1)}, f32[168,128]{1,0:T(8,128)S(1)}, u32[]{:S(2)}, u32[]{:S(2)}) collective-permute-start(f32[168,128]{1,0:T(8,128)S(1)} %add_add_fusion.1), channel_id=1, source_target_pairs={{0,16},{1,17},{16,0},{17,1},{2,18},{3,19},{18,2},{19,3},{4,20},{5,... | collective-permute-start | bytes 258056 | tf_op jit(solution)/shard_map/ppermute | solution.py:147
  66.1 4.8 %collective-permute-start.9 = (f32[168,128]{1,0:T(8,128)S(1)}, f32[168,128]{1,0:T(8,128)S(1)}, u32[]{:S(2)}, u32[]{:S(2)}) collective-permute-start(f32[168,128]{1,0:T(8,128)S(1)} %add_add_fusion.1), channel_id=1, source_target_pairs={{0,17},{1,16},{16,1},{17,0},{2,19},{3,18},{18,3},{19,2},{4,21},{5,... | collective-permute-start | bytes 258056 | tf_op jit(solution)/shard_map/ppermute | solution.py:147
  70.9 63.2 %all-to-all-start.2 = ((bf16[8,4,32,2048]{3,2,1,0:T(8,128)(2,1)}), bf16[8,4,32,2048]{3,2,1,0:T(8,128)(2,1)}, u32[]{:S(2)}, u32[]{:S(2)}) async-start(bf16[8,4,32,2048]{3,2,1,0:T(8,128)(2,1)} %get-tuple-element.50), calls=%async_computation.2 | async-start | bytes 8388608 | tf_op jit(solution)/shard_map/all_to_all | solution.py:455
  75.4 58.7 %copy-start.3 = (s32[4,16384]{1,0:T(4,128)S(1)}, s32[4,16384]{1,0:T(4,128)}, u32[]{:S(2)}) copy-start(s32[4,16384]{1,0:T(4,128)} %refs_8_.1) | copy-start | bytes 786436
  75.5 58.7 %copy-start.4 = (s32[4,16384]{1,0:T(4,128)S(1)}, s32[4,16384]{1,0:T(4,128)}, u32[]{:S(2)}) copy-start(s32[4,16384]{1,0:T(4,128)} %refs_9_.1) | copy-start | bytes 786436
  75.5 3.9 %collective-permute-start.10 = (f32[168,128]{1,0:T(8,128)S(1)}, f32[168,128]{1,0:T(8,128)S(1)}, u32[]{:S(2)}, u32[]{:S(2)}) collective-permute-start(f32[168,128]{1,0:T(8,128)S(1)} %add_add_fusion), channel_id=1, source_target_pairs={{0,32},{32,0},{64,96},{96,64},{1,33},{33,1},{65,97},{97,65},{2,34}... | collective-permute-start | bytes 258056 | tf_op jit(solution)/shard_map/ppermute | solution.py:147
  75.6 4.9 %collective-permute-start.11 = (f32[168,128]{1,0:T(8,128)S(1)}, f32[168,128]{1,0:T(8,128)S(1)}, u32[]{:S(2)}, u32[]{:S(2)}) collective-permute-start(f32[168,128]{1,0:T(8,128)S(1)} %add_add_fusion), channel_id=1, source_target_pairs={{0,64},{32,96},{64,0},{96,32},{1,65},{33,97},{65,1},{97,33},{2,66}... | collective-permute-start | bytes 258056 | tf_op jit(solution)/shard_map/ppermute | solution.py:147
  77.3 4.5 %collective-permute-start.12 = (f32[168,128]{1,0:T(8,128)S(1)}, f32[168,128]{1,0:T(8,128)S(1)}, u32[]{:S(2)}, u32[]{:S(2)}) collective-permute-start(f32[168,128]{1,0:T(8,128)S(1)} %add_add_fusion), channel_id=1, source_target_pairs={{0,96},{32,64},{64,32},{96,0},{1,97},{33,65},{65,33},{97,1},{2,98}... | collective-permute-start | bytes 258056 | tf_op jit(solution)/shard_map/ppermute | solution.py:147
  81.9 6.1 %collective-permute-start.13 = (f32[4,168,128]{2,1,0:T(8,128)S(1)}, f32[4,168,128]{2,1,0:T(8,128)S(1)}, u32[]{:S(2)}, u32[]{:S(2)}) collective-permute-start(f32[4,168,128]{2,1,0:T(8,128)S(1)} %pad_maximum_fusion.1.refs_1_), channel_id=1, source_target_pairs={{0,8},{8,0},{1,9},{9,1},{2,10},{10,2},{3,11},{11,3},{4,12},{12,4},... | collective-permute-start | bytes 1032200 | tf_op jit(solution)/shard_map/ppermute | solution.py:147
  88.0 1.6 %copy-start.2 = (bf16[512,2048]{1,0:T(8,128)(2,1)S(1)}, bf16[512,2048]{1,0:T(8,128)(2,1)}, u32[]{:S(2)}) copy-start(bf16[512,2048]{1,0:T(8,128)(2,1)} %get-tuple-element.49.refs_3_) | copy-start | bytes 6291460
  110.3 13.9 %collective-permute-start.14 = (f32[1,2048]{1,0:T(1,128)S(1)}, f32[1,2048]{1,0:T(1,128)S(1)}, u32[]{:S(2)}, u32[]{:S(2)}) collective-permute-start(f32[1,2048]{1,0:T(1,128)S(1)} %solve_continuation.1), channel_id=1, source_target_pairs={{0,1},{1,0},{2,3},{3,2},{4,5},{5,4},{6,7},{7,6},{8,9},{9,8},{10,11... | collective-permute-start | bytes 24584 | tf_op jit(solution)/shard_map/ppermute | solution.py:147
  124.3 5.7 %collective-permute-start.15 = (f32[2,2048]{1,0:T(2,128)S(1)}, f32[2,2048]{1,0:T(2,128)S(1)}, u32[]{:S(2)}, u32[]{:S(2)}) collective-permute-start(f32[2,2048]{1,0:T(2,128)S(1)} %pad_maximum_fusion.2.refs_0_), channel_id=1, source_target_pairs={{0,2},{2,0},{4,6},{6,4},{1,3},{3,1},{5,7},{7,5},{8,10},{10,8},{12,... | collective-permute-start | bytes 49160 | tf_op jit(solution)/shard_map/ppermute | solution.py:147
  124.4 9.8 %collective-permute-start.16 = (f32[2,2048]{1,0:T(2,128)S(1)}, f32[2,2048]{1,0:T(2,128)S(1)}, u32[]{:S(2)}, u32[]{:S(2)}) collective-permute-start(f32[2,2048]{1,0:T(2,128)S(1)} %pad_maximum_fusion.2.refs_0_), channel_id=1, source_target_pairs={{0,4},{2,6},{4,0},{6,2},{1,5},{3,7},{5,1},{7,3},{8,12},{10,14},{12... | collective-permute-start | bytes 49160 | tf_op jit(solution)/shard_map/ppermute | solution.py:147
  127.3 6.9 %collective-permute-start.17 = (f32[2,2048]{1,0:T(2,128)S(1)}, f32[2,2048]{1,0:T(2,128)S(1)}, u32[]{:S(2)}, u32[]{:S(2)}) collective-permute-start(f32[2,2048]{1,0:T(2,128)S(1)} %pad_maximum_fusion.2.refs_0_), channel_id=1, source_target_pairs={{0,6},{2,4},{4,2},{6,0},{1,7},{3,5},{5,3},{7,1},{8,14},{10,12},{12... | collective-permute-start | bytes 49160 | tf_op jit(solution)/shard_map/ppermute | solution.py:147
  134.2 2.2 %copy-start = (bf16[4,32,16384]{2,1,0:T(8,128)(2,1)S(1)}, bf16[4,32,16384]{2,1,0:T(8,128)(2,1)}, u32[]{:S(2)}) copy-start(bf16[4,32,16384]{2,1,0:T(8,128)(2,1)} %refs_6_.1) | copy-start | bytes 12582916

commit v6 on v5

--- a/solution.py
+++ b/solution.py
@@ -12,8 +12,8 @@
 RIDGE = 0.1
 LANES = 128
 BLOCK = 128
-TILE = 512
-INCREMENT_TILE = 512
+TILE = 2048
+INCREMENT_TILE = 1024
 DATE_TILE = 2048
 STRIKE_BITS = 7
 STRIKE_ROWS = 1 << STRIKE_BITS
@@ -159,9 +159,9 @@
     return (piece_of(0) + parts[0]) + (parts[1] + parts[2]), beside
 
 
-def sum_over_others(share, axes, beside):
-    parts, beside = lax.optimization_barrier((exchange_with_others(share, axes, 4), beside))
-    return (share + parts[0]) + (parts[1] + parts[2]), beside
+def sum_of_exchange(share, axes):
+    parts = exchange_with_others(share, axes, 4)
+    return (share + parts[0]) + (parts[1] + parts[2])
 
 
 def gathered_sum(share):
@@ -450,8 +450,10 @@
     )
     share, moved = sum_over_cores_and_z(kept, other, moved)
     sent, weights = increments(moved, corr_gen, basket, slab_part)
-    share, sent = sum_over_others(share, "x", sent)
-    share, sent = sum_over_others(share, ("ylo", "yhi"), sent)
+    share = sum_of_exchange(share, "x")
+    parts = exchange_with_others(share, ("ylo", "yhi"), 4)
+    parts, sent = lax.optimization_barrier((parts, sent))
+    share = (share + parts[0]) + (parts[1] + parts[2])
     gains = lax.all_to_all(sent, STOCK_AXES, 0, 0, tiled=True)
     near, far = gathered_sum(share)
     continuation = solve_continuation(near, far, basis, path_count)

time: 158 us -> 156 us (0.987)
  Pallas kernels: 40.8 us -> 38 us
    pallas_call x1, Pallas kernels: 6.69 us -> 4.67 us  [regression_sums(): pl.pallas_call(gram_kernel, out_shape=(pltpu.HBM((512, slab_part), bf16),...]
  transfers between devices with their start and end apart: 21 -> 21, of which waited for: 14 -> 13; matrix products, arithmetic and copies ran while one was open for 2% -> 2% of each run, Pallas kernels for 20% -> 18%
where the time goes in v6:
time: 156 us; the launch traced here: 155 us
  waiting for transfers between devices  49.9 us (32%)
  starting transfers between devices  46.1 us (30%)
  Pallas kernels  38 us (24%)
  blocking collectives  10.7 us (7%)
  local copies, waits for them, and re-layouts  7.29 us (5%)
  other arithmetic  2.4 us (2%)
    ppermute x18, waiting for transfers between devices, exchange_with_others(): lax.ppermute(sent, axes, [(i, i ^ flip) for i in range(count)])  34.8 us
    ppermute x18, starting transfers between devices, exchange_with_others(): lax.ppermute(sent, axes, [(i, i ^ flip) for i in range(count)])  29.7 us
    pallas_call x1, Pallas kernels, solve_continuation(): pl.pallas_call(lambda *refs: solve_kernel(*refs, scale=1.0 / path_count),...  20.8 us
    all_to_all x1, waiting for transfers between devices, per_device(): lax.all_to_all(jnp.concatenate([pieces, table], axis=2), STOCK_AXES, 0, 0...  15 us
    all_to_all x1, blocking collectives, per_device(): surface = lax.all_to_all(surface, PATH_AXES, 0, 0, tiled=True)  10.7 us
    pallas_call x1, Pallas kernels, surface_and_delta(): pl.pallas_call(surface_kernel, out_shape=(jax.ShapeDtypeStruct((32, local...  9.54 us
    all_to_all x1, starting transfers between devices, per_device(): lax.all_to_all(jnp.concatenate([pieces, table], axis=2), STOCK_AXES, 0, 0...  7.61 us
    pallas_call x1, Pallas kernels, regression_sums(): pl.pallas_call(gram_kernel, out_shape=(pltpu.HBM((512, slab_part), bf16),...  4.67 us
  transfers between devices with their start and end apart: 21, of which 13 were waited for; matrix products, arithmetic and copies ran while one was open for 2% of the time, Pallas kernels for 18%

profile of v6, /device:TPU:1, one launch (start us, length us, event | category | flops | bytes accessed | tf_op | source)
XLA Modules:
  0.0 155.3 jit_solution(2344589499525559626)
XLA Ops:
  0.6 1.3 copy.27
  2.0 0.0 copy-start.1
  2.0 1.1 pad_maximum_fusion
  3.1 7.6 %all-to-all-start = ((bf16[8,32,2176]{2,1,0:T(8,128)(2,1)}), bf16[8,32,2176]{2,1,0:T(8,128)(2,1)S(1)}, u32[]{:S(2)}, u32[]{:S(2)}) async-start(bf16[8,32,2176]{2,1,0:T(8,128)(2,1)} %pad_maximum_fusion), calls=%async_computation | async-start | bytes 2228224 | tf_op jit(solution)/shard_map/all_to_all | solution.py:436
  10.7 0.0 copy-start.8
  10.7 1.1 copy.28
  11.9 15.0 %all-to-all-done.moved_ref.table_ref = bf16[8,32,2176]{2,1,0:T(8,128)(2,1)S(1)} async-done(((bf16[8,32,2176]{2,1,0:T(8,128)(2,1)}), bf16[8,32,2176]{2,1,0:T(8,128)(2,1)S(1)}, u32[]{:S(2)}, u32[]{:S(2)}) %all-to-all-start) | async-done | bytes 1114144 | tf_op jit(solution)/shard_map/all_to_all | solution.py:436
  26.9 4.2 %all-to-all-start.1 = ((bf16[8,32,2048]{2,1,0:T(8,128)(2,1)}), bf16[8,32,2048]{2,1,0:T(8,128)(2,1)S(1)}, u32[]{:S(2)}, u32[]{:S(2)}) async-start(bf16[8,32,2048]{2,1,0:T(8,128)(2,1)} %bitcast.38), calls=%async_computation.1 | async-start | bytes 2097152 | tf_op jit(solution)/shard_map/all_to_all | solution.py:444
  31.1 0.1 pad_add_fusion.1.slab_ref
  31.2 0.1 copy.20.bias_ref
  31.4 0.0 copy-start.9
  31.4 4.7 %regression_sums.1 = (bf16[512,2048]{1,0:T(8,128)(2,1)}, f32[672,128]{1,0:T(8,128)}, f32[672,128]{1,0:T(8,128)}) custom-call(s32[2]{0:T(128)S(1)} %pad_add_fusion.1.slab_ref, bf16[8,32,2176]{2,1,0:T(8,128)(2,1)S(1)} %all-to-all-done.moved_ref.table_ref, bf16[8,32,2176]{2,1,0:T(8,128)(2,1)S(1)} %all-to-all-done.moved_ref.table_ref, f32[32,512]{1,0:T(8,128)} %weight_ref, ...), custom_call_target="tpu_custom_call" | custom-call | tf_op jit(solution)/shard_map/regression_sums/pallas_call | solution.py:109
  36.1 1.2 collective-permute-start
  37.3 1.5 collective-permute-done
  38.8 1.0 add.49
  39.8 1.7 %collective-permute-start.1 = (f32[168,128]{1,0:T(8,128)S(1)}, f32[168,128]{1,0:T(8,128)S(1)}, u32[]{:S(2)}, u32[]{:S(2)}) collective-permute-start(f32[168,128]{1,0:T(8,128)S(1)} %get-tuple-element.48), channel_id=1, source_target_pairs={{0,32},{32,0},{64,96},{96,64},{1,33},{33,1},{65,97},{97,65},{2,34}... | collective-permute-start | bytes 258056 | tf_op jit(solution)/shard_map/ppermute | solution.py:147
  41.5 3.3 %collective-permute-start.2 = (f32[168,128]{1,0:T(8,128)S(1)}, f32[168,128]{1,0:T(8,128)S(1)}, u32[]{:S(2)}, u32[]{:S(2)}) collective-permute-start(f32[168,128]{1,0:T(8,128)S(1)} %get-tuple-element.47), channel_id=1, source_target_pairs={{0,64},{32,96},{64,0},{96,32},{1,65},{33,97},{65,1},{97,33},{2,66}... | collective-permute-start | bytes 258056 | tf_op jit(solution)/shard_map/ppermute | solution.py:147
  44.8 0.0 collective-permute-start.3
  44.9 0.0 collective-permute-done.1
  44.9 4.1 %collective-permute-done.2 = f32[168,128]{1,0:T(8,128)S(1)} collective-permute-done((f32[168,128]{1,0:T(8,128)S(1)}, f32[168,128]{1,0:T(8,128)S(1)}, u32[]{:S(2)}, u32[]{:S(2)}) %collective-permute-start.2) | collective-permute-done | bytes 86048 | tf_op jit(solution)/shard_map/ppermute | solution.py:147
  49.0 2.2 %collective-permute-done.3 = f32[168,128]{1,0:T(8,128)S(1)} collective-permute-done((f32[168,128]{1,0:T(8,128)S(1)}, f32[168,128]{1,0:T(8,128)S(1)}, u32[]{:S(2)}, u32[]{:S(2)}) %collective-permute-start.3) | collective-permute-done | bytes 86048 | tf_op jit(solution)/shard_map/ppermute | solution.py:147
  51.2 0.0 all-to-all-done.1.moved_ref
  51.2 1.8 %collective-permute-start.4 = (f32[168,128]{1,0:T(8,128)S(1)}, f32[168,128]{1,0:T(8,128)S(1)}, u32[]{:S(2)}, u32[]{:S(2)}) collective-permute-start(f32[168,128]{1,0:T(8,128)S(1)} %fusion), channel_id=1, source_target_pairs={{0,2},{2,0},{4,6},{6,4},{1,3},{3,1},{5,7},{7,5},{8,10},{10,8},{12,... | collective-permute-start | bytes 258056 | tf_op jit(solution)/shard_map/ppermute | solution.py:147
  53.0 2.4 %collective-permute-start.5 = (f32[168,128]{1,0:T(8,128)S(1)}, f32[168,128]{1,0:T(8,128)S(1)}, u32[]{:S(2)}, u32[]{:S(2)}) collective-permute-start(f32[168,128]{1,0:T(8,128)S(1)} %fusion), channel_id=1, source_target_pairs={{0,4},{2,6},{4,0},{6,2},{1,5},{3,7},{5,1},{7,3},{8,12},{10,14},{12... | collective-permute-start | bytes 258056 | tf_op jit(solution)/shard_map/ppermute | solution.py:147
  55.4 0.1 collective-permute-start.6
  55.5 0.0 collective-permute-done.4
  55.5 3.2 %collective-permute-done.5 = f32[168,128]{1,0:T(8,128)S(1)} collective-permute-done((f32[168,128]{1,0:T(8,128)S(1)}, f32[168,128]{1,0:T(8,128)S(1)}, u32[]{:S(2)}, u32[]{:S(2)}) %collective-permute-start.5) | collective-permute-done | bytes 86048 | tf_op jit(solution)/shard_map/ppermute | solution.py:147
  58.7 2.2 %collective-permute-done.6 = f32[168,128]{1,0:T(8,128)S(1)} collective-permute-done((f32[168,128]{1,0:T(8,128)S(1)}, f32[168,128]{1,0:T(8,128)S(1)}, u32[]{:S(2)}, u32[]{:S(2)}) %collective-permute-start.6) | collective-permute-done | bytes 86048 | tf_op jit(solution)/shard_map/ppermute | solution.py:147
  60.9 2.8 %collective-permute-start.7 = (f32[168,128]{1,0:T(8,128)S(1)}, f32[168,128]{1,0:T(8,128)S(1)}, u32[]{:S(2)}, u32[]{:S(2)}) collective-permute-start(f32[168,128]{1,0:T(8,128)S(1)} %add_add_fusion.1), channel_id=1, source_target_pairs={{0,1},{1,0},{16,17},{17,16},{2,3},{3,2},{18,19},{19,18},{4,5},{5,4... | collective-permute-start | bytes 258056 | tf_op jit(solution)/shard_map/ppermute | solution.py:147
  63.7 0.4 collective-permute-start.8
  64.1 0.2 collective-permute-start.9
  64.3 0.1 copy.21.basket_ref
  64.4 3.0 %increments.1 = (bf16[8,4,32,2048]{3,2,1,0:T(8,128)(2,1)}, f32[256,128]{1,0:T(8,128)S(1)}) custom-call(bf16[8,32,2048]{2,1,0:T(8,128)(2,1)S(1)} %all-to-all-done.1.moved_ref, bf16[256,256]{1,0:T(8,128)(2,1)S(1)} %copy-done.5, f32[256,1]{1,0:T(8,128)S(1)} %copy.21.basket_ref), custom_call_target="tpu_custom_call" | custom-call | tf_op jit(solution)/shard_map/increments/pallas_call | solution.py:327
  67.5 0.0 collective-permute-done.7
  67.5 0.0 collective-permute-done.8
  67.5 1.4 collective-permute-done.9
  68.8 4.5 %all-to-all-start.2 = ((bf16[8,4,32,2048]{3,2,1,0:T(8,128)(2,1)}), bf16[8,4,32,2048]{3,2,1,0:T(8,128)(2,1)}, u32[]{:S(2)}, u32[]{:S(2)}) async-start(bf16[8,4,32,2048]{3,2,1,0:T(8,128)(2,1)} %get-tuple-element.42), calls=%async_computation.2 | async-start | bytes 8388608 | tf_op jit(solution)/shard_map/all_to_all | solution.py:457
  73.4 0.0 copy-start.3
  73.4 0.0 copy-start.4
  73.4 0.1 collective-permute-start.10
  73.5 1.7 %collective-permute-start.11 = (f32[168,128]{1,0:T(8,128)S(1)}, f32[168,128]{1,0:T(8,128)S(1)}, u32[]{:S(2)}, u32[]{:S(2)}) collective-permute-start(f32[168,128]{1,0:T(8,128)S(1)} %add_add_fusion), channel_id=1, source_target_pairs={{0,64},{32,96},{64,0},{96,32},{1,65},{33,97},{65,1},{97,33},{2,66}... | collective-permute-start | bytes 258056 | tf_op jit(solution)/shard_map/ppermute | solution.py:147
  75.2 2.2 %collective-permute-start.12 = (f32[168,128]{1,0:T(8,128)S(1)}, f32[168,128]{1,0:T(8,128)S(1)}, u32[]{:S(2)}, u32[]{:S(2)}) collective-permute-start(f32[168,128]{1,0:T(8,128)S(1)} %add_add_fusion), channel_id=1, source_target_pairs={{0,96},{32,64},{64,32},{96,0},{1,97},{33,65},{65,33},{97,1},{2,98}... | collective-permute-start | bytes 258056 | tf_op jit(solution)/shard_map/ppermute | solution.py:147
  77.4 1.1 collective-permute-done.11
  78.5 1.3 collective-permute-done.12
  79.8 4.8 %collective-permute-start.13 = (f32[4,168,128]{2,1,0:T(8,128)S(1)}, f32[4,168,128]{2,1,0:T(8,128)S(1)}, u32[]{:S(2)}, u32[]{:S(2)}) collective-permute-start(f32[4,168,128]{2,1,0:T(8,128)S(1)} %pad_maximum_fusion.1.refs_1_), channel_id=1, source_target_pairs={{0,8},{8,0},{1,9},{9,1},{2,10},{10,2},{3,11},{11,3},{4,12},{12,4},... | collective-permute-start | bytes 1032200 | tf_op jit(solution)/shard_map/ppermute | solution.py:147
  84.6 0.1 pad_add_fusion.refs_0_
  84.7 1.2 collective-permute-done.13.refs_2_
  85.9 1.6 %copy-done.2 = bf16[512,2048]{1,0:T(8,128)(2,1)S(1)} copy-done((bf16[512,2048]{1,0:T(8,128)(2,1)S(1)}, bf16[512,2048]{1,0:T(8,128)(2,1)}, u32[]{:S(2)}) %copy-start.2) | copy-done | bytes 2097176
  87.5 20.8 %solve_continuation.1 = f32[1,2048]{1,0:T(1,128)S(1)} custom-call(s32[2]{0:T(128)S(1)} %pad_add_fusion.refs_0_, f32[4,168,128]{2,1,0:T(8,128)S(1)} %pad_maximum_fusion.1.refs_1_, f32[4,168,128]{2,1,0:T(8,128)S(1)} %collective-permute-done.13.refs_2_, bf16[512,2048]{1,0:T(8,128)(2,1)S(1)} %copy-done.2), custom_call_target="tpu_custom_call" | custom-call | tf_op jit(solution)/shard_map/solve_continuation/pallas_call | solution.py:277
  108.3 3.2 %collective-permute-start.14 = (f32[1,2048]{1,0:T(1,128)S(1)}, f32[1,2048]{1,0:T(1,128)S(1)}, u32[]{:S(2)}, u32[]{:S(2)}) collective-permute-start(f32[1,2048]{1,0:T(1,128)S(1)} %solve_continuation.1), channel_id=1, source_target_pairs={{0,1},{1,0},{2,3},{3,2},{4,5},{5,4},{6,7},{7,6},{8,9},{9,8},{10,11... | collective-permute-start | bytes 24584 | tf_op jit(solution)/shard_map/ppermute | solution.py:147
  111.4 10.8 %collective-permute-done.14 = f32[1,2048]{1,0:T(1,128)S(1)} collective-permute-done((f32[1,2048]{1,0:T(1,128)S(1)}, f32[1,2048]{1,0:T(1,128)S(1)}, u32[]{:S(2)}, u32[]{:S(2)}) %collective-permute-start.14) | collective-permute-done | bytes 8224 | tf_op jit(solution)/shard_map/ppermute | solution.py:147
  122.2 0.1 collective-permute-start.15
  122.3 2.9 %collective-permute-start.16 = (f32[2,2048]{1,0:T(2,128)S(1)}, f32[2,2048]{1,0:T(2,128)S(1)}, u32[]{:S(2)}, u32[]{:S(2)}) collective-permute-start(f32[2,2048]{1,0:T(2,128)S(1)} %pad_maximum_fusion.2.refs_0_), channel_id=1, source_target_pairs={{0,4},{2,6},{4,0},{6,2},{1,5},{3,7},{5,1},{7,3},{8,12},{10,14},{12... | collective-permute-start | bytes 49160 | tf_op jit(solution)/shard_map/ppermute | solution.py:147
  125.2 0.9 collective-permute-start.17
  126.2 1.7 %collective-permute-done.15.refs_1_ = f32[2,2048]{1,0:T(2,128)S(1)} collective-permute-done((f32[2,2048]{1,0:T(2,128)S(1)}, f32[2,2048]{1,0:T(2,128)S(1)}, u32[]{:S(2)}, u32[]{:S(2)}) %collective-permute-start.15) | collective-permute-done | bytes 16416 | tf_op jit(solution)/shard_map/ppermute | solution.py:147
  127.9 4.2 %collective-permute-done.16.refs_2_ = f32[2,2048]{1,0:T(2,128)S(1)} collective-permute-done((f32[2,2048]{1,0:T(2,128)S(1)}, f32[2,2048]{1,0:T(2,128)S(1)}, u32[]{:S(2)}, u32[]{:S(2)}) %collective-permute-start.16) | collective-permute-done | bytes 16416 | tf_op jit(solution)/shard_map/ppermute | solution.py:147
  132.1 0.0 collective-permute-done.17.refs_3_
  132.1 0.0 all-to-all-done.2.refs_5_
  132.1 0.0 copy-start
  132.1 2.2 %copy-done = bf16[4,32,16384]{2,1,0:T(8,128)(2,1)S(1)} copy-done((bf16[4,32,16384]{2,1,0:T(8,128)(2,1)S(1)}, bf16[4,32,16384]{2,1,0:T(8,128)(2,1)}, u32[]{:S(2)}) %copy-start) | copy-done | bytes 4194328
  134.3 9.5 %surface_and_delta.1 = (f32[32,16384]{1,0:T(8,128)}, f32[16,4,128]{2,1,0:T(4,128)S(1)}) custom-call(s32[1]{0:T(128)} %bitcast.slab_ref, f32[2,2048]{1,0:T(2,128)S(1)} %pad_maximum_fusion.2.refs_0_, f32[2,2048]{1,0:T(2,128)S(1)} %collective-permute-done.15.refs_1_, f32[2,2048]{1,0:T(2,128)S(1)} %collective-permute-done.16.refs_2_, ...), custom_call_target="tpu_custom_call" | custom-call | tf_op jit(solution)/shard_map/surface_and_delta/pallas_call | solution.py:399
  143.8 10.7 %all_to_all.20 = f32[16,4,128]{2,1,0:T(4,128)S(1)} all-to-all(f32[16,4,128]{2,1,0:T(4,128)S(1)} %get-tuple-element.45), channel_id=1, replica_groups=mesh['z'=4,'ylo'=2,'core'=2,'x'=4,'yhi'=2] {'z','ylo','core'}, dimensions={0} | all-to-all | bytes 65536 | tf_op jit(solution)/shard_map/all_to_all | solution.py:465
  154.6 0.1 reshape.27
  154.7 0.6 copy.22
  (23 shorter events, 0.3 us)
Async XLA Ops:
  0.6 1.3 copy-start.7
  2.0 8.7 %copy-start.1 = (bf16[32,16384]{1,0:T(8,128)(2,1)S(1)}, bf16[32,16384]{1,0:T(8,128)(2,1)}, u32[]{:S(2)}) copy-start(bf16[32,16384]{1,0:T(8,128)(2,1)} %refs_4_.1) | copy-start | bytes 3145732
  3.1 8.7 %copy-start.6 = (bf16[16384]{0:T(1024)(128)(2,1)S(1)}, bf16[16384]{0:T(1024)(128)(2,1)}, u32[]{:S(2)}) copy-start(bf16[16384]{0:T(1024)(128)(2,1)} %param.16) | copy-start | bytes 98308
  3.1 23.8 %all-to-all-start = ((bf16[8,32,2176]{2,1,0:T(8,128)(2,1)}), bf16[8,32,2176]{2,1,0:T(8,128)(2,1)S(1)}, u32[]{:S(2)}, u32[]{:S(2)}) async-start(bf16[8,32,2176]{2,1,0:T(8,128)(2,1)} %pad_maximum_fusion), calls=%async_computation | async-start | bytes 2228224 | tf_op jit(solution)/shard_map/all_to_all | solution.py:436
  10.7 20.5 %copy-start.8 = (f32[512]{0:T(512)S(1)}, f32[512]{0:T(512)}, u32[]{:S(2)}) copy-start(f32[512]{0:T(512)} %param.15) | copy-start | bytes 6148
  26.9 24.2 %all-to-all-start.1 = ((bf16[8,32,2048]{2,1,0:T(8,128)(2,1)}), bf16[8,32,2048]{2,1,0:T(8,128)(2,1)S(1)}, u32[]{:S(2)}, u32[]{:S(2)}) async-start(bf16[8,32,2048]{2,1,0:T(8,128)(2,1)} %bitcast.38), calls=%async_computation.1 | async-start | bytes 2097152 | tf_op jit(solution)/shard_map/all_to_all | solution.py:444
  31.4 32.9 %copy-start.9 = (f32[256]{0:T(256)S(1)}, f32[256]{0:T(256)}, u32[]{:S(2)}) copy-start(f32[256]{0:T(256)} %param.21) | copy-start | bytes 3076
  36.1 28.3 %copy-start.5 = (bf16[256,256]{1,0:T(8,128)(2,1)S(1)}, bf16[256,256]{1,0:T(8,128)(2,1)}, u32[]{:S(2)}) copy-start(bf16[256,256]{1,0:T(8,128)(2,1)} %mixer_ref.1) | copy-start | bytes 393220
  36.1 2.7 %collective-permute-start = (f32[672,128]{1,0:T(8,128)}, f32[672,128]{1,0:T(8,128)S(1)}, u32[]{:S(2)}, u32[]{:S(2)}) collective-permute-start(f32[672,128]{1,0:T(8,128)} %get-tuple-element.30), channel_id=1, source_target_pairs={{0,8},{8,0},{1,9},{9,1},{2,10},{10,2},{3,11},{11,3},{4,12},{12,4},... | collective-permute-start | bytes 1032200 | tf_op jit(solution)/shard_map/ppermute | solution.py:147
  39.8 5.0 %collective-permute-start.1 = (f32[168,128]{1,0:T(8,128)S(1)}, f32[168,128]{1,0:T(8,128)S(1)}, u32[]{:S(2)}, u32[]{:S(2)}) collective-permute-start(f32[168,128]{1,0:T(8,128)S(1)} %get-tuple-element.48), channel_id=1, source_target_pairs={{0,32},{32,0},{64,96},{96,64},{1,33},{33,1},{65,97},{97,65},{2,34}... | collective-permute-start | bytes 258056 | tf_op jit(solution)/shard_map/ppermute | solution.py:147
  41.5 7.4 %collective-permute-start.2 = (f32[168,128]{1,0:T(8,128)S(1)}, f32[168,128]{1,0:T(8,128)S(1)}, u32[]{:S(2)}, u32[]{:S(2)}) collective-permute-start(f32[168,128]{1,0:T(8,128)S(1)} %get-tuple-element.47), channel_id=1, source_target_pairs={{0,64},{32,96},{64,0},{96,32},{1,65},{33,97},{65,1},{97,33},{2,66}... | collective-permute-start | bytes 258056 | tf_op jit(solution)/shard_map/ppermute | solution.py:147
  44.8 6.3 %collective-permute-start.3 = (f32[168,128]{1,0:T(8,128)S(1)}, f32[168,128]{1,0:T(8,128)S(1)}, u32[]{:S(2)}, u32[]{:S(2)}) collective-permute-start(f32[168,128]{1,0:T(8,128)S(1)} %get-tuple-element.46), channel_id=1, source_target_pairs={{0,96},{32,64},{64,32},{96,0},{1,97},{33,65},{65,33},{97,1},{2,98}... | collective-permute-start | bytes 258056 | tf_op jit(solution)/shard_map/ppermute | solution.py:147
  51.2 4.3 %collective-permute-start.4 = (f32[168,128]{1,0:T(8,128)S(1)}, f32[168,128]{1,0:T(8,128)S(1)}, u32[]{:S(2)}, u32[]{:S(2)}) collective-permute-start(f32[168,128]{1,0:T(8,128)S(1)} %fusion), channel_id=1, source_target_pairs={{0,2},{2,0},{4,6},{6,4},{1,3},{3,1},{5,7},{7,5},{8,10},{10,8},{12,... | collective-permute-start | bytes 258056 | tf_op jit(solution)/shard_map/ppermute | solution.py:147
  53.0 5.7 %collective-permute-start.5 = (f32[168,128]{1,0:T(8,128)S(1)}, f32[168,128]{1,0:T(8,128)S(1)}, u32[]{:S(2)}, u32[]{:S(2)}) collective-permute-start(f32[168,128]{1,0:T(8,128)S(1)} %fusion), channel_id=1, source_target_pairs={{0,4},{2,6},{4,0},{6,2},{1,5},{3,7},{5,1},{7,3},{8,12},{10,14},{12... | collective-permute-start | bytes 258056 | tf_op jit(solution)/shard_map/ppermute | solution.py:147
  55.4 5.5 %collective-permute-start.6 = (f32[168,128]{1,0:T(8,128)S(1)}, f32[168,128]{1,0:T(8,128)S(1)}, u32[]{:S(2)}, u32[]{:S(2)}) collective-permute-start(f32[168,128]{1,0:T(8,128)S(1)} %fusion), channel_id=1, source_target_pairs={{0,6},{2,4},{4,2},{6,0},{1,7},{3,5},{5,3},{7,1},{8,14},{10,12},{12... | collective-permute-start | bytes 258056 | tf_op jit(solution)/shard_map/ppermute | solution.py:147
  60.9 6.5 %collective-permute-start.7 = (f32[168,128]{1,0:T(8,128)S(1)}, f32[168,128]{1,0:T(8,128)S(1)}, u32[]{:S(2)}, u32[]{:S(2)}) collective-permute-start(f32[168,128]{1,0:T(8,128)S(1)} %add_add_fusion.1), channel_id=1, source_target_pairs={{0,1},{1,0},{16,17},{17,16},{2,3},{3,2},{18,19},{19,18},{4,5},{5,4... | collective-permute-start | bytes 258056 | tf_op jit(solution)/shard_map/ppermute | solution.py:147
  63.7 3.8 %collective-permute-start.8 = (f32[168,128]{1,0:T(8,128)S(1)}, f32[168,128]{1,0:T(8,128)S(1)}, u32[]{:S(2)}, u32[]{:S(2)}) collective-permute-start(f32[168,128]{1,0:T(8,128)S(1)} %add_add_fusion.1), channel_id=1, source_target_pairs={{0,16},{1,17},{16,0},{17,1},{2,18},{3,19},{18,2},{19,3},{4,20},{5,... | collective-permute-start | bytes 258056 | tf_op jit(solution)/shard_map/ppermute | solution.py:147
  64.1 4.8 %collective-permute-start.9 = (f32[168,128]{1,0:T(8,128)S(1)}, f32[168,128]{1,0:T(8,128)S(1)}, u32[]{:S(2)}, u32[]{:S(2)}) collective-permute-start(f32[168,128]{1,0:T(8,128)S(1)} %add_add_fusion.1), channel_id=1, source_target_pairs={{0,17},{1,16},{16,1},{17,0},{2,19},{3,18},{18,3},{19,2},{4,21},{5,... | collective-permute-start | bytes 258056 | tf_op jit(solution)/shard_map/ppermute | solution.py:147
  68.8 63.2 %all-to-all-start.2 = ((bf16[8,4,32,2048]{3,2,1,0:T(8,128)(2,1)}), bf16[8,4,32,2048]{3,2,1,0:T(8,128)(2,1)}, u32[]{:S(2)}, u32[]{:S(2)}) async-start(bf16[8,4,32,2048]{3,2,1,0:T(8,128)(2,1)} %get-tuple-element.42), calls=%async_computation.2 | async-start | bytes 8388608 | tf_op jit(solution)/shard_map/all_to_all | solution.py:457
  73.4 58.7 %copy-start.3 = (s32[4,16384]{1,0:T(4,128)S(1)}, s32[4,16384]{1,0:T(4,128)}, u32[]{:S(2)}) copy-start(s32[4,16384]{1,0:T(4,128)} %refs_8_.1) | copy-start | bytes 786436
  73.4 58.7 %copy-start.4 = (s32[4,16384]{1,0:T(4,128)S(1)}, s32[4,16384]{1,0:T(4,128)}, u32[]{:S(2)}) copy-start(s32[4,16384]{1,0:T(4,128)} %refs_9_.1) | copy-start | bytes 786436
  73.4 3.9 %collective-permute-start.10 = (f32[168,128]{1,0:T(8,128)S(1)}, f32[168,128]{1,0:T(8,128)S(1)}, u32[]{:S(2)}, u32[]{:S(2)}) collective-permute-start(f32[168,128]{1,0:T(8,128)S(1)} %add_add_fusion), channel_id=1, source_target_pairs={{0,32},{32,0},{64,96},{96,64},{1,33},{33,1},{65,97},{97,65},{2,34}... | collective-permute-start | bytes 258056 | tf_op jit(solution)/shard_map/ppermute | solution.py:147
  73.5 4.9 %collective-permute-start.11 = (f32[168,128]{1,0:T(8,128)S(1)}, f32[168,128]{1,0:T(8,128)S(1)}, u32[]{:S(2)}, u32[]{:S(2)}) collective-permute-start(f32[168,128]{1,0:T(8,128)S(1)} %add_add_fusion), channel_id=1, source_target_pairs={{0,64},{32,96},{64,0},{96,32},{1,65},{33,97},{65,1},{97,33},{2,66}... | collective-permute-start | bytes 258056 | tf_op jit(solution)/shard_map/ppermute | solution.py:147
  75.2 4.5 %collective-permute-start.12 = (f32[168,128]{1,0:T(8,128)S(1)}, f32[168,128]{1,0:T(8,128)S(1)}, u32[]{:S(2)}, u32[]{:S(2)}) collective-permute-start(f32[168,128]{1,0:T(8,128)S(1)} %add_add_fusion), channel_id=1, source_target_pairs={{0,96},{32,64},{64,32},{96,0},{1,97},{33,65},{65,33},{97,1},{2,98}... | collective-permute-start | bytes 258056 | tf_op jit(solution)/shard_map/ppermute | solution.py:147
  79.8 6.1 %collective-permute-start.13 = (f32[4,168,128]{2,1,0:T(8,128)S(1)}, f32[4,168,128]{2,1,0:T(8,128)S(1)}, u32[]{:S(2)}, u32[]{:S(2)}) collective-permute-start(f32[4,168,128]{2,1,0:T(8,128)S(1)} %pad_maximum_fusion.1.refs_1_), channel_id=1, source_target_pairs={{0,8},{8,0},{1,9},{9,1},{2,10},{10,2},{3,11},{11,3},{4,12},{12,4},... | collective-permute-start | bytes 1032200 | tf_op jit(solution)/shard_map/ppermute | solution.py:147
  85.9 1.6 %copy-start.2 = (bf16[512,2048]{1,0:T(8,128)(2,1)S(1)}, bf16[512,2048]{1,0:T(8,128)(2,1)}, u32[]{:S(2)}) copy-start(bf16[512,2048]{1,0:T(8,128)(2,1)} %get-tuple-element.41.refs_3_) | copy-start | bytes 6291460
  108.3 13.9 %collective-permute-start.14 = (f32[1,2048]{1,0:T(1,128)S(1)}, f32[1,2048]{1,0:T(1,128)S(1)}, u32[]{:S(2)}, u32[]{:S(2)}) collective-permute-start(f32[1,2048]{1,0:T(1,128)S(1)} %solve_continuation.1), channel_id=1, source_target_pairs={{0,1},{1,0},{2,3},{3,2},{4,5},{5,4},{6,7},{7,6},{8,9},{9,8},{10,11... | collective-permute-start | bytes 24584 | tf_op jit(solution)/shard_map/ppermute | solution.py:147
  122.2 5.7 %collective-permute-start.15 = (f32[2,2048]{1,0:T(2,128)S(1)}, f32[2,2048]{1,0:T(2,128)S(1)}, u32[]{:S(2)}, u32[]{:S(2)}) collective-permute-start(f32[2,2048]{1,0:T(2,128)S(1)} %pad_maximum_fusion.2.refs_0_), channel_id=1, source_target_pairs={{0,2},{2,0},{4,6},{6,4},{1,3},{3,1},{5,7},{7,5},{8,10},{10,8},{12,... | collective-permute-start | bytes 49160 | tf_op jit(solution)/shard_map/ppermute | solution.py:147
  122.3 9.8 %collective-permute-start.16 = (f32[2,2048]{1,0:T(2,128)S(1)}, f32[2,2048]{1,0:T(2,128)S(1)}, u32[]{:S(2)}, u32[]{:S(2)}) collective-permute-start(f32[2,2048]{1,0:T(2,128)S(1)} %pad_maximum_fusion.2.refs_0_), channel_id=1, source_target_pairs={{0,4},{2,6},{4,0},{6,2},{1,5},{3,7},{5,1},{7,3},{8,12},{10,14},{12... | collective-permute-start | bytes 49160 | tf_op jit(solution)/shard_map/ppermute | solution.py:147
  125.2 6.9 %collective-permute-start.17 = (f32[2,2048]{1,0:T(2,128)S(1)}, f32[2,2048]{1,0:T(2,128)S(1)}, u32[]{:S(2)}, u32[]{:S(2)}) collective-permute-start(f32[2,2048]{1,0:T(2,128)S(1)} %pad_maximum_fusion.2.refs_0_), channel_id=1, source_target_pairs={{0,6},{2,4},{4,2},{6,0},{1,7},{3,5},{5,3},{7,1},{8,14},{10,12},{12... | collective-permute-start | bytes 49160 | tf_op jit(solution)/shard_map/ppermute | solution.py:147
  132.1 2.2 %copy-start = (bf16[4,32,16384]{2,1,0:T(8,128)(2,1)S(1)}, bf16[4,32,16384]{2,1,0:T(8,128)(2,1)}, u32[]{:S(2)}) copy-start(bf16[4,32,16384]{2,1,0:T(8,128)(2,1)} %refs_6_.1) | copy-start | bytes 12582916

commit v7 on v6

--- a/solution.py
+++ b/solution.py
@@ -292,6 +292,10 @@
     )(at, near, far, basis)
 
 
+def in_hbm(x):
+    return pltpu.with_memory_space_constraint(x, pltpu.HBM)
+
+
 def increments_kernel(moved_ref, mixer_ref, basket_ref, sent_ref, weights_ref, buffer_ref, copied):
     copies = []
     for tile in range(moved_ref.shape[2] // INCREMENT_TILE):
@@ -421,7 +425,7 @@
         ),
         compiler_params=pltpu.CompilerParams(vmem_limit_bytes=32 << 20),
         name="surface_and_delta",
-    )(slab, *continuations, cotangent, gains, shocks, weights, exercise, bucket)
+    )(slab, *continuations, cotangent, gains, in_hbm(shocks), weights, exercise, bucket)
 
 
 def per_device(prices, loadings, basis_w, basis_bias, payoff, in_fit, cotangent, shocks, corr_gen,
@@ -442,8 +446,8 @@
     slabs, moved_prices, small = lax.optimization_barrier((slabs, moved_prices, small))
     basis_w, bias, payoff, in_fit, basket = small
     moved = lax.all_to_all(slabs, STOCK_AXES, 0, 0, tiled=True)
-    basis_w = pltpu.with_memory_space_constraint(basis_w, pltpu.HBM)
-    in_fit = pltpu.with_memory_space_constraint(in_fit, pltpu.HBM)
+    basis_w = in_hbm(basis_w)
+    in_fit = in_hbm(in_fit)
     place = jnp.stack([slab[0], lax.axis_index("core").astype(jnp.int32)])
     basis, kept, other = regression_sums(
         place, moved_prices, basis_w, bias, payoff, in_fit, slab_part

time: 156 us -> 155 us (level)
  local copies, waits for them, and re-layouts: 7.29 us -> 5.11 us
    unnamed x20 -> x18, local copies, waits for them, and re-layouts: 3.82 us -> 1.63 us
  transfers between devices with their start and end apart: 21 -> 21, of which waited for: 13 -> 13; matrix products, arithmetic and copies ran while one was open for 2% -> 2% of each run, Pallas kernels for 18% -> 19%
where the time goes in v7:
time: 155 us; the launch traced here: 154 us
  waiting for transfers between devices  49.9 us (32%)
  starting transfers between devices  46.1 us (30%)
  Pallas kernels  38.8 us (25%)
  blocking collectives  10.7 us (7%)
  local copies, waits for them, and re-layouts  5.11 us (3%)
  other arithmetic  2.4 us (2%)
    ppermute x18, waiting for transfers between devices, exchange_with_others(): lax.ppermute(sent, axes, [(i, i ^ flip) for i in range(count)])  34.8 us
    ppermute x18, starting transfers between devices, exchange_with_others(): lax.ppermute(sent, axes, [(i, i ^ flip) for i in range(count)])  29.8 us
    pallas_call x1, Pallas kernels, solve_continuation(): pl.pallas_call(lambda *refs: solve_kernel(*refs, scale=1.0 / path_count),...  20.8 us
    all_to_all x1, waiting for transfers between devices, per_device(): lax.all_to_all(jnp.concatenate([pieces, table], axis=2), STOCK_AXES, 0, 0...  15 us
    all_to_all x1, blocking collectives, per_device(): surface = lax.all_to_all(surface, PATH_AXES, 0, 0, tiled=True)  10.7 us
    pallas_call x1, Pallas kernels, surface_and_delta(): pl.pallas_call(surface_kernel, out_shape=(jax.ShapeDtypeStruct((32, local...  10.3 us
    all_to_all x1, starting transfers between devices, per_device(): lax.all_to_all(jnp.concatenate([pieces, table], axis=2), STOCK_AXES, 0, 0...  7.61 us
    pallas_call x1, Pallas kernels, regression_sums(): pl.pallas_call(gram_kernel, out_shape=(pltpu.HBM((512, slab_part), bf16),...  4.68 us
  transfers between devices with their start and end apart: 21, of which 13 were waited for; matrix products, arithmetic and copies ran while one was open for 2% of the time, Pallas kernels for 19%

profile of v7, /device:TPU:1, one launch (start us, length us, event | category | flops | bytes accessed | tf_op | source)
XLA Modules:
  0.0 153.8 jit_solution(2479642247346251665)
XLA Ops:
  0.6 1.3 copy.27
  2.0 0.0 copy-start
  2.0 1.1 pad_maximum_fusion
  3.1 7.6 %all-to-all-start = ((bf16[8,32,2176]{2,1,0:T(8,128)(2,1)}), bf16[8,32,2176]{2,1,0:T(8,128)(2,1)S(1)}, u32[]{:S(2)}, u32[]{:S(2)}) async-start(bf16[8,32,2176]{2,1,0:T(8,128)(2,1)} %pad_maximum_fusion), calls=%async_computation | async-start | bytes 2228224 | tf_op jit(solution)/shard_map/all_to_all | solution.py:440
  10.7 0.0 copy-start.7
  10.7 1.1 copy.28
  11.9 15.0 %all-to-all-done.moved_ref.table_ref = bf16[8,32,2176]{2,1,0:T(8,128)(2,1)S(1)} async-done(((bf16[8,32,2176]{2,1,0:T(8,128)(2,1)}), bf16[8,32,2176]{2,1,0:T(8,128)(2,1)S(1)}, u32[]{:S(2)}, u32[]{:S(2)}) %all-to-all-start) | async-done | bytes 1114144 | tf_op jit(solution)/shard_map/all_to_all | solution.py:440
  26.9 4.2 %all-to-all-start.1 = ((bf16[8,32,2048]{2,1,0:T(8,128)(2,1)}), bf16[8,32,2048]{2,1,0:T(8,128)(2,1)S(1)}, u32[]{:S(2)}, u32[]{:S(2)}) async-start(bf16[8,32,2048]{2,1,0:T(8,128)(2,1)} %bitcast.38), calls=%async_computation.1 | async-start | bytes 2097152 | tf_op jit(solution)/shard_map/all_to_all | solution.py:448
  31.1 0.1 pad_add_fusion.1.slab_ref
  31.2 0.1 copy.20.bias_ref
  31.4 0.0 copy-start.8
  31.4 4.7 %regression_sums.1 = (bf16[512,2048]{1,0:T(8,128)(2,1)}, f32[672,128]{1,0:T(8,128)}, f32[672,128]{1,0:T(8,128)}) custom-call(s32[2]{0:T(128)S(1)} %pad_add_fusion.1.slab_ref, bf16[8,32,2176]{2,1,0:T(8,128)(2,1)S(1)} %all-to-all-done.moved_ref.table_ref, bf16[8,32,2176]{2,1,0:T(8,128)(2,1)S(1)} %all-to-all-done.moved_ref.table_ref, f32[32,512]{1,0:T(8,128)} %weight_ref, ...), custom_call_target="tpu_custom_call" | custom-call | tf_op jit(solution)/shard_map/regression_sums/pallas_call | solution.py:109
  36.1 1.2 collective-permute-start
  37.3 1.5 collective-permute-done
  38.8 1.0 add.49
  39.8 1.7 %collective-permute-start.1 = (f32[168,128]{1,0:T(8,128)S(1)}, f32[168,128]{1,0:T(8,128)S(1)}, u32[]{:S(2)}, u32[]{:S(2)}) collective-permute-start(f32[168,128]{1,0:T(8,128)S(1)} %get-tuple-element.48), channel_id=1, source_target_pairs={{0,32},{32,0},{64,96},{96,64},{1,33},{33,1},{65,97},{97,65},{2,34}... | collective-permute-start | bytes 258056 | tf_op jit(solution)/shard_map/ppermute | solution.py:147
  41.6 3.3 %collective-permute-start.2 = (f32[168,128]{1,0:T(8,128)S(1)}, f32[168,128]{1,0:T(8,128)S(1)}, u32[]{:S(2)}, u32[]{:S(2)}) collective-permute-start(f32[168,128]{1,0:T(8,128)S(1)} %get-tuple-element.47), channel_id=1, source_target_pairs={{0,64},{32,96},{64,0},{96,32},{1,65},{33,97},{65,1},{97,33},{2,66}... | collective-permute-start | bytes 258056 | tf_op jit(solution)/shard_map/ppermute | solution.py:147
  44.9 0.0 collective-permute-start.3
  44.9 0.0 collective-permute-done.1
  44.9 4.1 %collective-permute-done.2 = f32[168,128]{1,0:T(8,128)S(1)} collective-permute-done((f32[168,128]{1,0:T(8,128)S(1)}, f32[168,128]{1,0:T(8,128)S(1)}, u32[]{:S(2)}, u32[]{:S(2)}) %collective-permute-start.2) | collective-permute-done | bytes 86048 | tf_op jit(solution)/shard_map/ppermute | solution.py:147
  49.0 2.2 %collective-permute-done.3 = f32[168,128]{1,0:T(8,128)S(1)} collective-permute-done((f32[168,128]{1,0:T(8,128)S(1)}, f32[168,128]{1,0:T(8,128)S(1)}, u32[]{:S(2)}, u32[]{:S(2)}) %collective-permute-start.3) | collective-permute-done | bytes 86048 | tf_op jit(solution)/shard_map/ppermute | solution.py:147
  51.2 0.0 all-to-all-done.1.moved_ref
  51.2 1.8 %collective-permute-start.4 = (f32[168,128]{1,0:T(8,128)S(1)}, f32[168,128]{1,0:T(8,128)S(1)}, u32[]{:S(2)}, u32[]{:S(2)}) collective-permute-start(f32[168,128]{1,0:T(8,128)S(1)} %fusion), channel_id=1, source_target_pairs={{0,2},{2,0},{4,6},{6,4},{1,3},{3,1},{5,7},{7,5},{8,10},{10,8},{12,... | collective-permute-start | bytes 258056 | tf_op jit(solution)/shard_map/ppermute | solution.py:147
  53.0 2.4 %collective-permute-start.5 = (f32[168,128]{1,0:T(8,128)S(1)}, f32[168,128]{1,0:T(8,128)S(1)}, u32[]{:S(2)}, u32[]{:S(2)}) collective-permute-start(f32[168,128]{1,0:T(8,128)S(1)} %fusion), channel_id=1, source_target_pairs={{0,4},{2,6},{4,0},{6,2},{1,5},{3,7},{5,1},{7,3},{8,12},{10,14},{12... | collective-permute-start | bytes 258056 | tf_op jit(solution)/shard_map/ppermute | solution.py:147
  55.4 0.1 collective-permute-start.6
  55.5 0.0 collective-permute-done.4
  55.5 3.2 %collective-permute-done.5 = f32[168,128]{1,0:T(8,128)S(1)} collective-permute-done((f32[168,128]{1,0:T(8,128)S(1)}, f32[168,128]{1,0:T(8,128)S(1)}, u32[]{:S(2)}, u32[]{:S(2)}) %collective-permute-start.5) | collective-permute-done | bytes 86048 | tf_op jit(solution)/shard_map/ppermute | solution.py:147
  58.7 2.2 %collective-permute-done.6 = f32[168,128]{1,0:T(8,128)S(1)} collective-permute-done((f32[168,128]{1,0:T(8,128)S(1)}, f32[168,128]{1,0:T(8,128)S(1)}, u32[]{:S(2)}, u32[]{:S(2)}) %collective-permute-start.6) | collective-permute-done | bytes 86048 | tf_op jit(solution)/shard_map/ppermute | solution.py:147
  60.9 2.8 %collective-permute-start.7 = (f32[168,128]{1,0:T(8,128)S(1)}, f32[168,128]{1,0:T(8,128)S(1)}, u32[]{:S(2)}, u32[]{:S(2)}) collective-permute-start(f32[168,128]{1,0:T(8,128)S(1)} %add_add_fusion.1), channel_id=1, source_target_pairs={{0,1},{1,0},{16,17},{17,16},{2,3},{3,2},{18,19},{19,18},{4,5},{5,4... | collective-permute-start | bytes 258056 | tf_op jit(solution)/shard_map/ppermute | solution.py:147
  63.7 0.4 collective-permute-start.8
  64.1 0.2 collective-permute-start.9
  64.3 0.1 copy.21.basket_ref
  64.4 3.1 %increments.1 = (bf16[8,4,32,2048]{3,2,1,0:T(8,128)(2,1)}, f32[256,128]{1,0:T(8,128)S(1)}) custom-call(bf16[8,32,2048]{2,1,0:T(8,128)(2,1)S(1)} %all-to-all-done.1.moved_ref, bf16[256,256]{1,0:T(8,128)(2,1)S(1)} %copy-done.4, f32[256,1]{1,0:T(8,128)S(1)} %copy.21.basket_ref), custom_call_target="tpu_custom_call" | custom-call | tf_op jit(solution)/shard_map/increments/pallas_call | solution.py:331
  67.5 0.0 collective-permute-done.7
  67.5 0.0 collective-permute-done.8
  67.5 1.3 collective-permute-done.9
  68.9 4.5 %all-to-all-start.2 = ((bf16[8,4,32,2048]{3,2,1,0:T(8,128)(2,1)}), bf16[8,4,32,2048]{3,2,1,0:T(8,128)(2,1)}, u32[]{:S(2)}, u32[]{:S(2)}) async-start(bf16[8,4,32,2048]{3,2,1,0:T(8,128)(2,1)} %get-tuple-element.42), calls=%async_computation.2 | async-start | bytes 8388608 | tf_op jit(solution)/shard_map/all_to_all | solution.py:461
  73.4 0.0 copy-start.2
  73.4 0.0 copy-start.3
  73.5 0.1 collective-permute-start.10
  73.6 1.7 %collective-permute-start.11 = (f32[168,128]{1,0:T(8,128)S(1)}, f32[168,128]{1,0:T(8,128)S(1)}, u32[]{:S(2)}, u32[]{:S(2)}) collective-permute-start(f32[168,128]{1,0:T(8,128)S(1)} %add_add_fusion), channel_id=1, source_target_pairs={{0,64},{32,96},{64,0},{96,32},{1,65},{33,97},{65,1},{97,33},{2,66}... | collective-permute-start | bytes 258056 | tf_op jit(solution)/shard_map/ppermute | solution.py:147
  75.2 2.2 %collective-permute-start.12 = (f32[168,128]{1,0:T(8,128)S(1)}, f32[168,128]{1,0:T(8,128)S(1)}, u32[]{:S(2)}, u32[]{:S(2)}) collective-permute-start(f32[168,128]{1,0:T(8,128)S(1)} %add_add_fusion), channel_id=1, source_target_pairs={{0,96},{32,64},{64,32},{96,0},{1,97},{33,65},{65,33},{97,1},{2,98}... | collective-permute-start | bytes 258056 | tf_op jit(solution)/shard_map/ppermute | solution.py:147
  77.4 0.0 collective-permute-done.10
  77.4 1.1 collective-permute-done.11
  78.5 1.3 collective-permute-done.12
  79.8 4.8 %collective-permute-start.13 = (f32[4,168,128]{2,1,0:T(8,128)S(1)}, f32[4,168,128]{2,1,0:T(8,128)S(1)}, u32[]{:S(2)}, u32[]{:S(2)}) collective-permute-start(f32[4,168,128]{2,1,0:T(8,128)S(1)} %pad_maximum_fusion.1.refs_1_), channel_id=1, source_target_pairs={{0,8},{8,0},{1,9},{9,1},{2,10},{10,2},{3,11},{11,3},{4,12},{12,4},... | collective-permute-start | bytes 1032200 | tf_op jit(solution)/shard_map/ppermute | solution.py:147
  84.6 0.1 pad_add_fusion.refs_0_
  84.7 1.2 collective-permute-done.13.refs_2_
  85.9 1.6 %copy-done.1 = bf16[512,2048]{1,0:T(8,128)(2,1)S(1)} copy-done((bf16[512,2048]{1,0:T(8,128)(2,1)S(1)}, bf16[512,2048]{1,0:T(8,128)(2,1)}, u32[]{:S(2)}) %copy-start.1) | copy-done | bytes 2097176
  87.5 20.8 %solve_continuation.1 = f32[1,2048]{1,0:T(1,128)S(1)} custom-call(s32[2]{0:T(128)S(1)} %pad_add_fusion.refs_0_, f32[4,168,128]{2,1,0:T(8,128)S(1)} %pad_maximum_fusion.1.refs_1_, f32[4,168,128]{2,1,0:T(8,128)S(1)} %collective-permute-done.13.refs_2_, bf16[512,2048]{1,0:T(8,128)(2,1)S(1)} %copy-done.1), custom_call_target="tpu_custom_call" | custom-call | tf_op jit(solution)/shard_map/solve_continuation/pallas_call | solution.py:277
  108.3 3.2 %collective-permute-start.14 = (f32[1,2048]{1,0:T(1,128)S(1)}, f32[1,2048]{1,0:T(1,128)S(1)}, u32[]{:S(2)}, u32[]{:S(2)}) collective-permute-start(f32[1,2048]{1,0:T(1,128)S(1)} %solve_continuation.1), channel_id=1, source_target_pairs={{0,1},{1,0},{2,3},{3,2},{4,5},{5,4},{6,7},{7,6},{8,9},{9,8},{10,11... | collective-permute-start | bytes 24584 | tf_op jit(solution)/shard_map/ppermute | solution.py:147
  111.4 10.8 %collective-permute-done.14 = f32[1,2048]{1,0:T(1,128)S(1)} collective-permute-done((f32[1,2048]{1,0:T(1,128)S(1)}, f32[1,2048]{1,0:T(1,128)S(1)}, u32[]{:S(2)}, u32[]{:S(2)}) %collective-permute-start.14) | collective-permute-done | bytes 8224 | tf_op jit(solution)/shard_map/ppermute | solution.py:147
  122.2 0.1 collective-permute-start.15
  122.3 2.9 %collective-permute-start.16 = (f32[2,2048]{1,0:T(2,128)S(1)}, f32[2,2048]{1,0:T(2,128)S(1)}, u32[]{:S(2)}, u32[]{:S(2)}) collective-permute-start(f32[2,2048]{1,0:T(2,128)S(1)} %pad_maximum_fusion.2.refs_0_), channel_id=1, source_target_pairs={{0,4},{2,6},{4,0},{6,2},{1,5},{3,7},{5,1},{7,3},{8,12},{10,14},{12... | collective-permute-start | bytes 49160 | tf_op jit(solution)/shard_map/ppermute | solution.py:147
  125.2 0.9 collective-permute-start.17
  126.2 1.7 %collective-permute-done.15.refs_1_ = f32[2,2048]{1,0:T(2,128)S(1)} collective-permute-done((f32[2,2048]{1,0:T(2,128)S(1)}, f32[2,2048]{1,0:T(2,128)S(1)}, u32[]{:S(2)}, u32[]{:S(2)}) %collective-permute-start.15) | collective-permute-done | bytes 16416 | tf_op jit(solution)/shard_map/ppermute | solution.py:147
  127.9 4.2 %collective-permute-done.16.refs_2_ = f32[2,2048]{1,0:T(2,128)S(1)} collective-permute-done((f32[2,2048]{1,0:T(2,128)S(1)}, f32[2,2048]{1,0:T(2,128)S(1)}, u32[]{:S(2)}, u32[]{:S(2)}) %collective-permute-start.16) | collective-permute-done | bytes 16416 | tf_op jit(solution)/shard_map/ppermute | solution.py:147
  132.1 0.0 collective-permute-done.17.refs_3_
  132.1 0.0 all-to-all-done.2.refs_5_
  132.1 0.0 copy-done.2
  132.1 10.3 %surface_and_delta.1 = (f32[32,16384]{1,0:T(8,128)}, f32[16,4,128]{2,1,0:T(4,128)S(1)}) custom-call(s32[1]{0:T(128)} %bitcast.slab_ref, f32[2,2048]{1,0:T(2,128)S(1)} %pad_maximum_fusion.2.refs_0_, f32[2,2048]{1,0:T(2,128)S(1)} %collective-permute-done.15.refs_1_, f32[2,2048]{1,0:T(2,128)S(1)} %collective-permute-done.16.refs_2_, ...), custom_call_target="tpu_custom_call" | custom-call | tf_op jit(solution)/shard_map/surface_and_delta/pallas_call | solution.py:403
  142.4 10.7 %all_to_all.20 = f32[16,4,128]{2,1,0:T(4,128)S(1)} all-to-all(f32[16,4,128]{2,1,0:T(4,128)S(1)} %get-tuple-element.45), channel_id=1, replica_groups=mesh['z'=4,'ylo'=2,'core'=2,'x'=4,'yhi'=2] {'z','ylo','core'}, dimensions={0} | all-to-all | bytes 65536 | tf_op jit(solution)/shard_map/all_to_all | solution.py:469
  153.1 0.1 reshape.27
  153.2 0.6 copy.22
  (21 shorter events, 0.3 us)
Async XLA Ops:
  0.6 1.3 copy-start.6
  2.0 8.7 %copy-start = (bf16[32,16384]{1,0:T(8,128)(2,1)S(1)}, bf16[32,16384]{1,0:T(8,128)(2,1)}, u32[]{:S(2)}) copy-start(bf16[32,16384]{1,0:T(8,128)(2,1)} %refs_4_.1) | copy-start | bytes 3145732
  3.1 8.7 %copy-start.5 = (bf16[16384]{0:T(1024)(128)(2,1)S(1)}, bf16[16384]{0:T(1024)(128)(2,1)}, u32[]{:S(2)}) copy-start(bf16[16384]{0:T(1024)(128)(2,1)} %param.16) | copy-start | bytes 98308
  3.1 23.8 %all-to-all-start = ((bf16[8,32,2176]{2,1,0:T(8,128)(2,1)}), bf16[8,32,2176]{2,1,0:T(8,128)(2,1)S(1)}, u32[]{:S(2)}, u32[]{:S(2)}) async-start(bf16[8,32,2176]{2,1,0:T(8,128)(2,1)} %pad_maximum_fusion), calls=%async_computation | async-start | bytes 2228224 | tf_op jit(solution)/shard_map/all_to_all | solution.py:440
  10.7 20.5 %copy-start.7 = (f32[512]{0:T(512)S(1)}, f32[512]{0:T(512)}, u32[]{:S(2)}) copy-start(f32[512]{0:T(512)} %param.15) | copy-start | bytes 6148
  26.9 24.3 %all-to-all-start.1 = ((bf16[8,32,2048]{2,1,0:T(8,128)(2,1)}), bf16[8,32,2048]{2,1,0:T(8,128)(2,1)S(1)}, u32[]{:S(2)}, u32[]{:S(2)}) async-start(bf16[8,32,2048]{2,1,0:T(8,128)(2,1)} %bitcast.38), calls=%async_computation.1 | async-start | bytes 2097152 | tf_op jit(solution)/shard_map/all_to_all | solution.py:448
  31.4 32.9 %copy-start.8 = (f32[256]{0:T(256)S(1)}, f32[256]{0:T(256)}, u32[]{:S(2)}) copy-start(f32[256]{0:T(256)} %param.21) | copy-start | bytes 3076
  36.1 28.3 %copy-start.4 = (bf16[256,256]{1,0:T(8,128)(2,1)S(1)}, bf16[256,256]{1,0:T(8,128)(2,1)}, u32[]{:S(2)}) copy-start(bf16[256,256]{1,0:T(8,128)(2,1)} %mixer_ref.1) | copy-start | bytes 393220
  36.1 2.7 %collective-permute-start = (f32[672,128]{1,0:T(8,128)}, f32[672,128]{1,0:T(8,128)S(1)}, u32[]{:S(2)}, u32[]{:S(2)}) collective-permute-start(f32[672,128]{1,0:T(8,128)} %get-tuple-element.30), channel_id=1, source_target_pairs={{0,8},{8,0},{1,9},{9,1},{2,10},{10,2},{3,11},{11,3},{4,12},{12,4},... | collective-permute-start | bytes 1032200 | tf_op jit(solution)/shard_map/ppermute | solution.py:147
  39.8 5.0 %collective-permute-start.1 = (f32[168,128]{1,0:T(8,128)S(1)}, f32[168,128]{1,0:T(8,128)S(1)}, u32[]{:S(2)}, u32[]{:S(2)}) collective-permute-start(f32[168,128]{1,0:T(8,128)S(1)} %get-tuple-element.48), channel_id=1, source_target_pairs={{0,32},{32,0},{64,96},{96,64},{1,33},{33,1},{65,97},{97,65},{2,34}... | collective-permute-start | bytes 258056 | tf_op jit(solution)/shard_map/ppermute | solution.py:147
  41.6 7.4 %collective-permute-start.2 = (f32[168,128]{1,0:T(8,128)S(1)}, f32[168,128]{1,0:T(8,128)S(1)}, u32[]{:S(2)}, u32[]{:S(2)}) collective-permute-start(f32[168,128]{1,0:T(8,128)S(1)} %get-tuple-element.47), channel_id=1, source_target_pairs={{0,64},{32,96},{64,0},{96,32},{1,65},{33,97},{65,1},{97,33},{2,66}... | collective-permute-start | bytes 258056 | tf_op jit(solution)/shard_map/ppermute | solution.py:147
  44.9 6.3 %collective-permute-start.3 = (f32[168,128]{1,0:T(8,128)S(1)}, f32[168,128]{1,0:T(8,128)S(1)}, u32[]{:S(2)}, u32[]{:S(2)}) collective-permute-start(f32[168,128]{1,0:T(8,128)S(1)} %get-tuple-element.46), channel_id=1, source_target_pairs={{0,96},{32,64},{64,32},{96,0},{1,97},{33,65},{65,33},{97,1},{2,98}... | collective-permute-start | bytes 258056 | tf_op jit(solution)/shard_map/ppermute | solution.py:147
  51.2 4.3 %collective-permute-start.4 = (f32[168,128]{1,0:T(8,128)S(1)}, f32[168,128]{1,0:T(8,128)S(1)}, u32[]{:S(2)}, u32[]{:S(2)}) collective-permute-start(f32[168,128]{1,0:T(8,128)S(1)} %fusion), channel_id=1, source_target_pairs={{0,2},{2,0},{4,6},{6,4},{1,3},{3,1},{5,7},{7,5},{8,10},{10,8},{12,... | collective-permute-start | bytes 258056 | tf_op jit(solution)/shard_map/ppermute | solution.py:147
  53.0 5.7 %collective-permute-start.5 = (f32[168,128]{1,0:T(8,128)S(1)}, f32[168,128]{1,0:T(8,128)S(1)}, u32[]{:S(2)}, u32[]{:S(2)}) collective-permute-start(f32[168,128]{1,0:T(8,128)S(1)} %fusion), channel_id=1, source_target_pairs={{0,4},{2,6},{4,0},{6,2},{1,5},{3,7},{5,1},{7,3},{8,12},{10,14},{12... | collective-permute-start | bytes 258056 | tf_op jit(solution)/shard_map/ppermute | solution.py:147
  55.4 5.5 %collective-permute-start.6 = (f32[168,128]{1,0:T(8,128)S(1)}, f32[168,128]{1,0:T(8,128)S(1)}, u32[]{:S(2)}, u32[]{:S(2)}) collective-permute-start(f32[168,128]{1,0:T(8,128)S(1)} %fusion), channel_id=1, source_target_pairs={{0,6},{2,4},{4,2},{6,0},{1,7},{3,5},{5,3},{7,1},{8,14},{10,12},{12... | collective-permute-start | bytes 258056 | tf_op jit(solution)/shard_map/ppermute | solution.py:147
  60.9 6.6 %collective-permute-start.7 = (f32[168,128]{1,0:T(8,128)S(1)}, f32[168,128]{1,0:T(8,128)S(1)}, u32[]{:S(2)}, u32[]{:S(2)}) collective-permute-start(f32[168,128]{1,0:T(8,128)S(1)} %add_add_fusion.1), channel_id=1, source_target_pairs={{0,1},{1,0},{16,17},{17,16},{2,3},{3,2},{18,19},{19,18},{4,5},{5,4... | collective-permute-start | bytes 258056 | tf_op jit(solution)/shard_map/ppermute | solution.py:147
  63.7 3.8 %collective-permute-start.8 = (f32[168,128]{1,0:T(8,128)S(1)}, f32[168,128]{1,0:T(8,128)S(1)}, u32[]{:S(2)}, u32[]{:S(2)}) collective-permute-start(f32[168,128]{1,0:T(8,128)S(1)} %add_add_fusion.1), channel_id=1, source_target_pairs={{0,16},{1,17},{16,0},{17,1},{2,18},{3,19},{18,2},{19,3},{4,20},{5,... | collective-permute-start | bytes 258056 | tf_op jit(solution)/shard_map/ppermute | solution.py:147
  64.1 4.8 %collective-permute-start.9 = (f32[168,128]{1,0:T(8,128)S(1)}, f32[168,128]{1,0:T(8,128)S(1)}, u32[]{:S(2)}, u32[]{:S(2)}) collective-permute-start(f32[168,128]{1,0:T(8,128)S(1)} %add_add_fusion.1), channel_id=1, source_target_pairs={{0,17},{1,16},{16,1},{17,0},{2,19},{3,18},{18,3},{19,2},{4,21},{5,... | collective-permute-start | bytes 258056 | tf_op jit(solution)/shard_map/ppermute | solution.py:147
  68.9 63.2 %all-to-all-start.2 = ((bf16[8,4,32,2048]{3,2,1,0:T(8,128)(2,1)}), bf16[8,4,32,2048]{3,2,1,0:T(8,128)(2,1)}, u32[]{:S(2)}, u32[]{:S(2)}) async-start(bf16[8,4,32,2048]{3,2,1,0:T(8,128)(2,1)} %get-tuple-element.42), calls=%async_computation.2 | async-start | bytes 8388608 | tf_op jit(solution)/shard_map/all_to_all | solution.py:461
  73.4 58.7 %copy-start.2 = (s32[4,16384]{1,0:T(4,128)S(1)}, s32[4,16384]{1,0:T(4,128)}, u32[]{:S(2)}) copy-start(s32[4,16384]{1,0:T(4,128)} %refs_8_.1) | copy-start | bytes 786436
  73.4 58.7 %copy-start.3 = (s32[4,16384]{1,0:T(4,128)S(1)}, s32[4,16384]{1,0:T(4,128)}, u32[]{:S(2)}) copy-start(s32[4,16384]{1,0:T(4,128)} %refs_9_.1) | copy-start | bytes 786436
  73.5 3.9 %collective-permute-start.10 = (f32[168,128]{1,0:T(8,128)S(1)}, f32[168,128]{1,0:T(8,128)S(1)}, u32[]{:S(2)}, u32[]{:S(2)}) collective-permute-start(f32[168,128]{1,0:T(8,128)S(1)} %add_add_fusion), channel_id=1, source_target_pairs={{0,32},{32,0},{64,96},{96,64},{1,33},{33,1},{65,97},{97,65},{2,34}... | collective-permute-start | bytes 258056 | tf_op jit(solution)/shard_map/ppermute | solution.py:147
  73.6 4.9 %collective-permute-start.11 = (f32[168,128]{1,0:T(8,128)S(1)}, f32[168,128]{1,0:T(8,128)S(1)}, u32[]{:S(2)}, u32[]{:S(2)}) collective-permute-start(f32[168,128]{1,0:T(8,128)S(1)} %add_add_fusion), channel_id=1, source_target_pairs={{0,64},{32,96},{64,0},{96,32},{1,65},{33,97},{65,1},{97,33},{2,66}... | collective-permute-start | bytes 258056 | tf_op jit(solution)/shard_map/ppermute | solution.py:147
  75.2 4.5 %collective-permute-start.12 = (f32[168,128]{1,0:T(8,128)S(1)}, f32[168,128]{1,0:T(8,128)S(1)}, u32[]{:S(2)}, u32[]{:S(2)}) collective-permute-start(f32[168,128]{1,0:T(8,128)S(1)} %add_add_fusion), channel_id=1, source_target_pairs={{0,96},{32,64},{64,32},{96,0},{1,97},{33,65},{65,33},{97,1},{2,98}... | collective-permute-start | bytes 258056 | tf_op jit(solution)/shard_map/ppermute | solution.py:147
  79.8 6.1 %collective-permute-start.13 = (f32[4,168,128]{2,1,0:T(8,128)S(1)}, f32[4,168,128]{2,1,0:T(8,128)S(1)}, u32[]{:S(2)}, u32[]{:S(2)}) collective-permute-start(f32[4,168,128]{2,1,0:T(8,128)S(1)} %pad_maximum_fusion.1.refs_1_), channel_id=1, source_target_pairs={{0,8},{8,0},{1,9},{9,1},{2,10},{10,2},{3,11},{11,3},{4,12},{12,4},... | collective-permute-start | bytes 1032200 | tf_op jit(solution)/shard_map/ppermute | solution.py:147
  85.9 1.6 %copy-start.1 = (bf16[512,2048]{1,0:T(8,128)(2,1)S(1)}, bf16[512,2048]{1,0:T(8,128)(2,1)}, u32[]{:S(2)}) copy-start(bf16[512,2048]{1,0:T(8,128)(2,1)} %get-tuple-element.41.refs_3_) | copy-start | bytes 6291460
  108.3 13.9 %collective-permute-start.14 = (f32[1,2048]{1,0:T(1,128)S(1)}, f32[1,2048]{1,0:T(1,128)S(1)}, u32[]{:S(2)}, u32[]{:S(2)}) collective-permute-start(f32[1,2048]{1,0:T(1,128)S(1)} %solve_continuation.1), channel_id=1, source_target_pairs={{0,1},{1,0},{2,3},{3,2},{4,5},{5,4},{6,7},{7,6},{8,9},{9,8},{10,11... | collective-permute-start | bytes 24584 | tf_op jit(solution)/shard_map/ppermute | solution.py:147
  122.2 5.7 %collective-permute-start.15 = (f32[2,2048]{1,0:T(2,128)S(1)}, f32[2,2048]{1,0:T(2,128)S(1)}, u32[]{:S(2)}, u32[]{:S(2)}) collective-permute-start(f32[2,2048]{1,0:T(2,128)S(1)} %pad_maximum_fusion.2.refs_0_), channel_id=1, source_target_pairs={{0,2},{2,0},{4,6},{6,4},{1,3},{3,1},{5,7},{7,5},{8,10},{10,8},{12,... | collective-permute-start | bytes 49160 | tf_op jit(solution)/shard_map/ppermute | solution.py:147
  122.3 9.8 %collective-permute-start.16 = (f32[2,2048]{1,0:T(2,128)S(1)}, f32[2,2048]{1,0:T(2,128)S(1)}, u32[]{:S(2)}, u32[]{:S(2)}) collective-permute-start(f32[2,2048]{1,0:T(2,128)S(1)} %pad_maximum_fusion.2.refs_0_), channel_id=1, source_target_pairs={{0,4},{2,6},{4,0},{6,2},{1,5},{3,7},{5,1},{7,3},{8,12},{10,14},{12... | collective-permute-start | bytes 49160 | tf_op jit(solution)/shard_map/ppermute | solution.py:147
  125.2 6.9 %collective-permute-start.17 = (f32[2,2048]{1,0:T(2,128)S(1)}, f32[2,2048]{1,0:T(2,128)S(1)}, u32[]{:S(2)}, u32[]{:S(2)}) collective-permute-start(f32[2,2048]{1,0:T(2,128)S(1)} %pad_maximum_fusion.2.refs_0_), channel_id=1, source_target_pairs={{0,6},{2,4},{4,2},{6,0},{1,7},{3,5},{5,3},{7,1},{8,14},{10,12},{12... | collective-permute-start | bytes 49160 | tf_op jit(solution)/shard_map/ppermute | solution.py:147

commit v8 on v7

--- a/solution.py
+++ b/solution.py
@@ -347,21 +347,27 @@
     )(moved, mixer, basket)
 
 
-def surface_kernel(slab_ref, *refs):
-    continuation_refs = refs[:4]
-    (cotangent_ref, gain_ref, shock_ref, weight_ref, exercise_ref, bucket_ref, delta_ref, share_ref,
-     continuation_ref, total_ref) = refs[4:]
+def surface_kernel(slab_ref, *refs, near):
     step = pl.program_id(0)
-
-    @pl.when(step == 0)
-    def _():
-        for flip in range(8):
-            continuation_ref[pl.ds(slab_ref[0] ^ flip, 1), :] = continuation_refs[flip // 2][
-                flip % 2:flip % 2 + 1, :
-            ]
-        total_ref[...] = jnp.zeros(total_ref.shape, f32)
-
-    continuation = continuation_ref[pl.ds(step, 1), :]
+    own = slab_ref[0]
+    if near:
+        (continuation_ref, cotangent_ref, gain_ref, shock_ref, weight_ref, exercise_ref, bucket_ref,
+         delta_ref, total_ref) = refs
+
+        @pl.when(step == 0)
+        def _():
+            total_ref[...] = jnp.zeros(total_ref.shape, f32)
+    else:
+        (far_refs, (before_ref, _, cotangent_ref, gain_ref, shock_ref, weight_ref, exercise_ref,
+                    bucket_ref, delta_ref, share_ref, continuation_ref, total_ref)) = refs[:3], refs[3:]
+
+        @pl.when(step == 0)
+        def _():
+            for flip in range(3):
+                continuation_ref[2 * flip + 2:2 * flip + 4, :] = far_refs[flip][...]
+            total_ref[...] = before_ref[...]
+
+    continuation = continuation_ref[pl.ds(slab_of_step(step, own, near) ^ own, 1), :]
     held = [exercise_ref[date:date + 1, :].astype(f32) * continuation for date in range(STEPS)]
     weights = [weight_ref[:, later:later + 1] for later in range(STEPS)]
     strikes = lax.broadcasted_iota(jnp.int32, (STRIKE_ROWS, DATE_TILE), 0).astype(f32).astype(bf16)
@@ -386,46 +392,76 @@
     delta_ref[...] = adjoint
     total_ref[...] = total
 
-    @pl.when(step == pl.num_programs(0) - 1)
-    def _():
-        owners = STRIKE_ROWS // 16
-        for g in range(NK // STRIKE_ROWS):
-            grouped = total[:, 32 * g:32 * g + 32].reshape(owners, 16, 32)
-            for q in range(4):
-                share_ref[g * owners:(g + 1) * owners, :, 32 * q:32 * q + 32] = grouped[
-                    :, 4 * q:4 * q + 4, :
-                ]
-
-
-def surface_and_delta(slab, continuations, cotangent, gains, shocks, weights, exercise, bucket):
+    if not near:
+        @pl.when(step == pl.num_programs(0) - 1)
+        def _():
+            owners = STRIKE_ROWS // 16
+            for g in range(NK // STRIKE_ROWS):
+                grouped = total[:, 32 * g:32 * g + 32].reshape(owners, 16, 32)
+                for q in range(4):
+                    share_ref[g * owners:(g + 1) * owners, :, 32 * q:32 * q + 32] = grouped[
+                        :, 4 * q:4 * q + 4, :
+                    ]
+
+
+def slab_of_step(step, own, near):
+    pair = own >> 1
+    return 2 * pair + step if near else 2 * ((pair + 1 + (step >> 1)) & 3) + (step & 1)
+
+
+def surface_call(slab, continuations, before, cotangent, gains, shocks, weights, exercise, bucket):
+    near = before is None
     local_paths = cotangent.shape[1]
-    whole = pl.BlockSpec((2, DATE_TILE), lambda i, s: (0, 0))
+    sums_shape = (STRIKE_ROWS, 32 * (NK // STRIKE_ROWS))
+
+    def whole(shape):
+        return pl.BlockSpec(shape, lambda i, s: (0,) * len(shape))
+
+    def at(i, s):
+        return slab_of_step(i, s[0], near)
+
+    delta_spec = pl.BlockSpec((32, DATE_TILE), lambda i, s: (0, at(i, s)))
+    delta_shape = jax.ShapeDtypeStruct((32, local_paths), f32)
+    shared_specs = [
+        pl.BlockSpec((32, DATE_TILE), lambda i, s: (0, at(i, s))),
+        pl.BlockSpec((1, STEPS, 32, DATE_TILE), lambda i, s: (at(i, s), 0, 0, 0)),
+        pl.BlockSpec((STEPS, 32, DATE_TILE), lambda i, s: (0, 0, at(i, s))),
+        pl.BlockSpec((32, LANES), lambda i, s: (s[0], 0)),
+        pl.BlockSpec((STEPS, DATE_TILE), lambda i, s: (0, at(i, s))),
+        pl.BlockSpec((STEPS, DATE_TILE), lambda i, s: (0, at(i, s))),
+    ]
+    rows = whole((2, DATE_TILE))
+    if near:
+        first_specs, first = [rows], continuations
+        outs = (delta_shape, jax.ShapeDtypeStruct(sums_shape, f32))
+        out_specs = (delta_spec, whole(sums_shape))
+        scratch = []
+    else:
+        delta, total = before
+        first_specs = [rows] * 3 + [whole(sums_shape), pl.BlockSpec(memory_space=pl.ANY)]
+        first = [*continuations, total, delta]
+        outs = (delta_shape, jax.ShapeDtypeStruct((16, 4, LANES), f32))
+        out_specs = (delta_spec, whole((16, 4, LANES)))
+        scratch = [pltpu.VMEM((8, DATE_TILE), f32), pltpu.VMEM(sums_shape, f32)]
     return pl.pallas_call(
-        surface_kernel,
-        out_shape=(
-            jax.ShapeDtypeStruct((32, local_paths), f32),
-            jax.ShapeDtypeStruct((16, 4, LANES), f32),
-        ),
+        lambda *refs: surface_kernel(*refs, near=near),
+        out_shape=outs,
         grid_spec=pltpu.PrefetchScalarGridSpec(
             num_scalar_prefetch=1,
-            grid=(local_paths // DATE_TILE,),
-            in_specs=[whole] * 4 + [
-                pl.BlockSpec((32, DATE_TILE), lambda i, s: (0, i)),
-                pl.BlockSpec((1, STEPS, 32, DATE_TILE), lambda i, s: (i, 0, 0, 0)),
-                pl.BlockSpec((STEPS, 32, DATE_TILE), lambda i, s: (0, 0, i)),
-                pl.BlockSpec((32, LANES), lambda i, s: (s[0], 0)),
-                pl.BlockSpec((STEPS, DATE_TILE), lambda i, s: (0, i)),
-                pl.BlockSpec((STEPS, DATE_TILE), lambda i, s: (0, i)),
-            ],
-            out_specs=(
-                pl.BlockSpec((32, DATE_TILE), lambda i, s: (0, i)),
-                pl.BlockSpec((16, 4, LANES), lambda i, s: (0, 0, 0)),
-            ),
-            scratch_shapes=[pltpu.VMEM((8, DATE_TILE), f32), pltpu.VMEM((STRIKE_ROWS, 32 * (NK // STRIKE_ROWS)), f32)],
-        ),
+            grid=(2 if near else 6,),
+            in_specs=first_specs + shared_specs,
+            out_specs=out_specs,
+            scratch_shapes=scratch,
+        ),
+        input_output_aliases={} if near else {5: 0},
         compiler_params=pltpu.CompilerParams(vmem_limit_bytes=32 << 20),
-        name="surface_and_delta",
-    )(slab, *continuations, cotangent, gains, in_hbm(shocks), weights, exercise, bucket)
+        name="surface_near" if near else "surface_far",
+    )(slab, *first, cotangent, gains, in_hbm(shocks), weights, exercise, bucket)
+
+
+def surface_and_delta(slab, continuations, *rest):
+    before = surface_call(slab, continuations[:1], None, *rest)
+    return surface_call(slab, continuations[1:], before, *rest)
 
 
 def per_device(prices, loadings, basis_w, basis_bias, payoff, in_fit, cotangent, shocks, corr_gen,

time: 155 us -> 156 us (level)
    ppermute x18, waiting for transfers between devices: 34.8 us -> 28.9 us  [exchange_with_others(): lax.ppermute(sent, axes, [(i, i ^ flip) for i in range(count)])]
    all_to_all x1, waiting for transfers between devices: 0.01 us -> 5.22 us  [per_device(): gains = lax.all_to_all(sent, STOCK_AXES, 0, 0, tiled=True)]
    pallas_call x1 -> x2, Pallas kernels: 10.3 us -> 11.5 us  [surface_call(): pl.pallas_call(lambda *refs: surface_kernel(*refs, near=near), out_shape=...]
  transfers between devices with their start and end apart: 21 -> 21, of which waited for: 13 -> 12; matrix products, arithmetic and copies ran while one was open for 2% -> 2% of each run, Pallas kernels for 19% -> 21%
where the time goes in v8:
time: 156 us; the launch traced here: 155 us
  waiting for transfers between devices  49.2 us (32%)
  starting transfers between devices  46.1 us (30%)
  Pallas kernels  40 us (26%)
  blocking collectives  11.2 us (7%)
  local copies, waits for them, and re-layouts  5.06 us (3%)
  other arithmetic  2.41 us (2%)
    ppermute x18, starting transfers between devices, exchange_with_others(): lax.ppermute(sent, axes, [(i, i ^ flip) for i in range(count)])  29.7 us
    ppermute x18, waiting for transfers between devices, exchange_with_others(): lax.ppermute(sent, axes, [(i, i ^ flip) for i in range(count)])  28.9 us
    pallas_call x1, Pallas kernels, solve_continuation(): pl.pallas_call(lambda *refs: solve_kernel(*refs, scale=1.0 / path_count),...  20.7 us
    all_to_all x1, waiting for transfers between devices, per_device(): lax.all_to_all(jnp.concatenate([pieces, table], axis=2), STOCK_AXES, 0, 0...  15.1 us
    pallas_call x2, Pallas kernels, surface_call(): pl.pallas_call(lambda *refs: surface_kernel(*refs, near=near), out_shape=...  11.5 us
    all_to_all x1, blocking collectives, per_device(): surface = lax.all_to_all(surface, PATH_AXES, 0, 0, tiled=True)  11.2 us
    all_to_all x1, starting transfers between devices, per_device(): lax.all_to_all(jnp.concatenate([pieces, table], axis=2), STOCK_AXES, 0, 0...  7.61 us
    all_to_all x1, waiting for transfers between devices, per_device(): gains = lax.all_to_all(sent, STOCK_AXES, 0, 0, tiled=True)  5.22 us
  transfers between devices with their start and end apart: 21, of which 12 were waited for; matrix products, arithmetic and copies ran while one was open for 2% of the time, Pallas kernels for 21%

profile of v8, /device:TPU:1, one launch (start us, length us, event | category | flops | bytes accessed | tf_op | source)
XLA Modules:
  0.0 154.9 jit_solution(13526160490350229469)
XLA Ops:
  0.6 1.3 copy.28
  2.0 0.0 copy-start
  2.0 1.1 pad_maximum_fusion
  3.1 7.6 %all-to-all-start = ((bf16[8,32,2176]{2,1,0:T(8,128)(2,1)}), bf16[8,32,2176]{2,1,0:T(8,128)(2,1)S(1)}, u32[]{:S(2)}, u32[]{:S(2)}) async-start(bf16[8,32,2176]{2,1,0:T(8,128)(2,1)} %pad_maximum_fusion), calls=%async_computation | async-start | bytes 2228224 | tf_op jit(solution)/shard_map/all_to_all | solution.py:476
  10.7 0.0 copy-start.7
  10.7 1.1 copy.29
  11.8 15.1 %all-to-all-done.moved_ref.table_ref = bf16[8,32,2176]{2,1,0:T(8,128)(2,1)S(1)} async-done(((bf16[8,32,2176]{2,1,0:T(8,128)(2,1)}), bf16[8,32,2176]{2,1,0:T(8,128)(2,1)S(1)}, u32[]{:S(2)}, u32[]{:S(2)}) %all-to-all-start) | async-done | bytes 1114144 | tf_op jit(solution)/shard_map/all_to_all | solution.py:476
  26.9 4.2 %all-to-all-start.1 = ((bf16[8,32,2048]{2,1,0:T(8,128)(2,1)}), bf16[8,32,2048]{2,1,0:T(8,128)(2,1)S(1)}, u32[]{:S(2)}, u32[]{:S(2)}) async-start(bf16[8,32,2048]{2,1,0:T(8,128)(2,1)} %bitcast.38), calls=%async_computation.1 | async-start | bytes 2097152 | tf_op jit(solution)/shard_map/all_to_all | solution.py:484
  31.1 0.1 pad_add_fusion.1.slab_ref
  31.2 0.1 copy.21.bias_ref
  31.4 0.0 copy-start.8
  31.4 4.7 %regression_sums.1 = (bf16[512,2048]{1,0:T(8,128)(2,1)}, f32[672,128]{1,0:T(8,128)}, f32[672,128]{1,0:T(8,128)}) custom-call(s32[2]{0:T(128)S(1)} %pad_add_fusion.1.slab_ref, bf16[8,32,2176]{2,1,0:T(8,128)(2,1)S(1)} %all-to-all-done.moved_ref.table_ref, bf16[8,32,2176]{2,1,0:T(8,128)(2,1)S(1)} %all-to-all-done.moved_ref.table_ref, f32[32,512]{1,0:T(8,128)} %weight_ref, ...), custom_call_target="tpu_custom_call" | custom-call | tf_op jit(solution)/shard_map/regression_sums/pallas_call | solution.py:109
  36.1 1.2 collective-permute-start
  37.3 1.5 collective-permute-done
  38.8 1.0 add.49
  39.8 1.7 %collective-permute-start.1 = (f32[168,128]{1,0:T(8,128)S(1)}, f32[168,128]{1,0:T(8,128)S(1)}, u32[]{:S(2)}, u32[]{:S(2)}) collective-permute-start(f32[168,128]{1,0:T(8,128)S(1)} %get-tuple-element.52), channel_id=1, source_target_pairs={{0,32},{32,0},{64,96},{96,64},{1,33},{33,1},{65,97},{97,65},{2,34}... | collective-permute-start | bytes 258056 | tf_op jit(solution)/shard_map/ppermute | solution.py:147
  41.5 3.3 %collective-permute-start.2 = (f32[168,128]{1,0:T(8,128)S(1)}, f32[168,128]{1,0:T(8,128)S(1)}, u32[]{:S(2)}, u32[]{:S(2)}) collective-permute-start(f32[168,128]{1,0:T(8,128)S(1)} %get-tuple-element.51), channel_id=1, source_target_pairs={{0,64},{32,96},{64,0},{96,32},{1,65},{33,97},{65,1},{97,33},{2,66}... | collective-permute-start | bytes 258056 | tf_op jit(solution)/shard_map/ppermute | solution.py:147
  44.8 0.0 collective-permute-start.3
  44.9 0.0 collective-permute-done.1
  44.9 4.1 %collective-permute-done.2 = f32[168,128]{1,0:T(8,128)S(1)} collective-permute-done((f32[168,128]{1,0:T(8,128)S(1)}, f32[168,128]{1,0:T(8,128)S(1)}, u32[]{:S(2)}, u32[]{:S(2)}) %collective-permute-start.2) | collective-permute-done | bytes 86048 | tf_op jit(solution)/shard_map/ppermute | solution.py:147
  49.0 2.2 %collective-permute-done.3 = f32[168,128]{1,0:T(8,128)S(1)} collective-permute-done((f32[168,128]{1,0:T(8,128)S(1)}, f32[168,128]{1,0:T(8,128)S(1)}, u32[]{:S(2)}, u32[]{:S(2)}) %collective-permute-start.3) | collective-permute-done | bytes 86048 | tf_op jit(solution)/shard_map/ppermute | solution.py:147
  51.2 0.0 all-to-all-done.1.moved_ref
  51.2 1.8 %collective-permute-start.4 = (f32[168,128]{1,0:T(8,128)S(1)}, f32[168,128]{1,0:T(8,128)S(1)}, u32[]{:S(2)}, u32[]{:S(2)}) collective-permute-start(f32[168,128]{1,0:T(8,128)S(1)} %fusion), channel_id=1, source_target_pairs={{0,2},{2,0},{4,6},{6,4},{1,3},{3,1},{5,7},{7,5},{8,10},{10,8},{12,... | collective-permute-start | bytes 258056 | tf_op jit(solution)/shard_map/ppermute | solution.py:147
  53.0 2.4 %collective-permute-start.5 = (f32[168,128]{1,0:T(8,128)S(1)}, f32[168,128]{1,0:T(8,128)S(1)}, u32[]{:S(2)}, u32[]{:S(2)}) collective-permute-start(f32[168,128]{1,0:T(8,128)S(1)} %fusion), channel_id=1, source_target_pairs={{0,4},{2,6},{4,0},{6,2},{1,5},{3,7},{5,1},{7,3},{8,12},{10,14},{12... | collective-permute-start | bytes 258056 | tf_op jit(solution)/shard_map/ppermute | solution.py:147
  55.4 0.1 collective-permute-start.6
  55.5 0.0 collective-permute-done.4
  55.5 3.2 %collective-permute-done.5 = f32[168,128]{1,0:T(8,128)S(1)} collective-permute-done((f32[168,128]{1,0:T(8,128)S(1)}, f32[168,128]{1,0:T(8,128)S(1)}, u32[]{:S(2)}, u32[]{:S(2)}) %collective-permute-start.5) | collective-permute-done | bytes 86048 | tf_op jit(solution)/shard_map/ppermute | solution.py:147
  58.7 2.2 %collective-permute-done.6 = f32[168,128]{1,0:T(8,128)S(1)} collective-permute-done((f32[168,128]{1,0:T(8,128)S(1)}, f32[168,128]{1,0:T(8,128)S(1)}, u32[]{:S(2)}, u32[]{:S(2)}) %collective-permute-start.6) | collective-permute-done | bytes 86048 | tf_op jit(solution)/shard_map/ppermute | solution.py:147
  60.9 2.8 %collective-permute-start.7 = (f32[168,128]{1,0:T(8,128)S(1)}, f32[168,128]{1,0:T(8,128)S(1)}, u32[]{:S(2)}, u32[]{:S(2)}) collective-permute-start(f32[168,128]{1,0:T(8,128)S(1)} %add_add_fusion.1), channel_id=1, source_target_pairs={{0,1},{1,0},{16,17},{17,16},{2,3},{3,2},{18,19},{19,18},{4,5},{5,4... | collective-permute-start | bytes 258056 | tf_op jit(solution)/shard_map/ppermute | solution.py:147
  63.7 0.4 collective-permute-start.8
  64.1 0.2 collective-permute-start.9
  64.3 0.1 copy.22.basket_ref
  64.4 3.0 %increments.1 = (bf16[8,4,32,2048]{3,2,1,0:T(8,128)(2,1)}, f32[256,128]{1,0:T(8,128)S(1)}) custom-call(bf16[8,32,2048]{2,1,0:T(8,128)(2,1)S(1)} %all-to-all-done.1.moved_ref, bf16[256,256]{1,0:T(8,128)(2,1)S(1)} %copy-done.4, f32[256,1]{1,0:T(8,128)S(1)} %copy.22.basket_ref), custom_call_target="tpu_custom_call" | custom-call | tf_op jit(solution)/shard_map/increments/pallas_call | solution.py:331
  67.5 0.0 collective-permute-done.7
  67.5 0.0 collective-permute-done.8
  67.5 1.4 collective-permute-done.9
  68.8 4.5 %all-to-all-start.2 = ((bf16[8,4,32,2048]{3,2,1,0:T(8,128)(2,1)}), bf16[8,4,32,2048]{3,2,1,0:T(8,128)(2,1)}, u32[]{:S(2)}, u32[]{:S(2)}) async-start(bf16[8,4,32,2048]{3,2,1,0:T(8,128)(2,1)} %get-tuple-element.44), calls=%async_computation.2 | async-start | bytes 8388608 | tf_op jit(solution)/shard_map/all_to_all | solution.py:497
  73.4 0.0 copy-start.2
  73.4 0.0 copy-start.3
  73.4 0.1 collective-permute-start.10
  73.5 1.7 %collective-permute-start.11 = (f32[168,128]{1,0:T(8,128)S(1)}, f32[168,128]{1,0:T(8,128)S(1)}, u32[]{:S(2)}, u32[]{:S(2)}) collective-permute-start(f32[168,128]{1,0:T(8,128)S(1)} %add_add_fusion), channel_id=1, source_target_pairs={{0,64},{32,96},{64,0},{96,32},{1,65},{33,97},{65,1},{97,33},{2,66}... | collective-permute-start | bytes 258056 | tf_op jit(solution)/shard_map/ppermute | solution.py:147
  75.2 2.2 %collective-permute-start.12 = (f32[168,128]{1,0:T(8,128)S(1)}, f32[168,128]{1,0:T(8,128)S(1)}, u32[]{:S(2)}, u32[]{:S(2)}) collective-permute-start(f32[168,128]{1,0:T(8,128)S(1)} %add_add_fusion), channel_id=1, source_target_pairs={{0,96},{32,64},{64,32},{96,0},{1,97},{33,65},{65,33},{97,1},{2,98}... | collective-permute-start | bytes 258056 | tf_op jit(solution)/shard_map/ppermute | solution.py:147
  77.4 0.0 collective-permute-done.10
  77.4 1.1 collective-permute-done.11
  78.5 1.3 collective-permute-done.12
  79.8 4.8 %collective-permute-start.13 = (f32[4,168,128]{2,1,0:T(8,128)S(1)}, f32[4,168,128]{2,1,0:T(8,128)S(1)}, u32[]{:S(2)}, u32[]{:S(2)}) collective-permute-start(f32[4,168,128]{2,1,0:T(8,128)S(1)} %pad_maximum_fusion.1.refs_1_), channel_id=1, source_target_pairs={{0,8},{8,0},{1,9},{9,1},{2,10},{10,2},{3,11},{11,3},{4,12},{12,4},... | collective-permute-start | bytes 1032200 | tf_op jit(solution)/shard_map/ppermute | solution.py:147
  84.6 0.1 pad_add_fusion.refs_0_
  84.7 1.2 collective-permute-done.13.refs_2_
  85.9 1.6 %copy-done.1 = bf16[512,2048]{1,0:T(8,128)(2,1)S(1)} copy-done((bf16[512,2048]{1,0:T(8,128)(2,1)S(1)}, bf16[512,2048]{1,0:T(8,128)(2,1)}, u32[]{:S(2)}) %copy-start.1) | copy-done | bytes 2097176
  87.5 20.7 %solve_continuation.1 = f32[1,2048]{1,0:T(1,128)S(1)} custom-call(s32[2]{0:T(128)S(1)} %pad_add_fusion.refs_0_, f32[4,168,128]{2,1,0:T(8,128)S(1)} %pad_maximum_fusion.1.refs_1_, f32[4,168,128]{2,1,0:T(8,128)S(1)} %collective-permute-done.13.refs_2_, bf16[512,2048]{1,0:T(8,128)(2,1)S(1)} %copy-done.1), custom_call_target="tpu_custom_call" | custom-call | tf_op jit(solution)/shard_map/solve_continuation/pallas_call | solution.py:277
  108.3 3.2 %collective-permute-start.14 = (f32[1,2048]{1,0:T(1,128)S(1)}, f32[1,2048]{1,0:T(1,128)S(1)}, u32[]{:S(2)}, u32[]{:S(2)}) collective-permute-start(f32[1,2048]{1,0:T(1,128)S(1)} %solve_continuation.1), channel_id=1, source_target_pairs={{0,1},{1,0},{2,3},{3,2},{4,5},{5,4},{6,7},{7,6},{8,9},{9,8},{10,11... | collective-permute-start | bytes 24584 | tf_op jit(solution)/shard_map/ppermute | solution.py:147
  111.4 10.8 %collective-permute-done.14 = f32[1,2048]{1,0:T(1,128)S(1)} collective-permute-done((f32[1,2048]{1,0:T(1,128)S(1)}, f32[1,2048]{1,0:T(1,128)S(1)}, u32[]{:S(2)}, u32[]{:S(2)}) %collective-permute-start.14) | collective-permute-done | bytes 8224 | tf_op jit(solution)/shard_map/ppermute | solution.py:147
  122.2 0.1 collective-permute-start.15
  122.3 2.9 %collective-permute-start.16 = (f32[2,2048]{1,0:T(2,128)S(1)}, f32[2,2048]{1,0:T(2,128)S(1)}, u32[]{:S(2)}, u32[]{:S(2)}) collective-permute-start(f32[2,2048]{1,0:T(2,128)S(1)} %pad_maximum_fusion.2.refs_1_), channel_id=1, source_target_pairs={{0,4},{2,6},{4,0},{6,2},{1,5},{3,7},{5,1},{7,3},{8,12},{10,14},{12... | collective-permute-start | bytes 49160 | tf_op jit(solution)/shard_map/ppermute | solution.py:147
  125.2 0.9 collective-permute-start.17
  126.1 5.2 %all-to-all-done.2.refs_3_.refs_7_ = bf16[8,4,32,2048]{3,2,1,0:T(8,128)(2,1)} async-done(((bf16[8,4,32,2048]{3,2,1,0:T(8,128)(2,1)}), bf16[8,4,32,2048]{3,2,1,0:T(8,128)(2,1)}, u32[]{:S(2)}, u32[]{:S(2)}) %all-to-all-start.2) | async-done | bytes 4194336 | tf_op jit(solution)/shard_map/all_to_all | solution.py:497
  131.4 3.4 %surface_near.1 = (f32[32,16384]{1,0:T(8,128)}, f32[128,64]{1,0:T(8,128)S(1)}) custom-call(s32[1]{0:T(128)} %bitcast.refs_0_, f32[2,2048]{1,0:T(2,128)S(1)} %pad_maximum_fusion.2.refs_1_, bf16[32,16384]{1,0:T(8,128)(2,1)S(1)} %copy-done, bf16[8,4,32,2048]{3,2,1,0:T(8,128)(2,1)} %all-to-all-done.2.refs_3_.refs_7_, bf16[4,32,16384]{2,1,0:T(8,128)(2,1)} %refs_8_.1, ...), custom_call_target="tpu_custom_call" | custom-call | tf_op jit(solution)/shard_map/surface_near/pallas_call | solution.py:446
  134.8 0.0 collective-permute-done.15.refs_1_
  134.8 0.0 collective-permute-done.16.refs_2_
  134.8 0.0 collective-permute-done.17.refs_3_
  134.8 8.2 %surface_far.1 = (f32[32,16384]{1,0:T(8,128)}, f32[16,4,128]{2,1,0:T(4,128)S(1)}) custom-call(s32[1]{0:T(128)} %bitcast.refs_0_, f32[2,2048]{1,0:T(2,128)S(1)} %collective-permute-done.15.refs_1_, f32[2,2048]{1,0:T(2,128)S(1)} %collective-permute-done.16.refs_2_, f32[2,2048]{1,0:T(2,128)S(1)} %collective-permute-done.17.refs_3_, ...), custom_call_target="tpu_custom_call", output_to_operand_aliasing={{0}: (5, {})} | custom-call | tf_op jit(solution)/shard_map/surface_far/pallas_call | solution.py:446
  142.9 11.2 %all_to_all.20 = f32[16,4,128]{2,1,0:T(4,128)S(1)} all-to-all(f32[16,4,128]{2,1,0:T(4,128)S(1)} %get-tuple-element.49), channel_id=1, replica_groups=mesh['z'=4,'ylo'=2,'core'=2,'x'=4,'yhi'=2] {'z','ylo','core'}, dimensions={0} | all-to-all | bytes 65536 | tf_op jit(solution)/shard_map/all_to_all | solution.py:505
  154.2 0.1 reshape.27
  154.3 0.6 copy.23
  (22 shorter events, 0.3 us)
Async XLA Ops:
  0.6 1.3 copy-start.6
  2.0 8.7 %copy-start = (bf16[32,16384]{1,0:T(8,128)(2,1)S(1)}, bf16[32,16384]{1,0:T(8,128)(2,1)}, u32[]{:S(2)}) copy-start(bf16[32,16384]{1,0:T(8,128)(2,1)} %refs_6_.3) | copy-start | bytes 3145732
  3.1 8.7 %copy-start.5 = (bf16[16384]{0:T(1024)(128)(2,1)S(1)}, bf16[16384]{0:T(1024)(128)(2,1)}, u32[]{:S(2)}) copy-start(bf16[16384]{0:T(1024)(128)(2,1)} %param.16) | copy-start | bytes 98308
  3.1 23.8 %all-to-all-start = ((bf16[8,32,2176]{2,1,0:T(8,128)(2,1)}), bf16[8,32,2176]{2,1,0:T(8,128)(2,1)S(1)}, u32[]{:S(2)}, u32[]{:S(2)}) async-start(bf16[8,32,2176]{2,1,0:T(8,128)(2,1)} %pad_maximum_fusion), calls=%async_computation | async-start | bytes 2228224 | tf_op jit(solution)/shard_map/all_to_all | solution.py:476
  10.7 20.5 %copy-start.7 = (f32[512]{0:T(512)S(1)}, f32[512]{0:T(512)}, u32[]{:S(2)}) copy-start(f32[512]{0:T(512)} %param.15) | copy-start | bytes 6148
  26.9 24.2 %all-to-all-start.1 = ((bf16[8,32,2048]{2,1,0:T(8,128)(2,1)}), bf16[8,32,2048]{2,1,0:T(8,128)(2,1)S(1)}, u32[]{:S(2)}, u32[]{:S(2)}) async-start(bf16[8,32,2048]{2,1,0:T(8,128)(2,1)} %bitcast.38), calls=%async_computation.1 | async-start | bytes 2097152 | tf_op jit(solution)/shard_map/all_to_all | solution.py:484
  31.4 32.9 %copy-start.8 = (f32[256]{0:T(256)S(1)}, f32[256]{0:T(256)}, u32[]{:S(2)}) copy-start(f32[256]{0:T(256)} %param.21) | copy-start | bytes 3076
  36.1 28.3 %copy-start.4 = (bf16[256,256]{1,0:T(8,128)(2,1)S(1)}, bf16[256,256]{1,0:T(8,128)(2,1)}, u32[]{:S(2)}) copy-start(bf16[256,256]{1,0:T(8,128)(2,1)} %mixer_ref.1) | copy-start | bytes 393220
  36.1 2.7 %collective-permute-start = (f32[672,128]{1,0:T(8,128)}, f32[672,128]{1,0:T(8,128)S(1)}, u32[]{:S(2)}, u32[]{:S(2)}) collective-permute-start(f32[672,128]{1,0:T(8,128)} %get-tuple-element.32), channel_id=1, source_target_pairs={{0,8},{8,0},{1,9},{9,1},{2,10},{10,2},{3,11},{11,3},{4,12},{12,4},... | collective-permute-start | bytes 1032200 | tf_op jit(solution)/shard_map/ppermute | solution.py:147
  39.8 5.0 %collective-permute-start.1 = (f32[168,128]{1,0:T(8,128)S(1)}, f32[168,128]{1,0:T(8,128)S(1)}, u32[]{:S(2)}, u32[]{:S(2)}) collective-permute-start(f32[168,128]{1,0:T(8,128)S(1)} %get-tuple-element.52), channel_id=1, source_target_pairs={{0,32},{32,0},{64,96},{96,64},{1,33},{33,1},{65,97},{97,65},{2,34}... | collective-permute-start | bytes 258056 | tf_op jit(solution)/shard_map/ppermute | solution.py:147
  41.5 7.4 %collective-permute-start.2 = (f32[168,128]{1,0:T(8,128)S(1)}, f32[168,128]{1,0:T(8,128)S(1)}, u32[]{:S(2)}, u32[]{:S(2)}) collective-permute-start(f32[168,128]{1,0:T(8,128)S(1)} %get-tuple-element.51), channel_id=1, source_target_pairs={{0,64},{32,96},{64,0},{96,32},{1,65},{33,97},{65,1},{97,33},{2,66}... | collective-permute-start | bytes 258056 | tf_op jit(solution)/shard_map/ppermute | solution.py:147
  44.8 6.3 %collective-permute-start.3 = (f32[168,128]{1,0:T(8,128)S(1)}, f32[168,128]{1,0:T(8,128)S(1)}, u32[]{:S(2)}, u32[]{:S(2)}) collective-permute-start(f32[168,128]{1,0:T(8,128)S(1)} %get-tuple-element.50), channel_id=1, source_target_pairs={{0,96},{32,64},{64,32},{96,0},{1,97},{33,65},{65,33},{97,1},{2,98}... | collective-permute-start | bytes 258056 | tf_op jit(solution)/shard_map/ppermute | solution.py:147
  51.2 4.3 %collective-permute-start.4 = (f32[168,128]{1,0:T(8,128)S(1)}, f32[168,128]{1,0:T(8,128)S(1)}, u32[]{:S(2)}, u32[]{:S(2)}) collective-permute-start(f32[168,128]{1,0:T(8,128)S(1)} %fusion), channel_id=1, source_target_pairs={{0,2},{2,0},{4,6},{6,4},{1,3},{3,1},{5,7},{7,5},{8,10},{10,8},{12,... | collective-permute-start | bytes 258056 | tf_op jit(solution)/shard_map/ppermute | solution.py:147
  53.0 5.7 %collective-permute-start.5 = (f32[168,128]{1,0:T(8,128)S(1)}, f32[168,128]{1,0:T(8,128)S(1)}, u32[]{:S(2)}, u32[]{:S(2)}) collective-permute-start(f32[168,128]{1,0:T(8,128)S(1)} %fusion), channel_id=1, source_target_pairs={{0,4},{2,6},{4,0},{6,2},{1,5},{3,7},{5,1},{7,3},{8,12},{10,14},{12... | collective-permute-start | bytes 258056 | tf_op jit(solution)/shard_map/ppermute | solution.py:147
  55.4 5.5 %collective-permute-start.6 = (f32[168,128]{1,0:T(8,128)S(1)}, f32[168,128]{1,0:T(8,128)S(1)}, u32[]{:S(2)}, u32[]{:S(2)}) collective-permute-start(f32[168,128]{1,0:T(8,128)S(1)} %fusion), channel_id=1, source_target_pairs={{0,6},{2,4},{4,2},{6,0},{1,7},{3,5},{5,3},{7,1},{8,14},{10,12},{12... | collective-permute-start | bytes 258056 | tf_op jit(solution)/shard_map/ppermute | solution.py:147
  60.9 6.5 %collective-permute-start.7 = (f32[168,128]{1,0:T(8,128)S(1)}, f32[168,128]{1,0:T(8,128)S(1)}, u32[]{:S(2)}, u32[]{:S(2)}) collective-permute-start(f32[168,128]{1,0:T(8,128)S(1)} %add_add_fusion.1), channel_id=1, source_target_pairs={{0,1},{1,0},{16,17},{17,16},{2,3},{3,2},{18,19},{19,18},{4,5},{5,4... | collective-permute-start | bytes 258056 | tf_op jit(solution)/shard_map/ppermute | solution.py:147
  63.7 3.8 %collective-permute-start.8 = (f32[168,128]{1,0:T(8,128)S(1)}, f32[168,128]{1,0:T(8,128)S(1)}, u32[]{:S(2)}, u32[]{:S(2)}) collective-permute-start(f32[168,128]{1,0:T(8,128)S(1)} %add_add_fusion.1), channel_id=1, source_target_pairs={{0,16},{1,17},{16,0},{17,1},{2,18},{3,19},{18,2},{19,3},{4,20},{5,... | collective-permute-start | bytes 258056 | tf_op jit(solution)/shard_map/ppermute | solution.py:147
  64.1 4.8 %collective-permute-start.9 = (f32[168,128]{1,0:T(8,128)S(1)}, f32[168,128]{1,0:T(8,128)S(1)}, u32[]{:S(2)}, u32[]{:S(2)}) collective-permute-start(f32[168,128]{1,0:T(8,128)S(1)} %add_add_fusion.1), channel_id=1, source_target_pairs={{0,17},{1,16},{16,1},{17,0},{2,19},{3,18},{18,3},{19,2},{4,21},{5,... | collective-permute-start | bytes 258056 | tf_op jit(solution)/shard_map/ppermute | solution.py:147
  68.8 62.5 %all-to-all-start.2 = ((bf16[8,4,32,2048]{3,2,1,0:T(8,128)(2,1)}), bf16[8,4,32,2048]{3,2,1,0:T(8,128)(2,1)}, u32[]{:S(2)}, u32[]{:S(2)}) async-start(bf16[8,4,32,2048]{3,2,1,0:T(8,128)(2,1)} %get-tuple-element.44), calls=%async_computation.2 | async-start | bytes 8388608 | tf_op jit(solution)/shard_map/all_to_all | solution.py:497
  73.4 58.0 %copy-start.2 = (s32[4,16384]{1,0:T(4,128)S(1)}, s32[4,16384]{1,0:T(4,128)}, u32[]{:S(2)}) copy-start(s32[4,16384]{1,0:T(4,128)} %refs_10_.1) | copy-start | bytes 786436
  73.4 58.0 %copy-start.3 = (s32[4,16384]{1,0:T(4,128)S(1)}, s32[4,16384]{1,0:T(4,128)}, u32[]{:S(2)}) copy-start(s32[4,16384]{1,0:T(4,128)} %refs_11_.1) | copy-start | bytes 786436
  73.4 3.9 %collective-permute-start.10 = (f32[168,128]{1,0:T(8,128)S(1)}, f32[168,128]{1,0:T(8,128)S(1)}, u32[]{:S(2)}, u32[]{:S(2)}) collective-permute-start(f32[168,128]{1,0:T(8,128)S(1)} %add_add_fusion), channel_id=1, source_target_pairs={{0,32},{32,0},{64,96},{96,64},{1,33},{33,1},{65,97},{97,65},{2,34}... | collective-permute-start | bytes 258056 | tf_op jit(solution)/shard_map/ppermute | solution.py:147
  73.5 4.9 %collective-permute-start.11 = (f32[168,128]{1,0:T(8,128)S(1)}, f32[168,128]{1,0:T(8,128)S(1)}, u32[]{:S(2)}, u32[]{:S(2)}) collective-permute-start(f32[168,128]{1,0:T(8,128)S(1)} %add_add_fusion), channel_id=1, source_target_pairs={{0,64},{32,96},{64,0},{96,32},{1,65},{33,97},{65,1},{97,33},{2,66}... | collective-permute-start | bytes 258056 | tf_op jit(solution)/shard_map/ppermute | solution.py:147
  75.2 4.5 %collective-permute-start.12 = (f32[168,128]{1,0:T(8,128)S(1)}, f32[168,128]{1,0:T(8,128)S(1)}, u32[]{:S(2)}, u32[]{:S(2)}) collective-permute-start(f32[168,128]{1,0:T(8,128)S(1)} %add_add_fusion), channel_id=1, source_target_pairs={{0,96},{32,64},{64,32},{96,0},{1,97},{33,65},{65,33},{97,1},{2,98}... | collective-permute-start | bytes 258056 | tf_op jit(solution)/shard_map/ppermute | solution.py:147
  79.8 6.1 %collective-permute-start.13 = (f32[4,168,128]{2,1,0:T(8,128)S(1)}, f32[4,168,128]{2,1,0:T(8,128)S(1)}, u32[]{:S(2)}, u32[]{:S(2)}) collective-permute-start(f32[4,168,128]{2,1,0:T(8,128)S(1)} %pad_maximum_fusion.1.refs_1_), channel_id=1, source_target_pairs={{0,8},{8,0},{1,9},{9,1},{2,10},{10,2},{3,11},{11,3},{4,12},{12,4},... | collective-permute-start | bytes 1032200 | tf_op jit(solution)/shard_map/ppermute | solution.py:147
  85.9 1.6 %copy-start.1 = (bf16[512,2048]{1,0:T(8,128)(2,1)S(1)}, bf16[512,2048]{1,0:T(8,128)(2,1)}, u32[]{:S(2)}) copy-start(bf16[512,2048]{1,0:T(8,128)(2,1)} %get-tuple-element.43.refs_3_) | copy-start | bytes 6291460
  108.3 13.9 %collective-permute-start.14 = (f32[1,2048]{1,0:T(1,128)S(1)}, f32[1,2048]{1,0:T(1,128)S(1)}, u32[]{:S(2)}, u32[]{:S(2)}) collective-permute-start(f32[1,2048]{1,0:T(1,128)S(1)} %solve_continuation.1), channel_id=1, source_target_pairs={{0,1},{1,0},{2,3},{3,2},{4,5},{5,4},{6,7},{7,6},{8,9},{9,8},{10,11... | collective-permute-start | bytes 24584 | tf_op jit(solution)/shard_map/ppermute | solution.py:147
  122.2 12.6 %collective-permute-start.15 = (f32[2,2048]{1,0:T(2,128)S(1)}, f32[2,2048]{1,0:T(2,128)S(1)}, u32[]{:S(2)}, u32[]{:S(2)}) collective-permute-start(f32[2,2048]{1,0:T(2,128)S(1)} %pad_maximum_fusion.2.refs_1_), channel_id=1, source_target_pairs={{0,2},{2,0},{4,6},{6,4},{1,3},{3,1},{5,7},{7,5},{8,10},{10,8},{12,... | collective-permute-start | bytes 49160 | tf_op jit(solution)/shard_map/ppermute | solution.py:147
  122.3 12.5 %collective-permute-start.16 = (f32[2,2048]{1,0:T(2,128)S(1)}, f32[2,2048]{1,0:T(2,128)S(1)}, u32[]{:S(2)}, u32[]{:S(2)}) collective-permute-start(f32[2,2048]{1,0:T(2,128)S(1)} %pad_maximum_fusion.2.refs_1_), channel_id=1, source_target_pairs={{0,4},{2,6},{4,0},{6,2},{1,5},{3,7},{5,1},{7,3},{8,12},{10,14},{12... | collective-permute-start | bytes 49160 | tf_op jit(solution)/shard_map/ppermute | solution.py:147
  125.2 9.6 %collective-permute-start.17 = (f32[2,2048]{1,0:T(2,128)S(1)}, f32[2,2048]{1,0:T(2,128)S(1)}, u32[]{:S(2)}, u32[]{:S(2)}) collective-permute-start(f32[2,2048]{1,0:T(2,128)S(1)} %pad_maximum_fusion.2.refs_1_), channel_id=1, source_target_pairs={{0,6},{2,4},{4,2},{6,0},{1,7},{3,5},{5,3},{7,1},{8,14},{10,12},{12... | collective-permute-start | bytes 49160 | tf_op jit(solution)/shard_map/ppermute | solution.py:147

commit v9 on v7

--- a/solution.py
+++ b/solution.py
@@ -372,7 +372,7 @@
         adjoint = base
         for later in range(STEPS - date):
             adjoint = adjoint + held[date + later] * weights[later]
-        terms = (adjoint * shock_ref[date].astype(f32)).astype(bf16).astype(f32)
+        terms = adjoint * shock_ref[date].astype(f32)
         bucket = bucket_ref[date:date + 1, :]
         column = (bucket & (STRIKE_ROWS - 1)).astype(f32).astype(bf16)
         chosen = jnp.where(strikes == column, jnp.bfloat16(1), jnp.bfloat16(0))
@@ -454,8 +454,8 @@
     )
     share, moved = sum_over_cores_and_z(kept, other, moved)
     sent, weights = increments(moved, corr_gen, basket, slab_part)
-    share = sum_of_exchange(share, "x")
-    parts = exchange_with_others(share, ("ylo", "yhi"), 4)
+    share = sum_of_exchange(share, ("ylo", "yhi"))
+    parts = exchange_with_others(share, "x", 4)
     parts, sent = lax.optimization_barrier((parts, sent))
     share = (share + parts[0]) + (parts[1] + parts[2])
     gains = lax.all_to_all(sent, STOCK_AXES, 0, 0, tiled=True)

time: 155 us -> 154 us (level)
  transfers between devices with their start and end apart: 21 -> 21, of which waited for: 13 -> 14; matrix products, arithmetic and copies ran while one was open for 2% -> 2% of each run, Pallas kernels for 19% -> 19%
where the time goes in v9:
time: 154 us
  waiting for transfers between devices  48.8 us (32%)
  starting transfers between devices  47 us (31%)
  Pallas kernels  38.8 us (25%)
  blocking collectives  10.8 us (7%)
  local copies, waits for them, and re-layouts  5.11 us (3%)
  other arithmetic  2.4 us (2%)
    ppermute x18, waiting for transfers between devices, exchange_with_others(): lax.ppermute(sent, axes, [(i, i ^ flip) for i in range(count)])  33.7 us
    ppermute x18, starting transfers between devices, exchange_with_others(): lax.ppermute(sent, axes, [(i, i ^ flip) for i in range(count)])  29.8 us
    pallas_call x1, Pallas kernels, solve_continuation(): pl.pallas_call(lambda *refs: solve_kernel(*refs, scale=1.0 / path_count),...  20.7 us
    all_to_all x1, waiting for transfers between devices, per_device(): lax.all_to_all(jnp.concatenate([pieces, table], axis=2), STOCK_AXES, 0, 0...  15 us
    all_to_all x1, blocking collectives, per_device(): surface = lax.all_to_all(surface, PATH_AXES, 0, 0, tiled=True)  10.8 us
    pallas_call x1, Pallas kernels, surface_and_delta(): pl.pallas_call(surface_kernel, out_shape=(jax.ShapeDtypeStruct((32, local...  10.3 us
    all_to_all x1, starting transfers between devices, per_device(): lax.all_to_all(jnp.concatenate([pieces, table], axis=2), STOCK_AXES, 0, 0...  7.61 us
    all_to_all x1, starting transfers between devices, per_device(): gains = lax.all_to_all(sent, STOCK_AXES, 0, 0, tiled=True)  5.33 us
  transfers between devices with their start and end apart: 21, of which 14 were waited for; matrix products, arithmetic and copies ran while one was open for 2% of the time, Pallas kernels for 19%

profile of v9, /device:TPU:1, one launch (start us, length us, event | category | flops | bytes accessed | tf_op | source)
XLA Modules:
  0.0 153.6 jit_solution(17908666801099859303)
XLA Ops:
  0.6 1.3 copy.27
  2.0 0.0 copy-start
  2.0 1.1 pad_maximum_fusion
  3.1 7.6 %all-to-all-start = ((bf16[8,32,2176]{2,1,0:T(8,128)(2,1)}), bf16[8,32,2176]{2,1,0:T(8,128)(2,1)S(1)}, u32[]{:S(2)}, u32[]{:S(2)}) async-start(bf16[8,32,2176]{2,1,0:T(8,128)(2,1)} %pad_maximum_fusion), calls=%async_computation | async-start | bytes 2228224 | tf_op jit(solution)/shard_map/all_to_all | solution.py:440
  10.7 0.0 copy-start.7
  10.7 1.1 copy.28
  11.9 15.0 %all-to-all-done.moved_ref.table_ref = bf16[8,32,2176]{2,1,0:T(8,128)(2,1)S(1)} async-done(((bf16[8,32,2176]{2,1,0:T(8,128)(2,1)}), bf16[8,32,2176]{2,1,0:T(8,128)(2,1)S(1)}, u32[]{:S(2)}, u32[]{:S(2)}) %all-to-all-start) | async-done | bytes 1114144 | tf_op jit(solution)/shard_map/all_to_all | solution.py:440
  26.9 4.2 %all-to-all-start.1 = ((bf16[8,32,2048]{2,1,0:T(8,128)(2,1)}), bf16[8,32,2048]{2,1,0:T(8,128)(2,1)S(1)}, u32[]{:S(2)}, u32[]{:S(2)}) async-start(bf16[8,32,2048]{2,1,0:T(8,128)(2,1)} %bitcast.38), calls=%async_computation.1 | async-start | bytes 2097152 | tf_op jit(solution)/shard_map/all_to_all | solution.py:448
  31.1 0.1 pad_add_fusion.1.slab_ref
  31.2 0.1 copy.20.bias_ref
  31.4 0.0 copy-start.8
  31.4 4.7 %regression_sums.1 = (bf16[512,2048]{1,0:T(8,128)(2,1)}, f32[672,128]{1,0:T(8,128)}, f32[672,128]{1,0:T(8,128)}) custom-call(s32[2]{0:T(128)S(1)} %pad_add_fusion.1.slab_ref, bf16[8,32,2176]{2,1,0:T(8,128)(2,1)S(1)} %all-to-all-done.moved_ref.table_ref, bf16[8,32,2176]{2,1,0:T(8,128)(2,1)S(1)} %all-to-all-done.moved_ref.table_ref, f32[32,512]{1,0:T(8,128)} %weight_ref, ...), custom_call_target="tpu_custom_call" | custom-call | tf_op jit(solution)/shard_map/regression_sums/pallas_call | solution.py:109
  36.1 1.2 collective-permute-start
  37.3 1.5 collective-permute-done
  38.8 1.0 add.49
  39.8 1.7 %collective-permute-start.1 = (f32[168,128]{1,0:T(8,128)S(1)}, f32[168,128]{1,0:T(8,128)S(1)}, u32[]{:S(2)}, u32[]{:S(2)}) collective-permute-start(f32[168,128]{1,0:T(8,128)S(1)} %get-tuple-element.48), channel_id=1, source_target_pairs={{0,32},{32,0},{64,96},{96,64},{1,33},{33,1},{65,97},{97,65},{2,34}... | collective-permute-start | bytes 258056 | tf_op jit(solution)/shard_map/ppermute | solution.py:147
  41.6 3.3 %collective-permute-start.2 = (f32[168,128]{1,0:T(8,128)S(1)}, f32[168,128]{1,0:T(8,128)S(1)}, u32[]{:S(2)}, u32[]{:S(2)}) collective-permute-start(f32[168,128]{1,0:T(8,128)S(1)} %get-tuple-element.47), channel_id=1, source_target_pairs={{0,64},{32,96},{64,0},{96,32},{1,65},{33,97},{65,1},{97,33},{2,66}... | collective-permute-start | bytes 258056 | tf_op jit(solution)/shard_map/ppermute | solution.py:147
  44.9 0.0 collective-permute-start.3
  44.9 0.0 collective-permute-done.1
  44.9 4.1 %collective-permute-done.2 = f32[168,128]{1,0:T(8,128)S(1)} collective-permute-done((f32[168,128]{1,0:T(8,128)S(1)}, f32[168,128]{1,0:T(8,128)S(1)}, u32[]{:S(2)}, u32[]{:S(2)}) %collective-permute-start.2) | collective-permute-done | bytes 86048 | tf_op jit(solution)/shard_map/ppermute | solution.py:147
  49.0 2.2 %collective-permute-done.3 = f32[168,128]{1,0:T(8,128)S(1)} collective-permute-done((f32[168,128]{1,0:T(8,128)S(1)}, f32[168,128]{1,0:T(8,128)S(1)}, u32[]{:S(2)}, u32[]{:S(2)}) %collective-permute-start.3) | collective-permute-done | bytes 86048 | tf_op jit(solution)/shard_map/ppermute | solution.py:147
  51.2 0.0 all-to-all-done.1.moved_ref
  51.2 3.3 %collective-permute-start.4 = (f32[168,128]{1,0:T(8,128)S(1)}, f32[168,128]{1,0:T(8,128)S(1)}, u32[]{:S(2)}, u32[]{:S(2)}) collective-permute-start(f32[168,128]{1,0:T(8,128)S(1)} %fusion), channel_id=1, source_target_pairs={{0,1},{1,0},{16,17},{17,16},{2,3},{3,2},{18,19},{19,18},{4,5},{5,4... | collective-permute-start | bytes 258056 | tf_op jit(solution)/shard_map/ppermute | solution.py:147
  54.5 0.4 collective-permute-start.5
  54.9 0.0 collective-permute-start.6
  54.9 1.5 collective-permute-done.4
  56.4 2.2 %collective-permute-done.5 = f32[168,128]{1,0:T(8,128)S(1)} collective-permute-done((f32[168,128]{1,0:T(8,128)S(1)}, f32[168,128]{1,0:T(8,128)S(1)}, u32[]{:S(2)}, u32[]{:S(2)}) %collective-permute-start.5) | collective-permute-done | bytes 86048 | tf_op jit(solution)/shard_map/ppermute | solution.py:147
  58.6 0.9 collective-permute-done.6
  59.5 1.3 collective-permute-start.7
  60.8 2.4 %collective-permute-start.8 = (f32[168,128]{1,0:T(8,128)S(1)}, f32[168,128]{1,0:T(8,128)S(1)}, u32[]{:S(2)}, u32[]{:S(2)}) collective-permute-start(f32[168,128]{1,0:T(8,128)S(1)} %add_add_fusion.1), channel_id=1, source_target_pairs={{0,4},{2,6},{4,0},{6,2},{1,5},{3,7},{5,1},{7,3},{8,12},{10,14},{12... | collective-permute-start | bytes 258056 | tf_op jit(solution)/shard_map/ppermute | solution.py:147
  63.2 0.2 collective-permute-start.9
  63.4 0.1 copy.21.basket_ref
  63.6 0.0 copy-done.4
  63.6 3.1 %increments.1 = (bf16[8,4,32,2048]{3,2,1,0:T(8,128)(2,1)}, f32[256,128]{1,0:T(8,128)S(1)}) custom-call(bf16[8,32,2048]{2,1,0:T(8,128)(2,1)S(1)} %all-to-all-done.1.moved_ref, bf16[256,256]{1,0:T(8,128)(2,1)S(1)} %copy-done.4, f32[256,1]{1,0:T(8,128)S(1)} %copy.21.basket_ref), custom_call_target="tpu_custom_call" | custom-call | tf_op jit(solution)/shard_map/increments/pallas_call | solution.py:331
  66.7 0.0 collective-permute-done.7
  66.7 0.0 collective-permute-done.8
  66.7 1.1 collective-permute-done.9
  67.8 5.3 %all-to-all-start.2 = ((bf16[8,4,32,2048]{3,2,1,0:T(8,128)(2,1)}), bf16[8,4,32,2048]{3,2,1,0:T(8,128)(2,1)}, u32[]{:S(2)}, u32[]{:S(2)}) async-start(bf16[8,4,32,2048]{3,2,1,0:T(8,128)(2,1)} %get-tuple-element.42), calls=%async_computation.2 | async-start | bytes 8388608 | tf_op jit(solution)/shard_map/all_to_all | solution.py:461
  73.1 0.0 copy-start.3
  73.1 0.1 collective-permute-start.10
  73.2 1.8 %collective-permute-start.11 = (f32[168,128]{1,0:T(8,128)S(1)}, f32[168,128]{1,0:T(8,128)S(1)}, u32[]{:S(2)}, u32[]{:S(2)}) collective-permute-start(f32[168,128]{1,0:T(8,128)S(1)} %add_add_fusion), channel_id=1, source_target_pairs={{0,64},{32,96},{64,0},{96,32},{1,65},{33,97},{65,1},{97,33},{2,66}... | collective-permute-start | bytes 258056 | tf_op jit(solution)/shard_map/ppermute | solution.py:147
  75.0 2.1 %collective-permute-start.12 = (f32[168,128]{1,0:T(8,128)S(1)}, f32[168,128]{1,0:T(8,128)S(1)}, u32[]{:S(2)}, u32[]{:S(2)}) collective-permute-start(f32[168,128]{1,0:T(8,128)S(1)} %add_add_fusion), channel_id=1, source_target_pairs={{0,96},{32,64},{64,32},{96,0},{1,97},{33,65},{65,33},{97,1},{2,98}... | collective-permute-start | bytes 258056 | tf_op jit(solution)/shard_map/ppermute | solution.py:147
  77.1 0.0 collective-permute-done.10
  77.1 1.1 collective-permute-done.11
  78.2 1.4 collective-permute-done.12
  79.6 4.8 %collective-permute-start.13 = (f32[4,168,128]{2,1,0:T(8,128)S(1)}, f32[4,168,128]{2,1,0:T(8,128)S(1)}, u32[]{:S(2)}, u32[]{:S(2)}) collective-permute-start(f32[4,168,128]{2,1,0:T(8,128)S(1)} %pad_maximum_fusion.1.refs_1_), channel_id=1, source_target_pairs={{0,8},{8,0},{1,9},{9,1},{2,10},{10,2},{3,11},{11,3},{4,12},{12,4},... | collective-permute-start | bytes 1032200 | tf_op jit(solution)/shard_map/ppermute | solution.py:147
  84.5 0.1 pad_add_fusion.refs_0_
  84.5 1.2 collective-permute-done.13.refs_2_
  85.7 1.6 %copy-done.1 = bf16[512,2048]{1,0:T(8,128)(2,1)S(1)} copy-done((bf16[512,2048]{1,0:T(8,128)(2,1)S(1)}, bf16[512,2048]{1,0:T(8,128)(2,1)}, u32[]{:S(2)}) %copy-start.1) | copy-done | bytes 2097176
  87.3 20.7 %solve_continuation.1 = f32[1,2048]{1,0:T(1,128)S(1)} custom-call(s32[2]{0:T(128)S(1)} %pad_add_fusion.refs_0_, f32[4,168,128]{2,1,0:T(8,128)S(1)} %pad_maximum_fusion.1.refs_1_, f32[4,168,128]{2,1,0:T(8,128)S(1)} %collective-permute-done.13.refs_2_, bf16[512,2048]{1,0:T(8,128)(2,1)S(1)} %copy-done.1), custom_call_target="tpu_custom_call" | custom-call | tf_op jit(solution)/shard_map/solve_continuation/pallas_call | solution.py:277
  108.1 3.2 %collective-permute-start.14 = (f32[1,2048]{1,0:T(1,128)S(1)}, f32[1,2048]{1,0:T(1,128)S(1)}, u32[]{:S(2)}, u32[]{:S(2)}) collective-permute-start(f32[1,2048]{1,0:T(1,128)S(1)} %solve_continuation.1), channel_id=1, source_target_pairs={{0,1},{1,0},{2,3},{3,2},{4,5},{5,4},{6,7},{7,6},{8,9},{9,8},{10,11... | collective-permute-start | bytes 24584 | tf_op jit(solution)/shard_map/ppermute | solution.py:147
  111.3 10.7 %collective-permute-done.14 = f32[1,2048]{1,0:T(1,128)S(1)} collective-permute-done((f32[1,2048]{1,0:T(1,128)S(1)}, f32[1,2048]{1,0:T(1,128)S(1)}, u32[]{:S(2)}, u32[]{:S(2)}) %collective-permute-start.14) | collective-permute-done | bytes 8224 | tf_op jit(solution)/shard_map/ppermute | solution.py:147
  122.0 0.1 collective-permute-start.15
  122.1 3.1 %collective-permute-start.16 = (f32[2,2048]{1,0:T(2,128)S(1)}, f32[2,2048]{1,0:T(2,128)S(1)}, u32[]{:S(2)}, u32[]{:S(2)}) collective-permute-start(f32[2,2048]{1,0:T(2,128)S(1)} %pad_maximum_fusion.2.refs_0_), channel_id=1, source_target_pairs={{0,4},{2,6},{4,0},{6,2},{1,5},{3,7},{5,1},{7,3},{8,12},{10,14},{12... | collective-permute-start | bytes 49160 | tf_op jit(solution)/shard_map/ppermute | solution.py:147
  125.1 0.8 collective-permute-start.17
  125.9 1.6 %collective-permute-done.15.refs_1_ = f32[2,2048]{1,0:T(2,128)S(1)} collective-permute-done((f32[2,2048]{1,0:T(2,128)S(1)}, f32[2,2048]{1,0:T(2,128)S(1)}, u32[]{:S(2)}, u32[]{:S(2)}) %collective-permute-start.15) | collective-permute-done | bytes 16416 | tf_op jit(solution)/shard_map/ppermute | solution.py:147
  127.6 4.2 %collective-permute-done.16.refs_2_ = f32[2,2048]{1,0:T(2,128)S(1)} collective-permute-done((f32[2,2048]{1,0:T(2,128)S(1)}, f32[2,2048]{1,0:T(2,128)S(1)}, u32[]{:S(2)}, u32[]{:S(2)}) %collective-permute-start.16) | collective-permute-done | bytes 16416 | tf_op jit(solution)/shard_map/ppermute | solution.py:147
  131.8 0.0 collective-permute-done.17.refs_3_
  131.8 0.0 all-to-all-done.2.refs_5_
  131.8 0.0 copy-done.2
  131.8 10.3 %surface_and_delta.1 = (f32[32,16384]{1,0:T(8,128)}, f32[16,4,128]{2,1,0:T(4,128)S(1)}) custom-call(s32[1]{0:T(128)} %bitcast.slab_ref, f32[2,2048]{1,0:T(2,128)S(1)} %pad_maximum_fusion.2.refs_0_, f32[2,2048]{1,0:T(2,128)S(1)} %collective-permute-done.15.refs_1_, f32[2,2048]{1,0:T(2,128)S(1)} %collective-permute-done.16.refs_2_, ...), custom_call_target="tpu_custom_call" | custom-call | tf_op jit(solution)/shard_map/surface_and_delta/pallas_call | solution.py:403
  142.1 10.8 %all_to_all.20 = f32[16,4,128]{2,1,0:T(4,128)S(1)} all-to-all(f32[16,4,128]{2,1,0:T(4,128)S(1)} %get-tuple-element.45), channel_id=1, replica_groups=mesh['z'=4,'ylo'=2,'core'=2,'x'=4,'yhi'=2] {'z','ylo','core'}, dimensions={0} | all-to-all | bytes 65536 | tf_op jit(solution)/shard_map/all_to_all | solution.py:469
  152.9 0.1 reshape.27
  153.0 0.6 copy.22
  (21 shorter events, 0.3 us)
Async XLA Ops:
  0.6 1.3 copy-start.6
  2.0 8.7 %copy-start = (bf16[32,16384]{1,0:T(8,128)(2,1)S(1)}, bf16[32,16384]{1,0:T(8,128)(2,1)}, u32[]{:S(2)}) copy-start(bf16[32,16384]{1,0:T(8,128)(2,1)} %refs_4_.1) | copy-start | bytes 3145732
  3.1 8.7 %copy-start.5 = (bf16[16384]{0:T(1024)(128)(2,1)S(1)}, bf16[16384]{0:T(1024)(128)(2,1)}, u32[]{:S(2)}) copy-start(bf16[16384]{0:T(1024)(128)(2,1)} %param.16) | copy-start | bytes 98308
  3.1 23.8 %all-to-all-start = ((bf16[8,32,2176]{2,1,0:T(8,128)(2,1)}), bf16[8,32,2176]{2,1,0:T(8,128)(2,1)S(1)}, u32[]{:S(2)}, u32[]{:S(2)}) async-start(bf16[8,32,2176]{2,1,0:T(8,128)(2,1)} %pad_maximum_fusion), calls=%async_computation | async-start | bytes 2228224 | tf_op jit(solution)/shard_map/all_to_all | solution.py:440
  10.7 20.5 %copy-start.7 = (f32[512]{0:T(512)S(1)}, f32[512]{0:T(512)}, u32[]{:S(2)}) copy-start(f32[512]{0:T(512)} %param.15) | copy-start | bytes 6148
  26.9 24.3 %all-to-all-start.1 = ((bf16[8,32,2048]{2,1,0:T(8,128)(2,1)}), bf16[8,32,2048]{2,1,0:T(8,128)(2,1)S(1)}, u32[]{:S(2)}, u32[]{:S(2)}) async-start(bf16[8,32,2048]{2,1,0:T(8,128)(2,1)} %bitcast.38), calls=%async_computation.1 | async-start | bytes 2097152 | tf_op jit(solution)/shard_map/all_to_all | solution.py:448
  31.4 32.1 %copy-start.8 = (f32[256]{0:T(256)S(1)}, f32[256]{0:T(256)}, u32[]{:S(2)}) copy-start(f32[256]{0:T(256)} %param.21) | copy-start | bytes 3076
  36.1 27.5 %copy-start.4 = (bf16[256,256]{1,0:T(8,128)(2,1)S(1)}, bf16[256,256]{1,0:T(8,128)(2,1)}, u32[]{:S(2)}) copy-start(bf16[256,256]{1,0:T(8,128)(2,1)} %mixer_ref.1) | copy-start | bytes 393220
  36.1 2.7 %collective-permute-start = (f32[672,128]{1,0:T(8,128)}, f32[672,128]{1,0:T(8,128)S(1)}, u32[]{:S(2)}, u32[]{:S(2)}) collective-permute-start(f32[672,128]{1,0:T(8,128)} %get-tuple-element.30), channel_id=1, source_target_pairs={{0,8},{8,0},{1,9},{9,1},{2,10},{10,2},{3,11},{11,3},{4,12},{12,4},... | collective-permute-start | bytes 1032200 | tf_op jit(solution)/shard_map/ppermute | solution.py:147
  39.8 5.0 %collective-permute-start.1 = (f32[168,128]{1,0:T(8,128)S(1)}, f32[168,128]{1,0:T(8,128)S(1)}, u32[]{:S(2)}, u32[]{:S(2)}) collective-permute-start(f32[168,128]{1,0:T(8,128)S(1)} %get-tuple-element.48), channel_id=1, source_target_pairs={{0,32},{32,0},{64,96},{96,64},{1,33},{33,1},{65,97},{97,65},{2,34}... | collective-permute-start | bytes 258056 | tf_op jit(solution)/shard_map/ppermute | solution.py:147
  41.6 7.4 %collective-permute-start.2 = (f32[168,128]{1,0:T(8,128)S(1)}, f32[168,128]{1,0:T(8,128)S(1)}, u32[]{:S(2)}, u32[]{:S(2)}) collective-permute-start(f32[168,128]{1,0:T(8,128)S(1)} %get-tuple-element.47), channel_id=1, source_target_pairs={{0,64},{32,96},{64,0},{96,32},{1,65},{33,97},{65,1},{97,33},{2,66}... | collective-permute-start | bytes 258056 | tf_op jit(solution)/shard_map/ppermute | solution.py:147
  44.9 6.3 %collective-permute-start.3 = (f32[168,128]{1,0:T(8,128)S(1)}, f32[168,128]{1,0:T(8,128)S(1)}, u32[]{:S(2)}, u32[]{:S(2)}) collective-permute-start(f32[168,128]{1,0:T(8,128)S(1)} %get-tuple-element.46), channel_id=1, source_target_pairs={{0,96},{32,64},{64,32},{96,0},{1,97},{33,65},{65,33},{97,1},{2,98}... | collective-permute-start | bytes 258056 | tf_op jit(solution)/shard_map/ppermute | solution.py:147
  51.2 5.2 %collective-permute-start.4 = (f32[168,128]{1,0:T(8,128)S(1)}, f32[168,128]{1,0:T(8,128)S(1)}, u32[]{:S(2)}, u32[]{:S(2)}) collective-permute-start(f32[168,128]{1,0:T(8,128)S(1)} %fusion), channel_id=1, source_target_pairs={{0,1},{1,0},{16,17},{17,16},{2,3},{3,2},{18,19},{19,18},{4,5},{5,4... | collective-permute-start | bytes 258056 | tf_op jit(solution)/shard_map/ppermute | solution.py:147
  54.5 4.0 %collective-permute-start.5 = (f32[168,128]{1,0:T(8,128)S(1)}, f32[168,128]{1,0:T(8,128)S(1)}, u32[]{:S(2)}, u32[]{:S(2)}) collective-permute-start(f32[168,128]{1,0:T(8,128)S(1)} %fusion), channel_id=1, source_target_pairs={{0,16},{1,17},{16,0},{17,1},{2,18},{3,19},{18,2},{19,3},{4,20},{5,... | collective-permute-start | bytes 258056 | tf_op jit(solution)/shard_map/ppermute | solution.py:147
  54.9 4.5 %collective-permute-start.6 = (f32[168,128]{1,0:T(8,128)S(1)}, f32[168,128]{1,0:T(8,128)S(1)}, u32[]{:S(2)}, u32[]{:S(2)}) collective-permute-start(f32[168,128]{1,0:T(8,128)S(1)} %fusion), channel_id=1, source_target_pairs={{0,17},{1,16},{16,1},{17,0},{2,19},{3,18},{18,3},{19,2},{4,21},{5,... | collective-permute-start | bytes 258056 | tf_op jit(solution)/shard_map/ppermute | solution.py:147
  59.5 7.2 %collective-permute-start.7 = (f32[168,128]{1,0:T(8,128)S(1)}, f32[168,128]{1,0:T(8,128)S(1)}, u32[]{:S(2)}, u32[]{:S(2)}) collective-permute-start(f32[168,128]{1,0:T(8,128)S(1)} %add_add_fusion.1), channel_id=1, source_target_pairs={{0,2},{2,0},{4,6},{6,4},{1,3},{3,1},{5,7},{7,5},{8,10},{10,8},{12,... | collective-permute-start | bytes 258056 | tf_op jit(solution)/shard_map/ppermute | solution.py:147
  60.8 5.9 %collective-permute-start.8 = (f32[168,128]{1,0:T(8,128)S(1)}, f32[168,128]{1,0:T(8,128)S(1)}, u32[]{:S(2)}, u32[]{:S(2)}) collective-permute-start(f32[168,128]{1,0:T(8,128)S(1)} %add_add_fusion.1), channel_id=1, source_target_pairs={{0,4},{2,6},{4,0},{6,2},{1,5},{3,7},{5,1},{7,3},{8,12},{10,14},{12... | collective-permute-start | bytes 258056 | tf_op jit(solution)/shard_map/ppermute | solution.py:147
  63.2 4.5 %collective-permute-start.9 = (f32[168,128]{1,0:T(8,128)S(1)}, f32[168,128]{1,0:T(8,128)S(1)}, u32[]{:S(2)}, u32[]{:S(2)}) collective-permute-start(f32[168,128]{1,0:T(8,128)S(1)} %add_add_fusion.1), channel_id=1, source_target_pairs={{0,6},{2,4},{4,2},{6,0},{1,7},{3,5},{5,3},{7,1},{8,14},{10,12},{12... | collective-permute-start | bytes 258056 | tf_op jit(solution)/shard_map/ppermute | solution.py:147
  67.8 64.0 %all-to-all-start.2 = ((bf16[8,4,32,2048]{3,2,1,0:T(8,128)(2,1)}), bf16[8,4,32,2048]{3,2,1,0:T(8,128)(2,1)}, u32[]{:S(2)}, u32[]{:S(2)}) async-start(bf16[8,4,32,2048]{3,2,1,0:T(8,128)(2,1)} %get-tuple-element.42), calls=%async_computation.2 | async-start | bytes 8388608 | tf_op jit(solution)/shard_map/all_to_all | solution.py:461
  73.1 58.7 %copy-start.2 = (s32[4,16384]{1,0:T(4,128)S(1)}, s32[4,16384]{1,0:T(4,128)}, u32[]{:S(2)}) copy-start(s32[4,16384]{1,0:T(4,128)} %refs_8_.1) | copy-start | bytes 786436
  73.1 58.7 %copy-start.3 = (s32[4,16384]{1,0:T(4,128)S(1)}, s32[4,16384]{1,0:T(4,128)}, u32[]{:S(2)}) copy-start(s32[4,16384]{1,0:T(4,128)} %refs_9_.1) | copy-start | bytes 786436
  73.1 3.9 %collective-permute-start.10 = (f32[168,128]{1,0:T(8,128)S(1)}, f32[168,128]{1,0:T(8,128)S(1)}, u32[]{:S(2)}, u32[]{:S(2)}) collective-permute-start(f32[168,128]{1,0:T(8,128)S(1)} %add_add_fusion), channel_id=1, source_target_pairs={{0,32},{32,0},{64,96},{96,64},{1,33},{33,1},{65,97},{97,65},{2,34}... | collective-permute-start | bytes 258056 | tf_op jit(solution)/shard_map/ppermute | solution.py:147
  73.2 4.9 %collective-permute-start.11 = (f32[168,128]{1,0:T(8,128)S(1)}, f32[168,128]{1,0:T(8,128)S(1)}, u32[]{:S(2)}, u32[]{:S(2)}) collective-permute-start(f32[168,128]{1,0:T(8,128)S(1)} %add_add_fusion), channel_id=1, source_target_pairs={{0,64},{32,96},{64,0},{96,32},{1,65},{33,97},{65,1},{97,33},{2,66}... | collective-permute-start | bytes 258056 | tf_op jit(solution)/shard_map/ppermute | solution.py:147
  75.0 4.5 %collective-permute-start.12 = (f32[168,128]{1,0:T(8,128)S(1)}, f32[168,128]{1,0:T(8,128)S(1)}, u32[]{:S(2)}, u32[]{:S(2)}) collective-permute-start(f32[168,128]{1,0:T(8,128)S(1)} %add_add_fusion), channel_id=1, source_target_pairs={{0,96},{32,64},{64,32},{96,0},{1,97},{33,65},{65,33},{97,1},{2,98}... | collective-permute-start | bytes 258056 | tf_op jit(solution)/shard_map/ppermute | solution.py:147
  79.6 6.1 %collective-permute-start.13 = (f32[4,168,128]{2,1,0:T(8,128)S(1)}, f32[4,168,128]{2,1,0:T(8,128)S(1)}, u32[]{:S(2)}, u32[]{:S(2)}) collective-permute-start(f32[4,168,128]{2,1,0:T(8,128)S(1)} %pad_maximum_fusion.1.refs_1_), channel_id=1, source_target_pairs={{0,8},{8,0},{1,9},{9,1},{2,10},{10,2},{3,11},{11,3},{4,12},{12,4},... | collective-permute-start | bytes 1032200 | tf_op jit(solution)/shard_map/ppermute | solution.py:147
  85.7 1.6 %copy-start.1 = (bf16[512,2048]{1,0:T(8,128)(2,1)S(1)}, bf16[512,2048]{1,0:T(8,128)(2,1)}, u32[]{:S(2)}) copy-start(bf16[512,2048]{1,0:T(8,128)(2,1)} %get-tuple-element.41.refs_3_) | copy-start | bytes 6291460
  108.1 13.9 %collective-permute-start.14 = (f32[1,2048]{1,0:T(1,128)S(1)}, f32[1,2048]{1,0:T(1,128)S(1)}, u32[]{:S(2)}, u32[]{:S(2)}) collective-permute-start(f32[1,2048]{1,0:T(1,128)S(1)} %solve_continuation.1), channel_id=1, source_target_pairs={{0,1},{1,0},{2,3},{3,2},{4,5},{5,4},{6,7},{7,6},{8,9},{9,8},{10,11... | collective-permute-start | bytes 24584 | tf_op jit(solution)/shard_map/ppermute | solution.py:147
  122.0 5.6 %collective-permute-start.15 = (f32[2,2048]{1,0:T(2,128)S(1)}, f32[2,2048]{1,0:T(2,128)S(1)}, u32[]{:S(2)}, u32[]{:S(2)}) collective-permute-start(f32[2,2048]{1,0:T(2,128)S(1)} %pad_maximum_fusion.2.refs_0_), channel_id=1, source_target_pairs={{0,2},{2,0},{4,6},{6,4},{1,3},{3,1},{5,7},{7,5},{8,10},{10,8},{12,... | collective-permute-start | bytes 49160 | tf_op jit(solution)/shard_map/ppermute | solution.py:147
  122.1 9.7 %collective-permute-start.16 = (f32[2,2048]{1,0:T(2,128)S(1)}, f32[2,2048]{1,0:T(2,128)S(1)}, u32[]{:S(2)}, u32[]{:S(2)}) collective-permute-start(f32[2,2048]{1,0:T(2,128)S(1)} %pad_maximum_fusion.2.refs_0_), channel_id=1, source_target_pairs={{0,4},{2,6},{4,0},{6,2},{1,5},{3,7},{5,1},{7,3},{8,12},{10,14},{12... | collective-permute-start | bytes 49160 | tf_op jit(solution)/shard_map/ppermute | solution.py:147
  125.1 6.7 %collective-permute-start.17 = (f32[2,2048]{1,0:T(2,128)S(1)}, f32[2,2048]{1,0:T(2,128)S(1)}, u32[]{:S(2)}, u32[]{:S(2)}) collective-permute-start(f32[2,2048]{1,0:T(2,128)S(1)} %pad_maximum_fusion.2.refs_0_), channel_id=1, source_target_pairs={{0,6},{2,4},{4,2},{6,0},{1,7},{3,5},{5,3},{7,1},{8,14},{10,12},{12... | collective-permute-start | bytes 49160 | tf_op jit(solution)/shard_map/ppermute | solution.py:147

commit v10 on v9

--- a/solution.py
+++ b/solution.py
@@ -150,10 +150,14 @@
 
 def sum_over_cores_and_z(kept, sent, beside):
     z = lax.axis_index("z")
-    mine = (kept + exchange_with_others(sent, "core", 2)[0]).reshape(4, PIECE, LANES)
+    kept = kept.reshape(4, PIECE, LANES)
+    received = exchange_with_others(sent, "core", 2)[0].reshape(4, PIECE, LANES)
 
     def piece_of(flip):
-        return lax.dynamic_index_in_dim(mine, z ^ flip, 0, False)
+        at = z ^ flip
+        return lax.dynamic_index_in_dim(kept, at, 0, False) + lax.dynamic_index_in_dim(
+            received, at, 0, False
+        )
 
     parts, beside = lax.optimization_barrier((exchange_with_others(None, "z", 4, piece_of), beside))
     return (piece_of(0) + parts[0]) + (parts[1] + parts[2]), beside

time: 154 us -> 155 us (level)
  transfers between devices with their start and end apart: 21 -> 21, of which waited for: 14 -> 14; matrix products, arithmetic and copies ran while one was open for 2% -> 2% of each run, Pallas kernels for 19% -> 18%
where the time goes in v10:
time: 155 us
  waiting for transfers between devices  47.9 us (31%)
  starting transfers between devices  47.1 us (30%)
  Pallas kernels  38.8 us (25%)
  blocking collectives  10.7 us (7%)
  local copies, waits for them, and re-layouts  5.98 us (4%)
  other arithmetic  3.29 us (2%)
    ppermute x18, waiting for transfers between devices, exchange_with_others(): lax.ppermute(sent, axes, [(i, i ^ flip) for i in range(count)])  32.8 us
    ppermute x18, starting transfers between devices, exchange_with_others(): lax.ppermute(sent, axes, [(i, i ^ flip) for i in range(count)])  29.8 us
    pallas_call x1, Pallas kernels, solve_continuation(): pl.pallas_call(lambda *refs: solve_kernel(*refs, scale=1.0 / path_count),...  20.8 us
    all_to_all x1, waiting for transfers between devices, per_device(): lax.all_to_all(jnp.concatenate([pieces, table], axis=2), STOCK_AXES, 0, 0...  15 us
    all_to_all x1, blocking collectives, per_device(): surface = lax.all_to_all(surface, PATH_AXES, 0, 0, tiled=True)  10.7 us
    pallas_call x1, Pallas kernels, surface_and_delta(): pl.pallas_call(surface_kernel, out_shape=(jax.ShapeDtypeStruct((32, local...  10.3 us
    all_to_all x1, starting transfers between devices, per_device(): lax.all_to_all(jnp.concatenate([pieces, table], axis=2), STOCK_AXES, 0, 0...  7.61 us
    all_to_all x1, starting transfers between devices, per_device(): gains = lax.all_to_all(sent, STOCK_AXES, 0, 0, tiled=True)  5.45 us
  transfers between devices with their start and end apart: 21, of which 14 were waited for; matrix products, arithmetic and copies ran while one was open for 2% of the time, Pallas kernels for 18%

profile of v10, /device:TPU:1, one launch (start us, length us, event | category | flops | bytes accessed | tf_op | source)
XLA Modules:
  0.0 154.6 jit_solution(7284261285208494819)
XLA Ops:
  0.6 1.3 copy.27
  2.0 0.0 copy-start
  2.0 1.1 pad_maximum_fusion
  3.1 7.6 %all-to-all-start = ((bf16[8,32,2176]{2,1,0:T(8,128)(2,1)}), bf16[8,32,2176]{2,1,0:T(8,128)(2,1)S(1)}, u32[]{:S(2)}, u32[]{:S(2)}) async-start(bf16[8,32,2176]{2,1,0:T(8,128)(2,1)} %pad_maximum_fusion), calls=%async_computation | async-start | bytes 2228224 | tf_op jit(solution)/shard_map/all_to_all | solution.py:444
  10.7 0.0 copy-start.7
  10.7 1.1 copy.28
  11.9 15.0 %all-to-all-done.moved_ref.table_ref = bf16[8,32,2176]{2,1,0:T(8,128)(2,1)S(1)} async-done(((bf16[8,32,2176]{2,1,0:T(8,128)(2,1)}), bf16[8,32,2176]{2,1,0:T(8,128)(2,1)S(1)}, u32[]{:S(2)}, u32[]{:S(2)}) %all-to-all-start) | async-done | bytes 1114144 | tf_op jit(solution)/shard_map/all_to_all | solution.py:444
  26.9 4.2 %all-to-all-start.1 = ((bf16[8,32,2048]{2,1,0:T(8,128)(2,1)}), bf16[8,32,2048]{2,1,0:T(8,128)(2,1)S(1)}, u32[]{:S(2)}, u32[]{:S(2)}) async-start(bf16[8,32,2048]{2,1,0:T(8,128)(2,1)} %bitcast.39), calls=%async_computation.1 | async-start | bytes 2097152 | tf_op jit(solution)/shard_map/all_to_all | solution.py:452
  31.1 0.1 pad_add_fusion.1.slab_ref
  31.2 0.1 copy.20.bias_ref
  31.4 0.0 copy-start.8
  31.4 4.7 %regression_sums.1 = (bf16[512,2048]{1,0:T(8,128)(2,1)}, f32[672,128]{1,0:T(8,128)}, f32[672,128]{1,0:T(8,128)}) custom-call(s32[2]{0:T(128)S(1)} %pad_add_fusion.1.slab_ref, bf16[8,32,2176]{2,1,0:T(8,128)(2,1)S(1)} %all-to-all-done.moved_ref.table_ref, bf16[8,32,2176]{2,1,0:T(8,128)(2,1)S(1)} %all-to-all-done.moved_ref.table_ref, f32[32,512]{1,0:T(8,128)} %weight_ref, ...), custom_call_target="tpu_custom_call" | custom-call | tf_op jit(solution)/shard_map/regression_sums/pallas_call | solution.py:109
  36.1 1.2 collective-permute-start
  37.3 1.5 collective-permute-done
  38.8 1.0 add_bitcast_fusion
  39.8 1.7 %collective-permute-start.1 = (f32[168,128]{1,0:T(8,128)S(1)}, f32[168,128]{1,0:T(8,128)S(1)}, u32[]{:S(2)}, u32[]{:S(2)}) collective-permute-start(f32[168,128]{1,0:T(8,128)S(1)} %get-tuple-element.48), channel_id=1, source_target_pairs={{0,32},{32,0},{64,96},{96,64},{1,33},{33,1},{65,97},{97,65},{2,34}... | collective-permute-start | bytes 258056 | tf_op jit(solution)/shard_map/ppermute | solution.py:147
  41.5 3.3 %collective-permute-start.2 = (f32[168,128]{1,0:T(8,128)S(1)}, f32[168,128]{1,0:T(8,128)S(1)}, u32[]{:S(2)}, u32[]{:S(2)}) collective-permute-start(f32[168,128]{1,0:T(8,128)S(1)} %get-tuple-element.47), channel_id=1, source_target_pairs={{0,64},{32,96},{64,0},{96,32},{1,65},{33,97},{65,1},{97,33},{2,66}... | collective-permute-start | bytes 258056 | tf_op jit(solution)/shard_map/ppermute | solution.py:147
  44.8 0.0 collective-permute-start.3
  44.8 0.0 collective-permute-done.1
  44.8 4.1 %collective-permute-done.2 = f32[168,128]{1,0:T(8,128)S(1)} collective-permute-done((f32[168,128]{1,0:T(8,128)S(1)}, f32[168,128]{1,0:T(8,128)S(1)}, u32[]{:S(2)}, u32[]{:S(2)}) %collective-permute-start.2) | collective-permute-done | bytes 86048 | tf_op jit(solution)/shard_map/ppermute | solution.py:147
  48.9 2.2 %collective-permute-done.3 = f32[168,128]{1,0:T(8,128)S(1)} collective-permute-done((f32[168,128]{1,0:T(8,128)S(1)}, f32[168,128]{1,0:T(8,128)S(1)}, u32[]{:S(2)}, u32[]{:S(2)}) %collective-permute-start.3) | collective-permute-done | bytes 86048 | tf_op jit(solution)/shard_map/ppermute | solution.py:147
  51.1 0.0 all-to-all-done.1.moved_ref
  51.1 0.9 fusion
  52.1 3.3 %collective-permute-start.4 = (f32[168,128]{1,0:T(8,128)S(1)}, f32[168,128]{1,0:T(8,128)S(1)}, u32[]{:S(2)}, u32[]{:S(2)}) collective-permute-start(f32[168,128]{1,0:T(8,128)S(1)} %fusion), channel_id=1, source_target_pairs={{0,1},{1,0},{16,17},{17,16},{2,3},{3,2},{18,19},{19,18},{4,5},{5,4... | collective-permute-start | bytes 258056 | tf_op jit(solution)/shard_map/ppermute | solution.py:147
  55.4 0.4 collective-permute-start.5
  55.8 0.0 collective-permute-start.6
  55.8 1.5 collective-permute-done.4
  57.3 2.2 %collective-permute-done.5 = f32[168,128]{1,0:T(8,128)S(1)} collective-permute-done((f32[168,128]{1,0:T(8,128)S(1)}, f32[168,128]{1,0:T(8,128)S(1)}, u32[]{:S(2)}, u32[]{:S(2)}) %collective-permute-start.5) | collective-permute-done | bytes 86048 | tf_op jit(solution)/shard_map/ppermute | solution.py:147
  59.4 0.9 collective-permute-done.6
  60.4 1.3 collective-permute-start.7
  61.7 2.4 %collective-permute-start.8 = (f32[168,128]{1,0:T(8,128)S(1)}, f32[168,128]{1,0:T(8,128)S(1)}, u32[]{:S(2)}, u32[]{:S(2)}) collective-permute-start(f32[168,128]{1,0:T(8,128)S(1)} %add_add_fusion.1), channel_id=1, source_target_pairs={{0,4},{2,6},{4,0},{6,2},{1,5},{3,7},{5,1},{7,3},{8,12},{10,14},{12... | collective-permute-start | bytes 258056 | tf_op jit(solution)/shard_map/ppermute | solution.py:147
  64.1 0.2 collective-permute-start.9
  64.3 0.1 copy.21.basket_ref
  64.4 0.0 copy-start.4
  64.5 0.9 copy-done.4
  65.4 3.1 %increments.1 = (bf16[8,4,32,2048]{3,2,1,0:T(8,128)(2,1)}, f32[256,128]{1,0:T(8,128)S(1)}) custom-call(bf16[8,32,2048]{2,1,0:T(8,128)(2,1)S(1)} %all-to-all-done.1.moved_ref, bf16[256,256]{1,0:T(8,128)(2,1)S(1)} %copy-done.4, f32[256,1]{1,0:T(8,128)S(1)} %copy.21.basket_ref), custom_call_target="tpu_custom_call" | custom-call | tf_op jit(solution)/shard_map/increments/pallas_call | solution.py:335
  68.4 0.0 collective-permute-done.7
  68.4 0.0 collective-permute-done.8
  68.4 0.2 collective-permute-done.9
  68.6 5.5 %all-to-all-start.2 = ((bf16[8,4,32,2048]{3,2,1,0:T(8,128)(2,1)}), bf16[8,4,32,2048]{3,2,1,0:T(8,128)(2,1)}, u32[]{:S(2)}, u32[]{:S(2)}) async-start(bf16[8,4,32,2048]{3,2,1,0:T(8,128)(2,1)} %get-tuple-element.42), calls=%async_computation.2 | async-start | bytes 8388608 | tf_op jit(solution)/shard_map/all_to_all | solution.py:465
  74.1 0.0 copy-start.3
  74.1 0.1 collective-permute-start.10
  74.2 1.7 %collective-permute-start.11 = (f32[168,128]{1,0:T(8,128)S(1)}, f32[168,128]{1,0:T(8,128)S(1)}, u32[]{:S(2)}, u32[]{:S(2)}) collective-permute-start(f32[168,128]{1,0:T(8,128)S(1)} %add_add_fusion), channel_id=1, source_target_pairs={{0,64},{32,96},{64,0},{96,32},{1,65},{33,97},{65,1},{97,33},{2,66}... | collective-permute-start | bytes 258056 | tf_op jit(solution)/shard_map/ppermute | solution.py:147
  75.9 2.2 %collective-permute-start.12 = (f32[168,128]{1,0:T(8,128)S(1)}, f32[168,128]{1,0:T(8,128)S(1)}, u32[]{:S(2)}, u32[]{:S(2)}) collective-permute-start(f32[168,128]{1,0:T(8,128)S(1)} %add_add_fusion), channel_id=1, source_target_pairs={{0,96},{32,64},{64,32},{96,0},{1,97},{33,65},{65,33},{97,1},{2,98}... | collective-permute-start | bytes 258056 | tf_op jit(solution)/shard_map/ppermute | solution.py:147
  78.1 1.1 collective-permute-done.11
  79.1 1.3 collective-permute-done.12
  80.5 4.8 %collective-permute-start.13 = (f32[4,168,128]{2,1,0:T(8,128)S(1)}, f32[4,168,128]{2,1,0:T(8,128)S(1)}, u32[]{:S(2)}, u32[]{:S(2)}) collective-permute-start(f32[4,168,128]{2,1,0:T(8,128)S(1)} %pad_maximum_fusion.1.refs_1_), channel_id=1, source_target_pairs={{0,8},{8,0},{1,9},{9,1},{2,10},{10,2},{3,11},{11,3},{4,12},{12,4},... | collective-permute-start | bytes 1032200 | tf_op jit(solution)/shard_map/ppermute | solution.py:147
  85.3 0.1 pad_add_fusion.refs_0_
  85.4 1.2 collective-permute-done.13.refs_2_
  86.6 1.6 %copy-done.1 = bf16[512,2048]{1,0:T(8,128)(2,1)S(1)} copy-done((bf16[512,2048]{1,0:T(8,128)(2,1)S(1)}, bf16[512,2048]{1,0:T(8,128)(2,1)}, u32[]{:S(2)}) %copy-start.1) | copy-done | bytes 2097176
  88.2 20.8 %solve_continuation.1 = f32[1,2048]{1,0:T(1,128)S(1)} custom-call(s32[2]{0:T(128)S(1)} %pad_add_fusion.refs_0_, f32[4,168,128]{2,1,0:T(8,128)S(1)} %pad_maximum_fusion.1.refs_1_, f32[4,168,128]{2,1,0:T(8,128)S(1)} %collective-permute-done.13.refs_2_, bf16[512,2048]{1,0:T(8,128)(2,1)S(1)} %copy-done.1), custom_call_target="tpu_custom_call" | custom-call | tf_op jit(solution)/shard_map/solve_continuation/pallas_call | solution.py:281
  108.9 3.2 %collective-permute-start.14 = (f32[1,2048]{1,0:T(1,128)S(1)}, f32[1,2048]{1,0:T(1,128)S(1)}, u32[]{:S(2)}, u32[]{:S(2)}) collective-permute-start(f32[1,2048]{1,0:T(1,128)S(1)} %solve_continuation.1), channel_id=1, source_target_pairs={{0,1},{1,0},{2,3},{3,2},{4,5},{5,4},{6,7},{7,6},{8,9},{9,8},{10,11... | collective-permute-start | bytes 24584 | tf_op jit(solution)/shard_map/ppermute | solution.py:147
  112.1 10.8 %collective-permute-done.14 = f32[1,2048]{1,0:T(1,128)S(1)} collective-permute-done((f32[1,2048]{1,0:T(1,128)S(1)}, f32[1,2048]{1,0:T(1,128)S(1)}, u32[]{:S(2)}, u32[]{:S(2)}) %collective-permute-start.14) | collective-permute-done | bytes 8224 | tf_op jit(solution)/shard_map/ppermute | solution.py:147
  123.0 0.1 collective-permute-start.15
  123.1 2.9 %collective-permute-start.16 = (f32[2,2048]{1,0:T(2,128)S(1)}, f32[2,2048]{1,0:T(2,128)S(1)}, u32[]{:S(2)}, u32[]{:S(2)}) collective-permute-start(f32[2,2048]{1,0:T(2,128)S(1)} %pad_maximum_fusion.2.refs_0_), channel_id=1, source_target_pairs={{0,4},{2,6},{4,0},{6,2},{1,5},{3,7},{5,1},{7,3},{8,12},{10,14},{12... | collective-permute-start | bytes 49160 | tf_op jit(solution)/shard_map/ppermute | solution.py:147
  126.0 0.9 collective-permute-start.17
  126.9 1.8 %collective-permute-done.15.refs_1_ = f32[2,2048]{1,0:T(2,128)S(1)} collective-permute-done((f32[2,2048]{1,0:T(2,128)S(1)}, f32[2,2048]{1,0:T(2,128)S(1)}, u32[]{:S(2)}, u32[]{:S(2)}) %collective-permute-start.15) | collective-permute-done | bytes 16416 | tf_op jit(solution)/shard_map/ppermute | solution.py:147
  128.7 4.1 %collective-permute-done.16.refs_2_ = f32[2,2048]{1,0:T(2,128)S(1)} collective-permute-done((f32[2,2048]{1,0:T(2,128)S(1)}, f32[2,2048]{1,0:T(2,128)S(1)}, u32[]{:S(2)}, u32[]{:S(2)}) %collective-permute-start.16) | collective-permute-done | bytes 16416 | tf_op jit(solution)/shard_map/ppermute | solution.py:147
  132.8 0.0 collective-permute-done.17.refs_3_
  132.8 0.0 all-to-all-done.2.refs_5_
  132.8 10.3 %surface_and_delta.1 = (f32[32,16384]{1,0:T(8,128)}, f32[16,4,128]{2,1,0:T(4,128)S(1)}) custom-call(s32[1]{0:T(128)} %bitcast.slab_ref, f32[2,2048]{1,0:T(2,128)S(1)} %pad_maximum_fusion.2.refs_0_, f32[2,2048]{1,0:T(2,128)S(1)} %collective-permute-done.15.refs_1_, f32[2,2048]{1,0:T(2,128)S(1)} %collective-permute-done.16.refs_2_, ...), custom_call_target="tpu_custom_call" | custom-call | tf_op jit(solution)/shard_map/surface_and_delta/pallas_call | solution.py:407
  143.1 10.7 %all_to_all.20 = f32[16,4,128]{2,1,0:T(4,128)S(1)} all-to-all(f32[16,4,128]{2,1,0:T(4,128)S(1)} %get-tuple-element.45), channel_id=1, replica_groups=mesh['z'=4,'ylo'=2,'core'=2,'x'=4,'yhi'=2] {'z','ylo','core'}, dimensions={0} | all-to-all | bytes 65536 | tf_op jit(solution)/shard_map/all_to_all | solution.py:473
  153.9 0.1 reshape.35
  154.0 0.6 copy.22
  (20 shorter events, 0.2 us)
Async XLA Ops:
  0.6 1.3 copy-start.6
  2.0 8.7 %copy-start = (bf16[32,16384]{1,0:T(8,128)(2,1)S(1)}, bf16[32,16384]{1,0:T(8,128)(2,1)}, u32[]{:S(2)}) copy-start(bf16[32,16384]{1,0:T(8,128)(2,1)} %refs_4_.1) | copy-start | bytes 3145732
  3.1 8.7 %copy-start.5 = (bf16[16384]{0:T(1024)(128)(2,1)S(1)}, bf16[16384]{0:T(1024)(128)(2,1)}, u32[]{:S(2)}) copy-start(bf16[16384]{0:T(1024)(128)(2,1)} %param.16) | copy-start | bytes 98308
  3.1 23.8 %all-to-all-start = ((bf16[8,32,2176]{2,1,0:T(8,128)(2,1)}), bf16[8,32,2176]{2,1,0:T(8,128)(2,1)S(1)}, u32[]{:S(2)}, u32[]{:S(2)}) async-start(bf16[8,32,2176]{2,1,0:T(8,128)(2,1)} %pad_maximum_fusion), calls=%async_computation | async-start | bytes 2228224 | tf_op jit(solution)/shard_map/all_to_all | solution.py:444
  10.7 20.5 %copy-start.7 = (f32[512]{0:T(512)S(1)}, f32[512]{0:T(512)}, u32[]{:S(2)}) copy-start(f32[512]{0:T(512)} %param.15) | copy-start | bytes 6148
  26.9 24.2 %all-to-all-start.1 = ((bf16[8,32,2048]{2,1,0:T(8,128)(2,1)}), bf16[8,32,2048]{2,1,0:T(8,128)(2,1)S(1)}, u32[]{:S(2)}, u32[]{:S(2)}) async-start(bf16[8,32,2048]{2,1,0:T(8,128)(2,1)} %bitcast.39), calls=%async_computation.1 | async-start | bytes 2097152 | tf_op jit(solution)/shard_map/all_to_all | solution.py:452
  31.4 32.9 %copy-start.8 = (f32[256]{0:T(256)S(1)}, f32[256]{0:T(256)}, u32[]{:S(2)}) copy-start(f32[256]{0:T(256)} %param.21) | copy-start | bytes 3076
  36.1 2.7 %collective-permute-start = (f32[672,128]{1,0:T(8,128)}, f32[672,128]{1,0:T(8,128)S(1)}, u32[]{:S(2)}, u32[]{:S(2)}) collective-permute-start(f32[672,128]{1,0:T(8,128)} %get-tuple-element.30), channel_id=1, source_target_pairs={{0,8},{8,0},{1,9},{9,1},{2,10},{10,2},{3,11},{11,3},{4,12},{12,4},... | collective-permute-start | bytes 1032200 | tf_op jit(solution)/shard_map/ppermute | solution.py:147
  39.8 5.0 %collective-permute-start.1 = (f32[168,128]{1,0:T(8,128)S(1)}, f32[168,128]{1,0:T(8,128)S(1)}, u32[]{:S(2)}, u32[]{:S(2)}) collective-permute-start(f32[168,128]{1,0:T(8,128)S(1)} %get-tuple-element.48), channel_id=1, source_target_pairs={{0,32},{32,0},{64,96},{96,64},{1,33},{33,1},{65,97},{97,65},{2,34}... | collective-permute-start | bytes 258056 | tf_op jit(solution)/shard_map/ppermute | solution.py:147
  41.5 7.4 %collective-permute-start.2 = (f32[168,128]{1,0:T(8,128)S(1)}, f32[168,128]{1,0:T(8,128)S(1)}, u32[]{:S(2)}, u32[]{:S(2)}) collective-permute-start(f32[168,128]{1,0:T(8,128)S(1)} %get-tuple-element.47), channel_id=1, source_target_pairs={{0,64},{32,96},{64,0},{96,32},{1,65},{33,97},{65,1},{97,33},{2,66}... | collective-permute-start | bytes 258056 | tf_op jit(solution)/shard_map/ppermute | solution.py:147
  44.8 6.3 %collective-permute-start.3 = (f32[168,128]{1,0:T(8,128)S(1)}, f32[168,128]{1,0:T(8,128)S(1)}, u32[]{:S(2)}, u32[]{:S(2)}) collective-permute-start(f32[168,128]{1,0:T(8,128)S(1)} %get-tuple-element.46), channel_id=1, source_target_pairs={{0,96},{32,64},{64,32},{96,0},{1,97},{33,65},{65,33},{97,1},{2,98}... | collective-permute-start | bytes 258056 | tf_op jit(solution)/shard_map/ppermute | solution.py:147
  52.1 5.2 %collective-permute-start.4 = (f32[168,128]{1,0:T(8,128)S(1)}, f32[168,128]{1,0:T(8,128)S(1)}, u32[]{:S(2)}, u32[]{:S(2)}) collective-permute-start(f32[168,128]{1,0:T(8,128)S(1)} %fusion), channel_id=1, source_target_pairs={{0,1},{1,0},{16,17},{17,16},{2,3},{3,2},{18,19},{19,18},{4,5},{5,4... | collective-permute-start | bytes 258056 | tf_op jit(solution)/shard_map/ppermute | solution.py:147
  55.4 4.0 %collective-permute-start.5 = (f32[168,128]{1,0:T(8,128)S(1)}, f32[168,128]{1,0:T(8,128)S(1)}, u32[]{:S(2)}, u32[]{:S(2)}) collective-permute-start(f32[168,128]{1,0:T(8,128)S(1)} %fusion), channel_id=1, source_target_pairs={{0,16},{1,17},{16,0},{17,1},{2,18},{3,19},{18,2},{19,3},{4,20},{5,... | collective-permute-start | bytes 258056 | tf_op jit(solution)/shard_map/ppermute | solution.py:147
  55.8 4.5 %collective-permute-start.6 = (f32[168,128]{1,0:T(8,128)S(1)}, f32[168,128]{1,0:T(8,128)S(1)}, u32[]{:S(2)}, u32[]{:S(2)}) collective-permute-start(f32[168,128]{1,0:T(8,128)S(1)} %fusion), channel_id=1, source_target_pairs={{0,17},{1,16},{16,1},{17,0},{2,19},{3,18},{18,3},{19,2},{4,21},{5,... | collective-permute-start | bytes 258056 | tf_op jit(solution)/shard_map/ppermute | solution.py:147
  60.4 8.1 %collective-permute-start.7 = (f32[168,128]{1,0:T(8,128)S(1)}, f32[168,128]{1,0:T(8,128)S(1)}, u32[]{:S(2)}, u32[]{:S(2)}) collective-permute-start(f32[168,128]{1,0:T(8,128)S(1)} %add_add_fusion.1), channel_id=1, source_target_pairs={{0,2},{2,0},{4,6},{6,4},{1,3},{3,1},{5,7},{7,5},{8,10},{10,8},{12,... | collective-permute-start | bytes 258056 | tf_op jit(solution)/shard_map/ppermute | solution.py:147
  61.7 6.8 %collective-permute-start.8 = (f32[168,128]{1,0:T(8,128)S(1)}, f32[168,128]{1,0:T(8,128)S(1)}, u32[]{:S(2)}, u32[]{:S(2)}) collective-permute-start(f32[168,128]{1,0:T(8,128)S(1)} %add_add_fusion.1), channel_id=1, source_target_pairs={{0,4},{2,6},{4,0},{6,2},{1,5},{3,7},{5,1},{7,3},{8,12},{10,14},{12... | collective-permute-start | bytes 258056 | tf_op jit(solution)/shard_map/ppermute | solution.py:147
  64.1 4.5 %collective-permute-start.9 = (f32[168,128]{1,0:T(8,128)S(1)}, f32[168,128]{1,0:T(8,128)S(1)}, u32[]{:S(2)}, u32[]{:S(2)}) collective-permute-start(f32[168,128]{1,0:T(8,128)S(1)} %add_add_fusion.1), channel_id=1, source_target_pairs={{0,6},{2,4},{4,2},{6,0},{1,7},{3,5},{5,3},{7,1},{8,14},{10,12},{12... | collective-permute-start | bytes 258056 | tf_op jit(solution)/shard_map/ppermute | solution.py:147
  64.4 0.9 copy-start.4
  68.6 64.2 %all-to-all-start.2 = ((bf16[8,4,32,2048]{3,2,1,0:T(8,128)(2,1)}), bf16[8,4,32,2048]{3,2,1,0:T(8,128)(2,1)}, u32[]{:S(2)}, u32[]{:S(2)}) async-start(bf16[8,4,32,2048]{3,2,1,0:T(8,128)(2,1)} %get-tuple-element.42), calls=%async_computation.2 | async-start | bytes 8388608 | tf_op jit(solution)/shard_map/all_to_all | solution.py:465
  74.1 58.7 %copy-start.2 = (s32[4,16384]{1,0:T(4,128)S(1)}, s32[4,16384]{1,0:T(4,128)}, u32[]{:S(2)}) copy-start(s32[4,16384]{1,0:T(4,128)} %refs_8_.1) | copy-start | bytes 786436
  74.1 58.7 %copy-start.3 = (s32[4,16384]{1,0:T(4,128)S(1)}, s32[4,16384]{1,0:T(4,128)}, u32[]{:S(2)}) copy-start(s32[4,16384]{1,0:T(4,128)} %refs_9_.1) | copy-start | bytes 786436
  74.1 3.9 %collective-permute-start.10 = (f32[168,128]{1,0:T(8,128)S(1)}, f32[168,128]{1,0:T(8,128)S(1)}, u32[]{:S(2)}, u32[]{:S(2)}) collective-permute-start(f32[168,128]{1,0:T(8,128)S(1)} %add_add_fusion), channel_id=1, source_target_pairs={{0,32},{32,0},{64,96},{96,64},{1,33},{33,1},{65,97},{97,65},{2,34}... | collective-permute-start | bytes 258056 | tf_op jit(solution)/shard_map/ppermute | solution.py:147
  74.2 4.9 %collective-permute-start.11 = (f32[168,128]{1,0:T(8,128)S(1)}, f32[168,128]{1,0:T(8,128)S(1)}, u32[]{:S(2)}, u32[]{:S(2)}) collective-permute-start(f32[168,128]{1,0:T(8,128)S(1)} %add_add_fusion), channel_id=1, source_target_pairs={{0,64},{32,96},{64,0},{96,32},{1,65},{33,97},{65,1},{97,33},{2,66}... | collective-permute-start | bytes 258056 | tf_op jit(solution)/shard_map/ppermute | solution.py:147
  75.9 4.5 %collective-permute-start.12 = (f32[168,128]{1,0:T(8,128)S(1)}, f32[168,128]{1,0:T(8,128)S(1)}, u32[]{:S(2)}, u32[]{:S(2)}) collective-permute-start(f32[168,128]{1,0:T(8,128)S(1)} %add_add_fusion), channel_id=1, source_target_pairs={{0,96},{32,64},{64,32},{96,0},{1,97},{33,65},{65,33},{97,1},{2,98}... | collective-permute-start | bytes 258056 | tf_op jit(solution)/shard_map/ppermute | solution.py:147
  80.5 6.1 %collective-permute-start.13 = (f32[4,168,128]{2,1,0:T(8,128)S(1)}, f32[4,168,128]{2,1,0:T(8,128)S(1)}, u32[]{:S(2)}, u32[]{:S(2)}) collective-permute-start(f32[4,168,128]{2,1,0:T(8,128)S(1)} %pad_maximum_fusion.1.refs_1_), channel_id=1, source_target_pairs={{0,8},{8,0},{1,9},{9,1},{2,10},{10,2},{3,11},{11,3},{4,12},{12,4},... | collective-permute-start | bytes 1032200 | tf_op jit(solution)/shard_map/ppermute | solution.py:147
  86.6 1.6 %copy-start.1 = (bf16[512,2048]{1,0:T(8,128)(2,1)S(1)}, bf16[512,2048]{1,0:T(8,128)(2,1)}, u32[]{:S(2)}) copy-start(bf16[512,2048]{1,0:T(8,128)(2,1)} %get-tuple-element.41.refs_3_) | copy-start | bytes 6291460
  108.9 14.0 %collective-permute-start.14 = (f32[1,2048]{1,0:T(1,128)S(1)}, f32[1,2048]{1,0:T(1,128)S(1)}, u32[]{:S(2)}, u32[]{:S(2)}) collective-permute-start(f32[1,2048]{1,0:T(1,128)S(1)} %solve_continuation.1), channel_id=1, source_target_pairs={{0,1},{1,0},{2,3},{3,2},{4,5},{5,4},{6,7},{7,6},{8,9},{9,8},{10,11... | collective-permute-start | bytes 24584 | tf_op jit(solution)/shard_map/ppermute | solution.py:147
  123.0 5.7 %collective-permute-start.15 = (f32[2,2048]{1,0:T(2,128)S(1)}, f32[2,2048]{1,0:T(2,128)S(1)}, u32[]{:S(2)}, u32[]{:S(2)}) collective-permute-start(f32[2,2048]{1,0:T(2,128)S(1)} %pad_maximum_fusion.2.refs_0_), channel_id=1, source_target_pairs={{0,2},{2,0},{4,6},{6,4},{1,3},{3,1},{5,7},{7,5},{8,10},{10,8},{12,... | collective-permute-start | bytes 49160 | tf_op jit(solution)/shard_map/ppermute | solution.py:147
  123.1 9.7 %collective-permute-start.16 = (f32[2,2048]{1,0:T(2,128)S(1)}, f32[2,2048]{1,0:T(2,128)S(1)}, u32[]{:S(2)}, u32[]{:S(2)}) collective-permute-start(f32[2,2048]{1,0:T(2,128)S(1)} %pad_maximum_fusion.2.refs_0_), channel_id=1, source_target_pairs={{0,4},{2,6},{4,0},{6,2},{1,5},{3,7},{5,1},{7,3},{8,12},{10,14},{12... | collective-permute-start | bytes 49160 | tf_op jit(solution)/shard_map/ppermute | solution.py:147
  126.0 6.8 %collective-permute-start.17 = (f32[2,2048]{1,0:T(2,128)S(1)}, f32[2,2048]{1,0:T(2,128)S(1)}, u32[]{:S(2)}, u32[]{:S(2)}) collective-permute-start(f32[2,2048]{1,0:T(2,128)S(1)} %pad_maximum_fusion.2.refs_0_), channel_id=1, source_target_pairs={{0,6},{2,4},{4,2},{6,0},{1,7},{3,5},{5,3},{7,1},{8,14},{10,12},{12... | collective-permute-start | bytes 49160 | tf_op jit(solution)/shard_map/ppermute | solution.py:147
